TPU v7x, 32 devices: a whole 2x2x4 slice. The times are simulated.
32 devices in a mesh: key: 4 (over x, core), head: 4 (over z), query: 2 (over y).
Axes of the slice: x: 2, y: 2, z: 4, core: 2. Of those that a mesh axis runs over, the one named last changes fastest.
Arguments:
- main_query: bfloat16 [4, 256, 24576], P(None, 'query', 'head'), may hold values from -64 to 64
- key_nope: bfloat16 [2048, 16384], P('key', 'head'), may hold values from -4 to 4
- key_rope: bfloat16 [2048, 64], P('key'), may hold values from -4 to 4
- query_pos: int32 [4, 256], P(None, 'query'), may hold values from 0 to 131071, as said below
- key_pos: int32 [2048], P('key'), may hold values from 0 to 131071, as said below
- key_count: int32 [64], P('key'), may hold values from 1 to 32, as said below
- index_query: bfloat16 [1024, 8192], P(('head', 'query')), may hold values from -16 to 16
- index_key: bfloat16 [2048, 128], P('key'), may hold values from -4 to 4
- index_weight: bfloat16 [1024, 64], P(('head', 'query')), may hold values from -0.5 to 0.5
- row_cotangent: float32 [1024], P(('head', 'query')), may hold values from 512 to 4096
Outputs:
- kl_rows: float32 [1024], P(('head', 'query'))
- grad_index_query: float32 [1024, 8192], P(('head', 'query'), 'key')
- grad_index_key: float32 [2048, 128], P('key')
Inputs may be any that keep to these rules, and one draw needn't show every extreme that they name: `query_pos`: increasing along the flattened order, distinct; the first query is at position 0 and the last at position 131071. `key_pos`: increasing, distinct; the first key is at position 0. `key_count`: some block is full and some block holds one live key.
All inputs are finite; a program needn't handle non-finite values.
Results may differ from a plain program's by a relative error of at most 0.002.
Values sent between devices are 32-bit elements; how exact they have to be, the bound alone decides.
No kernel may reach another device: no remote copies, remote signals or barrier semaphores. Data moves between devices by JAX's collectives and lax.ppermute only.
A program may use at most 128 MiB of HBM per device.

v0:
```python
import jax
import jax.numpy as jnp
from jax import lax
from jax.sharding import PartitionSpec as P

H = 128
DNOPE = 128
IH = 64
ID = 128
KBLOCK = 32
DQK = 192


neg_big = -1e30


def joined(value, axis, join):
    pieces = jax.tree.map(lambda part: lax.all_gather(part, axis), value)
    head = jax.tree.map(lambda part: part[0], pieces)
    tail = jax.tree.map(lambda part: part[1:], pieces)
    so_far, _ = lax.scan(lambda so_far, section: (join(so_far, section), None), head, tail)
    return so_far


def combine_softmax(first, second):
    top = jnp.maximum(first[0], second[0])
    total = first[1] * jnp.exp(first[0] - top) + second[1] * jnp.exp(second[0] - top)
    return (top, total)


def combine_index(first, second):
    top = jnp.maximum(first[0], second[0])
    total = first[1] * jnp.exp(first[0] - top) + second[1] * jnp.exp(second[0] - top)
    return (top, total, first[2] + second[2], first[3] + second[3])


def body(
    main_query,
    key_nope,
    key_rope,
    query_pos,
    key_pos,
    key_count,
    index_query,
    index_key,
    index_weight,
    row_cotangent,
):
    f32 = jnp.float32
    groups, half_rows, width = main_query.shape
    heads_here = width // DQK
    rows = groups * half_rows
    keys_here = key_nope.shape[0]
    scale_main = DQK ** (-0.5)
    scale_index = ID ** (-0.5)
    q_heads = main_query.reshape(rows, heads_here, DQK)
    k_heads = key_nope.reshape(keys_here, heads_here, DNOPE)
    slots = jnp.arange(keys_here, dtype=jnp.int32) % KBLOCK
    counts = jnp.repeat(key_count, KBLOCK, total_repeat_length=keys_here)
    key_live = slots < counts
    positions = query_pos.reshape(rows)
    valid = (key_pos[None, :] <= positions[:, None]) & key_live[None, :]
    scores = (
        jnp.einsum("thd,khd->htk", q_heads[:, :, :DNOPE], k_heads, preferred_element_type=f32)
        + jnp.einsum("thd,kd->htk", q_heads[:, :, DNOPE:], key_rope, preferred_element_type=f32)
    ) * scale_main
    local_top = jnp.max(jnp.where(valid[None], scores, neg_big), axis=-1)
    local_total = jnp.sum(
        jnp.where(valid[None], jnp.exp(scores - local_top[..., None]), 0.0), axis=-1
    )
    top, total = joined((local_top, local_total), "key", combine_softmax)
    probs = jnp.where(valid[None], jnp.exp(scores - top[..., None]), 0.0) / total[..., None]
    tile = jnp.sum(probs, axis=0).reshape(groups, half_rows, keys_here)
    group_index = lax.axis_index("head")
    mine = lax.psum_scatter(tile, "head", scatter_dimension=0, tiled=True)[0]
    target = (mine / H).T
    my_pos = lax.dynamic_index_in_dim(query_pos, group_index, 0, keepdims=False)
    valid_index = (key_pos[:, None] <= my_pos[None, :]) & key_live[:, None]
    flat_query = index_query.reshape(half_rows * IH, ID)
    z_vals = lax.dot_general(
        index_key, flat_query, (((1,), (1,)), ((), ())), preferred_element_type=f32
    )
    z_vals = z_vals.reshape(keys_here, half_rows, IH)
    weights = index_weight.astype(f32)
    logits = scale_index * jnp.sum(jnp.maximum(z_vals, 0.0) * weights[None], axis=-1)
    part_top = jnp.max(jnp.where(valid_index, logits, neg_big), axis=0)
    part_total = jnp.sum(jnp.where(valid_index, jnp.exp(logits - part_top[None, :]), 0.0), axis=0)
    safe = jnp.where(target > 0, target, 1.0)
    part_entropy = jnp.sum(jnp.where(target > 0, target * jnp.log(safe), 0.0), axis=0)
    part_cross = jnp.sum(jnp.where(valid_index, target * logits, 0.0), axis=0)
    index_top, index_total, entropy, cross = joined(
        (part_top, part_total, part_entropy, part_cross), "key", combine_index
    )
    lse = index_top + jnp.log(index_total)
    kl_rows = entropy - cross + lse
    qprob = jnp.where(valid_index, jnp.exp(logits - lse[None, :]), 0.0)
    grad_logits = row_cotangent[None, :] * (qprob - target)
    positive = (z_vals > 0).astype(f32)
    dz_vals = ((scale_index * grad_logits)[:, :, None] * weights[None] * positive).astype(
        jnp.bfloat16
    )
    dz_flat = dz_vals.reshape(keys_here, half_rows * IH)
    grad_terms = lax.dot_general(
        dz_flat, index_key, (((0,), (0,)), ((), ())), preferred_element_type=f32
    )
    grad_terms = grad_terms.reshape(half_rows, IH * ID)
    grad_query = lax.psum_scatter(grad_terms, "key", scatter_dimension=1, tiled=True)
    key_terms = jnp.dot(dz_flat, flat_query, preferred_element_type=f32)
    grad_key = lax.psum(key_terms, ("head", "query"))
    return (kl_rows, grad_query, grad_key)


def solution(mesh):
    return jax.shard_map(
        body,
        mesh=mesh,
        in_specs=(
            P(None, "query", "head"),
            P("key", "head"),
            P("key", None),
            P(None, "query"),
            P("key"),
            P("key"),
            P(("head", "query"), None),
            P("key", None),
            P(("head", "query"), None),
            P(("head", "query")),
        ),
        out_specs=(P(("head", "query")), P(("head", "query"), "key"), P("key", None)),
        check_vma=False,
    )
```

profile of v0, /device:TPU:0, one launch (start us, length us, event | category | flops | bytes accessed | tf_op | source)
XLA Modules:
  0.0 326.5 jit_solution(287575170702733805)
XLA Ops:
  7.2 1.9 fusion.35
  9.2 0.8 add_add_fusion.1
  9.9 4.3 %compare_select_fusion.3 = (s32[512,1]{0,1:T(1,128)S(1)}, s32[512,1]{0,1:T(1,128)S(1)}) fusion(s32[]{:T(128)} %bitcast.20, s32[]{:T(128)} %bitcast.21, s32[]{:T(128)} %bitcast.22, s32[]{:T(128)} %bitcast.23, s32[]{:T(128)} %bitcast.24, s32[]{:T(128)} %bitcast.26, s32[]{:T(128)} %bitcast.25, s32[512,1]{0,1:T(1,128)S(1)} %bitcast.158, s32[512,1]{0,1:T(1,128)S(1)} %bitcast.157), kind=kLoop, calls=%fused_computation.61 | loop fusion | flops 7168 | bytes 8220 | tf_op jit(solution)/shard_map/jit(_take)/gather | solution.py:59
  14.3 10.6 %copy.22 = bf16[4,128,6144]{1,0,2:T(4,128)(2,1)} copy(bf16[4,128,6144]{2,1,0:T(8,128)(2,1)} %param.16) | data formatting | bytes 12582912 | tf_op args[0]
  24.9 10.1 %reshape.209 = bf16[512,32,192]{0,2,1:T(8,128)(2,1)} reshape(bf16[4,128,6144]{1,0,2:T(4,128)(2,1)} %copy.22) | data formatting | bytes 12582912 | tf_op jit(solution)/shard_map/reshape | solution.py:56
  35.0 19.1 %fusion.13 = f32[32,512,512]{1,2,0:T(8,128)} fusion(bf16[512,32,192]{0,2,1:T(8,128)(2,1)} %reshape.209, bf16[512,4096]{1,0:T(8,128)(2,1)} %param.17), kind=kOutput, calls=%fused_computation.26 | convolution fusion | flops 2147483648 | bytes 41943040 | tf_op jit(solution)/shard_map/thd,khd->htk/dot_general | solution.py:64
  54.1 5.6 %fusion.30 = pred[512]{0:T(512)(128)(4,1)S(1)} fusion(pred[512]{0:T(512)(128)(4,1)S(1)} %get-tuple-element.110, pred[512]{0:T(512)(128)(4,1)S(1)} %get-tuple-element.109, pred[512]{0:T(512)(128)(4,1)S(1)} %get-tuple-element.108, pred[512]{0:T(512)(128)(4,1)S(1)} %get-tuple-element.107, pred[512]{0:T(512)(128)(4,1)S(1)} %get-tuple-element.106, ...), kind=kLoop, calls=%fused_computation.71 | loop fusion | flops 12800 | bytes 9268 | tf_op jit(solution)/shard_map/lt | solution.py:60
  60.0 23.2 %select_reduce_fusion.1 = (f32[32,512]{1,0:T(8,128)S(1)}, f32[32,512,512]{1,2,0:T(8,128)}) fusion(pred[512,512]{0,1:T(8,128)(4,1)S(1)} %compare_and_fusion, f32[32,512,512]{1,2,0:T(8,128)} %fusion.13, bf16[512,32,192]{0,2,1:T(8,128)(2,1)} %reshape.209, bf16[512,64]{0,1:T(8,128)(2,1)S(1)} %copy-done.5), kind=kOutput, calls=%fused_computation.22 | convolution fusion | flops 1107279872 | bytes 69599232 | tf_op jit(solution)/shard_map/thd,kd->htk/dot_general | solution.py:65
  83.2 14.0 %select_reduce_fusion = f32[32,512]{1,0:T(8,128)S(1)} fusion(f32[32,512,512]{1,2,0:T(8,128)} %get-tuple-element.169, f32[32,512]{1,0:T(8,128)S(1)} %get-tuple-element.168, pred[512,512]{0,1:T(8,128)(4,1)S(1)} %compare_and_fusion), kind=kLoop, calls=%fused_computation.21 | loop fusion | flops 25149440 | bytes 33947648 | tf_op jit(solution)/shard_map/reduce_sum | solution.py:68
  97.2 7.2 %all-gather.3 = f32[128,512]{1,0:T(8,128)S(1)} all-gather(f32[32,512]{1,0:T(8,128)S(1)} %select_reduce_fusion), channel_id=5, replica_groups=mesh['key'=4,'head'=4,'query'=2] {'key'}, dimensions={0}, use_global_device_ids=true | all-gather | bytes 327680 | tf_op jit(solution)/shard_map/all_gather | solution.py:18
  104.4 5.9 %all-gather.2 = f32[128,512]{1,0:T(8,128)S(1)} all-gather(f32[32,512]{1,0:T(8,128)S(1)} %get-tuple-element.168), channel_id=4, replica_groups=mesh['key'=4,'head'=4,'query'=2] {'key'}, dimensions={0}, use_global_device_ids=true | all-gather | bytes 327680 | tf_op jit(solution)/shard_map/all_gather | solution.py:18
  110.6 0.6 copy-done.2
  111.2 14.6 %fusion.12 = f32[512,512]{0,1:T(8,128)S(1)} fusion(f32[32,512,512]{1,2,0:T(8,128)} %get-tuple-element.169, f32[32,512]{1,0:T(8,128)} %copy-done.2, f32[32,512]{1,0:T(8,128)} %copy-done.3, pred[512,512]{0,1:T(8,128)(4,1)S(1)} %compare_and_fusion), kind=kLoop, calls=%fused_computation.23 | loop fusion | flops 33292288 | bytes 34996224 | tf_op jit(solution)/shard_map/reduce_sum | solution.py:73
  125.8 1.3 copy.27
  127.2 0.7 convert_element_type.7
  127.9 2.4 reshape.214
  130.3 6.7 %multiply_reduce_fusion = (f32[512,128]{0,1:T(8,128)S(1)}, f32[512,128,64]{0,1,2:T(8,128)}) fusion(f32[128,64]{0,1:T(8,128)S(1)} %convert_element_type.7, bf16[512,128]{1,0:T(8,128)(2,1)S(1)} %copy-done, bf16[128,8192]{1,0:T(8,128)(2,1)S(1)} %copy-done.1), kind=kOutput, calls=%fused_computation.25 | convolution fusion | flops 1086259200 | bytes 19300352 | tf_op jit(solution)/shard_map/dot_general | solution.py:80
  137.2 5.1 %all-gather.6 = f32[4,1,128]{2,1,0:T(1,128)S(1)} all-gather(f32[1,1,128]{2,1,0:T(1,128)S(1)} %bitcast.159), channel_id=2, replica_groups=mesh['key'=4,'head'=4,'query'=2] {'key'}, dimensions={0}, use_global_device_ids=true | all-gather | bytes 2560 | tf_op jit(solution)/shard_map/all_gather | solution.py:18
  142.3 13.6 %reduce-scatter.3.cloned.1.call-done = f32[1,128,512]{2,1,0:T(8,128)} async-done(((f32[4,128,512]{2,1,0:T(8,128)}), f32[1,128,512]{2,1,0:T(8,128)}) %reduce-scatter.3.cloned.1.call-update) | async-done | bytes 262160 | tf_op jit(solution)/shard_map/reduce_scatter | solution.py:75
  155.9 1.3 fusion.27
  157.1 5.2 %all-gather.9 = f32[4,1,128]{2,1,0:T(1,128)S(1)} all-gather(f32[1,1,128]{2,1,0:T(1,128)S(1)} %bitcast.163), channel_id=7, replica_groups=mesh['key'=4,'head'=4,'query'=2] {'key'}, dimensions={0}, use_global_device_ids=true | all-gather | bytes 2560 | tf_op jit(solution)/shard_map/all_gather | solution.py:18
  162.4 5.0 %all-gather.8 = f32[4,1,128]{2,1,0:T(1,128)S(1)} all-gather(f32[1,1,128]{2,1,0:T(1,128)S(1)} %bitcast.162), channel_id=6, replica_groups=mesh['key'=4,'head'=4,'query'=2] {'key'}, dimensions={0}, use_global_device_ids=true | all-gather | bytes 2560 | tf_op jit(solution)/shard_map/all_gather | solution.py:18
  167.4 5.0 %all-gather.7 = f32[4,1,128]{2,1,0:T(1,128)S(1)} all-gather(f32[1,1,128]{2,1,0:T(1,128)S(1)} %bitcast.161), channel_id=3, replica_groups=mesh['key'=4,'head'=4,'query'=2] {'key'}, dimensions={0}, use_global_device_ids=true | all-gather | bytes 2560 | tf_op jit(solution)/shard_map/all_gather | solution.py:18
  173.2 1.1 fusion.25
  174.4 9.5 %select_convert_fusion = bf16[512,128,64]{0,1,2:T(8,128)(2,1)} fusion(f32[512,128,64]{0,1,2:T(8,128)} %get-tuple-element.167, f32[512,128]{0,1:T(8,128)S(1)} %fusion.25, f32[128,64]{0,1:T(8,128)S(1)} %convert_element_type.7), kind=kLoop, calls=%fused_computation.24 | loop fusion | flops 16777216 | bytes 25460736 | tf_op jit(solution)/shard_map/convert_element_type | solution.py:99
  183.9 11.5 %copy.26 = bf16[512,128,64]{0,2,1:T(8,128)(2,1)} copy(bf16[512,128,64]{0,1,2:T(8,128)(2,1)} %select_convert_fusion) | data formatting | bytes 16777216 | tf_op jit(solution)/shard_map/convert_element_type | solution.py:99
  195.3 6.4 %fusion.37 = f32[512,128]{1,0:T(8,128)} fusion(bf16[512,8192]{0,1:T(8,128)(2,1)} %bitcast.147, bf16[8192,128]{1,0:T(8,128)(2,1)S(1)} %copy-done.4), kind=kOutput, calls=%fused_computation.91 | convolution fusion | flops 1073741824 | bytes 10747904 | tf_op jit(solution)/shard_map/dot_general | solution.py:108
  201.9 7.7 %fusion.36 = f32[8192,128]{1,0:T(8,128)} fusion(bf16[512,8192]{0,1:T(8,128)(2,1)} %bitcast.148, bf16[512,128]{1,0:T(8,128)(2,1)S(1)} %copy-done), kind=kOutput, calls=%fused_computation.90 | convolution fusion | flops 1073741824 | bytes 12713984 | tf_op jit(solution)/shard_map/dot_general | solution.py:103
  209.6 5.0 %reshape.213 = f32[128,8192]{1,0:T(8,128)} reshape(f32[8192,128]{1,0:T(8,128)} %fusion.36) | data formatting | bytes 8388608 | tf_op jit(solution)/shard_map/reshape | solution.py:106
  214.5 56.9 %all-reduce.2.cloned.1.call-done = f32[512,128]{1,0:T(8,128)} async-done(((f32[512,128]{1,0:T(8,128)}), f32[512,128]{1,0:T(8,128)}) %all-reduce.2.cloned.1.call-update) | async-done | bytes 262160 | tf_op jit(solution)/shard_map/psum | solution.py:109
  271.4 46.8 %reduce-scatter.5.cloned.1.call-done = f32[128,2048]{1,0:T(8,128)} async-done(((f32[128,8192]{1,0:T(8,128)}), f32[128,2048]{1,0:T(8,128)}) %reduce-scatter.5.cloned.1.call-update) | async-done | bytes 1048592 | tf_op jit(solution)/shard_map/reduce_scatter | solution.py:107
  318.3 1.7 copy.80
  (58 shorter events, 2.1 us)
Async XLA Ops:
  7.2 123.1 %copy-start = (bf16[512,128]{1,0:T(8,128)(2,1)S(1)}, bf16[512,128]{1,0:T(8,128)(2,1)}, u32[]{:S(2)}) copy-start(bf16[512,128]{1,0:T(8,128)(2,1)} %param.23) | copy-start | bytes 393220
  7.2 148.7 %reduce-scatter.3.cloned.1.call-start = ((), (), s32[]{:S(2)}) async-start(), calls=%async_computation.2 | async-start | bytes 1310720 | tf_op jit(solution)/shard_map/reduce_scatter | solution.py:75
  35.0 19.1 %copy-start.7 = (s32[4,128]{1,0:T(4,128)S(1)}, s32[4,128]{1,0:T(4,128)}, u32[]{:S(2)}) copy-start(s32[4,128]{1,0:T(4,128)} %constant.146.clone.1) | copy-start | bytes 6148
  35.0 24.7 %copy-start.6 = (s32[512]{0:T(512)S(1)}, s32[512]{0:T(512)}, u32[]{:S(2)}) copy-start(s32[512]{0:T(512)} %param.20) | copy-start | bytes 6148
  35.0 24.7 %copy-start.8 = (s32[4,128]{1,0:T(4,128)S(1)}, s32[4,128]{1,0:T(4,128)}, u32[]{:S(2)}) copy-start(s32[4,128]{1,0:T(4,128)} %param.19) | copy-start | bytes 6148
  35.0 24.9 %copy-start.5 = (bf16[512,64]{0,1:T(8,128)(2,1)S(1)}, bf16[512,64]{0,1:T(8,128)(2,1)}, u32[]{:S(2)}) copy-start(bf16[512,64]{0,1:T(8,128)(2,1)} %param.18) | copy-start | bytes 196612
  110.6 0.6 copy-start.2
  110.6 0.6 copy-start.3
  111.2 16.7 %copy-start.1 = (bf16[128,8192]{1,0:T(8,128)(2,1)S(1)}, bf16[128,8192]{1,0:T(8,128)(2,1)}, u32[]{:S(2)}) copy-start(bf16[128,8192]{1,0:T(8,128)(2,1)} %param.22) | copy-start | bytes 6291460
  127.1 144.3 %all-reduce.2.cloned.1.call-start = ((), (), s32[]{:S(2)}) async-start(), calls=%async_computation.4 | async-start | bytes 524288 | tf_op jit(solution)/shard_map/psum | solution.py:109
  130.3 42.9 %copy-start.9 = (f32[128]{0:T(128)S(1)}, f32[128]{0:T(128)}, u32[]{:S(2)}) copy-start(f32[128]{0:T(128)} %param.25) | copy-start | bytes 1540
  183.9 11.5 %copy-start.4 = (bf16[8192,128]{1,0:T(8,128)(2,1)S(1)}, bf16[8192,128]{1,0:T(8,128)(2,1)}, u32[]{:S(2)}) copy-start(bf16[8192,128]{1,0:T(8,128)(2,1)} %reshape.214) | copy-start | bytes 6291460
  201.8 116.4 %reduce-scatter.5.cloned.1.call-start = ((), (), s32[]{:S(2)}) async-start(), calls=%async_computation.3 | async-start | bytes 5242880 | tf_op jit(solution)/shard_map/reduce_scatter | solution.py:107
Sparse Core Ops, SparseCore 0:
  127.3 28.5 reduce-scatter.2
  201.9 69.4 all-reduce.1
  274.6 43.6 reduce-scatter.4
where the time goes:
time: 328 us; the launch traced here: 326 us
  waiting for transfers between devices  117 us (36%)
  matrix products  63.2 us (19%)
  other arithmetic  53.2 us (16%)
  local copies, waits for them, and re-layouts  45.2 us (14%)
  blocking collectives  33.5 us (10%)
  between operations  13.9 us (4%)
    psum x1, waiting for transfers between devices, body(): grad_key = lax.psum(key_terms, ('head', 'query'))  56.9 us
    reduce_scatter x1, waiting for transfers between devices, body(): lax.psum_scatter(grad_terms, 'key', scatter_dimension=1, tiled=True)  46.8 us
    all_gather x6, blocking collectives, joined(): pieces = jax.tree.map(lambda part: lax.all_gather(part, axis), value)  33.5 us
    dot_general x1, matrix products, body(): jnp.einsum('thd,kd->htk', q_heads[:, :, DNOPE:], key_rope, preferred_elem...  23.2 us
    dot_general x1, matrix products, body(): jnp.einsum('thd,khd->htk', q_heads[:, :, :DNOPE], k_heads, preferred_elem...  19.1 us
    reduce_sum x1, other arithmetic, body(): tile = jnp.sum(probs, axis=0).reshape(groups, half_rows, keys_here)  14.6 us
    reduce_sum x1, other arithmetic, body(): jnp.sum(jnp.where(valid[None], jnp.exp(scores - local_top[..., None]), 0....  14 us
    reduce_scatter x1, waiting for transfers between devices, body(): mine = lax.psum_scatter(tile, 'head', scatter_dimension=0, tiled=True)[0]  13.6 us
  transfers between devices with their start and end apart: 3, of which 3 were waited for; matrix products, arithmetic and copies ran while one was open for 7% of the time, Pallas kernels for 0%

commit v1 on v0

v1 whole, which is shorter than its diff:
```python
import functools
import math
import jax
import jax.numpy as jnp
from jax import lax
from jax.experimental import pallas as pl
from jax.experimental.pallas import tpu as pltpu
from jax.sharding import PartitionSpec as P

H = 128
DNOPE = 128
DROPE = 64
IH = 64
ID = 128
KBLOCK = 32
DQK = 192
LANES = 128
PAIR = 2 * DQK
NEG = -1e30
BIG = 2**30
LOG2E = math.log2(math.e)
SCALE_MAIN = DQK ** (-0.5) * LOG2E
SCALE_INDEX = ID ** (-0.5)
VMEM_LIMIT = 60 * 1024 * 1024

f32 = jnp.float32
bf16 = jnp.bfloat16


def dot_nt(a, b):
    return lax.dot_general(a, b, (((1,), (1,)), ((), ())), preferred_element_type=f32)


def dot_nn(a, b):
    return lax.dot_general(a, b, (((1,), (0,)), ((), ())), preferred_element_type=f32)


def params(*semantics):
    return pltpu.CompilerParams(
        dimension_semantics=semantics, vmem_limit_bytes=VMEM_LIMIT
    )


def cost(flops, bytes_accessed, transcendentals=0):
    return pl.CostEstimate(
        flops=int(flops), bytes_accessed=int(bytes_accessed), transcendentals=int(transcendentals)
    )


def key_limit_column(count_ref, pos_ref, keys):
    blocks = keys // KBLOCK
    lane = lax.broadcasted_iota(jnp.int32, (1, keys), 1)
    block = lane // KBLOCK
    limit = jnp.zeros((1, keys), jnp.int32)
    for b in range(blocks):
        limit = jnp.where(block == b, count_ref[b], limit)
    live = (lane % KBLOCK) < limit
    row = jnp.where(live, pos_ref[...], BIG)
    return jnp.transpose(jnp.broadcast_to(row, (8, keys)))[:, :1]


def main_keys(kn_ref, rope, parity):
    keys = rope.shape[0]
    zero = jnp.zeros((keys, DROPE), bf16)
    if parity == 0:
        return jnp.concatenate([kn_ref[:, :DNOPE], rope, zero], axis=1)
    return jnp.concatenate([zero, kn_ref[:, DNOPE:], rope], axis=1)


def stats_kernel(count_ref, q_ref, kn_ref, rope_ref, qpos_ref, kpos_ref, lse_ref, bias_ref):
    step = pl.program_id(0)
    keys = kn_ref.shape[0]
    groups, rows = q_ref.shape[0], q_ref.shape[1]

    @pl.when(step == 0)
    def _():
        column = key_limit_column(count_ref, kpos_ref, keys)
        for g in range(groups):
            valid = column <= qpos_ref[g : g + 1, :]
            bias_ref[:, g * rows : (g + 1) * rows] = jnp.where(valid, 0.0, NEG)

    rope = rope_ref[...]
    for parity in range(2):
        kk = main_keys(kn_ref, rope, parity)
        head = 2 * step + parity
        for c in range(groups // 2):
            q = q_ref[2 * c : 2 * c + 2, :, parity * LANES : parity * LANES + 2 * LANES]
            q = q.reshape(2 * rows, 2 * LANES)
            cols = slice(2 * c * rows, (2 * c + 2) * rows)
            s = dot_nt(kk, q) * SCALE_MAIN + bias_ref[:, cols]
            top = jnp.max(s, axis=0, keepdims=True)
            total = jnp.sum(jnp.exp2(s - top), axis=0, keepdims=True)
            lse_ref[pl.ds(head, 1), cols] = top + jnp.log2(total)


def main_stats(main_query, key_nope, key_rope, query_pos, key_pos, key_count):
    groups, rows, width = main_query.shape
    heads = width // DQK
    keys = key_nope.shape[0]
    total = groups * rows
    return pl.pallas_call(
        stats_kernel,
        grid_spec=pltpu.PrefetchScalarGridSpec(
            num_scalar_prefetch=1,
            grid=(heads // 2,),
            in_specs=[
                pl.BlockSpec((groups, rows, PAIR), lambda i, c: (0, 0, i)),
                pl.BlockSpec((keys, 2 * DNOPE), lambda i, c: (0, i)),
                pl.BlockSpec((keys, DROPE), lambda i, c: (0, 0)),
                pl.BlockSpec((groups, rows), lambda i, c: (0, 0)),
                pl.BlockSpec((1, keys), lambda i, c: (0, 0)),
            ],
            out_specs=pl.BlockSpec((heads, total), lambda i, c: (0, 0)),
            scratch_shapes=[pltpu.VMEM((keys, total), f32)],
        ),
        out_shape=jax.ShapeDtypeStruct((heads, total), f32),
        compiler_params=params("arbitrary"),
        cost_estimate=cost(
            heads * total * keys * 512, main_query.size * 2 + key_nope.size * 2, heads * total * keys
        ),
        name="main_stats",
    )(key_count, main_query, key_nope, key_rope, query_pos, key_pos.reshape(1, keys))


def target_kernel(n_lse, n_groups, count_ref, grp_ref, *refs):
    q_refs = refs[:n_groups]
    kn_ref, rope_ref, qpos_ref, kpos_ref = refs[n_groups : n_groups + 4]
    lse_refs = refs[n_groups + 4 : n_groups + 4 + n_lse * n_groups]
    out_refs = refs[n_groups + 4 + n_lse * n_groups : -1]
    glob_ref = refs[-1]
    step = pl.program_id(0)
    keys = kn_ref.shape[0]
    rows = q_refs[0].shape[1]

    @pl.when(step == 0)
    def _():
        for g in range(n_groups):
            parts = [r[...] for r in lse_refs[g * n_lse : (g + 1) * n_lse]]
            top = functools.reduce(jnp.maximum, parts)
            total = functools.reduce(jnp.add, [jnp.exp2(p - top) for p in parts])
            glob_ref[:, g * rows : (g + 1) * rows] = top + jnp.log2(total)
            out_refs[g][...] = jnp.zeros_like(out_refs[g])

    rope = rope_ref[...]
    acc = None
    for parity in range(2):
        kk = main_keys(kn_ref, rope, parity)
        lanes = slice(parity * LANES, parity * LANES + 2 * LANES)
        qs = [r[0, :, lanes] for r in q_refs]
        q = qs[0] if n_groups == 1 else jnp.concatenate(qs, axis=0)
        lse = glob_ref[pl.ds(2 * step + parity, 1), :]
        e = jnp.exp2(dot_nt(kk, q) * SCALE_MAIN - lse)
        acc = e if acc is None else acc + e
    for g in range(n_groups):
        out_refs[g][...] += acc[:, g * rows : (g + 1) * rows]

    @pl.when(step == pl.num_programs(0) - 1)
    def _():
        column = key_limit_column(count_ref, kpos_ref, keys)
        for g in range(n_groups):
            valid = column <= qpos_ref[pl.ds(grp_ref[g], 1), :]
            out_refs[g][...] = jnp.where(valid, out_refs[g][...], 0.0)


def head_sums(group_ids, main_query, key_nope, key_rope, query_pos, key_pos, key_count, lses):
    groups, rows, width = main_query.shape
    heads = width // DQK
    keys = key_nope.shape[0]
    n = len(group_ids)

    def group_q(g):
        return pl.BlockSpec((1, rows, PAIR), lambda i, c, grp: (grp[g], 0, i))

    def group_lse(g):
        return pl.BlockSpec((heads, rows), lambda i, c, grp: (0, grp[g]))

    return pl.pallas_call(
        functools.partial(target_kernel, len(lses), n),
        grid_spec=pltpu.PrefetchScalarGridSpec(
            num_scalar_prefetch=2,
            grid=(heads // 2,),
            in_specs=[group_q(g) for g in range(n)]
            + [
                pl.BlockSpec((keys, 2 * DNOPE), lambda i, c, grp: (0, i)),
                pl.BlockSpec((keys, DROPE), lambda i, c, grp: (0, 0)),
                pl.BlockSpec((groups, rows), lambda i, c, grp: (0, 0)),
                pl.BlockSpec((1, keys), lambda i, c, grp: (0, 0)),
            ]
            + [group_lse(g) for g in range(n) for _ in lses],
            out_specs=[pl.BlockSpec((keys, rows), lambda i, c, grp: (0, 0))] * n,
            scratch_shapes=[pltpu.VMEM((heads, n * rows), f32)],
        ),
        out_shape=[jax.ShapeDtypeStruct((keys, rows), f32)] * n,
        compiler_params=params("arbitrary"),
        cost_estimate=cost(
            heads * n * rows * keys * 512, main_query.size * n // 2 + key_nope.size * 2,
            heads * n * rows * keys,
        ),
        name="head_sums",
    )(
        key_count,
        jnp.stack(group_ids),
        *([main_query] * n),
        key_nope,
        key_rope,
        query_pos,
        key_pos.reshape(1, keys),
        *(list(lses) * n),
    )


def logits_kernel(count_ref, grp_ref, iq_ref, ik_ref, w_ref, qpos_ref, kpos_ref,
                  logits_ref, lse_ref, wm_ref, wt_ref):
    step = pl.program_id(0)
    keys = ik_ref.shape[0]
    rows = iq_ref.shape[0]
    per = iq_ref.shape[1] // ID

    @pl.when(step == 0)
    def _():
        wt_ref[...] = jnp.transpose(w_ref[...].astype(f32))
        logits_ref[...] = jnp.zeros_like(logits_ref)

    ik = ik_ref[...]
    total = None
    for p in range(per // 2):
        cols = [slice((2 * p + a) * ID, (2 * p + a + 1) * ID) for a in range(2)]
        q = jnp.concatenate([iq_ref[:, c] for c in cols], axis=0)
        z = dot_nt(ik, q)
        w = jnp.concatenate(
            [wt_ref[pl.ds(step * per + 2 * p + a, 1), :] for a in range(2)], axis=1
        )
        positive = z > 0
        masked = jnp.where(positive, w, 0.0)
        wm_ref[:, 2 * p * rows : (2 * p + 2) * rows] = masked.astype(bf16)
        r = z * masked
        r = r[:, :rows] + r[:, rows:]
        total = r if total is None else total + r
    logits_ref[...] += total

    @pl.when(step == pl.num_programs(0) - 1)
    def _():
        logits = logits_ref[...] * SCALE_INDEX
        logits_ref[...] = logits
        column = key_limit_column(count_ref, kpos_ref, keys)
        valid = column <= qpos_ref[pl.ds(grp_ref[0], 1), :]
        s = jnp.where(valid, logits * LOG2E, NEG)
        top = jnp.max(s, axis=0, keepdims=True)
        lse_ref[...] = top + jnp.log2(jnp.sum(jnp.exp2(s - top), axis=0, keepdims=True))


def index_logits(group_id, index_query, index_key, index_weight, query_pos, key_pos, key_count):
    rows, width = index_query.shape
    keys = index_key.shape[0]
    groups = query_pos.shape[0]
    per = 8
    steps = width // (per * ID)
    return pl.pallas_call(
        logits_kernel,
        grid_spec=pltpu.PrefetchScalarGridSpec(
            num_scalar_prefetch=2,
            grid=(steps,),
            in_specs=[
                pl.BlockSpec((rows, per * ID), lambda i, c, grp: (0, i)),
                pl.BlockSpec((keys, ID), lambda i, c, grp: (0, 0)),
                pl.BlockSpec((rows, width // ID), lambda i, c, grp: (0, 0)),
                pl.BlockSpec((groups, rows), lambda i, c, grp: (0, 0)),
                pl.BlockSpec((1, keys), lambda i, c, grp: (0, 0)),
            ],
            out_specs=[
                pl.BlockSpec((keys, rows), lambda i, c, grp: (0, 0)),
                pl.BlockSpec((1, rows), lambda i, c, grp: (0, 0)),
                pl.BlockSpec((keys, per * rows), lambda i, c, grp: (0, i)),
            ],
            scratch_shapes=[pltpu.VMEM((width // ID, rows), f32)],
        ),
        out_shape=[
            jax.ShapeDtypeStruct((keys, rows), f32),
            jax.ShapeDtypeStruct((1, rows), f32),
            jax.ShapeDtypeStruct((keys, (width // ID) * rows), bf16),
        ],
        compiler_params=params("arbitrary"),
        cost_estimate=cost(2 * keys * rows * width, rows * width * 2 + keys * rows * width // ID * 2),
        name="index_logits",
    )(key_count, group_id.reshape(1), index_query, index_key, index_weight, query_pos,
      key_pos.reshape(1, keys))


def combine_lse(parts):
    top = functools.reduce(jnp.maximum, parts)
    return top + jnp.log2(functools.reduce(jnp.add, [jnp.exp2(p - top) for p in parts]))


def grad_key_kernel(n_parts, n_lse, count_ref, grp_ref, *refs):
    parts = refs[:n_parts]
    lses = refs[n_parts : n_parts + n_lse]
    (logits_ref, cot_ref, qpos_ref, kpos_ref, wm_ref, iq_ref,
     sg_ref, gk_ref) = refs[n_parts + n_lse :]
    step = pl.program_id(0)
    keys, rows = logits_ref.shape
    per = iq_ref.shape[1] // ID

    @pl.when(step == 0)
    def _():
        column = key_limit_column(count_ref, kpos_ref, keys)
        valid = column <= qpos_ref[pl.ds(grp_ref[0], 1), :]
        target = functools.reduce(jnp.add, [p[...] for p in parts]) * (1.0 / H)
        logits = logits_ref[...]
        lse2 = combine_lse([r[...] for r in lses])
        qprob = jnp.where(valid, jnp.exp2(logits * LOG2E - lse2), 0.0)
        sg_ref[:keys, :] = SCALE_INDEX * (cot_ref[...] * (qprob - target))
        live = target > 0
        terms = jnp.where(live, target * (jnp.log(jnp.where(live, target, 1.0)) - logits), 0.0)
        kl = jnp.sum(terms, axis=0, keepdims=True)
        sg_ref[keys:, :] = jnp.broadcast_to(kl, (8, rows))
        gk_ref[...] = jnp.zeros_like(gk_ref)

    sg = sg_ref[:keys, :]
    total = None
    for p in range(per // 2):
        dz = []
        qs = []
        for a in range(2):
            j = 2 * p + a
            dz.append((sg * wm_ref[:, j * rows : (j + 1) * rows].astype(f32)).astype(bf16))
            qs.append(iq_ref[:, j * ID : (j + 1) * ID])
        t = dot_nn(jnp.concatenate(dz, axis=1), jnp.concatenate(qs, axis=0))
        total = t if total is None else total + t
    gk_ref[...] += total


def index_grad_key(group_id, parts, lses, logits, cotangent, wm, index_query,
                   query_pos, key_pos, key_count):
    rows, width = index_query.shape
    keys = logits.shape[0]
    groups = query_pos.shape[0]
    per = 8
    steps = width // (per * ID)
    whole = lambda i, c, grp: (0, 0)
    return pl.pallas_call(
        functools.partial(grad_key_kernel, len(parts), len(lses)),
        grid_spec=pltpu.PrefetchScalarGridSpec(
            num_scalar_prefetch=2,
            grid=(steps,),
            in_specs=[pl.BlockSpec((keys, rows), whole) for _ in parts]
            + [pl.BlockSpec((1, rows), whole) for _ in lses]
            + [
                pl.BlockSpec((keys, rows), whole),
                pl.BlockSpec((1, rows), whole),
                pl.BlockSpec((groups, rows), whole),
                pl.BlockSpec((1, keys), whole),
                pl.BlockSpec((keys, per * rows), lambda i, c, grp: (0, i)),
                pl.BlockSpec((rows, per * ID), lambda i, c, grp: (0, i)),
            ],
            out_specs=[
                pl.BlockSpec((keys + 8, rows), whole),
                pl.BlockSpec((keys, ID), whole),
            ],
        ),
        out_shape=[
            jax.ShapeDtypeStruct((keys + 8, rows), f32),
            jax.ShapeDtypeStruct((keys, ID), f32),
        ],
        compiler_params=params("arbitrary"),
        cost_estimate=cost(2 * keys * rows * width, rows * width * 2 + keys * rows * width // ID * 2),
        name="index_grad_key",
    )(key_count, group_id.reshape(1), *parts, *lses, logits, cotangent.reshape(1, rows),
      query_pos, key_pos.reshape(1, keys), wm, index_query)


def grad_query_kernel(n_shards, first, slot_ref, *refs):
    sgs = refs[:n_shards]
    iks = refs[n_shards : 2 * n_shards]
    iq_ref, w_ref = refs[2 * n_shards : 2 * n_shards + 2]
    rest = refs[2 * n_shards + 2 :]
    if first:
        gq_ref, kl_ref = rest
    else:
        gq_in_ref, kl_in_ref, gq_ref, kl_ref = rest
    rows = iq_ref.shape[0]
    heads = iq_ref.shape[1] // ID
    keys = iks[0].shape[0]
    weights = w_ref[...].astype(f32)
    col = lax.broadcasted_iota(jnp.int32, weights.shape, 1)
    base = slot_ref[0] * heads
    iq = jnp.concatenate([iq_ref[:, j * ID : (j + 1) * ID] for j in range(heads)], axis=0)
    ws = [
        jnp.sum(jnp.where(col == base + j, weights, 0.0), axis=1, keepdims=True)
        for j in range(heads)
    ]
    kl = functools.reduce(jnp.add, [s[keys : keys + 1, :] for s in sgs])
    kl_ref[...] = kl if first else kl_in_ref[...] + kl
    out = None
    for s_ref, ik_ref in zip(sgs, iks):
        ik = ik_ref[...].astype(bf16)
        sgt = jnp.transpose(s_ref[:keys, :])
        z = dot_nt(iq, ik)
        dz = jnp.concatenate(
            [
                jnp.where(z[j * rows : (j + 1) * rows] > 0, sgt * ws[j], 0.0).astype(bf16)
                for j in range(heads)
            ],
            axis=0,
        )
        g = dot_nn(dz, ik)
        out = g if out is None else out + g
    for j in range(heads):
        cols = slice(j * ID, (j + 1) * ID)
        g = out[j * rows : (j + 1) * rows]
        gq_ref[:, cols] = g if first else gq_in_ref[:, cols] + g


def index_grad_query(slot, n_slots, sgs, iks, index_query, index_weight, carry):
    rows, width = index_query.shape
    heads = width // ID
    mine = width // n_slots
    keys = iks[0].shape[0]
    whole = lambda i, s: (0, 0)
    first = carry is None
    carried = [] if first else list(carry)
    n = len(sgs)
    return pl.pallas_call(
        functools.partial(grad_query_kernel, n, first),
        grid_spec=pltpu.PrefetchScalarGridSpec(
            num_scalar_prefetch=1,
            grid=(1,),
            in_specs=[pl.BlockSpec((keys + 8, rows), whole) for _ in sgs]
            + [pl.BlockSpec((keys, ID), whole) for _ in iks]
            + [
                pl.BlockSpec((rows, mine), lambda i, s: (0, s[0])),
                pl.BlockSpec((rows, heads), whole),
            ]
            + ([] if first else [pl.BlockSpec((rows, mine), whole), pl.BlockSpec((1, rows), whole)]),
            out_specs=[pl.BlockSpec((rows, mine), whole), pl.BlockSpec((1, rows), whole)],
        ),
        out_shape=[
            jax.ShapeDtypeStruct((rows, mine), f32),
            jax.ShapeDtypeStruct((1, rows), f32),
        ],
        compiler_params=params("arbitrary"),
        cost_estimate=cost(4 * n * keys * rows * mine, n * (keys * ID * 8) + rows * mine * 8),
        name="index_grad_query",
    )(slot.reshape(1), *sgs, *iks, index_query, index_weight, *carried)


def swap(value, axis, mask, size):
    return lax.ppermute(value, axis, [(i, i ^ mask) for i in range(size)])


def rotate(value, axis, by, size):
    return lax.ppermute(value, axis, [(i, (i + by) % size) for i in range(size)])


def summed_copies(value, n_head, n_query):
    steps = [("query", m, n_query) for m in (1 << b for b in range(n_query.bit_length() - 1))]
    steps += [("head", (2 << b) - 1, n_head) for b in range(n_head.bit_length() - 1)]
    count = len(steps)
    if count == 0:
        return value
    rows = value.shape[0]
    unit = -(-rows // (8 * count)) * 8
    pieces = [value[i * unit : min((i + 1) * unit, rows)] for i in range(count)]
    pieces = [p for p in pieces if p.shape[0]]
    for s in range(count):
        moved = [swap(p, *steps[(i + s) % count]) for i, p in enumerate(pieces)]
        pieces = [p + m for p, m in zip(pieces, moved)]
    return jnp.concatenate(pieces, axis=0)


def body(n_key, n_head, n_query, main_query, key_nope, key_rope, query_pos, key_pos, key_count,
         index_query, index_key, index_weight, row_cotangent):
    groups, rows, _ = main_query.shape
    keys = key_nope.shape[0]
    z = lax.axis_index("head")
    slot = lax.axis_index("key")
    main = (main_query, key_nope, key_rope, query_pos, key_pos, key_count)

    lse = main_stats(*main)
    if n_key == 4:
        near = swap(lse, "key", 1, n_key)
        far = swap(lse, "key", 2, n_key)
        lses = [lse, near, far, swap(lse, "key", 3, n_key)]
    else:
        lses = [combine_lse(list(lax.all_gather(lse, "key")))]

    logits, index_lse, wm = index_logits(
        z, index_query, index_key, index_weight, query_pos, key_pos, key_count
    )
    index_lses = list(lax.all_gather(index_lse, "key")) if n_key != 4 else [index_lse] + [
        swap(index_lse, "key", m, n_key) for m in (1, 2, 3)
    ]
    if len(index_lses) > 4:
        index_lses = [combine_lse(index_lses)]

    if n_head == 4 and groups == 4:
        across = head_sums([(z + 2) % 4], *main, lses)[0]
        half = keys // 2
        low = rotate(across[:half], "head", 1, 4)
        high = rotate(across[half:], "head", 3, 4)
        up, down = head_sums([(z + 1) % 4, (z + 3) % 4], *main, lses)
        up = jnp.concatenate([up[:half] + low, up[half:]], axis=0)
        down = jnp.concatenate([down[:half], down[half:] + high], axis=0)
        from_below = rotate(up, "head", 1, 4)
        from_above = rotate(down, "head", 3, 4)
        own = head_sums([z], *main, lses)[0]
        parts = [own, from_below, from_above]
    else:
        tiles = jnp.stack([head_sums([jnp.int32(g)], *main, lses)[0] for g in range(groups)])
        parts = [lax.psum_scatter(tiles, "head", scatter_dimension=0, tiled=True)[0]]

    sg, grad_key = index_grad_key(
        z, parts, index_lses, logits, row_cotangent, wm, index_query, query_pos, key_pos, key_count
    )
    grad_key = summed_copies(grad_key, n_head, n_query)

    wide = index_key.astype(f32)
    if n_key == 4:
        ik_far = swap(wide, "key", 2, n_key)
        iks = [wide, swap(wide, "key", 1, n_key), ik_far, swap(ik_far, "key", 1, n_key)]
        sg_far = swap(sg, "key", 2, n_key)
        sgs = [sg, swap(sg, "key", 1, n_key), sg_far, swap(sg_far, "key", 1, n_key)]
        carry = None
        for lo in (0, 2):
            carry = index_grad_query(
                slot, n_key, sgs[lo : lo + 2], iks[lo : lo + 2], index_query, index_weight, carry
            )
    else:
        iks = list(lax.all_gather(wide, "key"))
        sgs = list(lax.all_gather(sg, "key"))
        carry = None
        for lo in range(0, n_key, 2):
            carry = index_grad_query(
                slot, n_key, sgs[lo : lo + 2], iks[lo : lo + 2], index_query, index_weight, carry
            )
    grad_query, kl = carry
    kl_rows = (kl + combine_lse(index_lses) * (1.0 / LOG2E)).reshape(rows)
    return kl_rows, grad_query, grad_key


def solution(mesh):
    return jax.shard_map(
        functools.partial(body, mesh.shape["key"], mesh.shape["head"], mesh.shape["query"]),
        mesh=mesh,
        in_specs=(
            P(None, "query", "head"),
            P("key", "head"),
            P("key", None),
            P(None, "query"),
            P("key"),
            P("key"),
            P(("head", "query"), None),
            P("key", None),
            P(("head", "query"), None),
            P(("head", "query")),
        ),
        out_specs=(P(("head", "query")), P(("head", "query"), "key"), P("key", None)),
        check_vma=False,
    )
```

time: 328 us -> 144 us (0.44)
  waiting for transfers between devices: 117 us -> 14.6 us
  Pallas kernels: 0 us -> 88.9 us
  matrix products: 63.2 us -> 0 us
  other arithmetic: 53.2 us -> 5.69 us
  local copies, waits for them, and re-layouts: 45.2 us -> 8.04 us
  blocking collectives: 33.5 us -> 0 us
  starting transfers between devices: 0.12 us -> 24 us
  between operations: 13.9 us -> 0.91 us
    pallas_call x0 -> x8, Pallas kernels: none -> 88.9 us  [the longest x3 40.8 us: head_sums(): pl.pallas_call(functools.partial(target_kernel, len(lses), n), grid_spec=...]
    dot_general x5 -> x0, matrix products: 63.2 us -> none  [the longest x1 23.2 us: body(): jnp.einsum('thd,kd->htk', q_heads[:, :, DNOPE:], key_rope, preferred_elem...]
    reduce_scatter x2 -> x0, waiting for transfers between devices: 60.4 us -> none  [the longest x1 46.8 us: body(): lax.psum_scatter(grad_terms, 'key', scatter_dimension=1, tiled=True)]
    psum x1 -> x0, waiting for transfers between devices: 56.9 us -> none  [body(): grad_key = lax.psum(key_terms, ('head', 'query'))]
    all_gather x6 -> x0, blocking collectives: 33.5 us -> none  [joined(): pieces = jax.tree.map(lambda part: lax.all_gather(part, axis), value)]
    reduce_sum x3 -> x0, other arithmetic: 29.8 us -> none  [the longest x1 14.6 us: body(): tile = jnp.sum(probs, axis=0).reshape(groups, half_rows, keys_here)]
    ppermute x0 -> x25, starting transfers between devices: none -> 24 us  [the longest x21 17.9 us: swap(): return lax.ppermute(value, axis, [(i, i ^ mask) for i in range(size)])]
    reshape x4 -> x0, local copies, waits for them, and re-layouts: 18.8 us -> none  [the longest x1 10.1 us: body(): q_heads = main_query.reshape(rows, heads_here, DQK)]
  transfers between devices with their start and end apart: 3 -> 25, of which waited for: 3 -> 9; matrix products, arithmetic and copies ran while one was open for 7% -> 4% of each run, Pallas kernels for 0% -> 37%
where the time goes in v1:
time: 144 us; the launch traced here: 142 us
  Pallas kernels  88.9 us (62%)
  starting transfers between devices  24 us (17%)
  waiting for transfers between devices  14.6 us (10%)
  local copies, waits for them, and re-layouts  8.04 us (6%)
  other arithmetic  5.69 us (4%)
    pallas_call x3, Pallas kernels, head_sums(): pl.pallas_call(functools.partial(target_kernel, len(lses), n), grid_spec=...  40.8 us
    ppermute x21, starting transfers between devices, swap(): return lax.ppermute(value, axis, [(i, i ^ mask) for i in range(size)])  17.9 us
    pallas_call x1, Pallas kernels, main_stats(): pl.pallas_call(stats_kernel, grid_spec=pltpu.PrefetchScalarGridSpec(num_s...  17.6 us
    ppermute x21, waiting for transfers between devices, swap(): return lax.ppermute(value, axis, [(i, i ^ mask) for i in range(size)])  14.6 us
    pallas_call x2, Pallas kernels, index_grad_query(): pl.pallas_call(functools.partial(grad_query_kernel, n, first), grid_spec=...  11 us
    pallas_call x1, Pallas kernels, index_grad_key(): pl.pallas_call(functools.partial(grad_key_kernel, len(parts), len(lses)),...  9.81 us
    pallas_call x1, Pallas kernels, index_logits(): pl.pallas_call(logits_kernel, grid_spec=pltpu.PrefetchScalarGridSpec(num_...  9.73 us
    ppermute x4, starting transfers between devices, rotate(): lax.ppermute(value, axis, [(i, (i + by) % size) for i in range(size)])  6.19 us
  transfers between devices with their start and end apart: 25, of which 9 were waited for; matrix products, arithmetic and copies ran while one was open for 4% of the time, Pallas kernels for 37%

profile of v1, /device:TPU:0, one launch (start us, length us, event | category | flops | bytes accessed | tf_op | source)
XLA Modules:
  0.0 142.2 jit_solution(9585994375714162349)
XLA Ops:
  0.6 1.6 %copy.14.rope_ref.refs_2_.refs_3_ = bf16[512,64]{1,0:T(8,128)(2,1)} copy(bf16[512,64]{0,1:T(8,128)(2,1)} %param.12) | data formatting | bytes 131072 | tf_op args[2]
  2.2 17.6 %main_stats.1.refs_5_.refs_6_.refs_10_ = f32[32,512]{1,0:T(8,128)} custom-call(s32[16]{0:T(128)} %count_ref.11, bf16[4,128,6144]{2,1,0:T(8,128)(2,1)} %refs_0_.5, bf16[512,4096]{1,0:T(8,128)(2,1)} %refs_1_.5, bf16[512,64]{1,0:T(8,128)(2,1)} %copy.14.rope_ref.refs_2_.refs_3_, s32[4,128]{1,0:T(4,128)} %refs_9_.1, s32[1,512]{1,0:T(1,128)} %bitcast.9), custom_call_target="tpu_custom_call" | custom-call | flops 4294967296 | bytes 10485760 | tf_op jit(solution)/shard_map/main_stats/pallas_call | solution.py:101
  20.4 2.5 %collective-permute-start.1 = (f32[32,512]{1,0:T(8,128)}, f32[32,512]{1,0:T(8,128)S(1)}, u32[]{:S(2)}, u32[]{:S(2)}) collective-permute-start(f32[32,512]{1,0:T(8,128)} %main_stats.1.refs_5_.refs_6_.refs_10_), channel_id=1, source_target_pairs={{0,16},{8,24},{16,0},{24,8},{1,17},{9,25},{17,1},{25,9},{2,18},{10... | collective-permute-start | bytes 196616 | tf_op jit(solution)/shard_map/ppermute | solution.py:447
  23.6 2.2 %collective-permute-done.1.refs_7_.refs_8_.refs_12_ = f32[32,512]{1,0:T(8,128)S(1)} collective-permute-done((f32[32,512]{1,0:T(8,128)}, f32[32,512]{1,0:T(8,128)S(1)}, u32[]{:S(2)}, u32[]{:S(2)}) %collective-permute-start.1) | collective-permute-done | bytes 65568 | tf_op jit(solution)/shard_map/ppermute | solution.py:447
  25.8 1.2 collective-permute-done.2.refs_8_.refs_9_.refs_13_
  27.7 13.3 %head_sums.5 = f32[512,128]{1,0:T(8,128)} custom-call(s32[16]{0:T(128)} %count_ref.11, s32[1]{0:T(128)} %bitcast.5.grp_ref, bf16[4,128,6144]{2,1,0:T(8,128)(2,1)} %refs_0_.5, bf16[512,4096]{1,0:T(8,128)(2,1)} %refs_1_.5, bf16[512,64]{1,0:T(8,128)(2,1)} %copy.14.rope_ref.refs_2_.refs_3_, s32[4,128]{1,0:T(4,128)} %refs_9_.1, s32[1,512]{1,0:T(1,128)} %bitcast.10, ...), custom_call_target="tpu_custom_call" | custom-call | flops 1073741824 | bytes 5767168 | tf_op jit(solution)/shard_map/head_sums/pallas_call | solution.py:177
  41.0 1.0 fusion.2
  42.0 1.7 %collective-permute-start.3 = (f32[256,128]{1,0:T(8,128)S(1)}, f32[256,128]{1,0:T(8,128)S(1)}, u32[]{:S(2)}, u32[]{:S(2)}) collective-permute-start(f32[256,128]{1,0:T(8,128)S(1)} %get-tuple-element.32), channel_id=1, source_target_pairs={{0,2},{2,4},{4,6},{6,0},{1,3},{3,5},{5,7},{7,1},{8,10},{10,12},{12... | collective-permute-start | bytes 393224 | tf_op jit(solution)/shard_map/ppermute | solution.py:451
  43.7 2.2 %collective-permute-start.5 = (f32[256,128]{1,0:T(8,128)S(1)}, f32[256,128]{1,0:T(8,128)S(1)}, u32[]{:S(2)}, u32[]{:S(2)}) collective-permute-start(f32[256,128]{1,0:T(8,128)S(1)} %get-tuple-element.31), channel_id=1, source_target_pairs={{0,6},{2,0},{4,2},{6,4},{1,7},{3,1},{5,3},{7,5},{8,14},{10,8},{12,... | collective-permute-start | bytes 393224 | tf_op jit(solution)/shard_map/ppermute | solution.py:451
  45.8 14.1 %head_sums.4 = (f32[512,128]{1,0:T(8,128)}, f32[512,128]{1,0:T(8,128)}) custom-call(s32[16]{0:T(128)} %count_ref.11, s32[2]{0:T(128)} %pad_add_fusion.grp_ref, bf16[4,128,6144]{2,1,0:T(8,128)(2,1)} %refs_0_.5, bf16[4,128,6144]{2,1,0:T(8,128)(2,1)} %refs_0_.5, bf16[512,4096]{1,0:T(8,128)(2,1)} %refs_1_.5, bf16[512,64]{1,0:T(8,128)(2,1)} %copy.14.rope_ref.refs_2_.refs_3_, ...), custom_call_target="tpu_custom_call" | custom-call | flops 2147483648 | bytes 7340032 | tf_op jit(solution)/shard_map/head_sums/pallas_call | solution.py:177
  60.0 1.2 slice_add_fusion.1
  61.2 1.9 %collective-permute-start.6 = (f32[512,128]{1,0:T(8,128)S(1)}, f32[512,128]{1,0:T(8,128)S(1)}, u32[]{:S(2)}, u32[]{:S(2)}) collective-permute-start(f32[512,128]{1,0:T(8,128)S(1)} %pad_maximum_fusion.1), channel_id=1, source_target_pairs={{0,6},{2,0},{4,2},{6,4},{1,7},{3,1},{5,3},{7,5},{8,14},{10,8},{12,... | collective-permute-start | bytes 786440 | tf_op jit(solution)/shard_map/ppermute | solution.py:451
  64.3 9.7 %index_logits.1 = (f32[512,128]{1,0:T(8,128)}, f32[1,128]{1,0:T(1,128)}, bf16[512,8192]{1,0:T(8,128)(2,1)}) custom-call(s32[16]{0:T(128)} %count_ref.11, s32[1]{0:T(128)} %bitcast.1.grp_ref, bf16[128,8192]{1,0:T(8,128)(2,1)} %refs_4_.5, bf16[512,128]{1,0:T(8,128)(2,1)} %ik_ref.1, bf16[128,64]{1,0:T(8,128)(2,1)} %copy.17.w_ref.refs_5_, s32[4,128]{1,0:T(4,128)} %refs_9_.1, ...), custom_call_target="tpu_custom_call" | custom-call | flops 1073741824 | bytes 10485760 | tf_op jit(solution)/shard_map/index_logits/pallas_call | solution.py:258
  74.0 1.5 %collective-permute-start.8 = (f32[1,128]{1,0:T(1,128)}, f32[1,128]{1,0:T(1,128)S(1)}, u32[]{:S(2)}, u32[]{:S(2)}) collective-permute-start(f32[1,128]{1,0:T(1,128)} %get-tuple-element.16.refs_3_), channel_id=1, source_target_pairs={{0,16},{8,24},{16,0},{24,8},{1,17},{9,25},{17,1},{25,9},{2,18},{10... | collective-permute-start | bytes 1544 | tf_op jit(solution)/shard_map/ppermute | solution.py:447
  75.9 13.3 %head_sums.3.refs_0_ = f32[512,128]{1,0:T(8,128)} custom-call(s32[16]{0:T(128)} %count_ref.11, s32[1]{0:T(128)} %bitcast.1.grp_ref, bf16[4,128,6144]{2,1,0:T(8,128)(2,1)} %refs_0_.5, bf16[512,4096]{1,0:T(8,128)(2,1)} %refs_1_.5, bf16[512,64]{1,0:T(8,128)(2,1)} %copy.14.rope_ref.refs_2_.refs_3_, s32[4,128]{1,0:T(4,128)} %refs_9_.1, s32[1,512]{1,0:T(1,128)} %bitcast.13, ...), custom_call_target="tpu_custom_call" | custom-call | flops 1073741824 | bytes 5767168 | tf_op jit(solution)/shard_map/head_sums/pallas_call | solution.py:177
  89.6 1.5 %collective-permute-start.12 = (f32[512,128]{1,0:T(8,128)S(1)}, f32[512,128]{1,0:T(8,128)S(1)}, u32[]{:S(2)}, u32[]{:S(2)}) collective-permute-start(f32[512,128]{1,0:T(8,128)S(1)} %convert_element_type.3.refs_2_), channel_id=1, source_target_pairs={{0,16},{8,24},{16,0},{24,8},{1,17},{9,25},{17,1},{25,9},{2,18},{10... | collective-permute-start | bytes 786440 | tf_op jit(solution)/shard_map/ppermute | solution.py:447
  91.9 9.8 %index_grad_key.1 = (f32[520,128]{1,0:T(8,128)}, f32[512,128]{1,0:T(8,128)}) custom-call(s32[16]{0:T(128)} %count_ref.11, s32[1]{0:T(128)} %bitcast.1.grp_ref, f32[512,128]{1,0:T(8,128)} %head_sums.3.refs_0_, f32[512,128]{1,0:T(8,128)} %copy-done.8, f32[512,128]{1,0:T(8,128)} %copy-done.7, f32[1,128]{1,0:T(1,128)} %get-tuple-element.16.refs_3_, ...), custom_call_target="tpu_custom_call" | custom-call | flops 1073741824 | bytes 10485760 | tf_op jit(solution)/shard_map/index_grad_key/pallas_call | solution.py:340
  101.7 0.9 slice.35
  102.6 3.6 %collective-permute-start.22 = (f32[160,128]{1,0:T(8,128)S(1)}, f32[160,128]{1,0:T(8,128)S(1)}, u32[]{:S(2)}, u32[]{:S(2)}) collective-permute-start(f32[160,128]{1,0:T(8,128)S(1)} %slice.35), channel_id=1, source_target_pairs={{0,6},{2,4},{4,2},{6,0},{1,7},{3,5},{5,3},{7,1},{8,14},{10,12},{12... | collective-permute-start | bytes 245768 | tf_op jit(solution)/shard_map/ppermute | solution.py:447
  106.2 0.9 fusion
  107.2 1.6 %collective-permute-start.16 = (f32[176,128]{1,0:T(8,128)S(1)}, f32[176,128]{1,0:T(8,128)S(1)}, u32[]{:S(2)}, u32[]{:S(2)}) collective-permute-start(f32[176,128]{1,0:T(8,128)S(1)} %get-tuple-element.27), channel_id=1, source_target_pairs={{0,1},{1,0},{2,3},{3,2},{4,5},{5,4},{6,7},{7,6},{8,9},{9,8},{10,11... | collective-permute-start | bytes 270344 | tf_op jit(solution)/shard_map/ppermute | solution.py:447
  108.9 0.9 slice_add_fusion.2
  109.8 2.0 %collective-permute-done.16 = f32[176,128]{1,0:T(8,128)S(1)} collective-permute-done((f32[176,128]{1,0:T(8,128)S(1)}, f32[176,128]{1,0:T(8,128)S(1)}, u32[]{:S(2)}, u32[]{:S(2)}) %collective-permute-start.16) | collective-permute-done | bytes 90144 | tf_op jit(solution)/shard_map/ppermute | solution.py:447
  112.4 0.9 collective-permute-done.19
  113.9 1.0 slice_add_fusion.4
  115.2 2.6 %collective-permute-done.23 = f32[160,128]{1,0:T(8,128)S(1)} collective-permute-done((f32[160,128]{1,0:T(8,128)S(1)}, f32[160,128]{1,0:T(8,128)S(1)}, u32[]{:S(2)}, u32[]{:S(2)}) %collective-permute-start.23) | collective-permute-done | bytes 81952 | tf_op jit(solution)/shard_map/ppermute | solution.py:447
  117.7 1.3 collective-permute-start.20
  119.7 4.5 %collective-permute-done.20 = f32[176,128]{1,0:T(8,128)S(1)} collective-permute-done((f32[176,128]{1,0:T(8,128)S(1)}, f32[176,128]{1,0:T(8,128)S(1)}, u32[]{:S(2)}, u32[]{:S(2)}) %collective-permute-start.20) | collective-permute-done | bytes 90144 | tf_op jit(solution)/shard_map/ppermute | solution.py:447
  124.9 2.0 %collective-permute-start.18 = (f32[176,128]{1,0:T(8,128)S(1)}, f32[176,128]{1,0:T(8,128)S(1)}, u32[]{:S(2)}, u32[]{:S(2)}) collective-permute-start(f32[176,128]{1,0:T(8,128)S(1)} %add.81), channel_id=1, source_target_pairs={{0,6},{2,4},{4,2},{6,0},{1,7},{3,5},{5,3},{7,1},{8,14},{10,12},{12... | collective-permute-start | bytes 270344 | tf_op jit(solution)/shard_map/ppermute | solution.py:447
  128.5 5.9 %index_grad_query.2 = (f32[128,2048]{1,0:T(8,128)}, f32[1,128]{1,0:T(1,128)}) custom-call(s32[1]{0:T(128)} %bitcast.slot_ref, f32[520,128]{1,0:T(8,128)} %get-tuple-element.19.refs_0_, f32[520,128]{1,0:T(8,128)} %copy-done.19, f32[512,128]{1,0:T(8,128)} %copy-done.9, f32[512,128]{1,0:T(8,128)} %copy-done.20, bf16[128,8192]{1,0:T(8,128)(2,1)} %refs_4_.5, ...), custom_call_target="tpu_custom_call" | custom-call | flops 1073741824 | bytes 3145728 | tf_op jit(solution)/shard_map/index_grad_query/pallas_call | solution.py:422
  136.0 5.1 %index_grad_query.3 = (f32[128,2048]{1,0:T(8,128)}, f32[1,128]{1,0:T(1,128)}) custom-call(s32[1]{0:T(128)} %bitcast.slot_ref, f32[520,128]{1,0:T(8,128)} %copy-done.3, f32[520,128]{1,0:T(8,128)} %copy-done.4, f32[512,128]{1,0:T(8,128)} %copy-done.5, f32[512,128]{1,0:T(8,128)} %copy-done.6, bf16[128,8192]{1,0:T(8,128)(2,1)} %refs_4_.5, ...), custom_call_target="tpu_custom_call" | custom-call | flops 1073741824 | bytes 3145728 | tf_op jit(solution)/shard_map/index_grad_query/pallas_call | solution.py:422
  141.0 1.1 add_bitcast_fusion
  (88 shorter events, 10.7 us)
Async XLA Ops:
  19.9 3.8 %collective-permute-start = (f32[32,512]{1,0:T(8,128)}, f32[32,512]{1,0:T(8,128)S(1)}, u32[]{:S(2)}, u32[]{:S(2)}) collective-permute-start(f32[32,512]{1,0:T(8,128)} %main_stats.1.refs_5_.refs_6_.refs_10_), channel_id=1, source_target_pairs={{0,8},{8,0},{16,24},{24,16},{1,9},{9,1},{17,25},{25,17},{2,10},{10... | collective-permute-start | bytes 196616 | tf_op jit(solution)/shard_map/ppermute | solution.py:447
  20.4 5.5 %collective-permute-start.1 = (f32[32,512]{1,0:T(8,128)}, f32[32,512]{1,0:T(8,128)S(1)}, u32[]{:S(2)}, u32[]{:S(2)}) collective-permute-start(f32[32,512]{1,0:T(8,128)} %main_stats.1.refs_5_.refs_6_.refs_10_), channel_id=1, source_target_pairs={{0,16},{8,24},{16,0},{24,8},{1,17},{9,25},{17,1},{25,9},{2,18},{10... | collective-permute-start | bytes 196616 | tf_op jit(solution)/shard_map/ppermute | solution.py:447
  22.8 4.2 %collective-permute-start.2 = (f32[32,512]{1,0:T(8,128)}, f32[32,512]{1,0:T(8,128)S(1)}, u32[]{:S(2)}, u32[]{:S(2)}) collective-permute-start(f32[32,512]{1,0:T(8,128)} %main_stats.1.refs_5_.refs_6_.refs_10_), channel_id=1, source_target_pairs={{0,24},{8,16},{16,8},{24,0},{1,25},{9,17},{17,9},{25,1},{2,26},{10... | collective-permute-start | bytes 196616 | tf_op jit(solution)/shard_map/ppermute | solution.py:447
  42.0 18.0 %collective-permute-start.3 = (f32[256,128]{1,0:T(8,128)S(1)}, f32[256,128]{1,0:T(8,128)S(1)}, u32[]{:S(2)}, u32[]{:S(2)}) collective-permute-start(f32[256,128]{1,0:T(8,128)S(1)} %get-tuple-element.32), channel_id=1, source_target_pairs={{0,2},{2,4},{4,6},{6,0},{1,3},{3,5},{5,7},{7,1},{8,10},{10,12},{12... | collective-permute-start | bytes 393224 | tf_op jit(solution)/shard_map/ppermute | solution.py:451
  43.6 19.9 %copy-start.11 = (bf16[128,64]{0,1:T(8,128)(2,1)S(1)}, bf16[128,64]{0,1:T(8,128)(2,1)}, u32[]{:S(2)}) copy-start(bf16[128,64]{0,1:T(8,128)(2,1)} %param.18) | copy-start | bytes 49156
  43.7 16.4 %collective-permute-start.5 = (f32[256,128]{1,0:T(8,128)S(1)}, f32[256,128]{1,0:T(8,128)S(1)}, u32[]{:S(2)}, u32[]{:S(2)}) collective-permute-start(f32[256,128]{1,0:T(8,128)S(1)} %get-tuple-element.31), channel_id=1, source_target_pairs={{0,6},{2,0},{4,2},{6,4},{1,7},{3,1},{5,3},{7,5},{8,14},{10,8},{12,... | collective-permute-start | bytes 393224 | tf_op jit(solution)/shard_map/ppermute | solution.py:451
  61.2 29.8 %collective-permute-start.6 = (f32[512,128]{1,0:T(8,128)S(1)}, f32[512,128]{1,0:T(8,128)S(1)}, u32[]{:S(2)}, u32[]{:S(2)}) collective-permute-start(f32[512,128]{1,0:T(8,128)S(1)} %pad_maximum_fusion.1), channel_id=1, source_target_pairs={{0,6},{2,0},{4,2},{6,4},{1,7},{3,1},{5,3},{7,5},{8,14},{10,8},{12,... | collective-permute-start | bytes 786440 | tf_op jit(solution)/shard_map/ppermute | solution.py:451
  63.1 28.0 %collective-permute-start.4 = (f32[512,128]{1,0:T(8,128)S(1)}, f32[512,128]{1,0:T(8,128)S(1)}, u32[]{:S(2)}, u32[]{:S(2)}) collective-permute-start(f32[512,128]{1,0:T(8,128)S(1)} %pad_maximum_fusion), channel_id=1, source_target_pairs={{0,2},{2,4},{4,6},{6,0},{1,3},{3,5},{5,7},{7,1},{8,10},{10,12},{12... | collective-permute-start | bytes 786440 | tf_op jit(solution)/shard_map/ppermute | solution.py:451
  74.0 15.2 %collective-permute-start.7 = (f32[1,128]{1,0:T(1,128)}, f32[1,128]{1,0:T(1,128)S(1)}, u32[]{:S(2)}, u32[]{:S(2)}) collective-permute-start(f32[1,128]{1,0:T(1,128)} %get-tuple-element.16.refs_3_), channel_id=1, source_target_pairs={{0,8},{8,0},{16,24},{24,16},{1,9},{9,1},{17,25},{25,17},{2,10},{10... | collective-permute-start | bytes 1544 | tf_op jit(solution)/shard_map/ppermute | solution.py:447
  74.0 15.6 %collective-permute-start.8 = (f32[1,128]{1,0:T(1,128)}, f32[1,128]{1,0:T(1,128)S(1)}, u32[]{:S(2)}, u32[]{:S(2)}) collective-permute-start(f32[1,128]{1,0:T(1,128)} %get-tuple-element.16.refs_3_), channel_id=1, source_target_pairs={{0,16},{8,24},{16,0},{24,8},{1,17},{9,25},{17,1},{25,9},{2,18},{10... | collective-permute-start | bytes 1544 | tf_op jit(solution)/shard_map/ppermute | solution.py:447
  75.5 15.6 %collective-permute-start.9 = (f32[1,128]{1,0:T(1,128)}, f32[1,128]{1,0:T(1,128)S(1)}, u32[]{:S(2)}, u32[]{:S(2)}) collective-permute-start(f32[1,128]{1,0:T(1,128)} %get-tuple-element.16.refs_3_), channel_id=1, source_target_pairs={{0,24},{8,16},{16,8},{24,0},{1,25},{9,17},{17,9},{25,1},{2,26},{10... | collective-permute-start | bytes 1544 | tf_op jit(solution)/shard_map/ppermute | solution.py:447
  75.9 25.8 %copy-start.9 = (f32[512,128]{1,0:T(8,128)}, f32[512,128]{1,0:T(8,128)S(1)}, u32[]{:S(2)}) copy-start(f32[512,128]{1,0:T(8,128)S(1)} %convert_element_type.3.refs_2_) | copy-start | bytes 786436
  89.2 37.6 %collective-permute-start.15 = (f32[512,128]{1,0:T(8,128)S(1)}, f32[512,128]{1,0:T(8,128)S(1)}, u32[]{:S(2)}, u32[]{:S(2)}) collective-permute-start(f32[512,128]{1,0:T(8,128)S(1)} %convert_element_type.3.refs_2_), channel_id=1, source_target_pairs={{0,8},{8,0},{16,24},{24,16},{1,9},{9,1},{17,25},{25,17},{2,10},{10... | collective-permute-start | bytes 786440 | tf_op jit(solution)/shard_map/ppermute | solution.py:447
  89.6 25.3 %collective-permute-start.12 = (f32[512,128]{1,0:T(8,128)S(1)}, f32[512,128]{1,0:T(8,128)S(1)}, u32[]{:S(2)}, u32[]{:S(2)}) collective-permute-start(f32[512,128]{1,0:T(8,128)S(1)} %convert_element_type.3.refs_2_), channel_id=1, source_target_pairs={{0,16},{8,24},{16,0},{24,8},{1,17},{9,25},{17,1},{25,9},{2,18},{10... | collective-permute-start | bytes 786440 | tf_op jit(solution)/shard_map/ppermute | solution.py:447
  101.7 39.3 %copy-start.12 = (f32[1,128]{1,0:T(1,128)S(1)}, f32[1,128]{1,0:T(1,128)}, u32[]{:S(2)}) copy-start(f32[1,128]{1,0:T(1,128)} %get-tuple-element.16.refs_3_) | copy-start | bytes 1540
  101.7 39.3 %copy-start.14 = (f32[1,128]{1,0:T(1,128)S(1)}, f32[1,128]{1,0:T(1,128)}, u32[]{:S(2)}) copy-start(f32[1,128]{1,0:T(1,128)} %copy-done.13) | copy-start | bytes 1540
  101.7 39.3 %copy-start.16 = (f32[1,128]{1,0:T(1,128)S(1)}, f32[1,128]{1,0:T(1,128)}, u32[]{:S(2)}) copy-start(f32[1,128]{1,0:T(1,128)} %copy-done.15) | copy-start | bytes 1540
  101.7 39.3 %copy-start.18 = (f32[1,128]{1,0:T(1,128)S(1)}, f32[1,128]{1,0:T(1,128)}, u32[]{:S(2)}) copy-start(f32[1,128]{1,0:T(1,128)} %copy-done.17) | copy-start | bytes 1540
  102.6 6.2 %collective-permute-start.22 = (f32[160,128]{1,0:T(8,128)S(1)}, f32[160,128]{1,0:T(8,128)S(1)}, u32[]{:S(2)}, u32[]{:S(2)}) collective-permute-start(f32[160,128]{1,0:T(8,128)S(1)} %slice.35), channel_id=1, source_target_pairs={{0,6},{2,4},{4,2},{6,0},{1,7},{3,5},{5,3},{7,1},{8,14},{10,12},{12... | collective-permute-start | bytes 245768 | tf_op jit(solution)/shard_map/ppermute | solution.py:447
  107.2 4.6 %collective-permute-start.16 = (f32[176,128]{1,0:T(8,128)S(1)}, f32[176,128]{1,0:T(8,128)S(1)}, u32[]{:S(2)}, u32[]{:S(2)}) collective-permute-start(f32[176,128]{1,0:T(8,128)S(1)} %get-tuple-element.27), channel_id=1, source_target_pairs={{0,1},{1,0},{2,3},{3,2},{4,5},{5,4},{6,7},{7,6},{8,9},{9,8},{10,11... | collective-permute-start | bytes 270344 | tf_op jit(solution)/shard_map/ppermute | solution.py:447
  108.8 4.5 %collective-permute-start.19 = (f32[176,128]{1,0:T(8,128)S(1)}, f32[176,128]{1,0:T(8,128)S(1)}, u32[]{:S(2)}, u32[]{:S(2)}) collective-permute-start(f32[176,128]{1,0:T(8,128)S(1)} %get-tuple-element.28), channel_id=1, source_target_pairs={{0,2},{2,0},{4,6},{6,4},{1,3},{3,1},{5,7},{7,5},{8,10},{10,8},{12,... | collective-permute-start | bytes 270344 | tf_op jit(solution)/shard_map/ppermute | solution.py:447
  108.9 18.9 %collective-permute-start.14 = (f32[520,128]{1,0:T(8,128)}, f32[520,128]{1,0:T(8,128)S(1)}, u32[]{:S(2)}, u32[]{:S(2)}) collective-permute-start(f32[520,128]{1,0:T(8,128)} %get-tuple-element.19.refs_0_), channel_id=1, source_target_pairs={{0,8},{8,0},{16,24},{24,16},{1,9},{9,1},{17,25},{25,17},{2,10},{10... | collective-permute-start | bytes 798728 | tf_op jit(solution)/shard_map/ppermute | solution.py:447
  111.8 7.9 %collective-permute-start.10 = (f32[520,128]{1,0:T(8,128)}, f32[520,128]{1,0:T(8,128)S(1)}, u32[]{:S(2)}, u32[]{:S(2)}) collective-permute-start(f32[520,128]{1,0:T(8,128)} %get-tuple-element.19.refs_0_), channel_id=1, source_target_pairs={{0,16},{8,24},{16,0},{24,8},{1,17},{9,25},{17,1},{25,9},{2,18},{10... | collective-permute-start | bytes 798728 | tf_op jit(solution)/shard_map/ppermute | solution.py:447
  113.3 4.4 %collective-permute-start.23 = (f32[160,128]{1,0:T(8,128)S(1)}, f32[160,128]{1,0:T(8,128)S(1)}, u32[]{:S(2)}, u32[]{:S(2)}) collective-permute-start(f32[160,128]{1,0:T(8,128)S(1)} %slice_add_fusion.2), channel_id=1, source_target_pairs={{0,1},{1,0},{2,3},{3,2},{4,5},{5,4},{6,7},{7,6},{8,9},{9,8},{10,11... | collective-permute-start | bytes 245768 | tf_op jit(solution)/shard_map/ppermute | solution.py:447
  114.9 20.3 %copy-start.5 = (f32[512,128]{1,0:T(8,128)}, f32[512,128]{1,0:T(8,128)S(1)}, u32[]{:S(2)}) copy-start(f32[512,128]{1,0:T(8,128)S(1)} %collective-permute-done.12.refs_2_) | copy-start | bytes 786436
  114.9 4.6 %collective-permute-start.17 = (f32[176,128]{1,0:T(8,128)S(1)}, f32[176,128]{1,0:T(8,128)S(1)}, u32[]{:S(2)}, u32[]{:S(2)}) collective-permute-start(f32[176,128]{1,0:T(8,128)S(1)} %get-tuple-element.25), channel_id=1, source_target_pairs={{0,2},{2,0},{4,6},{6,4},{1,3},{3,1},{5,7},{7,5},{8,10},{10,8},{12,... | collective-permute-start | bytes 270344 | tf_op jit(solution)/shard_map/ppermute | solution.py:447
  117.7 6.4 %collective-permute-start.20 = (f32[176,128]{1,0:T(8,128)S(1)}, f32[176,128]{1,0:T(8,128)S(1)}, u32[]{:S(2)}, u32[]{:S(2)}) collective-permute-start(f32[176,128]{1,0:T(8,128)S(1)} %get-tuple-element.26), channel_id=1, source_target_pairs={{0,6},{2,4},{4,2},{6,0},{1,7},{3,5},{5,3},{7,1},{8,14},{10,12},{12... | collective-permute-start | bytes 270344 | tf_op jit(solution)/shard_map/ppermute | solution.py:447
  119.5 5.4 %collective-permute-start.24 = (f32[160,128]{1,0:T(8,128)S(1)}, f32[160,128]{1,0:T(8,128)S(1)}, u32[]{:S(2)}, u32[]{:S(2)}) collective-permute-start(f32[160,128]{1,0:T(8,128)S(1)} %add.87), channel_id=1, source_target_pairs={{0,2},{2,0},{4,6},{6,4},{1,3},{3,1},{5,7},{7,5},{8,10},{10,8},{12,... | collective-permute-start | bytes 245768 | tf_op jit(solution)/shard_map/ppermute | solution.py:447
  119.7 15.5 %collective-permute-start.11 = (f32[520,128]{1,0:T(8,128)S(1)}, f32[520,128]{1,0:T(8,128)S(1)}, u32[]{:S(2)}, u32[]{:S(2)}) collective-permute-start(f32[520,128]{1,0:T(8,128)S(1)} %collective-permute-done.10.refs_0_), channel_id=1, source_target_pairs={{0,8},{8,0},{16,24},{24,16},{1,9},{9,1},{17,25},{25,17},{2,10},{10... | collective-permute-start | bytes 798728 | tf_op jit(solution)/shard_map/ppermute | solution.py:447
  124.2 11.0 %collective-permute-start.13 = (f32[512,128]{1,0:T(8,128)S(1)}, f32[512,128]{1,0:T(8,128)S(1)}, u32[]{:S(2)}, u32[]{:S(2)}) collective-permute-start(f32[512,128]{1,0:T(8,128)S(1)} %collective-permute-done.12.refs_2_), channel_id=1, source_target_pairs={{0,8},{8,0},{16,24},{24,16},{1,9},{9,1},{17,25},{25,17},{2,10},{10... | collective-permute-start | bytes 786440 | tf_op jit(solution)/shard_map/ppermute | solution.py:447
  124.9 9.5 %collective-permute-start.18 = (f32[176,128]{1,0:T(8,128)S(1)}, f32[176,128]{1,0:T(8,128)S(1)}, u32[]{:S(2)}, u32[]{:S(2)}) collective-permute-start(f32[176,128]{1,0:T(8,128)S(1)} %add.81), channel_id=1, source_target_pairs={{0,6},{2,4},{4,2},{6,0},{1,7},{3,5},{5,3},{7,1},{8,14},{10,12},{12... | collective-permute-start | bytes 270344 | tf_op jit(solution)/shard_map/ppermute | solution.py:447
  126.9 7.5 %collective-permute-start.21 = (f32[176,128]{1,0:T(8,128)S(1)}, f32[176,128]{1,0:T(8,128)S(1)}, u32[]{:S(2)}, u32[]{:S(2)}) collective-permute-start(f32[176,128]{1,0:T(8,128)S(1)} %add.84), channel_id=1, source_target_pairs={{0,1},{1,0},{2,3},{3,2},{4,5},{5,4},{6,7},{7,6},{8,9},{9,8},{10,11... | collective-permute-start | bytes 270344 | tf_op jit(solution)/shard_map/ppermute | solution.py:447
  (14 other events, 45.0 us)

commit v2 on v1

v2 whole, which is shorter than its diff:
```python
import functools
import math
import jax
import jax.numpy as jnp
from jax import lax
from jax.experimental import pallas as pl
from jax.experimental.pallas import tpu as pltpu
from jax.sharding import PartitionSpec as P

H = 128
DNOPE = 128
DROPE = 64
IH = 64
ID = 128
KBLOCK = 32
DQK = 192
LANES = 128
PAIR = 2 * DQK
NEG = -1e30
BIG = 2**30
LOG2E = math.log2(math.e)
SCALE_MAIN = DQK ** (-0.5) * LOG2E
SCALE_INDEX = ID ** (-0.5)
VMEM_LIMIT = 32 * 1024 * 1024

f32 = jnp.float32
bf16 = jnp.bfloat16
IN_VMEM = pl.BlockSpec(memory_space=pltpu.VMEM)


def dot_nt(a, b):
    return lax.dot_general(a, b, (((1,), (1,)), ((), ())), preferred_element_type=f32)


def dot_nn(a, b):
    return lax.dot_general(a, b, (((1,), (0,)), ((), ())), preferred_element_type=f32)


def params():
    return pltpu.CompilerParams(
        dimension_semantics=("arbitrary",), vmem_limit_bytes=VMEM_LIMIT
    )


def cost(flops, bytes_accessed, transcendentals=0):
    return pl.CostEstimate(
        flops=int(flops), bytes_accessed=int(bytes_accessed), transcendentals=int(transcendentals)
    )


def combine_lse(parts):
    if len(parts) == 1:
        return parts[0]
    top = functools.reduce(jnp.maximum, parts)
    return top + jnp.log2(functools.reduce(jnp.add, [jnp.exp2(p - top) for p in parts]))


def key_limit_column(count_ref, pos_ref, keys):
    blocks = keys // KBLOCK
    lane = lax.broadcasted_iota(jnp.int32, (1, keys), 1)
    block = lane // KBLOCK
    limit = jnp.zeros((1, keys), jnp.int32)
    for b in range(blocks):
        limit = jnp.where(block == b, count_ref[b], limit)
    live = (lane % KBLOCK) < limit
    row = jnp.where(live, pos_ref[...], BIG)
    return jnp.transpose(jnp.broadcast_to(row, (8, keys)))[:, :1]


def rope_setup(rope_t_ref, even_ref, odd_ref):
    rope = jnp.transpose(rope_t_ref[...].astype(f32)).astype(bf16)
    zero = jnp.zeros_like(rope)
    even_ref[...] = jnp.concatenate([rope, zero], axis=1)
    odd_ref[...] = jnp.concatenate([zero, rope], axis=1)


def main_keys(nope, parity, even_ref, odd_ref):
    if parity == 0:
        return jnp.concatenate([nope, even_ref[...]], axis=1)
    turned = jnp.concatenate([nope[:, DROPE:], nope[:, :DROPE]], axis=1)
    low = lax.broadcasted_iota(jnp.int32, turned.shape, 1) < DROPE
    first = jnp.where(low, jnp.zeros_like(turned), turned)
    second = jnp.where(low, turned, odd_ref[...])
    return jnp.concatenate([first, second], axis=1)


def stats_kernel(per, count_ref, q_ref, kn_ref, rope_ref, qpos_ref, kpos_ref, lse_ref,
                 bias_ref, even_ref, odd_ref, s0_ref, s1_ref):
    step = pl.program_id(0)
    keys = kn_ref.shape[0]
    groups, rows = q_ref.shape[0], q_ref.shape[1]

    @pl.when(step == 0)
    def _():
        rope_setup(rope_ref, even_ref, odd_ref)
        column = key_limit_column(count_ref, kpos_ref, keys)
        for g in range(groups):
            valid = column <= qpos_ref[g : g + 1, :]
            bias_ref[:, g * rows : (g + 1) * rows] = jnp.where(valid, 0.0, NEG)

    bufs = (s0_ref, s1_ref)
    units = [(p, a, c) for p in range(per) for a in range(2) for c in range(groups // 2)]
    tops = {}
    kept = {}

    def forward(u):
        p, a, c = units[u]
        if c == 0:
            lanes = slice((2 * p + a) * DNOPE, (2 * p + a + 1) * DNOPE)
            kept[0] = main_keys(kn_ref[:, lanes], a, even_ref, odd_ref)
        start = p * PAIR + a * LANES
        q = q_ref[2 * c : 2 * c + 2, :, start : start + 2 * LANES].reshape(2 * rows, 2 * LANES)
        cols = slice(2 * c * rows, (2 * c + 2) * rows)
        s = dot_nt(kept[0], q) * SCALE_MAIN + bias_ref[:, cols]
        bufs[u % 2][...] = s
        tops[u] = jnp.max(s, axis=0, keepdims=True)

    def finish(u):
        p, a, c = units[u]
        cols = slice(2 * c * rows, (2 * c + 2) * rows)
        total = jnp.sum(jnp.exp2(bufs[u % 2][...] - tops[u]), axis=0, keepdims=True)
        lse_ref[pl.ds(2 * per * step + 2 * p + a, 1), cols] = tops[u] + jnp.log2(total)

    forward(0)
    for u in range(1, len(units)):
        forward(u)
        finish(u - 1)
    finish(len(units) - 1)


def main_stats(main_query, key_nope, rope_t, query_pos, key_pos, key_count):
    groups, rows, width = main_query.shape
    heads = width // DQK
    keys = key_nope.shape[0]
    total = groups * rows
    per = 2
    return pl.pallas_call(
        functools.partial(stats_kernel, per),
        grid_spec=pltpu.PrefetchScalarGridSpec(
            num_scalar_prefetch=1,
            grid=(heads // (2 * per),),
            in_specs=[
                pl.BlockSpec((groups, rows, per * PAIR), lambda i, c: (0, 0, i)),
                pl.BlockSpec((keys, per * 2 * DNOPE), lambda i, c: (0, i)),
                IN_VMEM,
                IN_VMEM,
                IN_VMEM,
            ],
            out_specs=IN_VMEM,
            scratch_shapes=[
                pltpu.VMEM((keys, total), f32),
                pltpu.VMEM((keys, LANES), bf16),
                pltpu.VMEM((keys, LANES), bf16),
                pltpu.VMEM((keys, 2 * rows), f32),
                pltpu.VMEM((keys, 2 * rows), f32),
            ],
        ),
        out_shape=jax.ShapeDtypeStruct((heads, total), f32),
        compiler_params=params(),
        cost_estimate=cost(
            heads * total * keys * 512, main_query.size * 2 + key_nope.size * 2, heads * total * keys
        ),
        name="main_stats",
    )(key_count, main_query, key_nope, rope_t, query_pos, key_pos)


def target_kernel(n_lse, n_groups, per, count_ref, grp_ref, *refs):
    q_refs = refs[:n_groups]
    kn_ref, rope_ref, qpos_ref, kpos_ref = refs[n_groups : n_groups + 4]
    lse_refs = refs[n_groups + 4 : n_groups + 4 + n_lse]
    out_refs = refs[n_groups + 4 + n_lse : -3]
    glob_ref, even_ref, odd_ref = refs[-3:]
    step = pl.program_id(0)
    keys = kn_ref.shape[0]
    rows = q_refs[0].shape[1]

    @pl.when(step == 0)
    def _():
        rope_setup(rope_ref, even_ref, odd_ref)
        for g in range(n_groups):
            at = pl.ds(pl.multiple_of(grp_ref[g] * rows, rows), rows)
            glob_ref[:, g * rows : (g + 1) * rows] = combine_lse([r[:, at] for r in lse_refs])
            out_refs[g][...] = jnp.zeros_like(out_refs[g])

    for p in range(per):
        acc = None
        for a in range(2):
            lanes = slice((2 * p + a) * DNOPE, (2 * p + a + 1) * DNOPE)
            kk = main_keys(kn_ref[:, lanes], a, even_ref, odd_ref)
            start = p * PAIR + a * LANES
            qs = [r[0, :, start : start + 2 * LANES] for r in q_refs]
            q = qs[0] if n_groups == 1 else jnp.concatenate(qs, axis=0)
            lse = glob_ref[pl.ds(2 * per * step + 2 * p + a, 1), :]
            e = jnp.exp2(dot_nt(kk, q) * SCALE_MAIN - lse)
            acc = e if acc is None else acc + e
        for g in range(n_groups):
            out_refs[g][...] += acc[:, g * rows : (g + 1) * rows]

    @pl.when(step == pl.num_programs(0) - 1)
    def _():
        column = key_limit_column(count_ref, kpos_ref, keys)
        for g in range(n_groups):
            valid = column <= qpos_ref[pl.ds(grp_ref[g], 1), :]
            out_refs[g][...] = jnp.where(valid, out_refs[g][...], 0.0)


def head_sums(group_ids, main_query, key_nope, rope_t, query_pos, key_pos, key_count, lses):
    groups, rows, width = main_query.shape
    heads = width // DQK
    keys = key_nope.shape[0]
    n = len(group_ids)
    per = 4 // n

    def group_q(g):
        return pl.BlockSpec((1, rows, per * PAIR), lambda i, c, grp: (grp[g], 0, i))

    return pl.pallas_call(
        functools.partial(target_kernel, len(lses), n, per),
        grid_spec=pltpu.PrefetchScalarGridSpec(
            num_scalar_prefetch=2,
            grid=(heads // (2 * per),),
            in_specs=[group_q(g) for g in range(n)]
            + [pl.BlockSpec((keys, per * 2 * DNOPE), lambda i, c, grp: (0, i))]
            + [IN_VMEM] * (3 + len(lses)),
            out_specs=[IN_VMEM] * n,
            scratch_shapes=[
                pltpu.VMEM((heads, n * rows), f32),
                pltpu.VMEM((keys, LANES), bf16),
                pltpu.VMEM((keys, LANES), bf16),
            ],
        ),
        out_shape=[jax.ShapeDtypeStruct((keys, rows), f32)] * n,
        compiler_params=params(),
        cost_estimate=cost(
            heads * n * rows * keys * 512, main_query.size * n // 2 + key_nope.size * 2,
            heads * n * rows * keys,
        ),
        name="head_sums",
    )(
        key_count, jnp.stack(group_ids), *([main_query] * n), key_nope, rope_t, query_pos,
        key_pos, *lses,
    )


def logits_kernel(count_ref, grp_ref, iq_ref, ik_ref, wt_ref, qpos_ref, kpos_ref,
                  logits_ref, lse_ref, wm_ref, w_ref):
    step = pl.program_id(0)
    keys = ik_ref.shape[0]
    rows = iq_ref.shape[0]
    per = iq_ref.shape[1] // ID

    @pl.when(step == 0)
    def _():
        w_ref[...] = wt_ref[...].astype(f32)
        logits_ref[...] = jnp.zeros_like(logits_ref)

    for p in range(per // 2):
        q = jnp.concatenate(
            [iq_ref[:, (2 * p + a) * ID : (2 * p + a + 1) * ID] for a in range(2)], axis=0
        )
        z = dot_nt(ik_ref[...], q)
        w = jnp.concatenate(
            [w_ref[pl.ds(step * per + 2 * p + a, 1), :] for a in range(2)], axis=1
        )
        masked = jnp.where(z > 0, w, 0.0)
        wm_ref[:, 2 * p * rows : (2 * p + 2) * rows] = masked.astype(bf16)
        r = z * masked
        logits_ref[...] += r[:, :rows] + r[:, rows:]

    @pl.when(step == pl.num_programs(0) - 1)
    def _():
        logits = logits_ref[...] * SCALE_INDEX
        logits_ref[...] = logits
        column = key_limit_column(count_ref, kpos_ref, keys)
        valid = column <= qpos_ref[pl.ds(grp_ref[0], 1), :]
        s = jnp.where(valid, logits * LOG2E, NEG)
        top = jnp.max(s, axis=0, keepdims=True)
        lse_ref[...] = top + jnp.log2(jnp.sum(jnp.exp2(s - top), axis=0, keepdims=True))


def index_logits(group_id, index_query, index_key, weight_t, query_pos, key_pos, key_count):
    rows, width = index_query.shape
    keys = index_key.shape[0]
    per = 16
    steps = width // (per * ID)
    return pl.pallas_call(
        logits_kernel,
        grid_spec=pltpu.PrefetchScalarGridSpec(
            num_scalar_prefetch=2,
            grid=(steps,),
            in_specs=[
                pl.BlockSpec((rows, per * ID), lambda i, c, grp: (0, i)),
                IN_VMEM,
                IN_VMEM,
                IN_VMEM,
                IN_VMEM,
            ],
            out_specs=[
                IN_VMEM,
                IN_VMEM,
                pl.BlockSpec((keys, per * rows), lambda i, c, grp: (0, i)),
            ],
            scratch_shapes=[pltpu.VMEM((width // ID, rows), f32)],
        ),
        out_shape=[
            jax.ShapeDtypeStruct((keys, rows), f32),
            jax.ShapeDtypeStruct((1, rows), f32),
            jax.ShapeDtypeStruct((keys, (width // ID) * rows), bf16),
        ],
        compiler_params=params(),
        cost_estimate=cost(2 * keys * rows * width, rows * width * 2 + keys * rows * width // ID * 2),
        name="index_logits",
    )(key_count, group_id.reshape(1), index_query, index_key, weight_t, query_pos, key_pos)


def grad_key_kernel(n_parts, n_lse, count_ref, grp_ref, *refs):
    parts = refs[:n_parts]
    lses = refs[n_parts : n_parts + n_lse]
    (logits_ref, cot_ref, qpos_ref, kpos_ref, wm_ref, iq_ref,
     sg_ref, gk_ref) = refs[n_parts + n_lse :]
    step = pl.program_id(0)
    keys, rows = logits_ref.shape
    per = iq_ref.shape[1] // ID

    @pl.when(step == 0)
    def _():
        column = key_limit_column(count_ref, kpos_ref, keys)
        valid = column <= qpos_ref[pl.ds(grp_ref[0], 1), :]
        target = functools.reduce(jnp.add, [p[...] for p in parts]) * (1.0 / H)
        logits = logits_ref[...]
        lse2 = combine_lse([r[...] for r in lses])
        qprob = jnp.where(valid, jnp.exp2(logits * LOG2E - lse2), 0.0)
        sg_ref[:keys, :] = SCALE_INDEX * (cot_ref[...] * (qprob - target))
        live = target > 0
        terms = jnp.where(live, target * (jnp.log(jnp.where(live, target, 1.0)) - logits), 0.0)
        kl = jnp.sum(terms, axis=0, keepdims=True)
        sg_ref[keys:, :] = jnp.broadcast_to(kl, (8, rows))
        gk_ref[...] = jnp.zeros_like(gk_ref)

    for p in range(per // 2):
        dz = []
        qs = []
        for a in range(2):
            j = 2 * p + a
            wm = wm_ref[:, j * rows : (j + 1) * rows].astype(f32)
            dz.append((sg_ref[:keys, :] * wm).astype(bf16))
            qs.append(iq_ref[:, j * ID : (j + 1) * ID])
        gk_ref[...] += dot_nn(jnp.concatenate(dz, axis=1), jnp.concatenate(qs, axis=0))


def index_grad_key(group_id, parts, lses, logits, cotangent, wm, index_query,
                   query_pos, key_pos, key_count):
    rows, width = index_query.shape
    keys = logits.shape[0]
    per = 16
    steps = width // (per * ID)
    return pl.pallas_call(
        functools.partial(grad_key_kernel, len(parts), len(lses)),
        grid_spec=pltpu.PrefetchScalarGridSpec(
            num_scalar_prefetch=2,
            grid=(steps,),
            in_specs=[IN_VMEM] * (len(parts) + len(lses) + 4)
            + [
                pl.BlockSpec((keys, per * rows), lambda i, c, grp: (0, i)),
                pl.BlockSpec((rows, per * ID), lambda i, c, grp: (0, i)),
            ],
            out_specs=[IN_VMEM, IN_VMEM],
        ),
        out_shape=[
            jax.ShapeDtypeStruct((keys + 8, rows), f32),
            jax.ShapeDtypeStruct((keys, ID), f32),
        ],
        compiler_params=params(),
        cost_estimate=cost(2 * keys * rows * width, rows * width * 2 + keys * rows * width // ID * 2),
        name="index_grad_key",
    )(key_count, group_id.reshape(1), *parts, *lses, logits, cotangent, query_pos, key_pos, wm,
      index_query)


def grad_query_kernel(n_shards, first, n_lse, slot_ref, *refs):
    sgs = refs[:n_shards]
    iks = refs[n_shards : 2 * n_shards]
    iq_ref, w_ref = refs[2 * n_shards : 2 * n_shards + 2]
    rest = refs[2 * n_shards + 2 :]
    lses = rest[:n_lse]
    rest = rest[n_lse:]
    if first:
        gq_ref, kl_ref, ws_ref = rest
    else:
        gq_in_ref, kl_in_ref, gq_ref, kl_ref, ws_ref = rest
    rows = iq_ref.shape[0]
    heads = iq_ref.shape[1] // ID
    keys = iks[0].shape[0]
    ws_ref[...] = w_ref[...].astype(f32)
    mine = ws_ref[pl.ds(slot_ref[0] * heads, heads), :]
    ws = jnp.transpose(jnp.concatenate([mine, jnp.zeros((LANES - heads, rows), f32)], axis=0))
    kl = functools.reduce(jnp.add, [s[keys : keys + 1, :] for s in sgs])
    kl = kl if first else kl_in_ref[...] + kl
    if n_lse:
        kl = kl + combine_lse([r[...] for r in lses]) * (1.0 / LOG2E)
    kl_ref[...] = kl
    unit = min(heads, 4)
    iks = [ref[...].astype(bf16) for ref in iks]
    sgts = [jnp.transpose(ref[:keys, :]) for ref in sgs]
    for start in range(0, heads, unit):
        js = range(start, start + unit)
        iq = jnp.concatenate([iq_ref[:, j * ID : (j + 1) * ID] for j in js], axis=0)
        out = None
        for ik, sgt in zip(iks, sgts):
            z = dot_nt(iq, ik)
            dz = jnp.concatenate(
                [
                    jnp.where(z[i * rows : (i + 1) * rows] > 0, sgt * ws[:, j : j + 1], 0.0).astype(bf16)
                    for i, j in enumerate(js)
                ],
                axis=0,
            )
            g = dot_nn(dz, ik)
            out = g if out is None else out + g
        for i, j in enumerate(js):
            cols = slice(j * ID, (j + 1) * ID)
            g = out[i * rows : (i + 1) * rows]
            gq_ref[:, cols] = g if first else gq_in_ref[:, cols] + g


def index_grad_query(slot, n_slots, sgs, iks, index_query, weight_t, lses, carry):
    rows, width = index_query.shape
    heads = width // ID
    mine = width // n_slots
    keys = iks[0].shape[0]
    first = carry is None
    carried = [] if first else list(carry)
    n = len(sgs)
    return pl.pallas_call(
        functools.partial(grad_query_kernel, n, first, len(lses)),
        grid_spec=pltpu.PrefetchScalarGridSpec(
            num_scalar_prefetch=1,
            grid=(1,),
            in_specs=[IN_VMEM] * (2 * n)
            + [pl.BlockSpec((rows, mine), lambda i, s: (0, s[0]))]
            + [IN_VMEM] * (1 + len(lses) + len(carried)),
            out_specs=[IN_VMEM, IN_VMEM],
            scratch_shapes=[pltpu.VMEM((heads, rows), f32)],
        ),
        out_shape=[
            jax.ShapeDtypeStruct((rows, mine), f32),
            jax.ShapeDtypeStruct((1, rows), f32),
        ],
        compiler_params=params(),
        cost_estimate=cost(4 * n * keys * rows * mine, n * (keys * ID * 8) + rows * mine * 8),
        name="index_grad_query",
    )(slot.reshape(1), *sgs, *iks, index_query, weight_t, *lses, *carried)


def swap(value, axis, mask, size):
    return lax.ppermute(value, axis, [(i, i ^ mask) for i in range(size)])


def rotate(value, axis, by, size):
    return lax.ppermute(value, axis, [(i, (i + by) % size) for i in range(size)])


def summed_copies(value, n_head, n_query):
    steps = [("query", m, n_query) for m in (1 << b for b in range(n_query.bit_length() - 1))]
    steps += [("head", (2 << b) - 1, n_head) for b in range(n_head.bit_length() - 1)]
    count = len(steps)
    if count == 0:
        return value
    rows = value.shape[0]
    unit = -(-rows // (8 * count)) * 8
    pieces = [value[i * unit : min((i + 1) * unit, rows)] for i in range(count)]
    pieces = [p for p in pieces if p.shape[0]]
    for s in range(count):
        moved = [swap(p, *steps[(i + s) % count]) for i, p in enumerate(pieces)]
        pieces = [p + m for p, m in zip(pieces, moved)]
    return jnp.concatenate(pieces, axis=0)


def body(n_key, n_head, n_query, main_query, key_nope, key_rope, query_pos, key_pos, key_count,
         index_query, index_key, index_weight, row_cotangent):
    groups, rows, _ = main_query.shape
    keys = key_nope.shape[0]
    z = lax.axis_index("head")
    slot = lax.axis_index("key")
    key_row = key_pos.reshape(1, keys)
    main = (main_query, key_nope, key_rope.T, query_pos, key_row, key_count)
    weight_t = index_weight.T
    cotangent = row_cotangent.reshape(1, rows)

    def gathered(value):
        if n_key == 4:
            far = swap(value, "key", 2, n_key)
            return [value, swap(value, "key", 1, n_key), far, swap(far, "key", 1, n_key)]
        return list(lax.all_gather(value, "key"))

    iks = gathered(index_key.astype(f32))
    lse = main_stats(*main)
    lses = [lse] + [swap(lse, "key", m, n_key) for m in (1, 2, 3)] if n_key == 4 else [
        combine_lse(gathered(lse))
    ]
    logits, index_lse, wm = index_logits(
        z, index_query, index_key, weight_t, query_pos, key_row, key_count
    )
    index_lses = gathered(index_lse) if n_key == 4 else [combine_lse(gathered(index_lse))]

    if n_head == 4 and groups == 4:
        across = head_sums([(z + 2) % 4], *main, lses)[0]
        half = keys // 2
        low = rotate(across[:half], "head", 1, 4)
        high = rotate(across[half:], "head", 3, 4)
        up, down = head_sums([(z + 1) % 4, (z + 3) % 4], *main, lses)
        up = jnp.concatenate([up[:half] + low, up[half:]], axis=0)
        down = jnp.concatenate([down[:half], down[half:] + high], axis=0)
        from_below = rotate(up, "head", 1, 4)
        from_above = rotate(down, "head", 3, 4)
        own = head_sums([z], *main, lses)[0]
        parts = [own, from_below, from_above]
    else:
        tiles = jnp.stack([head_sums([jnp.int32(g)], *main, lses)[0] for g in range(groups)])
        parts = [lax.psum_scatter(tiles, "head", scatter_dimension=0, tiled=True)[0]]

    sg, grad_key = index_grad_key(
        z, parts, index_lses, logits, cotangent, wm, index_query, query_pos, key_row, key_count
    )
    grad_key = summed_copies(grad_key, n_head, n_query)
    sgs = gathered(sg)
    carry = None
    for lo in range(0, n_key, 2):
        last = lo + 2 >= n_key
        carry = index_grad_query(
            slot, n_key, sgs[lo : lo + 2], iks[lo : lo + 2], index_query, weight_t,
            index_lses if last else [], carry,
        )
    grad_query, kl = carry
    return kl.reshape(rows), grad_query, grad_key


def solution(mesh):
    return jax.shard_map(
        functools.partial(body, mesh.shape["key"], mesh.shape["head"], mesh.shape["query"]),
        mesh=mesh,
        in_specs=(
            P(None, "query", "head"),
            P("key", "head"),
            P("key", None),
            P(None, "query"),
            P("key"),
            P("key"),
            P(("head", "query"), None),
            P("key", None),
            P(("head", "query"), None),
            P(("head", "query")),
        ),
        out_specs=(P(("head", "query")), P(("head", "query"), "key"), P("key", None)),
        check_vma=False,
    )
```

time: 144 us -> 112 us (0.78)
  Pallas kernels: 88.9 us -> 43.5 us
  local copies, waits for them, and re-layouts: 8.04 us -> 19.6 us
  starting transfers between devices: 24 us -> 26.6 us
    pallas_call x6, Pallas kernels: 69.4 us -> 33.9 us  [the longest x3 14.8 us: head_sums(): pl.pallas_call(functools.partial(target_kernel, len(lses), n, per), grid_...]
    unnamed x44, local copies, waits for them, and re-layouts: 5.21 us -> 19.5 us
    pallas_call x1, Pallas kernels: 9.81 us -> 4.52 us  [index_grad_key(): pl.pallas_call(functools.partial(grad_key_kernel, len(parts), len(lses)),...]
    pallas_call x1, Pallas kernels: 9.73 us -> 5.06 us  [index_logits(): pl.pallas_call(logits_kernel, grid_spec=pltpu.PrefetchScalarGridSpec(num_...]
    ppermute x21, starting transfers between devices: 17.9 us -> 20.1 us  [swap(): return lax.ppermute(value, axis, [(i, i ^ mask) for i in range(size)])]
    slice x2, local copies, waits for them, and re-layouts: 1.84 us -> 0.02 us  [summed_copies(): pieces = [value[i * unit:min((i + 1) * unit, rows)] for i in range(count)]]
    add x8, other arithmetic: 1.94 us -> 3.49 us  [summed_copies(): pieces = [p + m for p, m in zip(pieces, moved)]]
  transfers between devices with their start and end apart: 25 -> 25, of which waited for: 9 -> 8; matrix products, arithmetic and copies ran while one was open for 4% -> 4% of each run, Pallas kernels for 37% -> 21%
where the time goes in v2:
time: 112 us; the launch traced here: 111 us
  Pallas kernels  43.5 us (39%)
  starting transfers between devices  26.6 us (24%)
  local copies, waits for them, and re-layouts  19.6 us (18%)
  waiting for transfers between devices  15.9 us (14%)
  other arithmetic  4.41 us (4%)
    ppermute x21, starting transfers between devices, swap(): return lax.ppermute(value, axis, [(i, i ^ mask) for i in range(size)])  20.1 us
    unnamed x44, local copies, waits for them, and re-layouts  19.5 us
    ppermute x21, waiting for transfers between devices, swap(): return lax.ppermute(value, axis, [(i, i ^ mask) for i in range(size)])  15.9 us
    pallas_call x3, Pallas kernels, head_sums(): pl.pallas_call(functools.partial(target_kernel, len(lses), n, per), grid_...  14.8 us
    pallas_call x1, Pallas kernels, main_stats(): pl.pallas_call(functools.partial(stats_kernel, per), grid_spec=pltpu.Pref...  11.9 us
    pallas_call x2, Pallas kernels, index_grad_query(): pl.pallas_call(functools.partial(grad_query_kernel, n, first, len(lses)),...  7.23 us
    ppermute x4, starting transfers between devices, rotate(): lax.ppermute(value, axis, [(i, (i + by) % size) for i in range(size)])  6.42 us
    pallas_call x1, Pallas kernels, index_logits(): pl.pallas_call(logits_kernel, grid_spec=pltpu.PrefetchScalarGridSpec(num_...  5.06 us
  transfers between devices with their start and end apart: 25, of which 8 were waited for; matrix products, arithmetic and copies ran while one was open for 4% of the time, Pallas kernels for 21%

profile of v2, /device:TPU:0, one launch (start us, length us, event | category | flops | bytes accessed | tf_op | source)
XLA Modules:
  0.0 111.0 jit_solution(3391017139693456290)
XLA Ops:
  0.6 2.8 %copy-done = bf16[4,128,6144]{2,1,0:T(8,128)(2,1)S(1)} copy-done((bf16[4,128,6144]{2,1,0:T(8,128)(2,1)S(1)}, bf16[4,128,6144]{2,1,0:T(8,128)(2,1)}, u32[]{:S(2)}) %copy-start) | copy-done | bytes 6291480
  3.4 2.2 %copy-done.2 = bf16[512,4096]{1,0:T(8,128)(2,1)S(1)} copy-done((bf16[512,4096]{1,0:T(8,128)(2,1)S(1)}, bf16[512,4096]{1,0:T(8,128)(2,1)}, u32[]{:S(2)}) %copy-start.2) | copy-done | bytes 4194328
  8.5 11.9 %main_stats.1.refs_5_.refs_6_ = f32[32,512]{1,0:T(8,128)S(1)} custom-call(s32[16]{0:T(128)S(1)} %copy-done.16, bf16[4,128,6144]{2,1,0:T(8,128)(2,1)S(1)} %copy-done, bf16[512,4096]{1,0:T(8,128)(2,1)S(1)} %copy-done.2, bf16[64,512]{1,0:T(8,128)(2,1)S(1)} %bitcast.12, s32[4,128]{1,0:T(4,128)S(1)} %copy-done.11, s32[1,512]{1,0:T(1,128)S(1)} %bitcast.16), custom_call_target="tpu_custom_call" | custom-call | flops 4294967296 | bytes 10485760 | tf_op jit(solution)/shard_map/main_stats/pallas_call | solution.py:137
  21.0 2.5 %collective-permute-start.1 = (f32[32,512]{1,0:T(8,128)S(1)}, f32[32,512]{1,0:T(8,128)S(1)}, u32[]{:S(2)}, u32[]{:S(2)}) collective-permute-start(f32[32,512]{1,0:T(8,128)S(1)} %main_stats.1.refs_5_.refs_6_), channel_id=1, source_target_pairs={{0,16},{8,24},{16,0},{24,8},{1,17},{9,25},{17,1},{25,9},{2,18},{10... | collective-permute-start | bytes 196616 | tf_op jit(solution)/shard_map/ppermute | solution.py:456
  23.6 2.6 %collective-permute-done.1.refs_7_.refs_8_ = f32[32,512]{1,0:T(8,128)S(1)} collective-permute-done((f32[32,512]{1,0:T(8,128)S(1)}, f32[32,512]{1,0:T(8,128)S(1)}, u32[]{:S(2)}, u32[]{:S(2)}) %collective-permute-start.1) | collective-permute-done | bytes 65568 | tf_op jit(solution)/shard_map/ppermute | solution.py:456
  26.2 1.4 %collective-permute-done.2.refs_8_.refs_9_ = f32[32,512]{1,0:T(8,128)S(1)} collective-permute-done((f32[32,512]{1,0:T(8,128)S(1)}, f32[32,512]{1,0:T(8,128)S(1)}, u32[]{:S(2)}, u32[]{:S(2)}) %collective-permute-start.2) | collective-permute-done | bytes 65568 | tf_op jit(solution)/shard_map/ppermute | solution.py:456
  27.6 2.8 %copy-done.1 = bf16[4,128,6144]{2,1,0:T(8,128)(2,1)S(1)} copy-done((bf16[4,128,6144]{2,1,0:T(8,128)(2,1)S(1)}, bf16[4,128,6144]{2,1,0:T(8,128)(2,1)}, u32[]{:S(2)}) %copy-start.1) | copy-done | bytes 6291480
  30.4 2.2 %copy-done.3 = bf16[512,4096]{1,0:T(8,128)(2,1)S(1)} copy-done((bf16[512,4096]{1,0:T(8,128)(2,1)S(1)}, bf16[512,4096]{1,0:T(8,128)(2,1)}, u32[]{:S(2)}) %copy-start.3) | copy-done | bytes 4194328
  32.6 4.5 %head_sums.5 = f32[512,128]{1,0:T(8,128)S(1)} custom-call(s32[16]{0:T(128)S(1)} %copy-done.17, s32[1]{0:T(128)} %bitcast.6.grp_ref, bf16[4,128,6144]{2,1,0:T(8,128)(2,1)S(1)} %copy-done.1, bf16[512,4096]{1,0:T(8,128)(2,1)S(1)} %copy-done.3, bf16[64,512]{1,0:T(8,128)(2,1)S(1)} %bitcast.13, s32[4,128]{1,0:T(4,128)S(1)} %copy-done.12, s32[1,512]{1,0:T(1,128)S(1)} %bitcast.17, ...), custom_call_target="tpu_custom_call" | custom-call | flops 1073741824 | bytes 5767168 | tf_op jit(solution)/shard_map/head_sums/pallas_call | solution.py:217
  37.1 1.6 %collective-permute-start.3 = (f32[256,128]{1,0:T(8,128)S(1)}, f32[256,128]{1,0:T(8,128)S(1)}, u32[]{:S(2)}, u32[]{:S(2)}) collective-permute-start(f32[256,128]{1,0:T(8,128)S(1)} %get-tuple-element.32), channel_id=1, source_target_pairs={{0,2},{2,4},{4,6},{6,0},{1,3},{3,5},{5,7},{7,1},{8,10},{10,12},{12... | collective-permute-start | bytes 393224 | tf_op jit(solution)/shard_map/ppermute | solution.py:460
  38.7 2.3 %collective-permute-start.5 = (f32[256,128]{1,0:T(8,128)S(1)}, f32[256,128]{1,0:T(8,128)S(1)}, u32[]{:S(2)}, u32[]{:S(2)}) collective-permute-start(f32[256,128]{1,0:T(8,128)S(1)} %get-tuple-element.31), channel_id=1, source_target_pairs={{0,6},{2,0},{4,2},{6,4},{1,7},{3,1},{5,3},{7,5},{8,14},{10,8},{12,... | collective-permute-start | bytes 393224 | tf_op jit(solution)/shard_map/ppermute | solution.py:460
  41.0 5.8 %head_sums.4 = (f32[512,128]{1,0:T(8,128)S(1)}, f32[512,128]{1,0:T(8,128)S(1)}) custom-call(s32[16]{0:T(128)S(1)} %copy-done.17, s32[2]{0:T(128)S(1)} %pad_add_fusion.grp_ref, bf16[4,128,6144]{2,1,0:T(8,128)(2,1)S(1)} %copy-done.1, bf16[4,128,6144]{2,1,0:T(8,128)(2,1)S(1)} %copy-done.1, bf16[512,4096]{1,0:T(8,128)(2,1)S(1)} %copy-done.3, ...), custom_call_target="tpu_custom_call" | custom-call | flops 2147483648 | bytes 7340032 | tf_op jit(solution)/shard_map/head_sums/pallas_call | solution.py:217
  47.0 2.2 %collective-permute-start.6 = (f32[512,128]{1,0:T(8,128)S(1)}, f32[512,128]{1,0:T(8,128)S(1)}, u32[]{:S(2)}, u32[]{:S(2)}) collective-permute-start(f32[512,128]{1,0:T(8,128)S(1)} %pad_maximum_fusion.1), channel_id=1, source_target_pairs={{0,6},{2,0},{4,2},{6,4},{1,7},{3,1},{5,3},{7,5},{8,14},{10,8},{12,... | collective-permute-start | bytes 786440 | tf_op jit(solution)/shard_map/ppermute | solution.py:460
  49.5 5.1 %index_logits.1 = (f32[512,128]{1,0:T(8,128)S(1)}, f32[1,128]{1,0:T(1,128)S(1)}, bf16[512,8192]{1,0:T(8,128)(2,1)S(1)}) custom-call(s32[16]{0:T(128)S(1)} %copy-done.17, s32[1]{0:T(128)} %bitcast.1.grp_ref, bf16[128,8192]{1,0:T(8,128)(2,1)S(1)} %copy-done.5, bf16[512,128]{1,0:T(8,128)(2,1)S(1)} %copy-done.10, bf16[64,128]{1,0:T(8,128)(2,1)S(1)} %bitcast.22, ...), custom_call_target="tpu_custom_call" | custom-call | flops 1073741824 | bytes 10485760 | tf_op jit(solution)/shard_map/index_logits/pallas_call | solution.py:286
  54.6 3.3 %copy-done.6 = bf16[512,8192]{1,0:T(8,128)(2,1)} copy-done((bf16[512,8192]{1,0:T(8,128)(2,1)}, bf16[512,8192]{1,0:T(8,128)(2,1)S(1)}, u32[]{:S(2)}) %copy-start.6) | copy-done | bytes 8388632
  57.9 1.4 %collective-permute-start.8 = (f32[1,128]{1,0:T(1,128)S(1)}, f32[1,128]{1,0:T(1,128)S(1)}, u32[]{:S(2)}, u32[]{:S(2)}) collective-permute-start(f32[1,128]{1,0:T(1,128)S(1)} %get-tuple-element.16.refs_3_.refs_6_), channel_id=1, source_target_pairs={{0,16},{8,24},{16,0},{24,8},{1,17},{9,25},{17,1},{25,9},{2,18},{10... | collective-permute-start | bytes 1544 | tf_op jit(solution)/shard_map/ppermute | solution.py:456
  59.9 1.5 %collective-permute-done.8.refs_5_.refs_8_ = f32[1,128]{1,0:T(1,128)S(1)} collective-permute-done((f32[1,128]{1,0:T(1,128)S(1)}, f32[1,128]{1,0:T(1,128)S(1)}, u32[]{:S(2)}, u32[]{:S(2)}) %collective-permute-start.8) | collective-permute-done | bytes 544 | tf_op jit(solution)/shard_map/ppermute | solution.py:456
  61.5 4.5 %head_sums.3.refs_0_ = f32[512,128]{1,0:T(8,128)S(1)} custom-call(s32[16]{0:T(128)S(1)} %copy-done.17, s32[1]{0:T(128)} %bitcast.1.grp_ref, bf16[4,128,6144]{2,1,0:T(8,128)(2,1)S(1)} %bitcast.11, bf16[512,4096]{1,0:T(8,128)(2,1)S(1)} %copy-done.4, bf16[64,512]{1,0:T(8,128)(2,1)S(1)} %bitcast.15, s32[4,128]{1,0:T(4,128)S(1)} %copy-done.12, ...), custom_call_target="tpu_custom_call" | custom-call | flops 1073741824 | bytes 5767168 | tf_op jit(solution)/shard_map/head_sums/pallas_call | solution.py:217
  66.0 1.5 %collective-permute-start.12 = (f32[512,128]{1,0:T(8,128)S(1)}, f32[512,128]{1,0:T(8,128)S(1)}, u32[]{:S(2)}, u32[]{:S(2)}) collective-permute-start(f32[512,128]{1,0:T(8,128)S(1)} %convert_element_type.3.refs_2_), channel_id=1, source_target_pairs={{0,16},{8,24},{16,0},{24,8},{1,17},{9,25},{17,1},{25,9},{2,18},{10... | collective-permute-start | bytes 786440 | tf_op jit(solution)/shard_map/ppermute | solution.py:456
  67.5 3.4 %copy-done.7 = bf16[512,8192]{1,0:T(8,128)(2,1)S(1)} copy-done((bf16[512,8192]{1,0:T(8,128)(2,1)S(1)}, bf16[512,8192]{1,0:T(8,128)(2,1)}, u32[]{:S(2)}) %copy-start.7) | copy-done | bytes 8388632
  70.9 4.5 %index_grad_key.1 = (f32[520,128]{1,0:T(8,128)}, f32[512,128]{1,0:T(8,128)S(1)}) custom-call(s32[16]{0:T(128)S(1)} %copy-done.17, s32[1]{0:T(128)} %bitcast.1.grp_ref, f32[512,128]{1,0:T(8,128)S(1)} %head_sums.3.refs_0_, f32[512,128]{1,0:T(8,128)S(1)} %collective-permute-done.4.refs_1_, f32[512,128]{1,0:T(8,128)S(1)} %collective-permute-done.6.refs_2_, ...), custom_call_target="tpu_custom_call" | custom-call | flops 1073741824 | bytes 10485760 | tf_op jit(solution)/shard_map/index_grad_key/pallas_call | solution.py:357
  75.5 3.8 %collective-permute-start.22 = (f32[160,128]{1,0:T(8,128)S(1)}, f32[160,128]{1,0:T(8,128)S(1)}, u32[]{:S(2)}, u32[]{:S(2)}) collective-permute-start(f32[160,128]{1,0:T(8,128)S(1)} %slice.35), channel_id=1, source_target_pairs={{0,6},{2,4},{4,2},{6,0},{1,7},{3,5},{5,3},{7,1},{8,14},{10,12},{12... | collective-permute-start | bytes 245768 | tf_op jit(solution)/shard_map/ppermute | solution.py:456
  79.3 1.6 %collective-permute-start.16 = (f32[176,128]{1,0:T(8,128)S(1)}, f32[176,128]{1,0:T(8,128)S(1)}, u32[]{:S(2)}, u32[]{:S(2)}) collective-permute-start(f32[176,128]{1,0:T(8,128)S(1)} %get-tuple-element.27), channel_id=1, source_target_pairs={{0,1},{1,0},{2,3},{3,2},{4,5},{5,4},{6,7},{7,6},{8,9},{9,8},{10,11... | collective-permute-start | bytes 270344 | tf_op jit(solution)/shard_map/ppermute | solution.py:456
  80.9 1.6 %collective-permute-done.22 = f32[160,128]{1,0:T(8,128)S(1)} collective-permute-done((f32[160,128]{1,0:T(8,128)S(1)}, f32[160,128]{1,0:T(8,128)S(1)}, u32[]{:S(2)}, u32[]{:S(2)}) %collective-permute-start.22) | collective-permute-done | bytes 81952 | tf_op jit(solution)/shard_map/ppermute | solution.py:456
  82.5 1.4 %collective-permute-done.16 = f32[176,128]{1,0:T(8,128)S(1)} collective-permute-done((f32[176,128]{1,0:T(8,128)S(1)}, f32[176,128]{1,0:T(8,128)S(1)}, u32[]{:S(2)}, u32[]{:S(2)}) %collective-permute-start.16) | collective-permute-done | bytes 90144 | tf_op jit(solution)/shard_map/ppermute | solution.py:456
  87.4 2.5 %collective-permute-done.23 = f32[160,128]{1,0:T(8,128)S(1)} collective-permute-done((f32[160,128]{1,0:T(8,128)S(1)}, f32[160,128]{1,0:T(8,128)S(1)}, u32[]{:S(2)}, u32[]{:S(2)}) %collective-permute-start.23) | collective-permute-done | bytes 81952 | tf_op jit(solution)/shard_map/ppermute | solution.py:456
  89.9 1.7 %collective-permute-start.20 = (f32[176,128]{1,0:T(8,128)S(1)}, f32[176,128]{1,0:T(8,128)}, u32[]{:S(2)}, u32[]{:S(2)}) collective-permute-start(f32[176,128]{1,0:T(8,128)S(1)} %get-tuple-element.26), channel_id=1, source_target_pairs={{0,6},{2,4},{4,2},{6,0},{1,7},{3,5},{5,3},{7,1},{8,14},{10,12},{12... | collective-permute-start | bytes 270344 | tf_op jit(solution)/shard_map/ppermute | solution.py:456
  92.3 4.0 %collective-permute-done.20 = f32[176,128]{1,0:T(8,128)} collective-permute-done((f32[176,128]{1,0:T(8,128)S(1)}, f32[176,128]{1,0:T(8,128)}, u32[]{:S(2)}, u32[]{:S(2)}) %collective-permute-start.20) | collective-permute-done | bytes 90144 | tf_op jit(solution)/shard_map/ppermute | solution.py:456
  98.2 1.7 %collective-permute-start.18 = (f32[176,128]{1,0:T(8,128)S(1)}, f32[176,128]{1,0:T(8,128)S(1)}, u32[]{:S(2)}, u32[]{:S(2)}) collective-permute-start(f32[176,128]{1,0:T(8,128)S(1)} %add.61), channel_id=1, source_target_pairs={{0,6},{2,4},{4,2},{6,0},{1,7},{3,5},{5,3},{7,1},{8,14},{10,12},{12... | collective-permute-start | bytes 270344 | tf_op jit(solution)/shard_map/ppermute | solution.py:456
  100.9 2.0 %collective-permute-start.21 = (f32[176,128]{1,0:T(8,128)S(1)}, f32[176,128]{1,0:T(8,128)S(1)}, u32[]{:S(2)}, u32[]{:S(2)}) collective-permute-start(f32[176,128]{1,0:T(8,128)S(1)} %add.64), channel_id=1, source_target_pairs={{0,1},{1,0},{2,3},{3,2},{4,5},{5,4},{6,7},{7,6},{8,9},{9,8},{10,11... | collective-permute-start | bytes 270344 | tf_op jit(solution)/shard_map/ppermute | solution.py:456
  102.9 3.9 %index_grad_query.2 = (f32[128,2048]{1,0:T(8,128)S(1)}, f32[1,128]{1,0:T(1,128)S(1)}) custom-call(s32[1]{0:T(128)} %bitcast.slot_ref, f32[520,128]{1,0:T(8,128)} %get-tuple-element.19.refs_0_, f32[520,128]{1,0:T(8,128)} %collective-permute-done.14.refs_1_, f32[512,128]{1,0:T(8,128)S(1)} %convert_element_type.3.refs_2_, ...), custom_call_target="tpu_custom_call" | custom-call | flops 1073741824 | bytes 3145728 | tf_op jit(solution)/shard_map/index_grad_query/pallas_call | solution.py:434
  107.6 3.4 %index_grad_query.3 = (f32[128,2048]{1,0:T(8,128)}, f32[1,128]{1,0:T(1,128)}) custom-call(s32[1]{0:T(128)} %bitcast.slot_ref, f32[520,128]{1,0:T(8,128)S(1)} %collective-permute-done.10.refs_0_, f32[520,128]{1,0:T(8,128)S(1)} %collective-permute-done.11.refs_1_, f32[512,128]{1,0:T(8,128)S(1)} %collective-permute-done.12.refs_2_, ...), custom_call_target="tpu_custom_call" | custom-call | flops 1073741824 | bytes 3145728 | tf_op jit(solution)/shard_map/index_grad_query/pallas_call | solution.py:434
  (88 shorter events, 12.3 us)
Async XLA Ops:
  8.5 19.1 %copy-start.9 = (bf16[512,64]{0,1:T(8,128)(2,1)S(1)}, bf16[512,64]{0,1:T(8,128)(2,1)}, u32[]{:S(2)}) copy-start(bf16[512,64]{0,1:T(8,128)(2,1)} %param.12) | copy-start | bytes 196612
  8.5 19.1 %copy-start.12 = (s32[4,128]{1,0:T(4,128)S(1)}, s32[4,128]{1,0:T(4,128)}, u32[]{:S(2)}) copy-start(s32[4,128]{1,0:T(4,128)} %refs_9_.1) | copy-start | bytes 6148
  8.5 19.1 %copy-start.14 = (s32[512]{0:T(512)S(1)}, s32[512]{0:T(512)}, u32[]{:S(2)}) copy-start(s32[512]{0:T(512)} %param.14) | copy-start | bytes 6148
  8.5 19.1 %copy-start.17 = (s32[16]{0:T(128)S(1)}, s32[16]{0:T(128)}, u32[]{:S(2)}) copy-start(s32[16]{0:T(128)} %count_ref.11) | copy-start | bytes 196
  20.4 3.2 %collective-permute-start = (f32[32,512]{1,0:T(8,128)S(1)}, f32[32,512]{1,0:T(8,128)S(1)}, u32[]{:S(2)}, u32[]{:S(2)}) collective-permute-start(f32[32,512]{1,0:T(8,128)S(1)} %main_stats.1.refs_5_.refs_6_), channel_id=1, source_target_pairs={{0,8},{8,0},{16,24},{24,16},{1,9},{9,1},{17,25},{25,17},{2,10},{10... | collective-permute-start | bytes 196616 | tf_op jit(solution)/shard_map/ppermute | solution.py:456
  21.0 5.2 %collective-permute-start.1 = (f32[32,512]{1,0:T(8,128)S(1)}, f32[32,512]{1,0:T(8,128)S(1)}, u32[]{:S(2)}, u32[]{:S(2)}) collective-permute-start(f32[32,512]{1,0:T(8,128)S(1)} %main_stats.1.refs_5_.refs_6_), channel_id=1, source_target_pairs={{0,16},{8,24},{16,0},{24,8},{1,17},{9,25},{17,1},{25,9},{2,18},{10... | collective-permute-start | bytes 196616 | tf_op jit(solution)/shard_map/ppermute | solution.py:456
  23.5 4.1 %collective-permute-start.2 = (f32[32,512]{1,0:T(8,128)S(1)}, f32[32,512]{1,0:T(8,128)S(1)}, u32[]{:S(2)}, u32[]{:S(2)}) collective-permute-start(f32[32,512]{1,0:T(8,128)S(1)} %main_stats.1.refs_5_.refs_6_), channel_id=1, source_target_pairs={{0,24},{8,16},{16,8},{24,0},{1,25},{9,17},{17,9},{25,1},{2,26},{10... | collective-permute-start | bytes 196616 | tf_op jit(solution)/shard_map/ppermute | solution.py:456
  37.1 9.8 %collective-permute-start.3 = (f32[256,128]{1,0:T(8,128)S(1)}, f32[256,128]{1,0:T(8,128)S(1)}, u32[]{:S(2)}, u32[]{:S(2)}) collective-permute-start(f32[256,128]{1,0:T(8,128)S(1)} %get-tuple-element.32), channel_id=1, source_target_pairs={{0,2},{2,4},{4,6},{6,0},{1,3},{3,5},{5,7},{7,1},{8,10},{10,12},{12... | collective-permute-start | bytes 393224 | tf_op jit(solution)/shard_map/ppermute | solution.py:460
  38.7 22.8 %slice-start = ((s8[6291456]{0:T(1024)(128)(4,1)}), s8[4194304]{0:T(1024)(128)(4,1)S(1)}, s32[]{:S(2)}) async-start(s8[6291456]{0:T(1024)(128)(4,1)} %bitcast.10), calls=%async_computation | async-start | bytes 8388608
  38.7 22.8 %slice-start.1 = ((s8[6291456]{0:T(1024)(128)(4,1)}), s8[2097152]{0:T(1024)(128)(4,1)S(1)}, s32[]{:S(2)}) async-start(s8[6291456]{0:T(1024)(128)(4,1)} %bitcast.10), calls=%async_computation.1 | async-start | bytes 4194304
  38.7 8.2 %collective-permute-start.5 = (f32[256,128]{1,0:T(8,128)S(1)}, f32[256,128]{1,0:T(8,128)S(1)}, u32[]{:S(2)}, u32[]{:S(2)}) collective-permute-start(f32[256,128]{1,0:T(8,128)S(1)} %get-tuple-element.31), channel_id=1, source_target_pairs={{0,6},{2,0},{4,2},{6,4},{1,7},{3,1},{5,3},{7,5},{8,14},{10,8},{12,... | collective-permute-start | bytes 393224 | tf_op jit(solution)/shard_map/ppermute | solution.py:460
  46.9 14.6 %copy-start.4 = (bf16[512,4096]{1,0:T(8,128)(2,1)S(1)}, bf16[512,4096]{1,0:T(8,128)(2,1)}, u32[]{:S(2)}) copy-start(bf16[512,4096]{1,0:T(8,128)(2,1)} %refs_1_.5) | copy-start | bytes 12582916
  47.0 20.5 %collective-permute-start.6 = (f32[512,128]{1,0:T(8,128)S(1)}, f32[512,128]{1,0:T(8,128)S(1)}, u32[]{:S(2)}, u32[]{:S(2)}) collective-permute-start(f32[512,128]{1,0:T(8,128)S(1)} %pad_maximum_fusion.1), channel_id=1, source_target_pairs={{0,6},{2,0},{4,2},{6,4},{1,7},{3,1},{5,3},{7,5},{8,14},{10,8},{12,... | collective-permute-start | bytes 786440 | tf_op jit(solution)/shard_map/ppermute | solution.py:460
  49.3 18.2 %collective-permute-start.4 = (f32[512,128]{1,0:T(8,128)S(1)}, f32[512,128]{1,0:T(8,128)S(1)}, u32[]{:S(2)}, u32[]{:S(2)}) collective-permute-start(f32[512,128]{1,0:T(8,128)S(1)} %pad_maximum_fusion), channel_id=1, source_target_pairs={{0,2},{2,4},{4,6},{6,0},{1,3},{3,5},{5,7},{7,1},{8,10},{10,12},{12... | collective-permute-start | bytes 786440 | tf_op jit(solution)/shard_map/ppermute | solution.py:460
  57.9 3.6 %collective-permute-start.8 = (f32[1,128]{1,0:T(1,128)S(1)}, f32[1,128]{1,0:T(1,128)S(1)}, u32[]{:S(2)}, u32[]{:S(2)}) collective-permute-start(f32[1,128]{1,0:T(1,128)S(1)} %get-tuple-element.16.refs_3_.refs_6_), channel_id=1, source_target_pairs={{0,16},{8,24},{16,0},{24,8},{1,17},{9,25},{17,1},{25,9},{2,18},{10... | collective-permute-start | bytes 1544 | tf_op jit(solution)/shard_map/ppermute | solution.py:456
  59.4 6.7 %collective-permute-start.7 = (f32[1,128]{1,0:T(1,128)S(1)}, f32[1,128]{1,0:T(1,128)S(1)}, u32[]{:S(2)}, u32[]{:S(2)}) collective-permute-start(f32[1,128]{1,0:T(1,128)S(1)} %get-tuple-element.16.refs_3_.refs_6_), channel_id=1, source_target_pairs={{0,8},{8,0},{16,24},{24,16},{1,9},{9,1},{17,25},{25,17},{2,10},{10... | collective-permute-start | bytes 1544 | tf_op jit(solution)/shard_map/ppermute | solution.py:456
  59.4 41.5 %collective-permute-start.15 = (f32[512,128]{1,0:T(8,128)S(1)}, f32[512,128]{1,0:T(8,128)}, u32[]{:S(2)}, u32[]{:S(2)}) collective-permute-start(f32[512,128]{1,0:T(8,128)S(1)} %convert_element_type.3.refs_2_), channel_id=1, source_target_pairs={{0,8},{8,0},{16,24},{24,16},{1,9},{9,1},{17,25},{25,17},{2,10},{10... | collective-permute-start | bytes 786440 | tf_op jit(solution)/shard_map/ppermute | solution.py:456
  61.5 6.0 %collective-permute-start.9 = (f32[1,128]{1,0:T(1,128)S(1)}, f32[1,128]{1,0:T(1,128)S(1)}, u32[]{:S(2)}, u32[]{:S(2)}) collective-permute-start(f32[1,128]{1,0:T(1,128)S(1)} %collective-permute-done.8.refs_5_.refs_8_), channel_id=1, source_target_pairs={{0,8},{8,0},{16,24},{24,16},{1,9},{9,1},{17,25},{25,17},{2,10},{10... | collective-permute-start | bytes 1544 | tf_op jit(solution)/shard_map/ppermute | solution.py:456
  66.0 20.1 %collective-permute-start.12 = (f32[512,128]{1,0:T(8,128)S(1)}, f32[512,128]{1,0:T(8,128)S(1)}, u32[]{:S(2)}, u32[]{:S(2)}) collective-permute-start(f32[512,128]{1,0:T(8,128)S(1)} %convert_element_type.3.refs_2_), channel_id=1, source_target_pairs={{0,16},{8,24},{16,0},{24,8},{1,17},{9,25},{17,1},{25,9},{2,18},{10... | collective-permute-start | bytes 786440 | tf_op jit(solution)/shard_map/ppermute | solution.py:456
  75.5 7.1 %collective-permute-start.22 = (f32[160,128]{1,0:T(8,128)S(1)}, f32[160,128]{1,0:T(8,128)S(1)}, u32[]{:S(2)}, u32[]{:S(2)}) collective-permute-start(f32[160,128]{1,0:T(8,128)S(1)} %slice.35), channel_id=1, source_target_pairs={{0,6},{2,4},{4,2},{6,0},{1,7},{3,5},{5,3},{7,1},{8,14},{10,12},{12... | collective-permute-start | bytes 245768 | tf_op jit(solution)/shard_map/ppermute | solution.py:456
  79.3 4.6 %collective-permute-start.16 = (f32[176,128]{1,0:T(8,128)S(1)}, f32[176,128]{1,0:T(8,128)S(1)}, u32[]{:S(2)}, u32[]{:S(2)}) collective-permute-start(f32[176,128]{1,0:T(8,128)S(1)} %get-tuple-element.27), channel_id=1, source_target_pairs={{0,1},{1,0},{2,3},{3,2},{4,5},{5,4},{6,7},{7,6},{8,9},{9,8},{10,11... | collective-permute-start | bytes 270344 | tf_op jit(solution)/shard_map/ppermute | solution.py:456
  80.9 4.5 %collective-permute-start.19 = (f32[176,128]{1,0:T(8,128)S(1)}, f32[176,128]{1,0:T(8,128)S(1)}, u32[]{:S(2)}, u32[]{:S(2)}) collective-permute-start(f32[176,128]{1,0:T(8,128)S(1)} %get-tuple-element.28), channel_id=1, source_target_pairs={{0,2},{2,0},{4,6},{6,4},{1,3},{3,1},{5,7},{7,5},{8,10},{10,8},{12,... | collective-permute-start | bytes 270344 | tf_op jit(solution)/shard_map/ppermute | solution.py:456
  82.5 20.4 %collective-permute-start.14 = (f32[520,128]{1,0:T(8,128)}, f32[520,128]{1,0:T(8,128)}, u32[]{:S(2)}, u32[]{:S(2)}) collective-permute-start(f32[520,128]{1,0:T(8,128)} %get-tuple-element.19.refs_0_), channel_id=1, source_target_pairs={{0,8},{8,0},{16,24},{24,16},{1,9},{9,1},{17,25},{25,17},{2,10},{10... | collective-permute-start | bytes 798728 | tf_op jit(solution)/shard_map/ppermute | solution.py:456
  83.9 8.3 %collective-permute-start.10 = (f32[520,128]{1,0:T(8,128)}, f32[520,128]{1,0:T(8,128)S(1)}, u32[]{:S(2)}, u32[]{:S(2)}) collective-permute-start(f32[520,128]{1,0:T(8,128)} %get-tuple-element.19.refs_0_), channel_id=1, source_target_pairs={{0,16},{8,24},{16,0},{24,8},{1,17},{9,25},{17,1},{25,9},{2,18},{10... | collective-permute-start | bytes 798728 | tf_op jit(solution)/shard_map/ppermute | solution.py:456
  85.4 4.4 %collective-permute-start.23 = (f32[160,128]{1,0:T(8,128)S(1)}, f32[160,128]{1,0:T(8,128)S(1)}, u32[]{:S(2)}, u32[]{:S(2)}) collective-permute-start(f32[160,128]{1,0:T(8,128)S(1)} %slice_add_fusion.2), channel_id=1, source_target_pairs={{0,1},{1,0},{2,3},{3,2},{4,5},{5,4},{6,7},{7,6},{8,9},{9,8},{10,11... | collective-permute-start | bytes 245768 | tf_op jit(solution)/shard_map/ppermute | solution.py:456
  86.1 6.1 %collective-permute-start.17 = (f32[176,128]{1,0:T(8,128)S(1)}, f32[176,128]{1,0:T(8,128)}, u32[]{:S(2)}, u32[]{:S(2)}) collective-permute-start(f32[176,128]{1,0:T(8,128)S(1)} %get-tuple-element.25), channel_id=1, source_target_pairs={{0,2},{2,0},{4,6},{6,4},{1,3},{3,1},{5,7},{7,5},{8,10},{10,8},{12,... | collective-permute-start | bytes 270344 | tf_op jit(solution)/shard_map/ppermute | solution.py:456
  89.9 6.5 %collective-permute-start.20 = (f32[176,128]{1,0:T(8,128)S(1)}, f32[176,128]{1,0:T(8,128)}, u32[]{:S(2)}, u32[]{:S(2)}) collective-permute-start(f32[176,128]{1,0:T(8,128)S(1)} %get-tuple-element.26), channel_id=1, source_target_pairs={{0,6},{2,4},{4,2},{6,0},{1,7},{3,5},{5,3},{7,1},{8,14},{10,12},{12... | collective-permute-start | bytes 270344 | tf_op jit(solution)/shard_map/ppermute | solution.py:456
  92.2 6.0 %collective-permute-start.24 = (f32[160,128]{1,0:T(8,128)}, f32[160,128]{1,0:T(8,128)}, u32[]{:S(2)}, u32[]{:S(2)}) collective-permute-start(f32[160,128]{1,0:T(8,128)} %add.67), channel_id=1, source_target_pairs={{0,2},{2,0},{4,6},{6,4},{1,3},{3,1},{5,7},{7,5},{8,10},{10,8},{12,... | collective-permute-start | bytes 245768 | tf_op jit(solution)/shard_map/ppermute | solution.py:456
  92.2 15.4 %collective-permute-start.11 = (f32[520,128]{1,0:T(8,128)S(1)}, f32[520,128]{1,0:T(8,128)S(1)}, u32[]{:S(2)}, u32[]{:S(2)}) collective-permute-start(f32[520,128]{1,0:T(8,128)S(1)} %collective-permute-done.10.refs_0_), channel_id=1, source_target_pairs={{0,8},{8,0},{16,24},{24,16},{1,9},{9,1},{17,25},{25,17},{2,10},{10... | collective-permute-start | bytes 798728 | tf_op jit(solution)/shard_map/ppermute | solution.py:456
  96.3 11.3 %collective-permute-start.13 = (f32[512,128]{1,0:T(8,128)S(1)}, f32[512,128]{1,0:T(8,128)S(1)}, u32[]{:S(2)}, u32[]{:S(2)}) collective-permute-start(f32[512,128]{1,0:T(8,128)S(1)} %collective-permute-done.12.refs_2_), channel_id=1, source_target_pairs={{0,8},{8,0},{16,24},{24,16},{1,9},{9,1},{17,25},{25,17},{2,10},{10... | collective-permute-start | bytes 786440 | tf_op jit(solution)/shard_map/ppermute | solution.py:456
  98.2 8.6 %collective-permute-start.18 = (f32[176,128]{1,0:T(8,128)S(1)}, f32[176,128]{1,0:T(8,128)S(1)}, u32[]{:S(2)}, u32[]{:S(2)}) collective-permute-start(f32[176,128]{1,0:T(8,128)S(1)} %add.61), channel_id=1, source_target_pairs={{0,6},{2,4},{4,2},{6,0},{1,7},{3,5},{5,3},{7,1},{8,14},{10,12},{12... | collective-permute-start | bytes 270344 | tf_op jit(solution)/shard_map/ppermute | solution.py:456
  100.9 5.9 %collective-permute-start.21 = (f32[176,128]{1,0:T(8,128)S(1)}, f32[176,128]{1,0:T(8,128)S(1)}, u32[]{:S(2)}, u32[]{:S(2)}) collective-permute-start(f32[176,128]{1,0:T(8,128)S(1)} %add.64), channel_id=1, source_target_pairs={{0,1},{1,0},{2,3},{3,2},{4,5},{5,4},{6,7},{7,6},{8,9},{9,8},{10,11... | collective-permute-start | bytes 270344 | tf_op jit(solution)/shard_map/ppermute | solution.py:456
  (15 other events, 67.8 us)

commit v3 on v2

--- a/solution.py
+++ b/solution.py
@@ -7,16 +7,18 @@
 from jax.experimental.pallas import tpu as pltpu
 from jax.sharding import PartitionSpec as P
 
+
 H = 128
 DNOPE = 128
 DROPE = 64
-IH = 64
 ID = 128
 KBLOCK = 32
 DQK = 192
 LANES = 128
 PAIR = 2 * DQK
 NEG = -1e30
+SMALL = 2.0**-90
+LARGE = 2.0**100
 BIG = 2**30
 LOG2E = math.log2(math.e)
 SCALE_MAIN = DQK ** (-0.5) * LOG2E
@@ -84,11 +86,12 @@
     return jnp.concatenate([first, second], axis=1)
 
 
-def stats_kernel(per, count_ref, q_ref, kn_ref, rope_ref, qpos_ref, kpos_ref, lse_ref,
-                 bias_ref, even_ref, odd_ref, s0_ref, s1_ref):
+def stats_kernel(per, count_ref, q_ref, kn_ref, rope_ref, qpos_ref, kpos_ref, q_hbm, kn_hbm,
+                 lse_ref, bias_ref, even_ref, odd_ref, none_ref, bad_ref, q_buf, kn_buf, sem):
     step = pl.program_id(0)
     keys = kn_ref.shape[0]
     groups, rows = q_ref.shape[0], q_ref.shape[1]
+    halves = [slice(2 * c * rows, (2 * c + 2) * rows) for c in range(groups // 2)]
 
     @pl.when(step == 0)
     def _():
@@ -97,35 +100,52 @@
         for g in range(groups):
             valid = column <= qpos_ref[g : g + 1, :]
             bias_ref[:, g * rows : (g + 1) * rows] = jnp.where(valid, 0.0, NEG)
-
-    bufs = (s0_ref, s1_ref)
-    units = [(p, a, c) for p in range(per) for a in range(2) for c in range(groups // 2)]
-    tops = {}
-    kept = {}
-
-    def forward(u):
-        p, a, c = units[u]
-        if c == 0:
+        none_ref[...] = jnp.where(jnp.max(bias_ref[...], axis=0, keepdims=True) < 0, 1.0, 0.0)
+        bad_ref[...] = jnp.zeros_like(bad_ref)
+
+    def scores(kk, q3, c):
+        q = q3.reshape(2 * rows, 2 * LANES)
+        return dot_nt(kk, q) * SCALE_MAIN + bias_ref[:, halves[c]]
+
+    for p in range(per):
+        for a in range(2):
             lanes = slice((2 * p + a) * DNOPE, (2 * p + a + 1) * DNOPE)
-            kept[0] = main_keys(kn_ref[:, lanes], a, even_ref, odd_ref)
-        start = p * PAIR + a * LANES
-        q = q_ref[2 * c : 2 * c + 2, :, start : start + 2 * LANES].reshape(2 * rows, 2 * LANES)
-        cols = slice(2 * c * rows, (2 * c + 2) * rows)
-        s = dot_nt(kept[0], q) * SCALE_MAIN + bias_ref[:, cols]
-        bufs[u % 2][...] = s
-        tops[u] = jnp.max(s, axis=0, keepdims=True)
-
-    def finish(u):
-        p, a, c = units[u]
-        cols = slice(2 * c * rows, (2 * c + 2) * rows)
-        total = jnp.sum(jnp.exp2(bufs[u % 2][...] - tops[u]), axis=0, keepdims=True)
-        lse_ref[pl.ds(2 * per * step + 2 * p + a, 1), cols] = tops[u] + jnp.log2(total)
-
-    forward(0)
-    for u in range(1, len(units)):
-        forward(u)
-        finish(u - 1)
-    finish(len(units) - 1)
+            kk = main_keys(kn_ref[:, lanes], a, even_ref, odd_ref)
+            start = p * PAIR + a * LANES
+            for c, cols in enumerate(halves):
+                q3 = q_ref[2 * c : 2 * c + 2, :, start : start + 2 * LANES]
+                total = jnp.sum(jnp.exp2(scores(kk, q3, c)), axis=0, keepdims=True)
+                fine = (total >= SMALL) & (total <= LARGE)
+                skip = none_ref[:, cols] > 0
+                bad_ref[:, cols] += jnp.where(fine | skip, 0.0, 1.0)
+                lse_ref[pl.ds(2 * per * step + 2 * p + a, 1), cols] = jnp.where(
+                    skip, NEG, jnp.log2(total)
+                )
+
+    last = step == pl.num_programs(0) - 1
+
+    @pl.when(last & (jnp.max(bad_ref[...]) > 0))
+    def _():
+        def again(i, carry):
+            q_at = pl.ds(pl.multiple_of(i * PAIR, LANES), PAIR)
+            k_at = pl.ds(pl.multiple_of(i * 2 * DNOPE, LANES), 2 * DNOPE)
+            q_copy = pltpu.make_async_copy(q_hbm.at[:, :, q_at], q_buf, sem.at[0])
+            k_copy = pltpu.make_async_copy(kn_hbm.at[:, k_at], kn_buf, sem.at[1])
+            q_copy.start()
+            k_copy.start()
+            q_copy.wait()
+            k_copy.wait()
+            for a in range(2):
+                kk = main_keys(kn_buf[:, a * DNOPE : (a + 1) * DNOPE], a, even_ref, odd_ref)
+                for c, cols in enumerate(halves):
+                    q3 = q_buf[2 * c : 2 * c + 2, :, a * LANES : a * LANES + 2 * LANES]
+                    s = scores(kk, q3, c)
+                    top = jnp.max(s, axis=0, keepdims=True)
+                    total = jnp.sum(jnp.exp2(s - top), axis=0, keepdims=True)
+                    lse_ref[pl.ds(2 * i + a, 1), cols] = top + jnp.log2(total)
+            return carry
+
+        lax.fori_loop(0, lse_ref.shape[0] // 2, again, 0)
 
 
 def main_stats(main_query, key_nope, rope_t, query_pos, key_pos, key_count):
@@ -142,17 +162,22 @@
             in_specs=[
                 pl.BlockSpec((groups, rows, per * PAIR), lambda i, c: (0, 0, i)),
                 pl.BlockSpec((keys, per * 2 * DNOPE), lambda i, c: (0, i)),
-                IN_VMEM,
-                IN_VMEM,
-                IN_VMEM,
+                pl.BlockSpec((DROPE, keys), lambda i, c: (0, 0)),
+                pl.BlockSpec((groups, rows), lambda i, c: (0, 0)),
+                pl.BlockSpec((1, keys), lambda i, c: (0, 0)),
+                pl.BlockSpec(memory_space=pltpu.HBM),
+                pl.BlockSpec(memory_space=pltpu.HBM),
             ],
             out_specs=IN_VMEM,
             scratch_shapes=[
                 pltpu.VMEM((keys, total), f32),
                 pltpu.VMEM((keys, LANES), bf16),
                 pltpu.VMEM((keys, LANES), bf16),
-                pltpu.VMEM((keys, 2 * rows), f32),
-                pltpu.VMEM((keys, 2 * rows), f32),
+                pltpu.VMEM((1, total), f32),
+                pltpu.VMEM((1, total), f32),
+                pltpu.VMEM((groups, rows, PAIR), bf16),
+                pltpu.VMEM((keys, 2 * DNOPE), bf16),
+                pltpu.SemaphoreType.DMA((2,)),
             ],
         ),
         out_shape=jax.ShapeDtypeStruct((heads, total), f32),
@@ -161,10 +186,10 @@
             heads * total * keys * 512, main_query.size * 2 + key_nope.size * 2, heads * total * keys
         ),
         name="main_stats",
-    )(key_count, main_query, key_nope, rope_t, query_pos, key_pos)
-
-
-def target_kernel(n_lse, n_groups, per, count_ref, grp_ref, *refs):
+    )(key_count, main_query, key_nope, rope_t, query_pos, key_pos, main_query, key_nope)
+
+
+def target_kernel(n_lse, n_groups, per, parts, count_ref, grp_ref, *refs):
     q_refs = refs[:n_groups]
     kn_ref, rope_ref, qpos_ref, kpos_ref = refs[n_groups : n_groups + 4]
     lse_refs = refs[n_groups + 4 : n_groups + 4 + n_lse]
@@ -173,6 +198,12 @@
     step = pl.program_id(0)
     keys = kn_ref.shape[0]
     rows = q_refs[0].shape[1]
+    size = keys // parts
+    tiles = [
+        (g, slice(i * size, (i + 1) * size), out_refs[g * parts + i])
+        for g in range(n_groups)
+        for i in range(parts)
+    ]
 
     @pl.when(step == 0)
     def _():
@@ -180,7 +211,8 @@
         for g in range(n_groups):
             at = pl.ds(pl.multiple_of(grp_ref[g] * rows, rows), rows)
             glob_ref[:, g * rows : (g + 1) * rows] = combine_lse([r[:, at] for r in lse_refs])
-            out_refs[g][...] = jnp.zeros_like(out_refs[g])
+        for ref in out_refs:
+            ref[...] = jnp.zeros_like(ref)
 
     for p in range(per):
         acc = None
@@ -193,18 +225,18 @@
             lse = glob_ref[pl.ds(2 * per * step + 2 * p + a, 1), :]
             e = jnp.exp2(dot_nt(kk, q) * SCALE_MAIN - lse)
             acc = e if acc is None else acc + e
-        for g in range(n_groups):
-            out_refs[g][...] += acc[:, g * rows : (g + 1) * rows]
+        for g, at, ref in tiles:
+            ref[...] += acc[at, g * rows : (g + 1) * rows]
 
     @pl.when(step == pl.num_programs(0) - 1)
     def _():
         column = key_limit_column(count_ref, kpos_ref, keys)
-        for g in range(n_groups):
-            valid = column <= qpos_ref[pl.ds(grp_ref[g], 1), :]
-            out_refs[g][...] = jnp.where(valid, out_refs[g][...], 0.0)
-
-
-def head_sums(group_ids, main_query, key_nope, rope_t, query_pos, key_pos, key_count, lses):
+        for g, at, ref in tiles:
+            valid = column[at] <= qpos_ref[pl.ds(grp_ref[g], 1), :]
+            ref[...] = jnp.where(valid, ref[...], 0.0)
+
+
+def head_sums(group_ids, main_query, key_nope, rope_t, query_pos, key_pos, key_count, lses, parts=1):
     groups, rows, width = main_query.shape
     heads = width // DQK
     keys = key_nope.shape[0]
@@ -215,21 +247,26 @@
         return pl.BlockSpec((1, rows, per * PAIR), lambda i, c, grp: (grp[g], 0, i))
 
     return pl.pallas_call(
-        functools.partial(target_kernel, len(lses), n, per),
+        functools.partial(target_kernel, len(lses), n, per, parts),
         grid_spec=pltpu.PrefetchScalarGridSpec(
             num_scalar_prefetch=2,
             grid=(heads // (2 * per),),
             in_specs=[group_q(g) for g in range(n)]
             + [pl.BlockSpec((keys, per * 2 * DNOPE), lambda i, c, grp: (0, i))]
-            + [IN_VMEM] * (3 + len(lses)),
-            out_specs=[IN_VMEM] * n,
+            + [
+                pl.BlockSpec((DROPE, keys), lambda i, c, grp: (0, 0)),
+                pl.BlockSpec((groups, rows), lambda i, c, grp: (0, 0)),
+                pl.BlockSpec((1, keys), lambda i, c, grp: (0, 0)),
+            ]
+            + [IN_VMEM] * len(lses),
+            out_specs=[IN_VMEM] * (n * parts),
             scratch_shapes=[
                 pltpu.VMEM((heads, n * rows), f32),
                 pltpu.VMEM((keys, LANES), bf16),
                 pltpu.VMEM((keys, LANES), bf16),
             ],
         ),
-        out_shape=[jax.ShapeDtypeStruct((keys, rows), f32)] * n,
+        out_shape=[jax.ShapeDtypeStruct((keys // parts, rows), f32)] * (n * parts),
         compiler_params=params(),
         cost_estimate=cost(
             heads * n * rows * keys * 512, main_query.size * n // 2 + key_nope.size * 2,
@@ -290,10 +327,10 @@
             grid=(steps,),
             in_specs=[
                 pl.BlockSpec((rows, per * ID), lambda i, c, grp: (0, i)),
-                IN_VMEM,
-                IN_VMEM,
-                IN_VMEM,
-                IN_VMEM,
+                pl.BlockSpec((keys, ID), lambda i, c, grp: (0, 0)),
+                pl.BlockSpec((width // ID, rows), lambda i, c, grp: (0, 0)),
+                pl.BlockSpec(query_pos.shape, lambda i, c, grp: (0, 0)),
+                pl.BlockSpec((1, keys), lambda i, c, grp: (0, 0)),
             ],
             out_specs=[
                 IN_VMEM,
@@ -305,7 +342,7 @@
         out_shape=[
             jax.ShapeDtypeStruct((keys, rows), f32),
             jax.ShapeDtypeStruct((1, rows), f32),
-            jax.ShapeDtypeStruct((keys, (width // ID) * rows), bf16),
+            pltpu.HBM((keys, (width // ID) * rows), bf16),
         ],
         compiler_params=params(),
         cost_estimate=cost(2 * keys * rows * width, rows * width * 2 + keys * rows * width // ID * 2),
@@ -359,8 +396,11 @@
         grid_spec=pltpu.PrefetchScalarGridSpec(
             num_scalar_prefetch=2,
             grid=(steps,),
-            in_specs=[IN_VMEM] * (len(parts) + len(lses) + 4)
+            in_specs=[IN_VMEM] * (len(parts) + len(lses) + 1)
             + [
+                pl.BlockSpec((1, rows), lambda i, c, grp: (0, 0)),
+                pl.BlockSpec(query_pos.shape, lambda i, c, grp: (0, 0)),
+                pl.BlockSpec((1, keys), lambda i, c, grp: (0, 0)),
                 pl.BlockSpec((keys, per * rows), lambda i, c, grp: (0, i)),
                 pl.BlockSpec((rows, per * ID), lambda i, c, grp: (0, i)),
             ],
@@ -437,8 +477,11 @@
             num_scalar_prefetch=1,
             grid=(1,),
             in_specs=[IN_VMEM] * (2 * n)
-            + [pl.BlockSpec((rows, mine), lambda i, s: (0, s[0]))]
-            + [IN_VMEM] * (1 + len(lses) + len(carried)),
+            + [
+                pl.BlockSpec((rows, mine), lambda i, s: (0, s[0])),
+                pl.BlockSpec(weight_t.shape, lambda i, s: (0, 0)),
+            ]
+            + [IN_VMEM] * (len(lses) + len(carried)),
             out_specs=[IN_VMEM, IN_VMEM],
             scratch_shapes=[pltpu.VMEM((heads, rows), f32)],
         ),
@@ -460,20 +503,24 @@
     return lax.ppermute(value, axis, [(i, (i + by) % size) for i in range(size)])
 
 
+def butterfly_lse(value, size):
+    pair = [value]
+    for bit in reversed(range(size.bit_length() - 1)):
+        here = combine_lse(pair)
+        pair = [here, swap(here, "key", 1 << bit, size)]
+    return pair
+
+
 def summed_copies(value, n_head, n_query):
-    steps = [("query", m, n_query) for m in (1 << b for b in range(n_query.bit_length() - 1))]
+    steps = [("query", 1 << b, n_query) for b in range(n_query.bit_length() - 1)]
     steps += [("head", (2 << b) - 1, n_head) for b in range(n_head.bit_length() - 1)]
-    count = len(steps)
-    if count == 0:
-        return value
-    rows = value.shape[0]
-    unit = -(-rows // (8 * count)) * 8
-    pieces = [value[i * unit : min((i + 1) * unit, rows)] for i in range(count)]
-    pieces = [p for p in pieces if p.shape[0]]
-    for s in range(count):
-        moved = [swap(p, *steps[(i + s) % count]) for i, p in enumerate(pieces)]
-        pieces = [p + m for p, m in zip(pieces, moved)]
-    return jnp.concatenate(pieces, axis=0)
+    for axis, mask, size in steps:
+        value = value + swap(value, axis, mask, size)
+    return value
+
+
+def in_hbm(*values):
+    return tuple(pltpu.with_memory_space_constraint(v, pltpu.HBM) for v in values)
 
 
 def body(n_key, n_head, n_query, main_query, key_nope, key_rope, query_pos, key_pos, key_count,
@@ -482,35 +529,38 @@
     keys = key_nope.shape[0]
     z = lax.axis_index("head")
     slot = lax.axis_index("key")
-    key_row = key_pos.reshape(1, keys)
-    main = (main_query, key_nope, key_rope.T, query_pos, key_row, key_count)
-    weight_t = index_weight.T
-    cotangent = row_cotangent.reshape(1, rows)
+    (main_query, key_nope, rope_t, query_pos, key_row, key_count, index_query, weight_t, cotangent,
+     narrow_key) = in_hbm(
+        main_query, key_nope, key_rope.T, query_pos, key_pos.reshape(1, keys), key_count,
+        index_query, index_weight.T, row_cotangent.reshape(1, rows), index_key,
+    )
+    main = (main_query, key_nope, rope_t, query_pos, key_row, key_count)
 
     def gathered(value):
         if n_key == 4:
+            near = swap(value, "key", 1, n_key)
             far = swap(value, "key", 2, n_key)
-            return [value, swap(value, "key", 1, n_key), far, swap(far, "key", 1, n_key)]
+            across = swap(far, "key", 1, n_key)
+            return [value, near, far, across]
         return list(lax.all_gather(value, "key"))
 
+    lse = main_stats(*main)
+    lses = butterfly_lse(lse, n_key)
+    logits, index_lse, wm = index_logits(
+        z, index_query, narrow_key, weight_t, query_pos, key_row, key_count
+    )
+    wm = in_hbm(wm)[0]
+    index_lses = butterfly_lse(index_lse, n_key)
     iks = gathered(index_key.astype(f32))
-    lse = main_stats(*main)
-    lses = [lse] + [swap(lse, "key", m, n_key) for m in (1, 2, 3)] if n_key == 4 else [
-        combine_lse(gathered(lse))
-    ]
-    logits, index_lse, wm = index_logits(
-        z, index_query, index_key, weight_t, query_pos, key_row, key_count
-    )
-    index_lses = gathered(index_lse) if n_key == 4 else [combine_lse(gathered(index_lse))]
 
     if n_head == 4 and groups == 4:
-        across = head_sums([(z + 2) % 4], *main, lses)[0]
+        low, high = head_sums([(z + 2) % 4], *main, lses, parts=2)
         half = keys // 2
-        low = rotate(across[:half], "head", 1, 4)
-        high = rotate(across[half:], "head", 3, 4)
+        low = rotate(low, "head", 1, 4)
+        high = rotate(high, "head", 3, 4)
         up, down = head_sums([(z + 1) % 4, (z + 3) % 4], *main, lses)
-        up = jnp.concatenate([up[:half] + low, up[half:]], axis=0)
-        down = jnp.concatenate([down[:half], down[half:] + high], axis=0)
+        up = up + jnp.pad(low, ((0, half), (0, 0)))
+        down = down + jnp.pad(high, ((half, 0), (0, 0)))
         from_below = rotate(up, "head", 1, 4)
         from_above = rotate(down, "head", 3, 4)
         own = head_sums([z], *main, lses)[0]
@@ -536,8 +586,13 @@
 
 
 def solution(mesh):
+    sizes = (mesh.shape["key"], mesh.shape["head"], mesh.shape["query"])
+
+    def step(*args):
+        return body(*sizes, *args)
+
     return jax.shard_map(
-        functools.partial(body, mesh.shape["key"], mesh.shape["head"], mesh.shape["query"]),
+        step,
         mesh=mesh,
         in_specs=(
             P(None, "query", "head"),

time: 112 us -> 124 us (1.11)
  the two profiles are of different devices: /device:TPU:0 before, /device:TPU:10 now
where the time goes in v3:
time: 124 us; the launch traced here: 123 us
  Pallas kernels  55.5 us (45%)
  starting transfers between devices  41 us (33%)
  waiting for transfers between devices  25 us (20%)
    ppermute x13, starting transfers between devices, swap(): return lax.ppermute(value, axis, [(i, i ^ mask) for i in range(size)])  36.6 us
    pallas_call x3, Pallas kernels, head_sums(): pl.pallas_call(functools.partial(target_kernel, len(lses), n, per, parts)...  21.3 us
    ppermute x13, waiting for transfers between devices, swap(): return lax.ppermute(value, axis, [(i, i ^ mask) for i in range(size)])  16.4 us
    pallas_call x1, Pallas kernels, main_stats(): pl.pallas_call(functools.partial(stats_kernel, per), grid_spec=pltpu.Pref...  11.3 us
    ppermute x4, waiting for transfers between devices, rotate(): lax.ppermute(value, axis, [(i, (i + by) % size) for i in range(size)])  8.57 us
    pallas_call x2, Pallas kernels, index_grad_query(): pl.pallas_call(functools.partial(grad_query_kernel, n, first, len(lses)),...  8.23 us
    pallas_call x1, Pallas kernels, index_logits(): pl.pallas_call(logits_kernel, grid_spec=pltpu.PrefetchScalarGridSpec(num_...  7.81 us
    pallas_call x1, Pallas kernels, index_grad_key(): pl.pallas_call(functools.partial(grad_key_kernel, len(parts), len(lses)),...  6.81 us
  transfers between devices with their start and end apart: 17, of which 6 were waited for; matrix products, arithmetic and copies ran while one was open for 0% of the time, Pallas kernels for 30%

profile of v3, /device:TPU:10, one launch (start us, length us, event | category | flops | bytes accessed | tf_op | source)
XLA Modules:
  0.0 123.3 jit_solution(4834011015620210218)
XLA Ops:
  0.6 11.3 %main_stats.1 = f32[32,512]{1,0:T(8,128)S(1)} custom-call(s32[16]{0:T(128)} %count_ref.11, bf16[4,128,6144]{2,1,0:T(8,128)(2,1)} %refs_0_.5, bf16[512,4096]{1,0:T(8,128)(2,1)} %refs_1_.5, bf16[64,512]{1,0:T(8,128)(2,1)} %bitcast.10, s32[4,128]{1,0:T(4,128)} %refs_7_.1, s32[1,512]{1,0:T(1,128)} %bitcast.14, bf16[4,128,6144]{2,1,0:T(8,128)(2,1)} %refs_0_.5, ...), custom_call_target="tpu_custom_call" | custom-call | flops 4294967296 | bytes 10485760 | tf_op jit(solution)/shard_map/main_stats/pallas_call | solution.py:157
  11.9 0.6 collective-permute-start
  12.5 7.8 %index_logits.1 = (f32[512,128]{1,0:T(8,128)S(1)}, f32[1,128]{1,0:T(1,128)S(1)}, bf16[512,8192]{1,0:T(8,128)(2,1)}) custom-call(s32[16]{0:T(128)} %count_ref.11, s32[1]{0:T(128)} %bitcast.1.grp_ref, bf16[128,8192]{1,0:T(8,128)(2,1)} %refs_4_.5, bf16[512,128]{1,0:T(8,128)(2,1)} %ik_ref.1, bf16[64,128]{1,0:T(8,128)(2,1)} %bitcast.20, s32[4,128]{1,0:T(4,128)} %refs_7_.1, ...), custom_call_target="tpu_custom_call" | custom-call | flops 1073741824 | bytes 10485760 | tf_op jit(solution)/shard_map/index_logits/pallas_call | solution.py:323
  20.4 1.5 %collective-permute-start.6 = (f32[1,128]{1,0:T(1,128)S(1)}, f32[1,128]{1,0:T(1,128)S(1)}, u32[]{:S(2)}, u32[]{:S(2)}) collective-permute-start(f32[1,128]{1,0:T(1,128)S(1)} %get-tuple-element.20), channel_id=1, source_target_pairs={{0,16},{8,24},{16,0},{24,8},{1,17},{9,25},{17,1},{25,9},{2,18},{10... | collective-permute-start | bytes 1544 | tf_op jit(solution)/shard_map/ppermute | solution.py:499
  21.9 0.1 collective-permute-start.1
  22.0 0.1 pad_add_fusion.2.grp_ref
  22.1 1.2 collective-permute-done.1.refs_6_.refs_7_
  23.2 6.3 %head_sums.5 = (f32[256,128]{1,0:T(8,128)S(1)}, f32[256,128]{1,0:T(8,128)S(1)}) custom-call(s32[16]{0:T(128)} %count_ref.11, s32[1]{0:T(128)} %bitcast.6.grp_ref, bf16[4,128,6144]{2,1,0:T(8,128)(2,1)} %refs_0_.5, bf16[512,4096]{1,0:T(8,128)(2,1)} %refs_1_.5, bf16[64,512]{1,0:T(8,128)(2,1)} %bitcast.11, s32[4,128]{1,0:T(4,128)} %refs_7_.1, ...), custom_call_target="tpu_custom_call" | custom-call | flops 1073741824 | bytes 5767168 | tf_op jit(solution)/shard_map/head_sums/pallas_call | solution.py:249
  29.5 0.5 collective-permute-start.4
  30.0 1.6 %collective-permute-start.2 = (f32[256,128]{1,0:T(8,128)S(1)}, f32[256,128]{1,0:T(8,128)S(1)}, u32[]{:S(2)}, u32[]{:S(2)}) collective-permute-start(f32[256,128]{1,0:T(8,128)S(1)} %get-tuple-element.17), channel_id=1, source_target_pairs={{0,2},{2,4},{4,6},{6,0},{1,3},{3,5},{5,7},{7,1},{8,10},{10,12},{12... | collective-permute-start | bytes 393224 | tf_op jit(solution)/shard_map/ppermute | solution.py:503
  31.6 8.8 %head_sums.4 = (f32[512,128]{1,0:T(8,128)S(1)}, f32[512,128]{1,0:T(8,128)S(1)}) custom-call(s32[16]{0:T(128)} %count_ref.11, s32[2]{0:T(128)S(1)} %pad_add_fusion.2.grp_ref, bf16[4,128,6144]{2,1,0:T(8,128)(2,1)} %refs_0_.5, bf16[4,128,6144]{2,1,0:T(8,128)(2,1)} %refs_0_.5, bf16[512,4096]{1,0:T(8,128)(2,1)} %refs_1_.5, bf16[64,512]{1,0:T(8,128)(2,1)} %bitcast.12, ...), custom_call_target="tpu_custom_call" | custom-call | flops 2147483648 | bytes 7340032 | tf_op jit(solution)/shard_map/head_sums/pallas_call | solution.py:249
  40.4 0.0 collective-permute-done.4
  40.5 2.1 %collective-permute-start.5 = (f32[512,128]{1,0:T(8,128)S(1)}, f32[512,128]{1,0:T(8,128)S(1)}, u32[]{:S(2)}, u32[]{:S(2)}) collective-permute-start(f32[512,128]{1,0:T(8,128)S(1)} %pad_add_fusion), channel_id=1, source_target_pairs={{0,6},{2,0},{4,2},{6,4},{1,7},{3,1},{5,3},{7,5},{8,14},{10,8},{12,... | collective-permute-start | bytes 786440 | tf_op jit(solution)/shard_map/ppermute | solution.py:503
  42.6 0.2 collective-permute-start.3
  42.8 0.1 collective-permute-start.7
  42.9 6.3 %head_sums.3.refs_0_ = f32[512,128]{1,0:T(8,128)S(1)} custom-call(s32[16]{0:T(128)} %count_ref.11, s32[1]{0:T(128)} %bitcast.1.grp_ref, bf16[4,128,6144]{2,1,0:T(8,128)(2,1)} %refs_0_.5, bf16[512,4096]{1,0:T(8,128)(2,1)} %refs_1_.5, bf16[64,512]{1,0:T(8,128)(2,1)} %bitcast.13, s32[4,128]{1,0:T(4,128)} %refs_7_.1, s32[1,512]{1,0:T(1,128)} %bitcast.18, ...), custom_call_target="tpu_custom_call" | custom-call | flops 1073741824 | bytes 5767168 | tf_op jit(solution)/shard_map/head_sums/pallas_call | solution.py:249
  49.2 0.0 copy-start
  49.2 8.6 %collective-permute-done.3.refs_1_ = f32[512,128]{1,0:T(8,128)S(1)} collective-permute-done((f32[512,128]{1,0:T(8,128)S(1)}, f32[512,128]{1,0:T(8,128)S(1)}, u32[]{:S(2)}, u32[]{:S(2)}) %collective-permute-start.3) | collective-permute-done | bytes 262176 | tf_op jit(solution)/shard_map/ppermute | solution.py:503
  57.8 6.8 %index_grad_key.1 = (f32[520,128]{1,0:T(8,128)S(1)}, f32[512,128]{1,0:T(8,128)S(1)}) custom-call(s32[16]{0:T(128)} %count_ref.11, s32[1]{0:T(128)} %bitcast.1.grp_ref, f32[512,128]{1,0:T(8,128)S(1)} %head_sums.3.refs_0_, f32[512,128]{1,0:T(8,128)S(1)} %collective-permute-done.3.refs_1_, f32[512,128]{1,0:T(8,128)S(1)} %collective-permute-done.5.refs_2_, ...), custom_call_target="tpu_custom_call" | custom-call | flops 1073741824 | bytes 10485760 | tf_op jit(solution)/shard_map/index_grad_key/pallas_call | solution.py:394
  64.6 31.1 %collective-permute-start.14 = (f32[512,128]{1,0:T(8,128)S(1)}, f32[512,128]{1,0:T(8,128)S(1)}, u32[]{:S(2)}, u32[]{:S(2)}) collective-permute-start(f32[512,128]{1,0:T(8,128)S(1)} %get-tuple-element.28), channel_id=1, source_target_pairs={{0,1},{1,0},{2,3},{3,2},{4,5},{5,4},{6,7},{7,6},{8,9},{9,8},{10,11... | collective-permute-start | bytes 786440 | tf_op jit(solution)/shard_map/ppermute | solution.py:499
  95.8 0.0 collective-permute-start.8
  95.8 2.1 %collective-permute-start.10 = (f32[512,128]{1,0:T(8,128)S(1)}, f32[512,128]{1,0:T(8,128)S(1)}, u32[]{:S(2)}, u32[]{:S(2)}) collective-permute-start(f32[512,128]{1,0:T(8,128)S(1)} %convert_element_type.7.refs_2_), channel_id=1, source_target_pairs={{0,16},{8,24},{16,0},{24,8},{1,17},{9,25},{17,1},{25,9},{2,18},{10... | collective-permute-start | bytes 786440 | tf_op jit(solution)/shard_map/ppermute | solution.py:499
  97.9 3.1 %collective-permute-done.14 = f32[512,128]{1,0:T(8,128)S(1)} collective-permute-done((f32[512,128]{1,0:T(8,128)S(1)}, f32[512,128]{1,0:T(8,128)S(1)}, u32[]{:S(2)}, u32[]{:S(2)}) %collective-permute-start.14) | collective-permute-done | bytes 262176 | tf_op jit(solution)/shard_map/ppermute | solution.py:499
  101.0 0.5 collective-permute-start.15
  101.6 0.5 collective-permute-start.13
  102.1 2.9 %collective-permute-done.8.refs_0_ = f32[520,128]{1,0:T(8,128)S(1)} collective-permute-done((f32[520,128]{1,0:T(8,128)S(1)}, f32[520,128]{1,0:T(8,128)S(1)}, u32[]{:S(2)}, u32[]{:S(2)}) %collective-permute-start.8) | collective-permute-done | bytes 266272 | tf_op jit(solution)/shard_map/ppermute | solution.py:499
  105.0 3.2 %collective-permute-done.10.refs_2_ = f32[512,128]{1,0:T(8,128)S(1)} collective-permute-done((f32[512,128]{1,0:T(8,128)S(1)}, f32[512,128]{1,0:T(8,128)S(1)}, u32[]{:S(2)}, u32[]{:S(2)}) %collective-permute-start.10) | collective-permute-done | bytes 262176 | tf_op jit(solution)/shard_map/ppermute | solution.py:499
  108.2 0.1 collective-permute-start.16
  108.3 3.8 %index_grad_query.2 = (f32[128,2048]{1,0:T(8,128)S(1)}, f32[1,128]{1,0:T(1,128)S(1)}) custom-call(s32[1]{0:T(128)} %bitcast.slot_ref, f32[520,128]{1,0:T(8,128)S(1)} %get-tuple-element.23.refs_0_, f32[520,128]{1,0:T(8,128)S(1)} %collective-permute-done.12.refs_1_, f32[512,128]{1,0:T(8,128)S(1)} %convert_element_type.7.refs_2_, ...), custom_call_target="tpu_custom_call" | custom-call | flops 1073741824 | bytes 3145728 | tf_op jit(solution)/shard_map/index_grad_query/pallas_call | solution.py:474
  112.1 4.4 %index_grad_query.3 = (f32[128,2048]{1,0:T(8,128)}, f32[1,128]{1,0:T(1,128)}) custom-call(s32[1]{0:T(128)} %bitcast.slot_ref, f32[520,128]{1,0:T(8,128)S(1)} %collective-permute-done.8.refs_0_, f32[520,128]{1,0:T(8,128)S(1)} %collective-permute-done.9.refs_1_, f32[512,128]{1,0:T(8,128)S(1)} %collective-permute-done.10.refs_2_, ...), custom_call_target="tpu_custom_call" | custom-call | flops 1073741824 | bytes 3145728 | tf_op jit(solution)/shard_map/index_grad_query/pallas_call | solution.py:474
  116.6 6.0 %collective-permute-done.16 = f32[512,128]{1,0:T(8,128)S(1)} collective-permute-done((f32[512,128]{1,0:T(8,128)S(1)}, f32[512,128]{1,0:T(8,128)S(1)}, u32[]{:S(2)}, u32[]{:S(2)}) %collective-permute-start.16) | collective-permute-done | bytes 262176 | tf_op jit(solution)/shard_map/ppermute | solution.py:499
  122.6 0.7 add.64
  (21 shorter events, 0.2 us)
Async XLA Ops:
  11.9 9.9 %collective-permute-start = (f32[32,512]{1,0:T(8,128)S(1)}, f32[32,512]{1,0:T(8,128)S(1)}, u32[]{:S(2)}, u32[]{:S(2)}) collective-permute-start(f32[32,512]{1,0:T(8,128)S(1)} %main_stats.1), channel_id=1, source_target_pairs={{0,16},{8,24},{16,0},{24,8},{1,17},{9,25},{17,1},{25,9},{2,18},{10... | collective-permute-start | bytes 196616 | tf_op jit(solution)/shard_map/ppermute | solution.py:499
  20.4 22.5 %collective-permute-start.6 = (f32[1,128]{1,0:T(1,128)S(1)}, f32[1,128]{1,0:T(1,128)S(1)}, u32[]{:S(2)}, u32[]{:S(2)}) collective-permute-start(f32[1,128]{1,0:T(1,128)S(1)} %get-tuple-element.20), channel_id=1, source_target_pairs={{0,16},{8,24},{16,0},{24,8},{1,17},{9,25},{17,1},{25,9},{2,18},{10... | collective-permute-start | bytes 1544 | tf_op jit(solution)/shard_map/ppermute | solution.py:499
  21.9 1.3 %collective-permute-start.1 = (f32[32,512]{1,0:T(8,128)S(1)}, f32[32,512]{1,0:T(8,128)S(1)}, u32[]{:S(2)}, u32[]{:S(2)}) collective-permute-start(f32[32,512]{1,0:T(8,128)S(1)} %multiply_add_fusion.refs_5_.refs_6_), channel_id=1, source_target_pairs={{0,8},{8,0},{16,24},{24,16},{1,9},{9,1},{17,25},{25,17},{2,10},{10... | collective-permute-start | bytes 196616 | tf_op jit(solution)/shard_map/ppermute | solution.py:499
  29.5 10.9 %collective-permute-start.4 = (f32[256,128]{1,0:T(8,128)S(1)}, f32[256,128]{1,0:T(8,128)S(1)}, u32[]{:S(2)}, u32[]{:S(2)}) collective-permute-start(f32[256,128]{1,0:T(8,128)S(1)} %get-tuple-element.19), channel_id=1, source_target_pairs={{0,6},{2,0},{4,2},{6,4},{1,7},{3,1},{5,3},{7,5},{8,14},{10,8},{12,... | collective-permute-start | bytes 393224 | tf_op jit(solution)/shard_map/ppermute | solution.py:503
  30.0 12.5 %collective-permute-start.2 = (f32[256,128]{1,0:T(8,128)S(1)}, f32[256,128]{1,0:T(8,128)S(1)}, u32[]{:S(2)}, u32[]{:S(2)}) collective-permute-start(f32[256,128]{1,0:T(8,128)S(1)} %get-tuple-element.17), channel_id=1, source_target_pairs={{0,2},{2,4},{4,6},{6,0},{1,3},{3,5},{5,7},{7,1},{8,10},{10,12},{12... | collective-permute-start | bytes 393224 | tf_op jit(solution)/shard_map/ppermute | solution.py:503
  40.5 8.8 %collective-permute-start.5 = (f32[512,128]{1,0:T(8,128)S(1)}, f32[512,128]{1,0:T(8,128)S(1)}, u32[]{:S(2)}, u32[]{:S(2)}) collective-permute-start(f32[512,128]{1,0:T(8,128)S(1)} %pad_add_fusion), channel_id=1, source_target_pairs={{0,6},{2,0},{4,2},{6,4},{1,7},{3,1},{5,3},{7,5},{8,14},{10,8},{12,... | collective-permute-start | bytes 786440 | tf_op jit(solution)/shard_map/ppermute | solution.py:503
  42.6 15.2 %collective-permute-start.3 = (f32[512,128]{1,0:T(8,128)S(1)}, f32[512,128]{1,0:T(8,128)S(1)}, u32[]{:S(2)}, u32[]{:S(2)}) collective-permute-start(f32[512,128]{1,0:T(8,128)S(1)} %pad_add_fusion.1), channel_id=1, source_target_pairs={{0,2},{2,4},{4,6},{6,0},{1,3},{3,5},{5,7},{7,1},{8,10},{10,12},{12... | collective-permute-start | bytes 786440 | tf_op jit(solution)/shard_map/ppermute | solution.py:503
  42.8 6.4 %collective-permute-start.7 = (f32[1,128]{1,0:T(1,128)S(1)}, f32[1,128]{1,0:T(1,128)S(1)}, u32[]{:S(2)}, u32[]{:S(2)}) collective-permute-start(f32[1,128]{1,0:T(1,128)S(1)} %multiply_add_fusion.1.refs_3_.refs_6_), channel_id=1, source_target_pairs={{0,8},{8,0},{16,24},{24,16},{1,9},{9,1},{17,25},{25,17},{2,10},{10... | collective-permute-start | bytes 1544 | tf_op jit(solution)/shard_map/ppermute | solution.py:499
  49.2 46.6 %copy-start = (bf16[512,128]{1,0:T(8,128)(2,1)S(1)}, bf16[512,128]{1,0:T(8,128)(2,1)}, u32[]{:S(2)}) copy-start(bf16[512,128]{1,0:T(8,128)(2,1)} %ik_ref.1) | copy-start | bytes 393220
  64.6 36.4 %collective-permute-start.14 = (f32[512,128]{1,0:T(8,128)S(1)}, f32[512,128]{1,0:T(8,128)S(1)}, u32[]{:S(2)}, u32[]{:S(2)}) collective-permute-start(f32[512,128]{1,0:T(8,128)S(1)} %get-tuple-element.28), channel_id=1, source_target_pairs={{0,1},{1,0},{2,3},{3,2},{4,5},{5,4},{6,7},{7,6},{8,9},{9,8},{10,11... | collective-permute-start | bytes 786440 | tf_op jit(solution)/shard_map/ppermute | solution.py:499
  95.8 9.3 %collective-permute-start.8 = (f32[520,128]{1,0:T(8,128)S(1)}, f32[520,128]{1,0:T(8,128)S(1)}, u32[]{:S(2)}, u32[]{:S(2)}) collective-permute-start(f32[520,128]{1,0:T(8,128)S(1)} %get-tuple-element.23.refs_0_), channel_id=1, source_target_pairs={{0,16},{8,24},{16,0},{24,8},{1,17},{9,25},{17,1},{25,9},{2,18},{10... | collective-permute-start | bytes 798728 | tf_op jit(solution)/shard_map/ppermute | solution.py:499
  95.8 12.4 %collective-permute-start.10 = (f32[512,128]{1,0:T(8,128)S(1)}, f32[512,128]{1,0:T(8,128)S(1)}, u32[]{:S(2)}, u32[]{:S(2)}) collective-permute-start(f32[512,128]{1,0:T(8,128)S(1)} %convert_element_type.7.refs_2_), channel_id=1, source_target_pairs={{0,16},{8,24},{16,0},{24,8},{1,17},{9,25},{17,1},{25,9},{2,18},{10... | collective-permute-start | bytes 786440 | tf_op jit(solution)/shard_map/ppermute | solution.py:499
  101.0 7.1 %collective-permute-start.15 = (f32[512,128]{1,0:T(8,128)S(1)}, f32[512,128]{1,0:T(8,128)S(1)}, u32[]{:S(2)}, u32[]{:S(2)}) collective-permute-start(f32[512,128]{1,0:T(8,128)S(1)} %add.62), channel_id=1, source_target_pairs={{0,2},{2,0},{4,6},{6,4},{1,3},{3,1},{5,7},{7,5},{8,10},{10,8},{12,... | collective-permute-start | bytes 786440 | tf_op jit(solution)/shard_map/ppermute | solution.py:499
  101.6 6.7 %collective-permute-start.12 = (f32[520,128]{1,0:T(8,128)S(1)}, f32[520,128]{1,0:T(8,128)S(1)}, u32[]{:S(2)}, u32[]{:S(2)}) collective-permute-start(f32[520,128]{1,0:T(8,128)S(1)} %get-tuple-element.23.refs_0_), channel_id=1, source_target_pairs={{0,8},{8,0},{16,24},{24,16},{1,9},{9,1},{17,25},{25,17},{2,10},{10... | collective-permute-start | bytes 798728 | tf_op jit(solution)/shard_map/ppermute | solution.py:499
  101.6 6.7 %collective-permute-start.13 = (f32[512,128]{1,0:T(8,128)S(1)}, f32[512,128]{1,0:T(8,128)S(1)}, u32[]{:S(2)}, u32[]{:S(2)}) collective-permute-start(f32[512,128]{1,0:T(8,128)S(1)} %convert_element_type.7.refs_2_), channel_id=1, source_target_pairs={{0,8},{8,0},{16,24},{24,16},{1,9},{9,1},{17,25},{25,17},{2,10},{10... | collective-permute-start | bytes 786440 | tf_op jit(solution)/shard_map/ppermute | solution.py:499
  105.0 7.1 %collective-permute-start.9 = (f32[520,128]{1,0:T(8,128)S(1)}, f32[520,128]{1,0:T(8,128)S(1)}, u32[]{:S(2)}, u32[]{:S(2)}) collective-permute-start(f32[520,128]{1,0:T(8,128)S(1)} %collective-permute-done.8.refs_0_), channel_id=1, source_target_pairs={{0,8},{8,0},{16,24},{24,16},{1,9},{9,1},{17,25},{25,17},{2,10},{10... | collective-permute-start | bytes 798728 | tf_op jit(solution)/shard_map/ppermute | solution.py:499
  108.2 4.0 %collective-permute-start.11 = (f32[512,128]{1,0:T(8,128)S(1)}, f32[512,128]{1,0:T(8,128)S(1)}, u32[]{:S(2)}, u32[]{:S(2)}) collective-permute-start(f32[512,128]{1,0:T(8,128)S(1)} %collective-permute-done.10.refs_2_), channel_id=1, source_target_pairs={{0,8},{8,0},{16,24},{24,16},{1,9},{9,1},{17,25},{25,17},{2,10},{10... | collective-permute-start | bytes 786440 | tf_op jit(solution)/shard_map/ppermute | solution.py:499
  108.2 14.4 %collective-permute-start.16 = (f32[512,128]{1,0:T(8,128)S(1)}, f32[512,128]{1,0:T(8,128)S(1)}, u32[]{:S(2)}, u32[]{:S(2)}) collective-permute-start(f32[512,128]{1,0:T(8,128)S(1)} %add.63), channel_id=1, source_target_pairs={{0,6},{2,4},{4,2},{6,0},{1,7},{3,5},{5,3},{7,1},{8,14},{10,12},{12... | collective-permute-start | bytes 786440 | tf_op jit(solution)/shard_map/ppermute | solution.py:499

commit v4 on v3

v4 whole, which is shorter than its diff:
```python
import functools
import math
import jax
import jax.numpy as jnp
from jax import lax
from jax.experimental import pallas as pl
from jax.experimental.pallas import tpu as pltpu
from jax.sharding import PartitionSpec as P


H = 128
DNOPE = 128
DROPE = 64
ID = 128
KBLOCK = 32
DQK = 192
LANES = 128
PAIR = 2 * DQK
NEG = -1e30
SMALL = 2.0**-90
LARGE = 2.0**100
BIG = 2**30
LOG2E = math.log2(math.e)
SCALE_MAIN = DQK ** (-0.5) * LOG2E
SCALE_INDEX = ID ** (-0.5)

f32 = jnp.float32
bf16 = jnp.bfloat16
IN_VMEM = pl.BlockSpec(memory_space=pltpu.VMEM)


def dot_nt(a, b):
    return lax.dot_general(a, b, (((1,), (1,)), ((), ())), preferred_element_type=f32)


def dot_nn(a, b):
    return lax.dot_general(a, b, (((1,), (0,)), ((), ())), preferred_element_type=f32)


def cost(flops, bytes_accessed, transcendentals=0):
    return pl.CostEstimate(
        flops=int(flops), bytes_accessed=int(bytes_accessed), transcendentals=int(transcendentals)
    )


def combine_lse(parts):
    if len(parts) == 1:
        return parts[0]
    top = functools.reduce(jnp.maximum, parts)
    return top + jnp.log2(functools.reduce(jnp.add, [jnp.exp2(p - top) for p in parts]))


def key_limit_column(count_ref, row, keys):
    lane = lax.broadcasted_iota(jnp.int32, (1, keys), 1)
    block = lane // KBLOCK
    limit = jnp.zeros((1, keys), jnp.int32)
    for b in range(keys // KBLOCK):
        limit = jnp.where(block == b, count_ref[b], limit)
    live = (lane % KBLOCK) < limit
    row = jnp.where(live, row, BIG)
    return jnp.transpose(jnp.broadcast_to(row, (8, keys)))[:, :1]


def main_keys(nope, parity, even_ref, odd_ref):
    if parity == 0:
        return jnp.concatenate([nope, even_ref[...]], axis=1)
    turned = jnp.concatenate([nope[:, DROPE:], nope[:, :DROPE]], axis=1)
    low = lax.broadcasted_iota(jnp.int32, turned.shape, 1) < DROPE
    first = jnp.where(low, jnp.zeros_like(turned), turned)
    second = jnp.where(low, turned, odd_ref[...])
    return jnp.concatenate([first, second], axis=1)


def lanes_at(index, width):
    return pl.ds(pl.multiple_of(index * width, LANES), width)


def stats_kernel(per, count_hbm, q_hbm, kn_hbm, rope_hbm, qpos_hbm, kpos_hbm,
                 lse_ref, q_ref, kk_ref, bias_ref,
                 kn_ref, rope_ref, qpos_ref, kpos_ref, even_ref, odd_ref, none_ref, bad_ref,
                 count_ref, small_sem, q_sem, kn_sem):
    keys = kn_ref.shape[0]
    groups, rows = q_ref.shape[0], q_ref.shape[1]
    pairs = q_ref.shape[2] // PAIR
    halves = [slice(2 * c * rows, (2 * c + 2) * rows) for c in range(groups // 2)]

    small = [
        pltpu.make_async_copy(src, dst, small_sem.at[i])
        for i, (src, dst) in enumerate(
            ((count_hbm, count_ref), (kpos_hbm, kpos_ref), (qpos_hbm, qpos_ref), (rope_hbm, rope_ref))
        )
    ]

    def large(i):
        q_at, k_at = lanes_at(i, PAIR), lanes_at(i, 2 * DNOPE)
        return (
            pltpu.make_async_copy(kn_hbm.at[:, k_at], kn_ref.at[:, k_at], kn_sem.at[i]),
            pltpu.make_async_copy(q_hbm.at[:, :, q_at], q_ref.at[:, :, q_at], q_sem.at[i]),
        )

    for copy in small:
        copy.start()
    for i in range(pairs):
        for copy in large(i):
            copy.start()
    for copy in small:
        copy.wait()

    rope = jnp.transpose(rope_ref[...].astype(f32)).astype(bf16)
    zero = jnp.zeros_like(rope)
    even_ref[...] = jnp.concatenate([rope, zero], axis=1)
    odd_ref[...] = jnp.concatenate([zero, rope], axis=1)
    column = key_limit_column(count_ref, kpos_ref[...], keys)
    for g in range(groups):
        valid = column <= qpos_ref[g : g + 1, :]
        bias = jnp.where(valid, 0.0, NEG)
        bias_ref[:, g * rows : (g + 1) * rows] = bias
        none_ref[:, g * rows : (g + 1) * rows] = jnp.where(
            jnp.max(bias, axis=0, keepdims=True) < 0, 1.0, 0.0
        )
    bad_ref[...] = jnp.zeros_like(bad_ref)

    def scores(kk, q3, c):
        q = q3.reshape(2 * rows, 2 * LANES)
        return dot_nt(kk, q) * SCALE_MAIN + bias_ref[:, halves[c]]

    def query(pair, a, c):
        at = pl.ds(pl.multiple_of(pair * PAIR + a * LANES, LANES), 2 * LANES)
        return q_ref[2 * c : 2 * c + 2, :, at]

    def step(i, carry):
        for p in range(per):
            pair = i * per + p
            for copy in large(pair):
                copy.wait()
        for p in range(per):
            pair = i * per + p
            for a in range(2):
                kk = main_keys(kn_ref[:, lanes_at(2 * pair + a, DNOPE)], a, even_ref, odd_ref)
                kk_ref[:, lanes_at(2 * pair + a, 2 * LANES)] = kk
                for c, cols in enumerate(halves):
                    s = scores(kk, query(pair, a, c), c)
                    total = jnp.sum(jnp.exp2(s), axis=0, keepdims=True)
                    fine = (total >= SMALL) & (total <= LARGE)
                    skip = none_ref[:, cols] > 0
                    bad_ref[:, cols] += jnp.where(fine | skip, 0.0, 1.0)
                    lse_ref[pl.ds(2 * pair + a, 1), cols] = jnp.where(skip, NEG, jnp.log2(total))
        return carry

    lax.fori_loop(0, pairs // per, step, 0)

    @pl.when(jnp.max(bad_ref[...]) > 0)
    def _():
        def again(pair, carry):
            for a in range(2):
                kk = kk_ref[:, lanes_at(2 * pair + a, 2 * LANES)]
                for c, cols in enumerate(halves):
                    s = scores(kk, query(pair, a, c), c)
                    top = jnp.max(s, axis=0, keepdims=True)
                    total = jnp.sum(jnp.exp2(s - top), axis=0, keepdims=True)
                    lse_ref[pl.ds(2 * pair + a, 1), cols] = top + jnp.log2(total)
            return carry

        lax.fori_loop(0, pairs, again, 0)


def main_stats(main_query, key_nope, rope_t, query_pos, key_pos, key_count):
    groups, rows, width = main_query.shape
    heads = width // DQK
    keys = key_nope.shape[0]
    total = groups * rows
    return pl.pallas_call(
        functools.partial(stats_kernel, 2),
        in_specs=[pl.BlockSpec(memory_space=pltpu.HBM)] * 6,
        out_specs=[IN_VMEM] * 4,
        out_shape=[
            jax.ShapeDtypeStruct((heads, total), f32),
            jax.ShapeDtypeStruct(main_query.shape, bf16),
            jax.ShapeDtypeStruct((keys, heads * 2 * LANES), bf16),
            jax.ShapeDtypeStruct((keys, total), f32),
        ],
        scratch_shapes=[
            pltpu.VMEM(key_nope.shape, bf16),
            pltpu.VMEM(rope_t.shape, bf16),
            pltpu.VMEM(query_pos.shape, jnp.int32),
            pltpu.VMEM(key_pos.shape, jnp.int32),
            pltpu.VMEM((keys, LANES), bf16),
            pltpu.VMEM((keys, LANES), bf16),
            pltpu.VMEM((1, total), f32),
            pltpu.VMEM((1, total), f32),
            pltpu.SMEM(key_count.shape, jnp.int32),
            pltpu.SemaphoreType.DMA((4,)),
            pltpu.SemaphoreType.DMA((heads // 2,)),
            pltpu.SemaphoreType.DMA((heads // 2,)),
        ],
        compiler_params=pltpu.CompilerParams(vmem_limit_bytes=16 * 1024 * 1024),
        cost_estimate=cost(
            heads * total * keys * 512, main_query.size * 2 + key_nope.size * 2, heads * total * keys
        ),
        name="main_stats",
    )(key_count, main_query, key_nope, rope_t, query_pos, key_pos)


def target_kernel(n_lse, shifts, per, parts, axis_size, q_ref, kk_ref, bias_ref, *refs):
    lse_refs = refs[:n_lse]
    out_refs = refs[n_lse:-1]
    glob_ref = refs[-1]
    n_groups = len(shifts)
    keys = kk_ref.shape[0]
    rows = q_ref.shape[1]
    pairs = q_ref.shape[2] // PAIR
    size = keys // parts
    me = lax.axis_index("head")
    ids = [lax.rem(me + shift, axis_size) for shift in shifts]
    tiles = [
        (g, slice(i * size, (i + 1) * size), out_refs[g * parts + i])
        for g in range(n_groups)
        for i in range(parts)
    ]
    for g in range(n_groups):
        at = lanes_at(ids[g], rows)
        glob_ref[:, g * rows : (g + 1) * rows] = combine_lse([r[:, at] for r in lse_refs])
    for ref in out_refs:
        ref[...] = jnp.zeros_like(ref)

    def step(i, carry):
        for p in range(per):
            pair = i * per + p
            acc = None
            for a in range(2):
                kk = kk_ref[:, lanes_at(2 * pair + a, 2 * LANES)]
                at = pl.ds(pl.multiple_of(pair * PAIR + a * LANES, LANES), 2 * LANES)
                qs = [q_ref[g, :, at] for g in ids]
                q = qs[0] if n_groups == 1 else jnp.concatenate(qs, axis=0)
                lse = glob_ref[pl.ds(2 * pair + a, 1), :]
                e = jnp.exp2(dot_nt(kk, q) * SCALE_MAIN - lse)
                acc = e if acc is None else acc + e
            for g, at, ref in tiles:
                ref[...] += acc[at, g * rows : (g + 1) * rows]
        return carry

    lax.fori_loop(0, pairs // per, step, 0)
    for g, at, ref in tiles:
        ref[...] = jnp.where(bias_ref[at, lanes_at(ids[g], rows)] < 0, 0.0, ref[...])


def head_sums(shifts, axis_size, q, kk, bias, lses, parts=1):
    _, rows, width = q.shape
    heads = width // DQK
    keys = kk.shape[0]
    n = len(shifts)
    return pl.pallas_call(
        functools.partial(target_kernel, len(lses), shifts, 4 // n, parts, axis_size),
        in_specs=[IN_VMEM] * (3 + len(lses)),
        out_specs=[IN_VMEM] * (n * parts),
        out_shape=[jax.ShapeDtypeStruct((keys // parts, rows), f32)] * (n * parts),
        scratch_shapes=[pltpu.VMEM((heads, n * rows), f32)],
        compiler_params=pltpu.CompilerParams(vmem_limit_bytes=16 * 1024 * 1024),
        cost_estimate=cost(
            heads * n * rows * keys * 512, heads * n * rows * keys // 16, heads * n * rows * keys
        ),
        name="head_sums",
    )(q, kk, bias, *lses)


def logits_kernel(per, iq_ref, ik_ref, wt_ref, bias_ref, logits_ref, lse_ref, wm_ref, w_ref):
    rows, width = iq_ref.shape
    w_ref[...] = wt_ref[...].astype(f32)
    logits_ref[...] = jnp.zeros_like(logits_ref)

    def step(i, carry):
        for p in range(per):
            first = 2 * (i * per + p)
            q = jnp.concatenate([iq_ref[:, lanes_at(first + a, ID)] for a in range(2)], axis=0)
            z = dot_nt(ik_ref[...], q)
            w = jnp.concatenate([w_ref[pl.ds(first + a, 1), :] for a in range(2)], axis=1)
            masked = jnp.where(z > 0, w, 0.0)
            wm_ref[:, lanes_at(i * per + p, 2 * rows)] = masked.astype(bf16)
            r = z * masked
            logits_ref[...] += r[:, :rows] + r[:, rows:]
        return carry

    lax.fori_loop(0, width // (2 * ID * per), step, 0)
    logits = logits_ref[...] * SCALE_INDEX
    logits_ref[...] = logits
    valid = bias_ref[:, lanes_at(lax.axis_index("head"), rows)] == 0
    s = jnp.where(valid, logits * LOG2E, NEG)
    top = jnp.max(s, axis=0, keepdims=True)
    lse_ref[...] = top + jnp.log2(jnp.sum(jnp.exp2(s - top), axis=0, keepdims=True))


def index_logits(index_query, index_key, weight_t, bias):
    rows, width = index_query.shape
    keys = index_key.shape[0]
    whole = lambda i: (0, 0)
    return pl.pallas_call(
        functools.partial(logits_kernel, 4),
        grid=(1,),
        in_specs=[
            IN_VMEM,
            pl.BlockSpec(index_key.shape, whole),
            pl.BlockSpec(weight_t.shape, whole),
            IN_VMEM,
        ],
        out_specs=[IN_VMEM] * 3,
        out_shape=[
            jax.ShapeDtypeStruct((keys, rows), f32),
            jax.ShapeDtypeStruct((1, rows), f32),
            jax.ShapeDtypeStruct((keys, (width // ID) * rows), bf16),
        ],
        scratch_shapes=[pltpu.VMEM((width // ID, rows), f32)],
        compiler_params=pltpu.CompilerParams(vmem_limit_bytes=16 * 1024 * 1024),
        cost_estimate=cost(2 * keys * rows * width, rows * width * 2 + keys * rows * width // ID * 2),
        name="index_logits",
    )(index_query, index_key, weight_t, bias)


def grad_key_kernel(n_parts, n_lse, per, *refs):
    parts = refs[:n_parts]
    lses = refs[n_parts : n_parts + n_lse]
    logits_ref, wm_ref, iq_ref, bias_ref, cot_ref, sg_ref, gk_ref = refs[n_parts + n_lse :]
    keys, rows = logits_ref.shape
    width = iq_ref.shape[1]

    valid = bias_ref[:, lanes_at(lax.axis_index("head"), rows)] == 0
    target = functools.reduce(jnp.add, [p[...] for p in parts]) * (1.0 / H)
    logits = logits_ref[...]
    lse2 = combine_lse([r[...] for r in lses])
    qprob = jnp.where(valid, jnp.exp2(logits * LOG2E - lse2), 0.0)
    sg_ref[:keys, :] = SCALE_INDEX * (cot_ref[...] * (qprob - target))
    live = target > 0
    terms = jnp.where(live, target * (jnp.log(jnp.where(live, target, 1.0)) - logits), 0.0)
    kl = jnp.sum(terms, axis=0, keepdims=True)
    sg_ref[keys:, :] = jnp.broadcast_to(kl, (8, rows))
    gk_ref[...] = jnp.zeros_like(gk_ref)

    def step(i, carry):
        for p in range(per):
            dz = []
            qs = []
            for a in range(2):
                j = 2 * (i * per + p) + a
                wm = wm_ref[:, lanes_at(j, rows)].astype(f32)
                dz.append((sg_ref[:keys, :] * wm).astype(bf16))
                qs.append(iq_ref[:, lanes_at(j, ID)])
            gk_ref[...] += dot_nn(jnp.concatenate(dz, axis=1), jnp.concatenate(qs, axis=0))
        return carry

    lax.fori_loop(0, width // (2 * ID * per), step, 0)


def index_grad_key(parts, lses, logits, wm, index_query, bias, cotangent):
    rows, width = index_query.shape
    keys = logits.shape[0]
    return pl.pallas_call(
        functools.partial(grad_key_kernel, len(parts), len(lses), 8),
        grid=(1,),
        in_specs=[IN_VMEM] * (len(parts) + len(lses) + 4)
        + [pl.BlockSpec((1, rows), lambda i: (0, 0))],
        out_specs=[IN_VMEM, IN_VMEM],
        out_shape=[
            jax.ShapeDtypeStruct((keys + 8, rows), f32),
            jax.ShapeDtypeStruct((keys, ID), f32),
        ],
        compiler_params=pltpu.CompilerParams(vmem_limit_bytes=16 * 1024 * 1024),
        cost_estimate=cost(2 * keys * rows * width, rows * width * 2 + keys * rows * width // ID * 2),
        name="index_grad_key",
    )(*parts, *lses, logits, wm, index_query, bias, cotangent)


def grad_query_kernel(n_shards, first, n_lse, *refs):
    sgs = refs[:n_shards]
    iks = refs[n_shards : 2 * n_shards]
    iq_ref, w_ref = refs[2 * n_shards : 2 * n_shards + 2]
    rest = refs[2 * n_shards + 2 :]
    lses = rest[:n_lse]
    rest = rest[n_lse:]
    if first:
        gq_ref, kl_ref, ws_ref = rest
    else:
        gq_in_ref, kl_in_ref, gq_ref, kl_ref, ws_ref = rest
    rows = iq_ref.shape[0]
    heads = gq_ref.shape[1] // ID
    keys = iks[0].shape[0]
    base = lax.axis_index("key") * heads
    ws_ref[...] = w_ref[...].astype(f32)
    mine = ws_ref[pl.ds(base, heads), :]
    ws = jnp.transpose(jnp.concatenate([mine, jnp.zeros((LANES - heads, rows), f32)], axis=0))
    kl = functools.reduce(jnp.add, [s[keys : keys + 1, :] for s in sgs])
    kl = kl if first else kl_in_ref[...] + kl
    if n_lse:
        kl = kl + combine_lse([r[...] for r in lses]) * (1.0 / LOG2E)
    kl_ref[...] = kl
    unit = min(heads, 4)
    iks = [ref[...].astype(bf16) for ref in iks]
    sgts = [jnp.transpose(ref[:keys, :]) for ref in sgs]
    for start in range(0, heads, unit):
        js = range(start, start + unit)
        iq = jnp.concatenate([iq_ref[:, lanes_at(base + j, ID)] for j in js], axis=0)
        out = None
        for ik, sgt in zip(iks, sgts):
            z = dot_nt(iq, ik)
            dz = jnp.concatenate(
                [
                    jnp.where(z[i * rows : (i + 1) * rows] > 0, sgt * ws[:, j : j + 1], 0.0).astype(bf16)
                    for i, j in enumerate(js)
                ],
                axis=0,
            )
            g = dot_nn(dz, ik)
            out = g if out is None else out + g
        for i, j in enumerate(js):
            cols = slice(j * ID, (j + 1) * ID)
            g = out[i * rows : (i + 1) * rows]
            gq_ref[:, cols] = g if first else gq_in_ref[:, cols] + g


def index_grad_query(n_slots, sgs, iks, index_query, weight_t, lses, carry):
    rows, width = index_query.shape
    heads = width // ID
    mine = width // n_slots
    keys = iks[0].shape[0]
    first = carry is None
    carried = [] if first else list(carry)
    n = len(sgs)
    return pl.pallas_call(
        functools.partial(grad_query_kernel, n, first, len(lses)),
        grid=(1,),
        in_specs=[IN_VMEM] * (2 * n + 1)
        + [pl.BlockSpec(weight_t.shape, lambda i: (0, 0))]
        + [IN_VMEM] * (len(lses) + len(carried)),
        out_specs=[IN_VMEM, IN_VMEM],
        out_shape=[
            jax.ShapeDtypeStruct((rows, mine), f32),
            jax.ShapeDtypeStruct((1, rows), f32),
        ],
        scratch_shapes=[pltpu.VMEM((heads, rows), f32)],
        compiler_params=pltpu.CompilerParams(vmem_limit_bytes=20 * 1024 * 1024),
        cost_estimate=cost(4 * n * keys * rows * mine, n * (keys * ID * 8) + rows * mine * 8),
        name="index_grad_query",
    )(*sgs, *iks, index_query, weight_t, *lses, *carried)


def swap(value, axis, mask, size):
    return lax.ppermute(value, axis, [(i, i ^ mask) for i in range(size)])


def rotate(value, axis, by, size):
    return lax.ppermute(value, axis, [(i, (i + by) % size) for i in range(size)])


def butterfly_lse(value, size):
    pair = [value]
    for bit in reversed(range(size.bit_length() - 1)):
        here = combine_lse(pair)
        pair = [here, swap(here, "key", 1 << bit, size)]
    return pair


def summed_copies(value, n_head, n_query):
    steps = [("query", 1 << b, n_query) for b in range(n_query.bit_length() - 1)]
    steps += [("head", (2 << b) - 1, n_head) for b in range(n_head.bit_length() - 1)]
    for axis, mask, size in steps:
        value = value + swap(value, axis, mask, size)
    return value


def in_hbm(*values):
    return tuple(pltpu.with_memory_space_constraint(v, pltpu.HBM) for v in values)


def body(n_key, n_head, n_query, main_query, key_nope, key_rope, query_pos, key_pos, key_count,
         index_query, index_key, index_weight, row_cotangent):
    groups, rows, _ = main_query.shape
    keys = key_nope.shape[0]
    main_query, key_nope, rope_t, query_pos, key_row, key_count, weight_t, cotangent, narrow = in_hbm(
        main_query, key_nope, key_rope.T, query_pos, key_pos.reshape(1, keys), key_count,
        index_weight.T, row_cotangent.reshape(1, rows), index_key,
    )

    def gathered(value):
        if n_key == 4:
            near = swap(value, "key", 1, n_key)
            far = swap(value, "key", 2, n_key)
            across = swap(far, "key", 1, n_key)
            return [value, near, far, across]
        return list(lax.all_gather(value, "key"))

    lse, q, kk, bias = main_stats(main_query, key_nope, rope_t, query_pos, key_row, key_count)
    lses = butterfly_lse(lse, n_key)
    logits, index_lse, wm = index_logits(index_query, narrow, weight_t, bias)
    index_lses = butterfly_lse(index_lse, n_key)
    iks = gathered(index_key.astype(f32))

    if n_head == 4 and groups == 4:
        low, high = head_sums([2], 4, q, kk, bias, lses, parts=2)
        half = keys // 2
        low = rotate(low, "head", 1, 4)
        high = rotate(high, "head", 3, 4)
        up, down = head_sums([1, 3], 4, q, kk, bias, lses)
        up = up + jnp.pad(low, ((0, half), (0, 0)))
        down = down + jnp.pad(high, ((half, 0), (0, 0)))
        from_below = rotate(up, "head", 1, 4)
        from_above = rotate(down, "head", 3, 4)
        own = head_sums([0], 4, q, kk, bias, lses)[0]
        parts = [own, from_below, from_above]
    else:
        tiles = jnp.stack([head_sums([g], groups, q, kk, bias, lses)[0] for g in range(groups)])
        tiles = jnp.roll(tiles, lax.axis_index("head"), axis=0)
        parts = [lax.psum_scatter(tiles, "head", scatter_dimension=0, tiled=True)[0]]

    sg, grad_key = index_grad_key(parts, index_lses, logits, wm, index_query, bias, cotangent)
    grad_key = summed_copies(grad_key, n_head, n_query)
    sgs = gathered(sg)
    carry = None
    for lo in range(0, n_key, 2):
        last = lo + 2 >= n_key
        carry = index_grad_query(
            n_key, sgs[lo : lo + 2], iks[lo : lo + 2], index_query, weight_t,
            index_lses if last else [], carry,
        )
    grad_query, kl = carry
    return kl.reshape(rows), grad_query, grad_key


def solution(mesh):
    sizes = (mesh.shape["key"], mesh.shape["head"], mesh.shape["query"])

    def step(*args):
        return body(*sizes, *args)

    return jax.shard_map(
        step,
        mesh=mesh,
        in_specs=(
            P(None, "query", "head"),
            P("key", "head"),
            P("key", None),
            P(None, "query"),
            P("key"),
            P("key"),
            P(("head", "query"), None),
            P("key", None),
            P(("head", "query"), None),
            P(("head", "query")),
        ),
        out_specs=(P(("head", "query")), P(("head", "query"), "key"), P("key", None)),
        check_vma=False,
    )
```

time: 124 us -> 98.5 us (0.79)
  the two profiles are of different devices: /device:TPU:10 before, /device:TPU:8 now
where the time goes in v4:
time: 98.5 us; the launch traced here: 98.2 us
  Pallas kernels  40.2 us (41%)
  waiting for transfers between devices  29.7 us (30%)
  starting transfers between devices  26.5 us (27%)
    ppermute x13, starting transfers between devices, swap(): return lax.ppermute(value, axis, [(i, i ^ mask) for i in range(size)])  22.1 us
    ppermute x13, waiting for transfers between devices, swap(): return lax.ppermute(value, axis, [(i, i ^ mask) for i in range(size)])  17.9 us
    pallas_call x1, Pallas kernels, main_stats(): pl.pallas_call(functools.partial(stats_kernel, 2), in_specs=[pl.BlockSpec...  12.4 us
    ppermute x4, waiting for transfers between devices, rotate(): lax.ppermute(value, axis, [(i, (i + by) % size) for i in range(size)])  11.9 us
    pallas_call x3, Pallas kernels, head_sums(): pl.pallas_call(functools.partial(target_kernel, len(lses), shifts, 4 // n...  10.4 us
    pallas_call x2, Pallas kernels, index_grad_query(): pl.pallas_call(functools.partial(grad_query_kernel, n, first, len(lses)),...  7.57 us
    pallas_call x1, Pallas kernels, index_logits(): pl.pallas_call(functools.partial(logits_kernel, 4), grid=(1,), in_specs=[...  5.44 us
    ppermute x4, starting transfers between devices, rotate(): lax.ppermute(value, axis, [(i, (i + by) % size) for i in range(size)])  4.39 us
  transfers between devices with their start and end apart: 17, of which 8 were waited for; matrix products, arithmetic and copies ran while one was open for 0% of the time, Pallas kernels for 24%

profile of v4, /device:TPU:8, one launch (start us, length us, event | category | flops | bytes accessed | tf_op | source)
XLA Modules:
  0.0 98.2 jit_solution(15326330215898232106)
XLA Ops:
  0.6 12.4 %main_stats.1 = (f32[32,512]{1,0:T(8,128)S(1)}, bf16[4,128,6144]{2,1,0:T(8,128)(2,1)S(1)}, bf16[512,8192]{1,0:T(8,128)(2,1)S(1)}, f32[512,512]{1,0:T(8,128)S(1)}) custom-call(s32[16]{0:T(128)} %count_hbm.1, bf16[4,128,6144]{2,1,0:T(8,128)(2,1)} %q_hbm.1, bf16[512,4096]{1,0:T(8,128)(2,1)} %kn_hbm.1, bf16[64,512]{1,0:T(8,128)(2,1)} %bitcast.9, ...), custom_call_target="tpu_custom_call" | custom-call | flops 4294967296 | bytes 10485760 | tf_op jit(solution)/shard_map/main_stats/pallas_call | solution.py:172
  13.1 1.6 %collective-permute-start = (f32[32,512]{1,0:T(8,128)S(1)}, f32[32,512]{1,0:T(8,128)S(1)}, u32[]{:S(2)}, u32[]{:S(2)}) collective-permute-start(f32[32,512]{1,0:T(8,128)S(1)} %get-tuple-element.23), channel_id=1, source_target_pairs={{0,16},{8,24},{16,0},{24,8},{1,17},{9,25},{17,1},{25,9},{2,18},{10... | collective-permute-start | bytes 196616 | tf_op jit(solution)/shard_map/ppermute | solution.py:445
  14.6 2.8 %collective-permute-done = f32[32,512]{1,0:T(8,128)S(1)} collective-permute-done((f32[32,512]{1,0:T(8,128)S(1)}, f32[32,512]{1,0:T(8,128)S(1)}, u32[]{:S(2)}, u32[]{:S(2)}) %collective-permute-start) | collective-permute-done | bytes 65568 | tf_op jit(solution)/shard_map/ppermute | solution.py:445
  17.4 0.1 collective-permute-start.1
  17.5 5.4 %index_logits.1 = (f32[512,128]{1,0:T(8,128)S(1)}, f32[1,128]{1,0:T(1,128)S(1)}, bf16[512,8192]{1,0:T(8,128)(2,1)S(1)}) custom-call(bf16[128,8192]{1,0:T(8,128)(2,1)S(1)} %copy-done, bf16[512,128]{1,0:T(8,128)(2,1)} %ik_ref.1, bf16[64,128]{1,0:T(8,128)(2,1)} %bitcast.5, f32[512,512]{1,0:T(8,128)S(1)} %get-tuple-element.22.bias_ref.refs_8_), custom_call_target="tpu_custom_call" | custom-call | flops 1073741824 | bytes 10485760 | tf_op jit(solution)/shard_map/index_logits/pallas_call | solution.py:296
  23.0 1.6 %collective-permute-start.6 = (f32[1,128]{1,0:T(1,128)S(1)}, f32[1,128]{1,0:T(1,128)S(1)}, u32[]{:S(2)}, u32[]{:S(2)}) collective-permute-start(f32[1,128]{1,0:T(1,128)S(1)} %get-tuple-element.28), channel_id=1, source_target_pairs={{0,16},{8,24},{16,0},{24,8},{1,17},{9,25},{17,1},{25,9},{2,18},{10... | collective-permute-start | bytes 1544 | tf_op jit(solution)/shard_map/ppermute | solution.py:445
  24.5 3.1 %head_sums.5 = (f32[256,128]{1,0:T(8,128)S(1)}, f32[256,128]{1,0:T(8,128)S(1)}) custom-call(bf16[4,128,6144]{2,1,0:T(8,128)(2,1)S(1)} %get-tuple-element.20.q_ref, bf16[512,8192]{1,0:T(8,128)(2,1)S(1)} %get-tuple-element.21.kk_ref, f32[512,512]{1,0:T(8,128)S(1)} %get-tuple-element.22.bias_ref.refs_8_, f32[32,512]{1,0:T(8,128)S(1)} %multiply_add_fusion.refs_0_, ...), custom_call_target="tpu_custom_call" | custom-call | flops 1073741824 | bytes 131072 | tf_op jit(solution)/shard_map/head_sums/pallas_call | solution.py:252
  27.6 0.5 collective-permute-start.4
  28.1 1.6 %collective-permute-start.2 = (f32[256,128]{1,0:T(8,128)S(1)}, f32[256,128]{1,0:T(8,128)S(1)}, u32[]{:S(2)}, u32[]{:S(2)}) collective-permute-start(f32[256,128]{1,0:T(8,128)S(1)} %get-tuple-element.25), channel_id=1, source_target_pairs={{0,2},{2,4},{4,6},{6,0},{1,3},{3,5},{5,7},{7,1},{8,10},{10,12},{12... | collective-permute-start | bytes 393224 | tf_op jit(solution)/shard_map/ppermute | solution.py:449
  29.7 4.3 %head_sums.4 = (f32[512,128]{1,0:T(8,128)S(1)}, f32[512,128]{1,0:T(8,128)S(1)}) custom-call(bf16[4,128,6144]{2,1,0:T(8,128)(2,1)S(1)} %get-tuple-element.20.q_ref, bf16[512,8192]{1,0:T(8,128)(2,1)S(1)} %get-tuple-element.21.kk_ref, f32[512,512]{1,0:T(8,128)S(1)} %get-tuple-element.22.bias_ref.refs_8_, f32[32,512]{1,0:T(8,128)S(1)} %multiply_add_fusion.refs_0_, ...), custom_call_target="tpu_custom_call" | custom-call | flops 2147483648 | bytes 262144 | tf_op jit(solution)/shard_map/head_sums/pallas_call | solution.py:252
  34.0 0.0 collective-permute-done.4
  34.0 2.1 %collective-permute-start.5 = (f32[512,128]{1,0:T(8,128)S(1)}, f32[512,128]{1,0:T(8,128)S(1)}, u32[]{:S(2)}, u32[]{:S(2)}) collective-permute-start(f32[512,128]{1,0:T(8,128)S(1)} %pad_add_fusion), channel_id=1, source_target_pairs={{0,6},{2,0},{4,2},{6,4},{1,7},{3,1},{5,3},{7,5},{8,14},{10,8},{12,... | collective-permute-start | bytes 786440 | tf_op jit(solution)/shard_map/ppermute | solution.py:449
  36.1 2.1 %collective-permute-done.2 = f32[256,128]{1,0:T(8,128)S(1)} collective-permute-done((f32[256,128]{1,0:T(8,128)S(1)}, f32[256,128]{1,0:T(8,128)S(1)}, u32[]{:S(2)}, u32[]{:S(2)}) %collective-permute-start.2) | collective-permute-done | bytes 131104 | tf_op jit(solution)/shard_map/ppermute | solution.py:449
  38.2 0.2 collective-permute-start.3
  38.4 0.1 collective-permute-start.7
  38.5 3.1 %head_sums.3.refs_0_ = f32[512,128]{1,0:T(8,128)S(1)} custom-call(bf16[4,128,6144]{2,1,0:T(8,128)(2,1)S(1)} %get-tuple-element.20.q_ref, bf16[512,8192]{1,0:T(8,128)(2,1)S(1)} %get-tuple-element.21.kk_ref, f32[512,512]{1,0:T(8,128)S(1)} %get-tuple-element.22.bias_ref.refs_8_, f32[32,512]{1,0:T(8,128)S(1)} %multiply_add_fusion.refs_0_, ...), custom_call_target="tpu_custom_call" | custom-call | flops 1073741824 | bytes 131072 | tf_op jit(solution)/shard_map/head_sums/pallas_call | solution.py:252
  41.6 1.4 %collective-permute-done.5.refs_2_ = f32[512,128]{1,0:T(8,128)S(1)} collective-permute-done((f32[512,128]{1,0:T(8,128)S(1)}, f32[512,128]{1,0:T(8,128)S(1)}, u32[]{:S(2)}, u32[]{:S(2)}) %collective-permute-start.5) | collective-permute-done | bytes 262176 | tf_op jit(solution)/shard_map/ppermute | solution.py:449
  43.0 8.4 %collective-permute-done.3.refs_1_ = f32[512,128]{1,0:T(8,128)S(1)} collective-permute-done((f32[512,128]{1,0:T(8,128)S(1)}, f32[512,128]{1,0:T(8,128)S(1)}, u32[]{:S(2)}, u32[]{:S(2)}) %collective-permute-start.3) | collective-permute-done | bytes 262176 | tf_op jit(solution)/shard_map/ppermute | solution.py:449
  51.4 4.3 %index_grad_key.1 = (f32[520,128]{1,0:T(8,128)S(1)}, f32[512,128]{1,0:T(8,128)S(1)}) custom-call(f32[512,128]{1,0:T(8,128)S(1)} %head_sums.3.refs_0_, f32[512,128]{1,0:T(8,128)S(1)} %collective-permute-done.3.refs_1_, f32[512,128]{1,0:T(8,128)S(1)} %collective-permute-done.5.refs_2_, f32[1,128]{1,0:T(1,128)S(1)} %multiply_add_fusion.1.refs_3_.refs_6_, ...), custom_call_target="tpu_custom_call" | custom-call | flops 1073741824 | bytes 10485760 | tf_op jit(solution)/shard_map/index_grad_key/pallas_call | solution.py:355
  55.8 14.8 %collective-permute-start.14 = (f32[512,128]{1,0:T(8,128)S(1)}, f32[512,128]{1,0:T(8,128)S(1)}, u32[]{:S(2)}, u32[]{:S(2)}) collective-permute-start(f32[512,128]{1,0:T(8,128)S(1)} %get-tuple-element.36), channel_id=1, source_target_pairs={{0,1},{1,0},{2,3},{3,2},{4,5},{5,4},{6,7},{7,6},{8,9},{9,8},{10,11... | collective-permute-start | bytes 786440 | tf_op jit(solution)/shard_map/ppermute | solution.py:445
  70.6 0.3 collective-permute-start.8
  70.9 1.8 %collective-permute-start.10 = (f32[512,128]{1,0:T(8,128)S(1)}, f32[512,128]{1,0:T(8,128)S(1)}, u32[]{:S(2)}, u32[]{:S(2)}) collective-permute-start(f32[512,128]{1,0:T(8,128)S(1)} %convert_element_type.7.refs_2_), channel_id=1, source_target_pairs={{0,16},{8,24},{16,0},{24,8},{1,17},{9,25},{17,1},{25,9},{2,18},{10... | collective-permute-start | bytes 786440 | tf_op jit(solution)/shard_map/ppermute | solution.py:445
  72.7 3.1 %collective-permute-done.14 = f32[512,128]{1,0:T(8,128)S(1)} collective-permute-done((f32[512,128]{1,0:T(8,128)S(1)}, f32[512,128]{1,0:T(8,128)S(1)}, u32[]{:S(2)}, u32[]{:S(2)}) %collective-permute-start.14) | collective-permute-done | bytes 262176 | tf_op jit(solution)/shard_map/ppermute | solution.py:445
  75.9 0.5 collective-permute-start.15
  76.4 0.5 collective-permute-start.13
  76.9 3.0 %collective-permute-done.8.refs_0_ = f32[520,128]{1,0:T(8,128)S(1)} collective-permute-done((f32[520,128]{1,0:T(8,128)S(1)}, f32[520,128]{1,0:T(8,128)S(1)}, u32[]{:S(2)}, u32[]{:S(2)}) %collective-permute-start.8) | collective-permute-done | bytes 266272 | tf_op jit(solution)/shard_map/ppermute | solution.py:445
  79.9 3.1 %collective-permute-done.10.refs_2_ = f32[512,128]{1,0:T(8,128)S(1)} collective-permute-done((f32[512,128]{1,0:T(8,128)S(1)}, f32[512,128]{1,0:T(8,128)S(1)}, u32[]{:S(2)}, u32[]{:S(2)}) %collective-permute-start.10) | collective-permute-done | bytes 262176 | tf_op jit(solution)/shard_map/ppermute | solution.py:445
  83.0 0.9 collective-permute-start.16
  83.9 3.5 %index_grad_query.2 = (f32[128,2048]{1,0:T(8,128)S(1)}, f32[1,128]{1,0:T(1,128)S(1)}) custom-call(f32[520,128]{1,0:T(8,128)S(1)} %get-tuple-element.31.refs_0_, f32[520,128]{1,0:T(8,128)S(1)} %collective-permute-done.12.refs_1_, f32[512,128]{1,0:T(8,128)S(1)} %convert_element_type.7.refs_2_, f32[512,128]{1,0:T(8,128)S(1)} %collective-permute-done.13.refs_3_, ...), custom_call_target="tpu_custom_call" | custom-call | flops 1073741824 | bytes 3145728 | tf_op jit(solution)/shard_map/index_grad_query/pallas_call | solution.py:426
  87.4 4.1 %index_grad_query.3 = (f32[128,2048]{1,0:T(8,128)}, f32[1,128]{1,0:T(1,128)}) custom-call(f32[520,128]{1,0:T(8,128)S(1)} %collective-permute-done.8.refs_0_, f32[520,128]{1,0:T(8,128)S(1)} %collective-permute-done.9.refs_1_, f32[512,128]{1,0:T(8,128)S(1)} %collective-permute-done.10.refs_2_, f32[512,128]{1,0:T(8,128)S(1)} %collective-permute-done.11.refs_3_, ...), custom_call_target="tpu_custom_call" | custom-call | flops 1073741824 | bytes 3145728 | tf_op jit(solution)/shard_map/index_grad_query/pallas_call | solution.py:426
  91.5 5.9 %collective-permute-done.16 = f32[512,128]{1,0:T(8,128)S(1)} collective-permute-done((f32[512,128]{1,0:T(8,128)S(1)}, f32[512,128]{1,0:T(8,128)S(1)}, u32[]{:S(2)}, u32[]{:S(2)}) %collective-permute-start.16) | collective-permute-done | bytes 262176 | tf_op jit(solution)/shard_map/ppermute | solution.py:445
  97.4 0.7 add.39
  (22 shorter events, 0.2 us)
Async XLA Ops:
  0.6 16.9 %copy-start = (bf16[128,8192]{1,0:T(8,128)(2,1)S(1)}, bf16[128,8192]{1,0:T(8,128)(2,1)}, u32[]{:S(2)}) copy-start(bf16[128,8192]{1,0:T(8,128)(2,1)} %refs_4_.3) | copy-start | bytes 6291460
  13.1 4.3 %collective-permute-start = (f32[32,512]{1,0:T(8,128)S(1)}, f32[32,512]{1,0:T(8,128)S(1)}, u32[]{:S(2)}, u32[]{:S(2)}) collective-permute-start(f32[32,512]{1,0:T(8,128)S(1)} %get-tuple-element.23), channel_id=1, source_target_pairs={{0,16},{8,24},{16,0},{24,8},{1,17},{9,25},{17,1},{25,9},{2,18},{10... | collective-permute-start | bytes 196616 | tf_op jit(solution)/shard_map/ppermute | solution.py:445
  17.4 7.1 %collective-permute-start.1 = (f32[32,512]{1,0:T(8,128)S(1)}, f32[32,512]{1,0:T(8,128)S(1)}, u32[]{:S(2)}, u32[]{:S(2)}) collective-permute-start(f32[32,512]{1,0:T(8,128)S(1)} %multiply_add_fusion.refs_0_), channel_id=1, source_target_pairs={{0,8},{8,0},{16,24},{24,16},{1,9},{9,1},{17,25},{25,17},{2,10},{10... | collective-permute-start | bytes 196616 | tf_op jit(solution)/shard_map/ppermute | solution.py:445
  23.0 15.4 %collective-permute-start.6 = (f32[1,128]{1,0:T(1,128)S(1)}, f32[1,128]{1,0:T(1,128)S(1)}, u32[]{:S(2)}, u32[]{:S(2)}) collective-permute-start(f32[1,128]{1,0:T(1,128)S(1)} %get-tuple-element.28), channel_id=1, source_target_pairs={{0,16},{8,24},{16,0},{24,8},{1,17},{9,25},{17,1},{25,9},{2,18},{10... | collective-permute-start | bytes 1544 | tf_op jit(solution)/shard_map/ppermute | solution.py:445
  27.6 6.4 %collective-permute-start.4 = (f32[256,128]{1,0:T(8,128)S(1)}, f32[256,128]{1,0:T(8,128)S(1)}, u32[]{:S(2)}, u32[]{:S(2)}) collective-permute-start(f32[256,128]{1,0:T(8,128)S(1)} %get-tuple-element.27), channel_id=1, source_target_pairs={{0,6},{2,0},{4,2},{6,4},{1,7},{3,1},{5,3},{7,5},{8,14},{10,8},{12,... | collective-permute-start | bytes 393224 | tf_op jit(solution)/shard_map/ppermute | solution.py:449
  28.1 10.0 %collective-permute-start.2 = (f32[256,128]{1,0:T(8,128)S(1)}, f32[256,128]{1,0:T(8,128)S(1)}, u32[]{:S(2)}, u32[]{:S(2)}) collective-permute-start(f32[256,128]{1,0:T(8,128)S(1)} %get-tuple-element.25), channel_id=1, source_target_pairs={{0,2},{2,4},{4,6},{6,0},{1,3},{3,5},{5,7},{7,1},{8,10},{10,12},{12... | collective-permute-start | bytes 393224 | tf_op jit(solution)/shard_map/ppermute | solution.py:449
  34.0 9.0 %collective-permute-start.5 = (f32[512,128]{1,0:T(8,128)S(1)}, f32[512,128]{1,0:T(8,128)S(1)}, u32[]{:S(2)}, u32[]{:S(2)}) collective-permute-start(f32[512,128]{1,0:T(8,128)S(1)} %pad_add_fusion), channel_id=1, source_target_pairs={{0,6},{2,0},{4,2},{6,4},{1,7},{3,1},{5,3},{7,5},{8,14},{10,8},{12,... | collective-permute-start | bytes 786440 | tf_op jit(solution)/shard_map/ppermute | solution.py:449
  38.2 13.2 %collective-permute-start.3 = (f32[512,128]{1,0:T(8,128)S(1)}, f32[512,128]{1,0:T(8,128)S(1)}, u32[]{:S(2)}, u32[]{:S(2)}) collective-permute-start(f32[512,128]{1,0:T(8,128)S(1)} %pad_add_fusion.1), channel_id=1, source_target_pairs={{0,2},{2,4},{4,6},{6,0},{1,3},{3,5},{5,7},{7,1},{8,10},{10,12},{12... | collective-permute-start | bytes 786440 | tf_op jit(solution)/shard_map/ppermute | solution.py:449
  38.4 3.2 %collective-permute-start.7 = (f32[1,128]{1,0:T(1,128)S(1)}, f32[1,128]{1,0:T(1,128)S(1)}, u32[]{:S(2)}, u32[]{:S(2)}) collective-permute-start(f32[1,128]{1,0:T(1,128)S(1)} %multiply_add_fusion.1.refs_3_.refs_6_), channel_id=1, source_target_pairs={{0,8},{8,0},{16,24},{24,16},{1,9},{9,1},{17,25},{25,17},{2,10},{10... | collective-permute-start | bytes 1544 | tf_op jit(solution)/shard_map/ppermute | solution.py:445
  51.4 19.5 %copy-start.1 = (bf16[512,128]{1,0:T(8,128)(2,1)S(1)}, bf16[512,128]{1,0:T(8,128)(2,1)}, u32[]{:S(2)}) copy-start(bf16[512,128]{1,0:T(8,128)(2,1)} %ik_ref.1) | copy-start | bytes 393220
  55.8 20.1 %collective-permute-start.14 = (f32[512,128]{1,0:T(8,128)S(1)}, f32[512,128]{1,0:T(8,128)S(1)}, u32[]{:S(2)}, u32[]{:S(2)}) collective-permute-start(f32[512,128]{1,0:T(8,128)S(1)} %get-tuple-element.36), channel_id=1, source_target_pairs={{0,1},{1,0},{2,3},{3,2},{4,5},{5,4},{6,7},{7,6},{8,9},{9,8},{10,11... | collective-permute-start | bytes 786440 | tf_op jit(solution)/shard_map/ppermute | solution.py:445
  70.6 9.3 %collective-permute-start.8 = (f32[520,128]{1,0:T(8,128)S(1)}, f32[520,128]{1,0:T(8,128)S(1)}, u32[]{:S(2)}, u32[]{:S(2)}) collective-permute-start(f32[520,128]{1,0:T(8,128)S(1)} %get-tuple-element.31.refs_0_), channel_id=1, source_target_pairs={{0,16},{8,24},{16,0},{24,8},{1,17},{9,25},{17,1},{25,9},{2,18},{10... | collective-permute-start | bytes 798728 | tf_op jit(solution)/shard_map/ppermute | solution.py:445
  70.9 12.1 %collective-permute-start.10 = (f32[512,128]{1,0:T(8,128)S(1)}, f32[512,128]{1,0:T(8,128)S(1)}, u32[]{:S(2)}, u32[]{:S(2)}) collective-permute-start(f32[512,128]{1,0:T(8,128)S(1)} %convert_element_type.7.refs_2_), channel_id=1, source_target_pairs={{0,16},{8,24},{16,0},{24,8},{1,17},{9,25},{17,1},{25,9},{2,18},{10... | collective-permute-start | bytes 786440 | tf_op jit(solution)/shard_map/ppermute | solution.py:445
  75.9 7.1 %collective-permute-start.15 = (f32[512,128]{1,0:T(8,128)S(1)}, f32[512,128]{1,0:T(8,128)S(1)}, u32[]{:S(2)}, u32[]{:S(2)}) collective-permute-start(f32[512,128]{1,0:T(8,128)S(1)} %add.37), channel_id=1, source_target_pairs={{0,2},{2,0},{4,6},{6,4},{1,3},{3,1},{5,7},{7,5},{8,10},{10,8},{12,... | collective-permute-start | bytes 786440 | tf_op jit(solution)/shard_map/ppermute | solution.py:445
  76.4 7.5 %collective-permute-start.12 = (f32[520,128]{1,0:T(8,128)S(1)}, f32[520,128]{1,0:T(8,128)S(1)}, u32[]{:S(2)}, u32[]{:S(2)}) collective-permute-start(f32[520,128]{1,0:T(8,128)S(1)} %get-tuple-element.31.refs_0_), channel_id=1, source_target_pairs={{0,8},{8,0},{16,24},{24,16},{1,9},{9,1},{17,25},{25,17},{2,10},{10... | collective-permute-start | bytes 798728 | tf_op jit(solution)/shard_map/ppermute | solution.py:445
  76.4 7.5 %collective-permute-start.13 = (f32[512,128]{1,0:T(8,128)S(1)}, f32[512,128]{1,0:T(8,128)S(1)}, u32[]{:S(2)}, u32[]{:S(2)}) collective-permute-start(f32[512,128]{1,0:T(8,128)S(1)} %convert_element_type.7.refs_2_), channel_id=1, source_target_pairs={{0,8},{8,0},{16,24},{24,16},{1,9},{9,1},{17,25},{25,17},{2,10},{10... | collective-permute-start | bytes 786440 | tf_op jit(solution)/shard_map/ppermute | solution.py:445
  79.9 7.5 %collective-permute-start.9 = (f32[520,128]{1,0:T(8,128)S(1)}, f32[520,128]{1,0:T(8,128)S(1)}, u32[]{:S(2)}, u32[]{:S(2)}) collective-permute-start(f32[520,128]{1,0:T(8,128)S(1)} %collective-permute-done.8.refs_0_), channel_id=1, source_target_pairs={{0,8},{8,0},{16,24},{24,16},{1,9},{9,1},{17,25},{25,17},{2,10},{10... | collective-permute-start | bytes 798728 | tf_op jit(solution)/shard_map/ppermute | solution.py:445
  83.0 4.4 %collective-permute-start.11 = (f32[512,128]{1,0:T(8,128)S(1)}, f32[512,128]{1,0:T(8,128)S(1)}, u32[]{:S(2)}, u32[]{:S(2)}) collective-permute-start(f32[512,128]{1,0:T(8,128)S(1)} %collective-permute-done.10.refs_2_), channel_id=1, source_target_pairs={{0,8},{8,0},{16,24},{24,16},{1,9},{9,1},{17,25},{25,17},{2,10},{10... | collective-permute-start | bytes 786440 | tf_op jit(solution)/shard_map/ppermute | solution.py:445
  83.0 14.4 %collective-permute-start.16 = (f32[512,128]{1,0:T(8,128)S(1)}, f32[512,128]{1,0:T(8,128)S(1)}, u32[]{:S(2)}, u32[]{:S(2)}) collective-permute-start(f32[512,128]{1,0:T(8,128)S(1)} %add.38), channel_id=1, source_target_pairs={{0,6},{2,4},{4,2},{6,0},{1,7},{3,5},{5,3},{7,1},{8,14},{10,12},{12... | collective-permute-start | bytes 786440 | tf_op jit(solution)/shard_map/ppermute | solution.py:445

commit v5 on v4

--- a/solution.py
+++ b/solution.py
@@ -201,17 +201,17 @@
     )(key_count, main_query, key_nope, rope_t, query_pos, key_pos)
 
 
-def target_kernel(n_lse, shifts, per, parts, axis_size, q_ref, kk_ref, bias_ref, *refs):
+def target_kernel(n_lse, masks, per, parts, q_ref, kk_ref, bias_ref, *refs):
     lse_refs = refs[:n_lse]
     out_refs = refs[n_lse:-1]
     glob_ref = refs[-1]
-    n_groups = len(shifts)
+    n_groups = len(masks)
     keys = kk_ref.shape[0]
     rows = q_ref.shape[1]
     pairs = q_ref.shape[2] // PAIR
     size = keys // parts
     me = lax.axis_index("head")
-    ids = [lax.rem(me + shift, axis_size) for shift in shifts]
+    ids = [lax.bitwise_xor(me, mask) for mask in masks]
     tiles = [
         (g, slice(i * size, (i + 1) * size), out_refs[g * parts + i])
         for g in range(n_groups)
@@ -244,13 +244,13 @@
         ref[...] = jnp.where(bias_ref[at, lanes_at(ids[g], rows)] < 0, 0.0, ref[...])
 
 
-def head_sums(shifts, axis_size, q, kk, bias, lses, parts=1):
+def head_sums(masks, q, kk, bias, lses, parts=1):
     _, rows, width = q.shape
     heads = width // DQK
     keys = kk.shape[0]
-    n = len(shifts)
+    n = len(masks)
     return pl.pallas_call(
-        functools.partial(target_kernel, len(lses), shifts, 4 // n, parts, axis_size),
+        functools.partial(target_kernel, len(lses), masks, 4 // n, parts),
         in_specs=[IN_VMEM] * (3 + len(lses)),
         out_specs=[IN_VMEM] * (n * parts),
         out_shape=[jax.ShapeDtypeStruct((keys // parts, rows), f32)] * (n * parts),
@@ -318,7 +318,7 @@
 def grad_key_kernel(n_parts, n_lse, per, *refs):
     parts = refs[:n_parts]
     lses = refs[n_parts : n_parts + n_lse]
-    logits_ref, wm_ref, iq_ref, bias_ref, cot_ref, sg_ref, gk_ref = refs[n_parts + n_lse :]
+    logits_ref, wm_ref, iq_ref, bias_ref, cot_ref, sg_ref, lo_ref, hi_ref = refs[n_parts + n_lse :]
     keys, rows = logits_ref.shape
     width = iq_ref.shape[1]
 
@@ -332,7 +332,8 @@
     terms = jnp.where(live, target * (jnp.log(jnp.where(live, target, 1.0)) - logits), 0.0)
     kl = jnp.sum(terms, axis=0, keepdims=True)
     sg_ref[keys:, :] = jnp.broadcast_to(kl, (8, rows))
-    gk_ref[...] = jnp.zeros_like(gk_ref)
+    lo_ref[...] = jnp.zeros_like(lo_ref)
+    hi_ref[...] = jnp.zeros_like(hi_ref)
 
     def step(i, carry):
         for p in range(per):
@@ -343,7 +344,9 @@
                 wm = wm_ref[:, lanes_at(j, rows)].astype(f32)
                 dz.append((sg_ref[:keys, :] * wm).astype(bf16))
                 qs.append(iq_ref[:, lanes_at(j, ID)])
-            gk_ref[...] += dot_nn(jnp.concatenate(dz, axis=1), jnp.concatenate(qs, axis=0))
+            g = dot_nn(jnp.concatenate(dz, axis=1), jnp.concatenate(qs, axis=0))
+            lo_ref[...] += g[: keys // 2]
+            hi_ref[...] += g[keys // 2 :]
         return carry
 
     lax.fori_loop(0, width // (2 * ID * per), step, 0)
@@ -357,10 +360,11 @@
         grid=(1,),
         in_specs=[IN_VMEM] * (len(parts) + len(lses) + 4)
         + [pl.BlockSpec((1, rows), lambda i: (0, 0))],
-        out_specs=[IN_VMEM, IN_VMEM],
+        out_specs=[IN_VMEM] * 3,
         out_shape=[
             jax.ShapeDtypeStruct((keys + 8, rows), f32),
-            jax.ShapeDtypeStruct((keys, ID), f32),
+            jax.ShapeDtypeStruct((keys // 2, ID), f32),
+            jax.ShapeDtypeStruct((keys // 2, ID), f32),
         ],
         compiler_params=pltpu.CompilerParams(vmem_limit_bytes=16 * 1024 * 1024),
         cost_estimate=cost(2 * keys * rows * width, rows * width * 2 + keys * rows * width // ID * 2),
@@ -445,10 +449,6 @@
     return lax.ppermute(value, axis, [(i, i ^ mask) for i in range(size)])
 
 
-def rotate(value, axis, by, size):
-    return lax.ppermute(value, axis, [(i, (i + by) % size) for i in range(size)])
-
-
 def butterfly_lse(value, size):
     pair = [value]
     for bit in reversed(range(size.bit_length() - 1)):
@@ -457,12 +457,16 @@
     return pair
 
 
-def summed_copies(value, n_head, n_query):
-    steps = [("query", 1 << b, n_query) for b in range(n_query.bit_length() - 1)]
-    steps += [("head", (2 << b) - 1, n_head) for b in range(n_head.bit_length() - 1)]
-    for axis, mask, size in steps:
-        value = value + swap(value, axis, mask, size)
-    return value
+def summed_copies(pieces, n_head, n_query):
+    steps = [("head", (2 << b) - 1, n_head) for b in reversed(range(n_head.bit_length() - 1))]
+    steps += [("query", 1 << b, n_query) for b in range(n_query.bit_length() - 1)]
+    steps = steps[:1] + steps[2:] + steps[1:2]
+    for number in range(len(steps)):
+        moved = []
+        for i, piece in enumerate(pieces):
+            moved.append(swap(piece, *steps[(number - i) % len(steps)]))
+        pieces = [piece + other for piece, other in zip(pieces, moved)]
+    return jnp.concatenate(pieces, axis=0)
 
 
 def in_hbm(*values):
@@ -492,24 +496,25 @@
     index_lses = butterfly_lse(index_lse, n_key)
     iks = gathered(index_key.astype(f32))
 
+    half = keys // 2
     if n_head == 4 and groups == 4:
-        low, high = head_sums([2], 4, q, kk, bias, lses, parts=2)
-        half = keys // 2
-        low = rotate(low, "head", 1, 4)
-        high = rotate(high, "head", 3, 4)
-        up, down = head_sums([1, 3], 4, q, kk, bias, lses)
-        up = up + jnp.pad(low, ((0, half), (0, 0)))
-        down = down + jnp.pad(high, ((half, 0), (0, 0)))
-        from_below = rotate(up, "head", 1, 4)
-        from_above = rotate(down, "head", 3, 4)
-        own = head_sums([0], 4, q, kk, bias, lses)[0]
-        parts = [own, from_below, from_above]
+        low, high = head_sums([2], q, kk, bias, lses, parts=2)
+        low = swap(low, "head", 1, 4)
+        high = swap(high, "head", 3, 4)
+        up, down = head_sums([1, 3], q, kk, bias, lses)
+        up = up + jnp.pad(high, ((half, 0), (0, 0)))
+        down = down + jnp.pad(low, ((0, half), (0, 0)))
+        from_up = swap(up, "head", 1, 4)
+        from_down = swap(down, "head", 3, 4)
+        own = head_sums([0], q, kk, bias, lses)[0]
+        parts = [own, from_up, from_down]
     else:
-        tiles = jnp.stack([head_sums([g], groups, q, kk, bias, lses)[0] for g in range(groups)])
-        tiles = jnp.roll(tiles, lax.axis_index("head"), axis=0)
+        z = lax.axis_index("head")
+        tiles = jnp.stack([head_sums([g], q, kk, bias, lses)[0] for g in range(groups)])
+        tiles = tiles[jnp.bitwise_xor(jnp.arange(groups), z)]
         parts = [lax.psum_scatter(tiles, "head", scatter_dimension=0, tiled=True)[0]]
 
-    sg, grad_key = index_grad_key(parts, index_lses, logits, wm, index_query, bias, cotangent)
+    sg, *grad_key = index_grad_key(parts, index_lses, logits, wm, index_query, bias, cotangent)
     grad_key = summed_copies(grad_key, n_head, n_query)
     sgs = gathered(sg)
     carry = None

time: 98.5 us -> 99.4 us (level)
  the two profiles are of different devices: /device:TPU:8 before, /device:TPU:0 now
where the time goes in v5:
time: 99.4 us; the launch traced here: 99.1 us
  Pallas kernels  40.1 us (40%)
  starting transfers between devices  34.4 us (35%)
  waiting for transfers between devices  22.8 us (23%)
    ppermute x20, starting transfers between devices, swap(): return lax.ppermute(value, axis, [(i, i ^ mask) for i in range(size)])  34.4 us
    ppermute x20, waiting for transfers between devices, swap(): return lax.ppermute(value, axis, [(i, i ^ mask) for i in range(size)])  22.8 us
    pallas_call x1, Pallas kernels, main_stats(): pl.pallas_call(functools.partial(stats_kernel, 2), in_specs=[pl.BlockSpec...  12.4 us
    pallas_call x3, Pallas kernels, head_sums(): pl.pallas_call(functools.partial(target_kernel, len(lses), masks, 4 // n,...  10.4 us
    pallas_call x2, Pallas kernels, index_grad_query(): pl.pallas_call(functools.partial(grad_query_kernel, n, first, len(lses)),...  7.57 us
    pallas_call x1, Pallas kernels, index_logits(): pl.pallas_call(functools.partial(logits_kernel, 4), grid=(1,), in_specs=[...  5.44 us
    pallas_call x1, Pallas kernels, index_grad_key(): pl.pallas_call(functools.partial(grad_key_kernel, len(parts), len(lses),...  4.31 us
  transfers between devices with their start and end apart: 20, of which 9 were waited for; matrix products, arithmetic and copies ran while one was open for 1% of the time, Pallas kernels for 24%

profile of v5, /device:TPU:0, one launch (start us, length us, event | category | flops | bytes accessed | tf_op | source)
XLA Modules:
  0.0 99.1 jit_solution(41028426183341349)
XLA Ops:
  0.7 12.4 %main_stats.1 = (f32[32,512]{1,0:T(8,128)S(1)}, bf16[4,128,6144]{2,1,0:T(8,128)(2,1)S(1)}, bf16[512,8192]{1,0:T(8,128)(2,1)S(1)}, f32[512,512]{1,0:T(8,128)S(1)}) custom-call(s32[16]{0:T(128)} %count_hbm.1, bf16[4,128,6144]{2,1,0:T(8,128)(2,1)} %q_hbm.1, bf16[512,4096]{1,0:T(8,128)(2,1)} %kn_hbm.1, bf16[64,512]{1,0:T(8,128)(2,1)} %bitcast.9, ...), custom_call_target="tpu_custom_call" | custom-call | flops 4294967296 | bytes 10485760 | tf_op jit(solution)/shard_map/main_stats/pallas_call | solution.py:172
  13.1 3.0 %collective-permute-start = (f32[32,512]{1,0:T(8,128)S(1)}, f32[32,512]{1,0:T(8,128)S(1)}, u32[]{:S(2)}, u32[]{:S(2)}) collective-permute-start(f32[32,512]{1,0:T(8,128)S(1)} %get-tuple-element.24), channel_id=1, source_target_pairs={{0,16},{8,24},{16,0},{24,8},{1,17},{9,25},{17,1},{25,9},{2,18},{10... | collective-permute-start | bytes 196616 | tf_op jit(solution)/shard_map/ppermute | solution.py:449
  16.1 2.2 %collective-permute-done = f32[32,512]{1,0:T(8,128)S(1)} collective-permute-done((f32[32,512]{1,0:T(8,128)S(1)}, f32[32,512]{1,0:T(8,128)S(1)}, u32[]{:S(2)}, u32[]{:S(2)}) %collective-permute-start) | collective-permute-done | bytes 65568 | tf_op jit(solution)/shard_map/ppermute | solution.py:449
  18.4 0.1 collective-permute-start.1
  18.5 5.4 %index_logits.1 = (f32[512,128]{1,0:T(8,128)S(1)}, f32[1,128]{1,0:T(1,128)S(1)}, bf16[512,8192]{1,0:T(8,128)(2,1)S(1)}) custom-call(bf16[128,8192]{1,0:T(8,128)(2,1)S(1)} %copy-done, bf16[512,128]{1,0:T(8,128)(2,1)} %ik_ref.1, bf16[64,128]{1,0:T(8,128)(2,1)} %bitcast.5, f32[512,512]{1,0:T(8,128)S(1)} %get-tuple-element.23.bias_ref.refs_8_), custom_call_target="tpu_custom_call" | custom-call | flops 1073741824 | bytes 10485760 | tf_op jit(solution)/shard_map/index_logits/pallas_call | solution.py:296
  23.9 2.1 %collective-permute-start.6 = (f32[1,128]{1,0:T(1,128)S(1)}, f32[1,128]{1,0:T(1,128)S(1)}, u32[]{:S(2)}, u32[]{:S(2)}) collective-permute-start(f32[1,128]{1,0:T(1,128)S(1)} %get-tuple-element.29), channel_id=1, source_target_pairs={{0,16},{8,24},{16,0},{24,8},{1,17},{9,25},{17,1},{25,9},{2,18},{10... | collective-permute-start | bytes 1544 | tf_op jit(solution)/shard_map/ppermute | solution.py:449
  26.1 0.1 collective-permute-start.10
  26.1 3.1 %head_sums.5 = (f32[256,128]{1,0:T(8,128)S(1)}, f32[256,128]{1,0:T(8,128)S(1)}) custom-call(bf16[4,128,6144]{2,1,0:T(8,128)(2,1)S(1)} %get-tuple-element.21.q_ref, bf16[512,8192]{1,0:T(8,128)(2,1)S(1)} %get-tuple-element.22.kk_ref, f32[512,512]{1,0:T(8,128)S(1)} %get-tuple-element.23.bias_ref.refs_8_, f32[32,512]{1,0:T(8,128)S(1)} %multiply_add_fusion.refs_0_, ...), custom_call_target="tpu_custom_call" | custom-call | flops 1073741824 | bytes 131072 | tf_op jit(solution)/shard_map/head_sums/pallas_call | solution.py:252
  29.2 2.1 %collective-permute-start.4 = (f32[256,128]{1,0:T(8,128)S(1)}, f32[256,128]{1,0:T(8,128)S(1)}, u32[]{:S(2)}, u32[]{:S(2)}) collective-permute-start(f32[256,128]{1,0:T(8,128)S(1)} %get-tuple-element.28), channel_id=1, source_target_pairs={{0,2},{2,0},{4,6},{6,4},{1,3},{3,1},{5,7},{7,5},{8,10},{10,8},{12,... | collective-permute-start | bytes 393224 | tf_op jit(solution)/shard_map/ppermute | solution.py:449
  31.4 2.5 %collective-permute-start.2 = (f32[256,128]{1,0:T(8,128)S(1)}, f32[256,128]{1,0:T(8,128)S(1)}, u32[]{:S(2)}, u32[]{:S(2)}) collective-permute-start(f32[256,128]{1,0:T(8,128)S(1)} %get-tuple-element.26), channel_id=1, source_target_pairs={{0,6},{2,4},{4,2},{6,0},{1,7},{3,5},{5,3},{7,1},{8,14},{10,12},{12... | collective-permute-start | bytes 393224 | tf_op jit(solution)/shard_map/ppermute | solution.py:449
  33.8 4.3 %head_sums.4 = (f32[512,128]{1,0:T(8,128)S(1)}, f32[512,128]{1,0:T(8,128)S(1)}) custom-call(bf16[4,128,6144]{2,1,0:T(8,128)(2,1)S(1)} %get-tuple-element.21.q_ref, bf16[512,8192]{1,0:T(8,128)(2,1)S(1)} %get-tuple-element.22.kk_ref, f32[512,512]{1,0:T(8,128)S(1)} %get-tuple-element.23.bias_ref.refs_8_, f32[32,512]{1,0:T(8,128)S(1)} %multiply_add_fusion.refs_0_, ...), custom_call_target="tpu_custom_call" | custom-call | flops 2147483648 | bytes 262144 | tf_op jit(solution)/shard_map/head_sums/pallas_call | solution.py:252
  38.2 3.5 %collective-permute-start.5 = (f32[512,128]{1,0:T(8,128)S(1)}, f32[512,128]{1,0:T(8,128)S(1)}, u32[]{:S(2)}, u32[]{:S(2)}) collective-permute-start(f32[512,128]{1,0:T(8,128)S(1)} %pad_add_fusion), channel_id=1, source_target_pairs={{0,6},{2,4},{4,2},{6,0},{1,7},{3,5},{5,3},{7,1},{8,14},{10,12},{12... | collective-permute-start | bytes 786440 | tf_op jit(solution)/shard_map/ppermute | solution.py:449
  41.6 0.1 collective-permute-start.3
  41.7 0.1 collective-permute-start.7
  41.8 3.1 %head_sums.3.refs_0_ = f32[512,128]{1,0:T(8,128)S(1)} custom-call(bf16[4,128,6144]{2,1,0:T(8,128)(2,1)S(1)} %get-tuple-element.21.q_ref, bf16[512,8192]{1,0:T(8,128)(2,1)S(1)} %get-tuple-element.22.kk_ref, f32[512,512]{1,0:T(8,128)S(1)} %get-tuple-element.23.bias_ref.refs_8_, f32[32,512]{1,0:T(8,128)S(1)} %multiply_add_fusion.refs_0_, ...), custom_call_target="tpu_custom_call" | custom-call | flops 1073741824 | bytes 131072 | tf_op jit(solution)/shard_map/head_sums/pallas_call | solution.py:252
  44.9 4.3 %collective-permute-done.5.refs_2_ = f32[512,128]{1,0:T(8,128)S(1)} collective-permute-done((f32[512,128]{1,0:T(8,128)S(1)}, f32[512,128]{1,0:T(8,128)S(1)}, u32[]{:S(2)}, u32[]{:S(2)}) %collective-permute-start.5) | collective-permute-done | bytes 262176 | tf_op jit(solution)/shard_map/ppermute | solution.py:449
  49.2 3.8 %collective-permute-done.3.refs_1_ = f32[512,128]{1,0:T(8,128)S(1)} collective-permute-done((f32[512,128]{1,0:T(8,128)S(1)}, f32[512,128]{1,0:T(8,128)S(1)}, u32[]{:S(2)}, u32[]{:S(2)}) %collective-permute-start.3) | collective-permute-done | bytes 262176 | tf_op jit(solution)/shard_map/ppermute | solution.py:449
  52.9 4.3 %index_grad_key.1 = (f32[520,128]{1,0:T(8,128)S(1)}, f32[256,128]{1,0:T(8,128)S(1)}, f32[256,128]{1,0:T(8,128)S(1)}) custom-call(f32[512,128]{1,0:T(8,128)S(1)} %head_sums.3.refs_0_, f32[512,128]{1,0:T(8,128)S(1)} %collective-permute-done.3.refs_1_, f32[512,128]{1,0:T(8,128)S(1)} %collective-permute-done.5.refs_2_, ...), custom_call_target="tpu_custom_call" | custom-call | flops 1073741824 | bytes 10485760 | tf_op jit(solution)/shard_map/index_grad_key/pallas_call | solution.py:358
  57.3 1.8 %collective-permute-start.14 = (f32[256,128]{1,0:T(8,128)S(1)}, f32[256,128]{1,0:T(8,128)S(1)}, u32[]{:S(2)}, u32[]{:S(2)}) collective-permute-start(f32[256,128]{1,0:T(8,128)S(1)} %get-tuple-element.37), channel_id=1, source_target_pairs={{0,6},{2,4},{4,2},{6,0},{1,7},{3,5},{5,3},{7,1},{8,14},{10,12},{12... | collective-permute-start | bytes 393224 | tf_op jit(solution)/shard_map/ppermute | solution.py:449
  59.1 1.5 %collective-permute-start.8 = (f32[520,128]{1,0:T(8,128)S(1)}, f32[520,128]{1,0:T(8,128)S(1)}, u32[]{:S(2)}, u32[]{:S(2)}) collective-permute-start(f32[520,128]{1,0:T(8,128)S(1)} %get-tuple-element.32.refs_0_), channel_id=1, source_target_pairs={{0,16},{8,24},{16,0},{24,8},{1,17},{9,25},{17,1},{25,9},{2,18},{10... | collective-permute-start | bytes 798728 | tf_op jit(solution)/shard_map/ppermute | solution.py:449
  60.5 5.0 %collective-permute-done.14 = f32[256,128]{1,0:T(8,128)S(1)} collective-permute-done((f32[256,128]{1,0:T(8,128)S(1)}, f32[256,128]{1,0:T(8,128)S(1)}, u32[]{:S(2)}, u32[]{:S(2)}) %collective-permute-start.14) | collective-permute-done | bytes 131104 | tf_op jit(solution)/shard_map/ppermute | solution.py:449
  65.5 1.1 %collective-permute-done.17 = f32[256,128]{1,0:T(8,128)S(1)} collective-permute-done((f32[256,128]{1,0:T(8,128)S(1)}, f32[256,128]{1,0:T(8,128)S(1)}, u32[]{:S(2)}, u32[]{:S(2)}) %collective-permute-start.17) | collective-permute-done | bytes 131104 | tf_op jit(solution)/shard_map/ppermute | solution.py:449
  66.7 14.8 %collective-permute-start.15 = (f32[256,128]{1,0:T(8,128)S(1)}, f32[256,128]{1,0:T(8,128)S(1)}, u32[]{:S(2)}, u32[]{:S(2)}) collective-permute-start(f32[256,128]{1,0:T(8,128)S(1)} %add.46), channel_id=1, source_target_pairs={{0,1},{1,0},{2,3},{3,2},{4,5},{5,4},{6,7},{7,6},{8,9},{9,8},{10,11... | collective-permute-start | bytes 393224 | tf_op jit(solution)/shard_map/ppermute | solution.py:449
  81.5 1.9 %collective-permute-start.18 = (f32[256,128]{1,0:T(8,128)S(1)}, f32[256,128]{1,0:T(8,128)S(1)}, u32[]{:S(2)}, u32[]{:S(2)}) collective-permute-start(f32[256,128]{1,0:T(8,128)S(1)} %add.49), channel_id=1, source_target_pairs={{0,6},{2,4},{4,2},{6,0},{1,7},{3,5},{5,3},{7,1},{8,14},{10,12},{12... | collective-permute-start | bytes 393224 | tf_op jit(solution)/shard_map/ppermute | solution.py:449
  83.4 1.2 %collective-permute-done.15 = f32[256,128]{1,0:T(8,128)S(1)} collective-permute-done((f32[256,128]{1,0:T(8,128)S(1)}, f32[256,128]{1,0:T(8,128)S(1)}, u32[]{:S(2)}, u32[]{:S(2)}) %collective-permute-start.15) | collective-permute-done | bytes 131104 | tf_op jit(solution)/shard_map/ppermute | solution.py:449
  84.7 3.7 %collective-permute-done.18 = f32[256,128]{1,0:T(8,128)S(1)} collective-permute-done((f32[256,128]{1,0:T(8,128)S(1)}, f32[256,128]{1,0:T(8,128)S(1)}, u32[]{:S(2)}, u32[]{:S(2)}) %collective-permute-start.18) | collective-permute-done | bytes 131104 | tf_op jit(solution)/shard_map/ppermute | solution.py:449
  88.3 0.8 collective-permute-start.16
  89.3 3.5 %index_grad_query.2 = (f32[128,2048]{1,0:T(8,128)S(1)}, f32[1,128]{1,0:T(1,128)S(1)}) custom-call(f32[520,128]{1,0:T(8,128)S(1)} %get-tuple-element.32.refs_0_, f32[520,128]{1,0:T(8,128)S(1)} %collective-permute-done.12.refs_1_, f32[512,128]{1,0:T(8,128)S(1)} %convert_element_type.7.refs_2_, f32[512,128]{1,0:T(8,128)S(1)} %collective-permute-done.13.refs_3_, ...), custom_call_target="tpu_custom_call" | custom-call | flops 1073741824 | bytes 3145728 | tf_op jit(solution)/shard_map/index_grad_query/pallas_call | solution.py:430
  92.7 0.5 collective-permute-done.16
  93.3 0.9 collective-permute-done.19
  94.2 0.7 pad_maximum_fusion
  95.0 4.1 %index_grad_query.3 = (f32[128,2048]{1,0:T(8,128)}, f32[1,128]{1,0:T(1,128)}) custom-call(f32[520,128]{1,0:T(8,128)S(1)} %collective-permute-done.8.refs_0_, f32[520,128]{1,0:T(8,128)S(1)} %collective-permute-done.9.refs_1_, f32[512,128]{1,0:T(8,128)S(1)} %collective-permute-done.10.refs_2_, f32[512,128]{1,0:T(8,128)S(1)} %collective-permute-done.11.refs_3_, ...), custom_call_target="tpu_custom_call" | custom-call | flops 1073741824 | bytes 3145728 | tf_op jit(solution)/shard_map/index_grad_query/pallas_call | solution.py:430
  (32 shorter events, 0.3 us)
Async XLA Ops:
  0.6 17.9 %copy-start = (bf16[128,8192]{1,0:T(8,128)(2,1)S(1)}, bf16[128,8192]{1,0:T(8,128)(2,1)}, u32[]{:S(2)}) copy-start(bf16[128,8192]{1,0:T(8,128)(2,1)} %refs_4_.3) | copy-start | bytes 6291460
  0.6 25.4 %copy-start.1 = (bf16[512,128]{1,0:T(8,128)(2,1)S(1)}, bf16[512,128]{1,0:T(8,128)(2,1)}, u32[]{:S(2)}) copy-start(bf16[512,128]{1,0:T(8,128)(2,1)} %ik_ref.1) | copy-start | bytes 393220
  13.1 5.3 %collective-permute-start = (f32[32,512]{1,0:T(8,128)S(1)}, f32[32,512]{1,0:T(8,128)S(1)}, u32[]{:S(2)}, u32[]{:S(2)}) collective-permute-start(f32[32,512]{1,0:T(8,128)S(1)} %get-tuple-element.24), channel_id=1, source_target_pairs={{0,16},{8,24},{16,0},{24,8},{1,17},{9,25},{17,1},{25,9},{2,18},{10... | collective-permute-start | bytes 196616 | tf_op jit(solution)/shard_map/ppermute | solution.py:449
  18.4 7.7 %collective-permute-start.1 = (f32[32,512]{1,0:T(8,128)S(1)}, f32[32,512]{1,0:T(8,128)S(1)}, u32[]{:S(2)}, u32[]{:S(2)}) collective-permute-start(f32[32,512]{1,0:T(8,128)S(1)} %multiply_add_fusion.refs_0_), channel_id=1, source_target_pairs={{0,8},{8,0},{16,24},{24,16},{1,9},{9,1},{17,25},{25,17},{2,10},{10... | collective-permute-start | bytes 196616 | tf_op jit(solution)/shard_map/ppermute | solution.py:449
  23.9 17.8 %collective-permute-start.6 = (f32[1,128]{1,0:T(1,128)S(1)}, f32[1,128]{1,0:T(1,128)S(1)}, u32[]{:S(2)}, u32[]{:S(2)}) collective-permute-start(f32[1,128]{1,0:T(1,128)S(1)} %get-tuple-element.29), channel_id=1, source_target_pairs={{0,16},{8,24},{16,0},{24,8},{1,17},{9,25},{17,1},{25,9},{2,18},{10... | collective-permute-start | bytes 1544 | tf_op jit(solution)/shard_map/ppermute | solution.py:449
  26.1 55.4 %collective-permute-start.10 = (f32[512,128]{1,0:T(8,128)S(1)}, f32[512,128]{1,0:T(8,128)S(1)}, u32[]{:S(2)}, u32[]{:S(2)}) collective-permute-start(f32[512,128]{1,0:T(8,128)S(1)} %convert_element_type.7.refs_2_), channel_id=1, source_target_pairs={{0,16},{8,24},{16,0},{24,8},{1,17},{9,25},{17,1},{25,9},{2,18},{10... | collective-permute-start | bytes 786440 | tf_op jit(solution)/shard_map/ppermute | solution.py:449
  29.2 8.9 %collective-permute-start.4 = (f32[256,128]{1,0:T(8,128)S(1)}, f32[256,128]{1,0:T(8,128)S(1)}, u32[]{:S(2)}, u32[]{:S(2)}) collective-permute-start(f32[256,128]{1,0:T(8,128)S(1)} %get-tuple-element.28), channel_id=1, source_target_pairs={{0,2},{2,0},{4,6},{6,4},{1,3},{3,1},{5,7},{7,5},{8,10},{10,8},{12,... | collective-permute-start | bytes 393224 | tf_op jit(solution)/shard_map/ppermute | solution.py:449
  31.4 10.2 %collective-permute-start.2 = (f32[256,128]{1,0:T(8,128)S(1)}, f32[256,128]{1,0:T(8,128)S(1)}, u32[]{:S(2)}, u32[]{:S(2)}) collective-permute-start(f32[256,128]{1,0:T(8,128)S(1)} %get-tuple-element.26), channel_id=1, source_target_pairs={{0,6},{2,4},{4,2},{6,0},{1,7},{3,5},{5,3},{7,1},{8,14},{10,12},{12... | collective-permute-start | bytes 393224 | tf_op jit(solution)/shard_map/ppermute | solution.py:449
  38.2 11.0 %collective-permute-start.5 = (f32[512,128]{1,0:T(8,128)S(1)}, f32[512,128]{1,0:T(8,128)S(1)}, u32[]{:S(2)}, u32[]{:S(2)}) collective-permute-start(f32[512,128]{1,0:T(8,128)S(1)} %pad_add_fusion), channel_id=1, source_target_pairs={{0,6},{2,4},{4,2},{6,0},{1,7},{3,5},{5,3},{7,1},{8,14},{10,12},{12... | collective-permute-start | bytes 786440 | tf_op jit(solution)/shard_map/ppermute | solution.py:449
  41.6 11.3 %collective-permute-start.3 = (f32[512,128]{1,0:T(8,128)S(1)}, f32[512,128]{1,0:T(8,128)S(1)}, u32[]{:S(2)}, u32[]{:S(2)}) collective-permute-start(f32[512,128]{1,0:T(8,128)S(1)} %pad_add_fusion.1), channel_id=1, source_target_pairs={{0,2},{2,0},{4,6},{6,4},{1,3},{3,1},{5,7},{7,5},{8,10},{10,8},{12,... | collective-permute-start | bytes 786440 | tf_op jit(solution)/shard_map/ppermute | solution.py:449
  41.7 3.2 %collective-permute-start.7 = (f32[1,128]{1,0:T(1,128)S(1)}, f32[1,128]{1,0:T(1,128)S(1)}, u32[]{:S(2)}, u32[]{:S(2)}) collective-permute-start(f32[1,128]{1,0:T(1,128)S(1)} %multiply_add_fusion.1.refs_3_.refs_6_), channel_id=1, source_target_pairs={{0,8},{8,0},{16,24},{24,16},{1,9},{9,1},{17,25},{25,17},{2,10},{10... | collective-permute-start | bytes 1544 | tf_op jit(solution)/shard_map/ppermute | solution.py:449
  57.3 8.2 %collective-permute-start.14 = (f32[256,128]{1,0:T(8,128)S(1)}, f32[256,128]{1,0:T(8,128)S(1)}, u32[]{:S(2)}, u32[]{:S(2)}) collective-permute-start(f32[256,128]{1,0:T(8,128)S(1)} %get-tuple-element.37), channel_id=1, source_target_pairs={{0,6},{2,4},{4,2},{6,0},{1,7},{3,5},{5,3},{7,1},{8,14},{10,12},{12... | collective-permute-start | bytes 393224 | tf_op jit(solution)/shard_map/ppermute | solution.py:449
  59.1 24.3 %collective-permute-start.8 = (f32[520,128]{1,0:T(8,128)S(1)}, f32[520,128]{1,0:T(8,128)S(1)}, u32[]{:S(2)}, u32[]{:S(2)}) collective-permute-start(f32[520,128]{1,0:T(8,128)S(1)} %get-tuple-element.32.refs_0_), channel_id=1, source_target_pairs={{0,16},{8,24},{16,0},{24,8},{1,17},{9,25},{17,1},{25,9},{2,18},{10... | collective-permute-start | bytes 798728 | tf_op jit(solution)/shard_map/ppermute | solution.py:449
  60.5 6.1 %collective-permute-start.17 = (f32[256,128]{1,0:T(8,128)S(1)}, f32[256,128]{1,0:T(8,128)S(1)}, u32[]{:S(2)}, u32[]{:S(2)}) collective-permute-start(f32[256,128]{1,0:T(8,128)S(1)} %get-tuple-element.38), channel_id=1, source_target_pairs={{0,2},{2,0},{4,6},{6,4},{1,3},{3,1},{5,7},{7,5},{8,10},{10,8},{12,... | collective-permute-start | bytes 393224 | tf_op jit(solution)/shard_map/ppermute | solution.py:449
  60.5 28.6 %collective-permute-start.13 = (f32[512,128]{1,0:T(8,128)S(1)}, f32[512,128]{1,0:T(8,128)S(1)}, u32[]{:S(2)}, u32[]{:S(2)}) collective-permute-start(f32[512,128]{1,0:T(8,128)S(1)} %convert_element_type.7.refs_2_), channel_id=1, source_target_pairs={{0,8},{8,0},{16,24},{24,16},{1,9},{9,1},{17,25},{25,17},{2,10},{10... | collective-permute-start | bytes 786440 | tf_op jit(solution)/shard_map/ppermute | solution.py:449
  65.5 23.8 %collective-permute-start.12 = (f32[520,128]{1,0:T(8,128)S(1)}, f32[520,128]{1,0:T(8,128)S(1)}, u32[]{:S(2)}, u32[]{:S(2)}) collective-permute-start(f32[520,128]{1,0:T(8,128)S(1)} %get-tuple-element.32.refs_0_), channel_id=1, source_target_pairs={{0,8},{8,0},{16,24},{24,16},{1,9},{9,1},{17,25},{25,17},{2,10},{10... | collective-permute-start | bytes 798728 | tf_op jit(solution)/shard_map/ppermute | solution.py:449
  66.7 18.0 %collective-permute-start.15 = (f32[256,128]{1,0:T(8,128)S(1)}, f32[256,128]{1,0:T(8,128)S(1)}, u32[]{:S(2)}, u32[]{:S(2)}) collective-permute-start(f32[256,128]{1,0:T(8,128)S(1)} %add.46), channel_id=1, source_target_pairs={{0,1},{1,0},{2,3},{3,2},{4,5},{5,4},{6,7},{7,6},{8,9},{9,8},{10,11... | collective-permute-start | bytes 393224 | tf_op jit(solution)/shard_map/ppermute | solution.py:449
  81.5 6.8 %collective-permute-start.18 = (f32[256,128]{1,0:T(8,128)S(1)}, f32[256,128]{1,0:T(8,128)S(1)}, u32[]{:S(2)}, u32[]{:S(2)}) collective-permute-start(f32[256,128]{1,0:T(8,128)S(1)} %add.49), channel_id=1, source_target_pairs={{0,6},{2,4},{4,2},{6,0},{1,7},{3,5},{5,3},{7,1},{8,14},{10,12},{12... | collective-permute-start | bytes 393224 | tf_op jit(solution)/shard_map/ppermute | solution.py:449
  83.4 11.6 %collective-permute-start.9 = (f32[520,128]{1,0:T(8,128)S(1)}, f32[520,128]{1,0:T(8,128)S(1)}, u32[]{:S(2)}, u32[]{:S(2)}) collective-permute-start(f32[520,128]{1,0:T(8,128)S(1)} %collective-permute-done.8.refs_0_), channel_id=1, source_target_pairs={{0,8},{8,0},{16,24},{24,16},{1,9},{9,1},{17,25},{25,17},{2,10},{10... | collective-permute-start | bytes 798728 | tf_op jit(solution)/shard_map/ppermute | solution.py:449
  84.6 10.3 %collective-permute-start.11 = (f32[512,128]{1,0:T(8,128)S(1)}, f32[512,128]{1,0:T(8,128)S(1)}, u32[]{:S(2)}, u32[]{:S(2)}) collective-permute-start(f32[512,128]{1,0:T(8,128)S(1)} %collective-permute-done.10.refs_2_), channel_id=1, source_target_pairs={{0,8},{8,0},{16,24},{24,16},{1,9},{9,1},{17,25},{25,17},{2,10},{10... | collective-permute-start | bytes 786440 | tf_op jit(solution)/shard_map/ppermute | solution.py:449
  88.3 5.0 %collective-permute-start.16 = (f32[256,128]{1,0:T(8,128)S(1)}, f32[256,128]{1,0:T(8,128)S(1)}, u32[]{:S(2)}, u32[]{:S(2)}) collective-permute-start(f32[256,128]{1,0:T(8,128)S(1)} %add.47), channel_id=1, source_target_pairs={{0,2},{2,0},{4,6},{6,4},{1,3},{3,1},{5,7},{7,5},{8,10},{10,8},{12,... | collective-permute-start | bytes 393224 | tf_op jit(solution)/shard_map/ppermute | solution.py:449
  89.2 5.0 %collective-permute-start.19 = (f32[256,128]{1,0:T(8,128)S(1)}, f32[256,128]{1,0:T(8,128)S(1)}, u32[]{:S(2)}, u32[]{:S(2)}) collective-permute-start(f32[256,128]{1,0:T(8,128)S(1)} %add.50), channel_id=1, source_target_pairs={{0,1},{1,0},{2,3},{3,2},{4,5},{5,4},{6,7},{7,6},{8,9},{9,8},{10,11... | collective-permute-start | bytes 393224 | tf_op jit(solution)/shard_map/ppermute | solution.py:449

commit v6 on v5

--- a/solution.py
+++ b/solution.py
@@ -496,18 +496,14 @@
     index_lses = butterfly_lse(index_lse, n_key)
     iks = gathered(index_key.astype(f32))
 
-    half = keys // 2
     if n_head == 4 and groups == 4:
-        low, high = head_sums([2], q, kk, bias, lses, parts=2)
-        low = swap(low, "head", 1, 4)
-        high = swap(high, "head", 3, 4)
+        across = head_sums([2], q, kk, bias, lses)[0]
+        from_across = swap(across, "head", 2, 4)
         up, down = head_sums([1, 3], q, kk, bias, lses)
-        up = up + jnp.pad(high, ((half, 0), (0, 0)))
-        down = down + jnp.pad(low, ((0, half), (0, 0)))
         from_up = swap(up, "head", 1, 4)
         from_down = swap(down, "head", 3, 4)
         own = head_sums([0], q, kk, bias, lses)[0]
-        parts = [own, from_up, from_down]
+        parts = [own, from_up, from_down, from_across]
     else:
         z = lax.axis_index("head")
         tiles = jnp.stack([head_sums([g], q, kk, bias, lses)[0] for g in range(groups)])

time: 99.4 us -> 105 us (1.056)
  waiting for transfers between devices: 22.8 us -> 30.5 us
  starting transfers between devices: 34.4 us -> 32.4 us
    ppermute x20 -> x19, waiting for transfers between devices: 22.8 us -> 30.5 us  [swap(): return lax.ppermute(value, axis, [(i, i ^ mask) for i in range(size)])]
    ppermute x20 -> x19, starting transfers between devices: 34.4 us -> 32.4 us  [swap(): return lax.ppermute(value, axis, [(i, i ^ mask) for i in range(size)])]
  transfers between devices with their start and end apart: 20 -> 19, of which waited for: 9 -> 9; matrix products, arithmetic and copies ran while one was open for 1% -> 1% of each run, Pallas kernels for 24% -> 23%
where the time goes in v6:
time: 105 us
  Pallas kernels  40.2 us (38%)
  starting transfers between devices  32.4 us (31%)
  waiting for transfers between devices  30.5 us (29%)
    ppermute x19, starting transfers between devices, swap(): return lax.ppermute(value, axis, [(i, i ^ mask) for i in range(size)])  32.4 us
    ppermute x19, waiting for transfers between devices, swap(): return lax.ppermute(value, axis, [(i, i ^ mask) for i in range(size)])  30.5 us
    pallas_call x1, Pallas kernels, main_stats(): pl.pallas_call(functools.partial(stats_kernel, 2), in_specs=[pl.BlockSpec...  12.4 us
    pallas_call x3, Pallas kernels, head_sums(): pl.pallas_call(functools.partial(target_kernel, len(lses), masks, 4 // n,...  10.4 us
    pallas_call x2, Pallas kernels, index_grad_query(): pl.pallas_call(functools.partial(grad_query_kernel, n, first, len(lses)),...  7.57 us
    pallas_call x1, Pallas kernels, index_logits(): pl.pallas_call(functools.partial(logits_kernel, 4), grid=(1,), in_specs=[...  5.44 us
    pallas_call x1, Pallas kernels, index_grad_key(): pl.pallas_call(functools.partial(grad_key_kernel, len(parts), len(lses),...  4.32 us
  transfers between devices with their start and end apart: 19, of which 9 were waited for; matrix products, arithmetic and copies ran while one was open for 1% of the time, Pallas kernels for 23%

profile of v6, /device:TPU:0, one launch (start us, length us, event | category | flops | bytes accessed | tf_op | source)
XLA Modules:
  0.0 104.8 jit_solution(2649446643660627843)
XLA Ops:
  0.7 12.4 %main_stats.1 = (f32[32,512]{1,0:T(8,128)S(1)}, bf16[4,128,6144]{2,1,0:T(8,128)(2,1)S(1)}, bf16[512,8192]{1,0:T(8,128)(2,1)S(1)}, f32[512,512]{1,0:T(8,128)S(1)}) custom-call(s32[16]{0:T(128)} %count_hbm.1, bf16[4,128,6144]{2,1,0:T(8,128)(2,1)} %q_hbm.1, bf16[512,4096]{1,0:T(8,128)(2,1)} %kn_hbm.1, bf16[64,512]{1,0:T(8,128)(2,1)} %bitcast.9, ...), custom_call_target="tpu_custom_call" | custom-call | flops 4294967296 | bytes 10485760 | tf_op jit(solution)/shard_map/main_stats/pallas_call | solution.py:172
  13.1 3.0 %collective-permute-start = (f32[32,512]{1,0:T(8,128)S(1)}, f32[32,512]{1,0:T(8,128)S(1)}, u32[]{:S(2)}, u32[]{:S(2)}) collective-permute-start(f32[32,512]{1,0:T(8,128)S(1)} %get-tuple-element.22), channel_id=1, source_target_pairs={{0,16},{8,24},{16,0},{24,8},{1,17},{9,25},{17,1},{25,9},{2,18},{10... | collective-permute-start | bytes 196616 | tf_op jit(solution)/shard_map/ppermute | solution.py:449
  16.1 2.2 %collective-permute-done = f32[32,512]{1,0:T(8,128)S(1)} collective-permute-done((f32[32,512]{1,0:T(8,128)S(1)}, f32[32,512]{1,0:T(8,128)S(1)}, u32[]{:S(2)}, u32[]{:S(2)}) %collective-permute-start) | collective-permute-done | bytes 65568 | tf_op jit(solution)/shard_map/ppermute | solution.py:449
  18.4 0.1 collective-permute-start.1
  18.5 5.4 %index_logits.1 = (f32[512,128]{1,0:T(8,128)S(1)}, f32[1,128]{1,0:T(1,128)S(1)}, bf16[512,8192]{1,0:T(8,128)(2,1)S(1)}) custom-call(bf16[128,8192]{1,0:T(8,128)(2,1)S(1)} %copy-done, bf16[512,128]{1,0:T(8,128)(2,1)} %ik_ref.1, bf16[64,128]{1,0:T(8,128)(2,1)} %bitcast.5, f32[512,512]{1,0:T(8,128)S(1)} %get-tuple-element.21.bias_ref.refs_9_), custom_call_target="tpu_custom_call" | custom-call | flops 1073741824 | bytes 10485760 | tf_op jit(solution)/shard_map/index_logits/pallas_call | solution.py:296
  23.9 2.1 %collective-permute-start.5 = (f32[1,128]{1,0:T(1,128)S(1)}, f32[1,128]{1,0:T(1,128)S(1)}, u32[]{:S(2)}, u32[]{:S(2)}) collective-permute-start(f32[1,128]{1,0:T(1,128)S(1)} %get-tuple-element.25), channel_id=1, source_target_pairs={{0,16},{8,24},{16,0},{24,8},{1,17},{9,25},{17,1},{25,9},{2,18},{10... | collective-permute-start | bytes 1544 | tf_op jit(solution)/shard_map/ppermute | solution.py:449
  26.1 0.1 collective-permute-start.9
  26.1 4.3 %head_sums.4 = (f32[512,128]{1,0:T(8,128)S(1)}, f32[512,128]{1,0:T(8,128)S(1)}) custom-call(bf16[4,128,6144]{2,1,0:T(8,128)(2,1)S(1)} %get-tuple-element.19.q_ref, bf16[512,8192]{1,0:T(8,128)(2,1)S(1)} %get-tuple-element.20.kk_ref, f32[512,512]{1,0:T(8,128)S(1)} %get-tuple-element.21.bias_ref.refs_9_, f32[32,512]{1,0:T(8,128)S(1)} %multiply_add_fusion.refs_0_, ...), custom_call_target="tpu_custom_call" | custom-call | flops 2147483648 | bytes 262144 | tf_op jit(solution)/shard_map/head_sums/pallas_call | solution.py:252
  30.5 2.1 %collective-permute-start.2 = (f32[512,128]{1,0:T(8,128)S(1)}, f32[512,128]{1,0:T(8,128)S(1)}, u32[]{:S(2)}, u32[]{:S(2)}) collective-permute-start(f32[512,128]{1,0:T(8,128)S(1)} %get-tuple-element.23), channel_id=1, source_target_pairs={{0,2},{2,0},{4,6},{6,4},{1,3},{3,1},{5,7},{7,5},{8,10},{10,8},{12,... | collective-permute-start | bytes 786440 | tf_op jit(solution)/shard_map/ppermute | solution.py:449
  32.6 2.5 %collective-permute-start.3 = (f32[512,128]{1,0:T(8,128)S(1)}, f32[512,128]{1,0:T(8,128)S(1)}, u32[]{:S(2)}, u32[]{:S(2)}) collective-permute-start(f32[512,128]{1,0:T(8,128)S(1)} %get-tuple-element.24), channel_id=1, source_target_pairs={{0,6},{2,4},{4,2},{6,0},{1,7},{3,5},{5,3},{7,1},{8,14},{10,12},{12... | collective-permute-start | bytes 786440 | tf_op jit(solution)/shard_map/ppermute | solution.py:449
  35.1 3.1 %head_sums.5 = f32[512,128]{1,0:T(8,128)S(1)} custom-call(bf16[4,128,6144]{2,1,0:T(8,128)(2,1)S(1)} %get-tuple-element.19.q_ref, bf16[512,8192]{1,0:T(8,128)(2,1)S(1)} %get-tuple-element.20.kk_ref, f32[512,512]{1,0:T(8,128)S(1)} %get-tuple-element.21.bias_ref.refs_9_, f32[32,512]{1,0:T(8,128)S(1)} %multiply_add_fusion.refs_0_, ...), custom_call_target="tpu_custom_call" | custom-call | flops 1073741824 | bytes 131072 | tf_op jit(solution)/shard_map/head_sums/pallas_call | solution.py:252
  38.2 0.2 collective-permute-start.4
  38.4 0.1 collective-permute-start.6
  38.4 3.1 %head_sums.3.refs_0_ = f32[512,128]{1,0:T(8,128)S(1)} custom-call(bf16[4,128,6144]{2,1,0:T(8,128)(2,1)S(1)} %get-tuple-element.19.q_ref, bf16[512,8192]{1,0:T(8,128)(2,1)S(1)} %get-tuple-element.20.kk_ref, f32[512,512]{1,0:T(8,128)S(1)} %get-tuple-element.21.bias_ref.refs_9_, f32[32,512]{1,0:T(8,128)S(1)} %multiply_add_fusion.refs_0_, ...), custom_call_target="tpu_custom_call" | custom-call | flops 1073741824 | bytes 131072 | tf_op jit(solution)/shard_map/head_sums/pallas_call | solution.py:252
  41.5 6.4 %collective-permute-done.3.refs_2_ = f32[512,128]{1,0:T(8,128)S(1)} collective-permute-done((f32[512,128]{1,0:T(8,128)S(1)}, f32[512,128]{1,0:T(8,128)S(1)}, u32[]{:S(2)}, u32[]{:S(2)}) %collective-permute-start.3) | collective-permute-done | bytes 262176 | tf_op jit(solution)/shard_map/ppermute | solution.py:449
  48.0 10.2 %collective-permute-done.4.refs_3_ = f32[512,128]{1,0:T(8,128)S(1)} collective-permute-done((f32[512,128]{1,0:T(8,128)S(1)}, f32[512,128]{1,0:T(8,128)S(1)}, u32[]{:S(2)}, u32[]{:S(2)}) %collective-permute-start.4) | collective-permute-done | bytes 262176 | tf_op jit(solution)/shard_map/ppermute | solution.py:449
  58.2 4.3 %index_grad_key.1 = (f32[520,128]{1,0:T(8,128)S(1)}, f32[256,128]{1,0:T(8,128)S(1)}, f32[256,128]{1,0:T(8,128)S(1)}) custom-call(f32[512,128]{1,0:T(8,128)S(1)} %head_sums.3.refs_0_, f32[512,128]{1,0:T(8,128)S(1)} %collective-permute-done.2.refs_1_, f32[512,128]{1,0:T(8,128)S(1)} %collective-permute-done.3.refs_2_, ...), custom_call_target="tpu_custom_call" | custom-call | flops 1073741824 | bytes 10485760 | tf_op jit(solution)/shard_map/index_grad_key/pallas_call | solution.py:358
  62.5 2.7 %collective-permute-start.13 = (f32[256,128]{1,0:T(8,128)S(1)}, f32[256,128]{1,0:T(8,128)S(1)}, u32[]{:S(2)}, u32[]{:S(2)}) collective-permute-start(f32[256,128]{1,0:T(8,128)S(1)} %get-tuple-element.33), channel_id=1, source_target_pairs={{0,6},{2,4},{4,2},{6,0},{1,7},{3,5},{5,3},{7,1},{8,14},{10,12},{12... | collective-permute-start | bytes 393224 | tf_op jit(solution)/shard_map/ppermute | solution.py:449
  65.2 1.5 %collective-permute-start.7 = (f32[520,128]{1,0:T(8,128)S(1)}, f32[520,128]{1,0:T(8,128)S(1)}, u32[]{:S(2)}, u32[]{:S(2)}) collective-permute-start(f32[520,128]{1,0:T(8,128)S(1)} %get-tuple-element.28.refs_0_), channel_id=1, source_target_pairs={{0,16},{8,24},{16,0},{24,8},{1,17},{9,25},{17,1},{25,9},{2,18},{10... | collective-permute-start | bytes 798728 | tf_op jit(solution)/shard_map/ppermute | solution.py:449
  66.7 3.9 %collective-permute-done.13 = f32[256,128]{1,0:T(8,128)S(1)} collective-permute-done((f32[256,128]{1,0:T(8,128)S(1)}, f32[256,128]{1,0:T(8,128)S(1)}, u32[]{:S(2)}, u32[]{:S(2)}) %collective-permute-start.13) | collective-permute-done | bytes 131104 | tf_op jit(solution)/shard_map/ppermute | solution.py:449
  70.7 1.4 %collective-permute-done.16 = f32[256,128]{1,0:T(8,128)S(1)} collective-permute-done((f32[256,128]{1,0:T(8,128)S(1)}, f32[256,128]{1,0:T(8,128)S(1)}, u32[]{:S(2)}, u32[]{:S(2)}) %collective-permute-start.16) | collective-permute-done | bytes 131104 | tf_op jit(solution)/shard_map/ppermute | solution.py:449
  72.1 14.7 %collective-permute-start.14 = (f32[256,128]{1,0:T(8,128)S(1)}, f32[256,128]{1,0:T(8,128)S(1)}, u32[]{:S(2)}, u32[]{:S(2)}) collective-permute-start(f32[256,128]{1,0:T(8,128)S(1)} %add.34), channel_id=1, source_target_pairs={{0,1},{1,0},{2,3},{3,2},{4,5},{5,4},{6,7},{7,6},{8,9},{9,8},{10,11... | collective-permute-start | bytes 393224 | tf_op jit(solution)/shard_map/ppermute | solution.py:449
  86.8 2.1 %collective-permute-start.17 = (f32[256,128]{1,0:T(8,128)S(1)}, f32[256,128]{1,0:T(8,128)S(1)}, u32[]{:S(2)}, u32[]{:S(2)}) collective-permute-start(f32[256,128]{1,0:T(8,128)S(1)} %add.37), channel_id=1, source_target_pairs={{0,6},{2,4},{4,2},{6,0},{1,7},{3,5},{5,3},{7,1},{8,14},{10,12},{12... | collective-permute-start | bytes 393224 | tf_op jit(solution)/shard_map/ppermute | solution.py:449
  88.9 0.8 collective-permute-done.14
  89.7 4.0 %collective-permute-done.17 = f32[256,128]{1,0:T(8,128)S(1)} collective-permute-done((f32[256,128]{1,0:T(8,128)S(1)}, f32[256,128]{1,0:T(8,128)S(1)}, u32[]{:S(2)}, u32[]{:S(2)}) %collective-permute-start.17) | collective-permute-done | bytes 131104 | tf_op jit(solution)/shard_map/ppermute | solution.py:449
  93.7 1.2 %collective-permute-start.15 = (f32[256,128]{1,0:T(8,128)S(1)}, f32[256,128]{1,0:T(8,128)S(1)}, u32[]{:S(2)}, u32[]{:S(2)}) collective-permute-start(f32[256,128]{1,0:T(8,128)S(1)} %add.35), channel_id=1, source_target_pairs={{0,2},{2,0},{4,6},{6,4},{1,3},{3,1},{5,7},{7,5},{8,10},{10,8},{12,... | collective-permute-start | bytes 393224 | tf_op jit(solution)/shard_map/ppermute | solution.py:449
  94.9 0.1 collective-permute-start.18
  95.0 3.5 %index_grad_query.2 = (f32[128,2048]{1,0:T(8,128)S(1)}, f32[1,128]{1,0:T(1,128)S(1)}) custom-call(f32[520,128]{1,0:T(8,128)S(1)} %get-tuple-element.28.refs_0_, f32[520,128]{1,0:T(8,128)S(1)} %collective-permute-done.11.refs_1_, f32[512,128]{1,0:T(8,128)S(1)} %convert_element_type.3.refs_2_, f32[512,128]{1,0:T(8,128)S(1)} %collective-permute-done.12.refs_3_, ...), custom_call_target="tpu_custom_call" | custom-call | flops 1073741824 | bytes 3145728 | tf_op jit(solution)/shard_map/index_grad_query/pallas_call | solution.py:430
  98.5 0.2 collective-permute-done.15
  98.7 1.2 %collective-permute-done.18 = f32[256,128]{1,0:T(8,128)S(1)} collective-permute-done((f32[256,128]{1,0:T(8,128)S(1)}, f32[256,128]{1,0:T(8,128)S(1)}, u32[]{:S(2)}, u32[]{:S(2)}) %collective-permute-start.18) | collective-permute-done | bytes 131104 | tf_op jit(solution)/shard_map/ppermute | solution.py:449
  100.0 0.7 pad_maximum_fusion
  100.7 4.1 %index_grad_query.3 = (f32[128,2048]{1,0:T(8,128)}, f32[1,128]{1,0:T(1,128)}) custom-call(f32[520,128]{1,0:T(8,128)S(1)} %collective-permute-done.7.refs_0_, f32[520,128]{1,0:T(8,128)S(1)} %collective-permute-done.8.refs_1_, f32[512,128]{1,0:T(8,128)S(1)} %collective-permute-done.9.refs_2_, f32[512,128]{1,0:T(8,128)S(1)} %collective-permute-done.10.refs_3_, ...), custom_call_target="tpu_custom_call" | custom-call | flops 1073741824 | bytes 3145728 | tf_op jit(solution)/shard_map/index_grad_query/pallas_call | solution.py:430
  (28 shorter events, 0.2 us)
Async XLA Ops:
  0.6 17.9 %copy-start = (bf16[128,8192]{1,0:T(8,128)(2,1)S(1)}, bf16[128,8192]{1,0:T(8,128)(2,1)}, u32[]{:S(2)}) copy-start(bf16[128,8192]{1,0:T(8,128)(2,1)} %refs_4_.3) | copy-start | bytes 6291460
  0.6 25.4 %copy-start.1 = (bf16[512,128]{1,0:T(8,128)(2,1)S(1)}, bf16[512,128]{1,0:T(8,128)(2,1)}, u32[]{:S(2)}) copy-start(bf16[512,128]{1,0:T(8,128)(2,1)} %ik_ref.1) | copy-start | bytes 393220
  13.1 5.3 %collective-permute-start = (f32[32,512]{1,0:T(8,128)S(1)}, f32[32,512]{1,0:T(8,128)S(1)}, u32[]{:S(2)}, u32[]{:S(2)}) collective-permute-start(f32[32,512]{1,0:T(8,128)S(1)} %get-tuple-element.22), channel_id=1, source_target_pairs={{0,16},{8,24},{16,0},{24,8},{1,17},{9,25},{17,1},{25,9},{2,18},{10... | collective-permute-start | bytes 196616 | tf_op jit(solution)/shard_map/ppermute | solution.py:449
  18.4 7.7 %collective-permute-start.1 = (f32[32,512]{1,0:T(8,128)S(1)}, f32[32,512]{1,0:T(8,128)S(1)}, u32[]{:S(2)}, u32[]{:S(2)}) collective-permute-start(f32[32,512]{1,0:T(8,128)S(1)} %multiply_add_fusion.refs_0_), channel_id=1, source_target_pairs={{0,8},{8,0},{16,24},{24,16},{1,9},{9,1},{17,25},{25,17},{2,10},{10... | collective-permute-start | bytes 196616 | tf_op jit(solution)/shard_map/ppermute | solution.py:449
  23.9 14.4 %collective-permute-start.5 = (f32[1,128]{1,0:T(1,128)S(1)}, f32[1,128]{1,0:T(1,128)S(1)}, u32[]{:S(2)}, u32[]{:S(2)}) collective-permute-start(f32[1,128]{1,0:T(1,128)S(1)} %get-tuple-element.25), channel_id=1, source_target_pairs={{0,16},{8,24},{16,0},{24,8},{1,17},{9,25},{17,1},{25,9},{2,18},{10... | collective-permute-start | bytes 1544 | tf_op jit(solution)/shard_map/ppermute | solution.py:449
  26.1 60.7 %collective-permute-start.9 = (f32[512,128]{1,0:T(8,128)S(1)}, f32[512,128]{1,0:T(8,128)S(1)}, u32[]{:S(2)}, u32[]{:S(2)}) collective-permute-start(f32[512,128]{1,0:T(8,128)S(1)} %convert_element_type.3.refs_2_), channel_id=1, source_target_pairs={{0,16},{8,24},{16,0},{24,8},{1,17},{9,25},{17,1},{25,9},{2,18},{10... | collective-permute-start | bytes 786440 | tf_op jit(solution)/shard_map/ppermute | solution.py:449
  30.5 11.0 %collective-permute-start.2 = (f32[512,128]{1,0:T(8,128)S(1)}, f32[512,128]{1,0:T(8,128)S(1)}, u32[]{:S(2)}, u32[]{:S(2)}) collective-permute-start(f32[512,128]{1,0:T(8,128)S(1)} %get-tuple-element.23), channel_id=1, source_target_pairs={{0,2},{2,0},{4,6},{6,4},{1,3},{3,1},{5,7},{7,5},{8,10},{10,8},{12,... | collective-permute-start | bytes 786440 | tf_op jit(solution)/shard_map/ppermute | solution.py:449
  32.6 15.3 %collective-permute-start.3 = (f32[512,128]{1,0:T(8,128)S(1)}, f32[512,128]{1,0:T(8,128)S(1)}, u32[]{:S(2)}, u32[]{:S(2)}) collective-permute-start(f32[512,128]{1,0:T(8,128)S(1)} %get-tuple-element.24), channel_id=1, source_target_pairs={{0,6},{2,4},{4,2},{6,0},{1,7},{3,5},{5,3},{7,1},{8,14},{10,12},{12... | collective-permute-start | bytes 786440 | tf_op jit(solution)/shard_map/ppermute | solution.py:449
  38.2 20.0 %collective-permute-start.4 = (f32[512,128]{1,0:T(8,128)S(1)}, f32[512,128]{1,0:T(8,128)S(1)}, u32[]{:S(2)}, u32[]{:S(2)}) collective-permute-start(f32[512,128]{1,0:T(8,128)S(1)} %head_sums.5), channel_id=1, source_target_pairs={{0,4},{2,6},{4,0},{6,2},{1,5},{3,7},{5,1},{7,3},{8,12},{10,14},{12... | collective-permute-start | bytes 786440 | tf_op jit(solution)/shard_map/ppermute | solution.py:449
  38.4 3.2 %collective-permute-start.6 = (f32[1,128]{1,0:T(1,128)S(1)}, f32[1,128]{1,0:T(1,128)S(1)}, u32[]{:S(2)}, u32[]{:S(2)}) collective-permute-start(f32[1,128]{1,0:T(1,128)S(1)} %multiply_add_fusion.1.refs_4_.refs_6_), channel_id=1, source_target_pairs={{0,8},{8,0},{16,24},{24,16},{1,9},{9,1},{17,25},{25,17},{2,10},{10... | collective-permute-start | bytes 1544 | tf_op jit(solution)/shard_map/ppermute | solution.py:449
  62.5 8.1 %collective-permute-start.13 = (f32[256,128]{1,0:T(8,128)S(1)}, f32[256,128]{1,0:T(8,128)S(1)}, u32[]{:S(2)}, u32[]{:S(2)}) collective-permute-start(f32[256,128]{1,0:T(8,128)S(1)} %get-tuple-element.33), channel_id=1, source_target_pairs={{0,6},{2,4},{4,2},{6,0},{1,7},{3,5},{5,3},{7,1},{8,14},{10,12},{12... | collective-permute-start | bytes 393224 | tf_op jit(solution)/shard_map/ppermute | solution.py:449
  65.2 23.7 %collective-permute-start.7 = (f32[520,128]{1,0:T(8,128)S(1)}, f32[520,128]{1,0:T(8,128)S(1)}, u32[]{:S(2)}, u32[]{:S(2)}) collective-permute-start(f32[520,128]{1,0:T(8,128)S(1)} %get-tuple-element.28.refs_0_), channel_id=1, source_target_pairs={{0,16},{8,24},{16,0},{24,8},{1,17},{9,25},{17,1},{25,9},{2,18},{10... | collective-permute-start | bytes 798728 | tf_op jit(solution)/shard_map/ppermute | solution.py:449
  66.7 5.4 %collective-permute-start.16 = (f32[256,128]{1,0:T(8,128)S(1)}, f32[256,128]{1,0:T(8,128)S(1)}, u32[]{:S(2)}, u32[]{:S(2)}) collective-permute-start(f32[256,128]{1,0:T(8,128)S(1)} %get-tuple-element.34), channel_id=1, source_target_pairs={{0,2},{2,0},{4,6},{6,4},{1,3},{3,1},{5,7},{7,5},{8,10},{10,8},{12,... | collective-permute-start | bytes 393224 | tf_op jit(solution)/shard_map/ppermute | solution.py:449
  66.7 28.2 %collective-permute-start.12 = (f32[512,128]{1,0:T(8,128)S(1)}, f32[512,128]{1,0:T(8,128)S(1)}, u32[]{:S(2)}, u32[]{:S(2)}) collective-permute-start(f32[512,128]{1,0:T(8,128)S(1)} %convert_element_type.3.refs_2_), channel_id=1, source_target_pairs={{0,8},{8,0},{16,24},{24,16},{1,9},{9,1},{17,25},{25,17},{2,10},{10... | collective-permute-start | bytes 786440 | tf_op jit(solution)/shard_map/ppermute | solution.py:449
  70.6 24.4 %collective-permute-start.11 = (f32[520,128]{1,0:T(8,128)S(1)}, f32[520,128]{1,0:T(8,128)S(1)}, u32[]{:S(2)}, u32[]{:S(2)}) collective-permute-start(f32[520,128]{1,0:T(8,128)S(1)} %get-tuple-element.28.refs_0_), channel_id=1, source_target_pairs={{0,8},{8,0},{16,24},{24,16},{1,9},{9,1},{17,25},{25,17},{2,10},{10... | collective-permute-start | bytes 798728 | tf_op jit(solution)/shard_map/ppermute | solution.py:449
  72.1 17.6 %collective-permute-start.14 = (f32[256,128]{1,0:T(8,128)S(1)}, f32[256,128]{1,0:T(8,128)S(1)}, u32[]{:S(2)}, u32[]{:S(2)}) collective-permute-start(f32[256,128]{1,0:T(8,128)S(1)} %add.34), channel_id=1, source_target_pairs={{0,1},{1,0},{2,3},{3,2},{4,5},{5,4},{6,7},{7,6},{8,9},{9,8},{10,11... | collective-permute-start | bytes 393224 | tf_op jit(solution)/shard_map/ppermute | solution.py:449
  86.8 6.9 %collective-permute-start.17 = (f32[256,128]{1,0:T(8,128)S(1)}, f32[256,128]{1,0:T(8,128)S(1)}, u32[]{:S(2)}, u32[]{:S(2)}) collective-permute-start(f32[256,128]{1,0:T(8,128)S(1)} %add.37), channel_id=1, source_target_pairs={{0,6},{2,4},{4,2},{6,0},{1,7},{3,5},{5,3},{7,1},{8,14},{10,12},{12... | collective-permute-start | bytes 393224 | tf_op jit(solution)/shard_map/ppermute | solution.py:449
  88.9 11.7 %collective-permute-start.8 = (f32[520,128]{1,0:T(8,128)S(1)}, f32[520,128]{1,0:T(8,128)S(1)}, u32[]{:S(2)}, u32[]{:S(2)}) collective-permute-start(f32[520,128]{1,0:T(8,128)S(1)} %collective-permute-done.7.refs_0_), channel_id=1, source_target_pairs={{0,8},{8,0},{16,24},{24,16},{1,9},{9,1},{17,25},{25,17},{2,10},{10... | collective-permute-start | bytes 798728 | tf_op jit(solution)/shard_map/ppermute | solution.py:449
  89.7 11.0 %collective-permute-start.10 = (f32[512,128]{1,0:T(8,128)S(1)}, f32[512,128]{1,0:T(8,128)S(1)}, u32[]{:S(2)}, u32[]{:S(2)}) collective-permute-start(f32[512,128]{1,0:T(8,128)S(1)} %collective-permute-done.9.refs_2_), channel_id=1, source_target_pairs={{0,8},{8,0},{16,24},{24,16},{1,9},{9,1},{17,25},{25,17},{2,10},{10... | collective-permute-start | bytes 786440 | tf_op jit(solution)/shard_map/ppermute | solution.py:449
  93.7 5.0 %collective-permute-start.15 = (f32[256,128]{1,0:T(8,128)S(1)}, f32[256,128]{1,0:T(8,128)S(1)}, u32[]{:S(2)}, u32[]{:S(2)}) collective-permute-start(f32[256,128]{1,0:T(8,128)S(1)} %add.35), channel_id=1, source_target_pairs={{0,2},{2,0},{4,6},{6,4},{1,3},{3,1},{5,7},{7,5},{8,10},{10,8},{12,... | collective-permute-start | bytes 393224 | tf_op jit(solution)/shard_map/ppermute | solution.py:449
  94.9 5.0 %collective-permute-start.18 = (f32[256,128]{1,0:T(8,128)S(1)}, f32[256,128]{1,0:T(8,128)S(1)}, u32[]{:S(2)}, u32[]{:S(2)}) collective-permute-start(f32[256,128]{1,0:T(8,128)S(1)} %add.38), channel_id=1, source_target_pairs={{0,1},{1,0},{2,3},{3,2},{4,5},{5,4},{6,7},{7,6},{8,9},{9,8},{10,11... | collective-permute-start | bytes 393224 | tf_op jit(solution)/shard_map/ppermute | solution.py:449

commit v7 on v5

--- a/solution.py
+++ b/solution.py
@@ -75,10 +75,10 @@
     return pl.ds(pl.multiple_of(index * width, LANES), width)
 
 
-def stats_kernel(per, count_hbm, q_hbm, kn_hbm, rope_hbm, qpos_hbm, kpos_hbm,
-                 lse_ref, q_ref, kk_ref, bias_ref,
+def stats_kernel(per, count_hbm, q_hbm, kn_hbm, rope_hbm, qpos_hbm, kpos_hbm, iq_hbm,
+                 lse_ref, q_ref, kk_ref, bias_ref, iq_ref,
                  kn_ref, rope_ref, qpos_ref, kpos_ref, even_ref, odd_ref, none_ref, bad_ref,
-                 count_ref, small_sem, q_sem, kn_sem):
+                 count_ref, small_sem, q_sem, kn_sem, iq_sem):
     keys = kn_ref.shape[0]
     groups, rows = q_ref.shape[0], q_ref.shape[1]
     pairs = q_ref.shape[2] // PAIR
@@ -103,6 +103,8 @@
     for i in range(pairs):
         for copy in large(i):
             copy.start()
+    index_copy = pltpu.make_async_copy(iq_hbm, iq_ref, iq_sem)
+    index_copy.start()
     for copy in small:
         copy.wait()
 
@@ -148,6 +150,7 @@
         return carry
 
     lax.fori_loop(0, pairs // per, step, 0)
+    index_copy.wait()
 
     @pl.when(jnp.max(bad_ref[...]) > 0)
     def _():
@@ -164,20 +167,21 @@
         lax.fori_loop(0, pairs, again, 0)
 
 
-def main_stats(main_query, key_nope, rope_t, query_pos, key_pos, key_count):
+def main_stats(main_query, key_nope, rope_t, query_pos, key_pos, key_count, index_query):
     groups, rows, width = main_query.shape
     heads = width // DQK
     keys = key_nope.shape[0]
     total = groups * rows
     return pl.pallas_call(
         functools.partial(stats_kernel, 2),
-        in_specs=[pl.BlockSpec(memory_space=pltpu.HBM)] * 6,
-        out_specs=[IN_VMEM] * 4,
+        in_specs=[pl.BlockSpec(memory_space=pltpu.HBM)] * 7,
+        out_specs=[IN_VMEM] * 5,
         out_shape=[
             jax.ShapeDtypeStruct((heads, total), f32),
             jax.ShapeDtypeStruct(main_query.shape, bf16),
             jax.ShapeDtypeStruct((keys, heads * 2 * LANES), bf16),
             jax.ShapeDtypeStruct((keys, total), f32),
+            jax.ShapeDtypeStruct(index_query.shape, bf16),
         ],
         scratch_shapes=[
             pltpu.VMEM(key_nope.shape, bf16),
@@ -192,13 +196,14 @@
             pltpu.SemaphoreType.DMA((4,)),
             pltpu.SemaphoreType.DMA((heads // 2,)),
             pltpu.SemaphoreType.DMA((heads // 2,)),
+            pltpu.SemaphoreType.DMA,
         ],
         compiler_params=pltpu.CompilerParams(vmem_limit_bytes=16 * 1024 * 1024),
         cost_estimate=cost(
             heads * total * keys * 512, main_query.size * 2 + key_nope.size * 2, heads * total * keys
         ),
         name="main_stats",
-    )(key_count, main_query, key_nope, rope_t, query_pos, key_pos)
+    )(key_count, main_query, key_nope, rope_t, query_pos, key_pos, index_query)
 
 
 def target_kernel(n_lse, masks, per, parts, q_ref, kk_ref, bias_ref, *refs):
@@ -477,9 +482,10 @@
          index_query, index_key, index_weight, row_cotangent):
     groups, rows, _ = main_query.shape
     keys = key_nope.shape[0]
-    main_query, key_nope, rope_t, query_pos, key_row, key_count, weight_t, cotangent, narrow = in_hbm(
+    (main_query, key_nope, rope_t, query_pos, key_row, key_count, weight_t, cotangent, narrow,
+     index_query) = in_hbm(
         main_query, key_nope, key_rope.T, query_pos, key_pos.reshape(1, keys), key_count,
-        index_weight.T, row_cotangent.reshape(1, rows), index_key,
+        index_weight.T, row_cotangent.reshape(1, rows), index_key, index_query,
     )
 
     def gathered(value):
@@ -490,9 +496,11 @@
             return [value, near, far, across]
         return list(lax.all_gather(value, "key"))
 
-    lse, q, kk, bias = main_stats(main_query, key_nope, rope_t, query_pos, key_row, key_count)
+    lse, q, kk, bias, iq = main_stats(
+        main_query, key_nope, rope_t, query_pos, key_row, key_count, index_query
+    )
     lses = butterfly_lse(lse, n_key)
-    logits, index_lse, wm = index_logits(index_query, narrow, weight_t, bias)
+    logits, index_lse, wm = index_logits(iq, narrow, weight_t, bias)
     index_lses = butterfly_lse(index_lse, n_key)
     iks = gathered(index_key.astype(f32))
 
@@ -514,14 +522,14 @@
         tiles = tiles[jnp.bitwise_xor(jnp.arange(groups), z)]
         parts = [lax.psum_scatter(tiles, "head", scatter_dimension=0, tiled=True)[0]]
 
-    sg, *grad_key = index_grad_key(parts, index_lses, logits, wm, index_query, bias, cotangent)
+    sg, *grad_key = index_grad_key(parts, index_lses, logits, wm, iq, bias, cotangent)
     grad_key = summed_copies(grad_key, n_head, n_query)
     sgs = gathered(sg)
     carry = None
     for lo in range(0, n_key, 2):
         last = lo + 2 >= n_key
         carry = index_grad_query(
-            n_key, sgs[lo : lo + 2], iks[lo : lo + 2], index_query, weight_t,
+            n_key, sgs[lo : lo + 2], iks[lo : lo + 2], iq, weight_t,
             index_lses if last else [], carry,
         )
     grad_query, kl = carry

time: 99.4 us -> 99.4 us (level)
  no operation moved by 1% of the time
where the time goes in v7:
time: 99.4 us; the launch traced here: 99 us
  Pallas kernels  40 us (40%)
  starting transfers between devices  34.2 us (34%)
  waiting for transfers between devices  23 us (23%)
    ppermute x20, starting transfers between devices, swap(): return lax.ppermute(value, axis, [(i, i ^ mask) for i in range(size)])  34.2 us
    ppermute x20, waiting for transfers between devices, swap(): return lax.ppermute(value, axis, [(i, i ^ mask) for i in range(size)])  23 us
    pallas_call x1, Pallas kernels, main_stats(): pl.pallas_call(functools.partial(stats_kernel, 2), in_specs=[pl.BlockSpec...  12.3 us
    pallas_call x3, Pallas kernels, head_sums(): pl.pallas_call(functools.partial(target_kernel, len(lses), masks, 4 // n,...  10.4 us
    pallas_call x2, Pallas kernels, index_grad_query(): pl.pallas_call(functools.partial(grad_query_kernel, n, first, len(lses)),...  7.57 us
    pallas_call x1, Pallas kernels, index_logits(): pl.pallas_call(functools.partial(logits_kernel, 4), grid=(1,), in_specs=[...  5.44 us
    pallas_call x1, Pallas kernels, index_grad_key(): pl.pallas_call(functools.partial(grad_key_kernel, len(parts), len(lses),...  4.3 us
  transfers between devices with their start and end apart: 20, of which 9 were waited for; matrix products, arithmetic and copies ran while one was open for 1% of the time, Pallas kernels for 24%

profile of v7, /device:TPU:0, one launch (start us, length us, event | category | flops | bytes accessed | tf_op | source)
XLA Modules:
  0.0 99.0 jit_solution(11883867783171770529)
XLA Ops:
  0.6 12.3 %main_stats.1 = (f32[32,512]{1,0:T(8,128)S(1)}, bf16[4,128,6144]{2,1,0:T(8,128)(2,1)S(1)}, bf16[512,8192]{1,0:T(8,128)(2,1)S(1)}, f32[512,512]{1,0:T(8,128)S(1)}, bf16[128,8192]{1,0:T(8,128)(2,1)S(1)}) custom-call(s32[16]{0:T(128)} %count_hbm.1, bf16[4,128,6144]{2,1,0:T(8,128)(2,1)} %q_hbm.1, bf16[512,4096]{1,0:T(8,128)(2,1)} %kn_hbm.1, ...), custom_call_target="tpu_custom_call" | custom-call | flops 4294967296 | bytes 10485760 | tf_op jit(solution)/shard_map/main_stats/pallas_call | solution.py:175
  13.0 3.0 %collective-permute-start = (f32[32,512]{1,0:T(8,128)S(1)}, f32[32,512]{1,0:T(8,128)S(1)}, u32[]{:S(2)}, u32[]{:S(2)}) collective-permute-start(f32[32,512]{1,0:T(8,128)S(1)} %get-tuple-element.25), channel_id=1, source_target_pairs={{0,16},{8,24},{16,0},{24,8},{1,17},{9,25},{17,1},{25,9},{2,18},{10... | collective-permute-start | bytes 196616 | tf_op jit(solution)/shard_map/ppermute | solution.py:454
  16.0 2.2 %collective-permute-done = f32[32,512]{1,0:T(8,128)S(1)} collective-permute-done((f32[32,512]{1,0:T(8,128)S(1)}, f32[32,512]{1,0:T(8,128)S(1)}, u32[]{:S(2)}, u32[]{:S(2)}) %collective-permute-start) | collective-permute-done | bytes 65568 | tf_op jit(solution)/shard_map/ppermute | solution.py:454
  18.3 0.1 collective-permute-start.1
  18.4 5.4 %index_logits.1 = (f32[512,128]{1,0:T(8,128)S(1)}, f32[1,128]{1,0:T(1,128)S(1)}, bf16[512,8192]{1,0:T(8,128)(2,1)S(1)}) custom-call(bf16[128,8192]{1,0:T(8,128)(2,1)S(1)} %get-tuple-element.30.iq_ref.refs_7_.refs_4_, bf16[512,128]{1,0:T(8,128)(2,1)} %ik_ref.1, bf16[64,128]{1,0:T(8,128)(2,1)} %bitcast.5, f32[512,512]{1,0:T(8,128)S(1)} %get-tuple-element.24.bias_ref.refs_8_), custom_call_target="tpu_custom_call" | custom-call | flops 1073741824 | bytes 10485760 | tf_op jit(solution)/shard_map/index_logits/pallas_call | solution.py:301
  23.8 2.1 %collective-permute-start.6 = (f32[1,128]{1,0:T(1,128)S(1)}, f32[1,128]{1,0:T(1,128)S(1)}, u32[]{:S(2)}, u32[]{:S(2)}) collective-permute-start(f32[1,128]{1,0:T(1,128)S(1)} %get-tuple-element.31), channel_id=1, source_target_pairs={{0,16},{8,24},{16,0},{24,8},{1,17},{9,25},{17,1},{25,9},{2,18},{10... | collective-permute-start | bytes 1544 | tf_op jit(solution)/shard_map/ppermute | solution.py:454
  25.9 0.1 collective-permute-start.10
  26.0 3.1 %head_sums.5 = (f32[256,128]{1,0:T(8,128)S(1)}, f32[256,128]{1,0:T(8,128)S(1)}) custom-call(bf16[4,128,6144]{2,1,0:T(8,128)(2,1)S(1)} %get-tuple-element.22.q_ref, bf16[512,8192]{1,0:T(8,128)(2,1)S(1)} %get-tuple-element.23.kk_ref, f32[512,512]{1,0:T(8,128)S(1)} %get-tuple-element.24.bias_ref.refs_8_, f32[32,512]{1,0:T(8,128)S(1)} %multiply_add_fusion.refs_0_, ...), custom_call_target="tpu_custom_call" | custom-call | flops 1073741824 | bytes 131072 | tf_op jit(solution)/shard_map/head_sums/pallas_call | solution.py:257
  29.1 2.1 %collective-permute-start.4 = (f32[256,128]{1,0:T(8,128)S(1)}, f32[256,128]{1,0:T(8,128)S(1)}, u32[]{:S(2)}, u32[]{:S(2)}) collective-permute-start(f32[256,128]{1,0:T(8,128)S(1)} %get-tuple-element.29), channel_id=1, source_target_pairs={{0,2},{2,0},{4,6},{6,4},{1,3},{3,1},{5,7},{7,5},{8,10},{10,8},{12,... | collective-permute-start | bytes 393224 | tf_op jit(solution)/shard_map/ppermute | solution.py:454
  31.2 2.5 %collective-permute-start.2 = (f32[256,128]{1,0:T(8,128)S(1)}, f32[256,128]{1,0:T(8,128)S(1)}, u32[]{:S(2)}, u32[]{:S(2)}) collective-permute-start(f32[256,128]{1,0:T(8,128)S(1)} %get-tuple-element.27), channel_id=1, source_target_pairs={{0,6},{2,4},{4,2},{6,0},{1,7},{3,5},{5,3},{7,1},{8,14},{10,12},{12... | collective-permute-start | bytes 393224 | tf_op jit(solution)/shard_map/ppermute | solution.py:454
  33.7 4.3 %head_sums.4 = (f32[512,128]{1,0:T(8,128)S(1)}, f32[512,128]{1,0:T(8,128)S(1)}) custom-call(bf16[4,128,6144]{2,1,0:T(8,128)(2,1)S(1)} %get-tuple-element.22.q_ref, bf16[512,8192]{1,0:T(8,128)(2,1)S(1)} %get-tuple-element.23.kk_ref, f32[512,512]{1,0:T(8,128)S(1)} %get-tuple-element.24.bias_ref.refs_8_, f32[32,512]{1,0:T(8,128)S(1)} %multiply_add_fusion.refs_0_, ...), custom_call_target="tpu_custom_call" | custom-call | flops 2147483648 | bytes 262144 | tf_op jit(solution)/shard_map/head_sums/pallas_call | solution.py:257
  38.1 3.4 %collective-permute-start.5 = (f32[512,128]{1,0:T(8,128)S(1)}, f32[512,128]{1,0:T(8,128)S(1)}, u32[]{:S(2)}, u32[]{:S(2)}) collective-permute-start(f32[512,128]{1,0:T(8,128)S(1)} %pad_add_fusion), channel_id=1, source_target_pairs={{0,6},{2,4},{4,2},{6,0},{1,7},{3,5},{5,3},{7,1},{8,14},{10,12},{12... | collective-permute-start | bytes 786440 | tf_op jit(solution)/shard_map/ppermute | solution.py:454
  41.5 0.1 collective-permute-start.3
  41.6 0.1 collective-permute-start.7
  41.7 3.0 %head_sums.3.refs_0_ = f32[512,128]{1,0:T(8,128)S(1)} custom-call(bf16[4,128,6144]{2,1,0:T(8,128)(2,1)S(1)} %get-tuple-element.22.q_ref, bf16[512,8192]{1,0:T(8,128)(2,1)S(1)} %get-tuple-element.23.kk_ref, f32[512,512]{1,0:T(8,128)S(1)} %get-tuple-element.24.bias_ref.refs_8_, f32[32,512]{1,0:T(8,128)S(1)} %multiply_add_fusion.refs_0_, ...), custom_call_target="tpu_custom_call" | custom-call | flops 1073741824 | bytes 131072 | tf_op jit(solution)/shard_map/head_sums/pallas_call | solution.py:257
  44.7 4.4 %collective-permute-done.5.refs_2_ = f32[512,128]{1,0:T(8,128)S(1)} collective-permute-done((f32[512,128]{1,0:T(8,128)S(1)}, f32[512,128]{1,0:T(8,128)S(1)}, u32[]{:S(2)}, u32[]{:S(2)}) %collective-permute-start.5) | collective-permute-done | bytes 262176 | tf_op jit(solution)/shard_map/ppermute | solution.py:454
  49.1 3.7 %collective-permute-done.3.refs_1_ = f32[512,128]{1,0:T(8,128)S(1)} collective-permute-done((f32[512,128]{1,0:T(8,128)S(1)}, f32[512,128]{1,0:T(8,128)S(1)}, u32[]{:S(2)}, u32[]{:S(2)}) %collective-permute-start.3) | collective-permute-done | bytes 262176 | tf_op jit(solution)/shard_map/ppermute | solution.py:454
  52.8 4.3 %index_grad_key.1 = (f32[520,128]{1,0:T(8,128)S(1)}, f32[256,128]{1,0:T(8,128)S(1)}, f32[256,128]{1,0:T(8,128)S(1)}) custom-call(f32[512,128]{1,0:T(8,128)S(1)} %head_sums.3.refs_0_, f32[512,128]{1,0:T(8,128)S(1)} %collective-permute-done.3.refs_1_, f32[512,128]{1,0:T(8,128)S(1)} %collective-permute-done.5.refs_2_, ...), custom_call_target="tpu_custom_call" | custom-call | flops 1073741824 | bytes 10485760 | tf_op jit(solution)/shard_map/index_grad_key/pallas_call | solution.py:363
  57.1 1.9 %collective-permute-start.14 = (f32[256,128]{1,0:T(8,128)S(1)}, f32[256,128]{1,0:T(8,128)S(1)}, u32[]{:S(2)}, u32[]{:S(2)}) collective-permute-start(f32[256,128]{1,0:T(8,128)S(1)} %get-tuple-element.39), channel_id=1, source_target_pairs={{0,6},{2,4},{4,2},{6,0},{1,7},{3,5},{5,3},{7,1},{8,14},{10,12},{12... | collective-permute-start | bytes 393224 | tf_op jit(solution)/shard_map/ppermute | solution.py:454
  59.0 1.5 %collective-permute-start.8 = (f32[520,128]{1,0:T(8,128)S(1)}, f32[520,128]{1,0:T(8,128)S(1)}, u32[]{:S(2)}, u32[]{:S(2)}) collective-permute-start(f32[520,128]{1,0:T(8,128)S(1)} %get-tuple-element.34.refs_0_), channel_id=1, source_target_pairs={{0,16},{8,24},{16,0},{24,8},{1,17},{9,25},{17,1},{25,9},{2,18},{10... | collective-permute-start | bytes 798728 | tf_op jit(solution)/shard_map/ppermute | solution.py:454
  60.5 4.9 %collective-permute-done.14 = f32[256,128]{1,0:T(8,128)S(1)} collective-permute-done((f32[256,128]{1,0:T(8,128)S(1)}, f32[256,128]{1,0:T(8,128)S(1)}, u32[]{:S(2)}, u32[]{:S(2)}) %collective-permute-start.14) | collective-permute-done | bytes 131104 | tf_op jit(solution)/shard_map/ppermute | solution.py:454
  65.4 1.3 %collective-permute-done.17 = f32[256,128]{1,0:T(8,128)S(1)} collective-permute-done((f32[256,128]{1,0:T(8,128)S(1)}, f32[256,128]{1,0:T(8,128)S(1)}, u32[]{:S(2)}, u32[]{:S(2)}) %collective-permute-start.17) | collective-permute-done | bytes 131104 | tf_op jit(solution)/shard_map/ppermute | solution.py:454
  66.7 14.8 %collective-permute-start.15 = (f32[256,128]{1,0:T(8,128)S(1)}, f32[256,128]{1,0:T(8,128)S(1)}, u32[]{:S(2)}, u32[]{:S(2)}) collective-permute-start(f32[256,128]{1,0:T(8,128)S(1)} %add.46), channel_id=1, source_target_pairs={{0,1},{1,0},{2,3},{3,2},{4,5},{5,4},{6,7},{7,6},{8,9},{9,8},{10,11... | collective-permute-start | bytes 393224 | tf_op jit(solution)/shard_map/ppermute | solution.py:454
  81.5 1.8 %collective-permute-start.18 = (f32[256,128]{1,0:T(8,128)S(1)}, f32[256,128]{1,0:T(8,128)S(1)}, u32[]{:S(2)}, u32[]{:S(2)}) collective-permute-start(f32[256,128]{1,0:T(8,128)S(1)} %add.49), channel_id=1, source_target_pairs={{0,6},{2,4},{4,2},{6,0},{1,7},{3,5},{5,3},{7,1},{8,14},{10,12},{12... | collective-permute-start | bytes 393224 | tf_op jit(solution)/shard_map/ppermute | solution.py:454
  83.3 1.2 %collective-permute-done.15 = f32[256,128]{1,0:T(8,128)S(1)} collective-permute-done((f32[256,128]{1,0:T(8,128)S(1)}, f32[256,128]{1,0:T(8,128)S(1)}, u32[]{:S(2)}, u32[]{:S(2)}) %collective-permute-start.15) | collective-permute-done | bytes 131104 | tf_op jit(solution)/shard_map/ppermute | solution.py:454
  84.6 3.8 %collective-permute-done.18 = f32[256,128]{1,0:T(8,128)S(1)} collective-permute-done((f32[256,128]{1,0:T(8,128)S(1)}, f32[256,128]{1,0:T(8,128)S(1)}, u32[]{:S(2)}, u32[]{:S(2)}) %collective-permute-start.18) | collective-permute-done | bytes 131104 | tf_op jit(solution)/shard_map/ppermute | solution.py:454
  88.3 0.8 collective-permute-start.16
  89.2 3.5 %index_grad_query.2 = (f32[128,2048]{1,0:T(8,128)S(1)}, f32[1,128]{1,0:T(1,128)S(1)}) custom-call(f32[520,128]{1,0:T(8,128)S(1)} %get-tuple-element.34.refs_0_, f32[520,128]{1,0:T(8,128)S(1)} %collective-permute-done.12.refs_1_, f32[512,128]{1,0:T(8,128)S(1)} %convert_element_type.7.refs_2_, f32[512,128]{1,0:T(8,128)S(1)} %collective-permute-done.13.refs_3_, ...), custom_call_target="tpu_custom_call" | custom-call | flops 1073741824 | bytes 3145728 | tf_op jit(solution)/shard_map/index_grad_query/pallas_call | solution.py:435
  92.7 0.6 collective-permute-done.16
  93.3 0.8 collective-permute-done.19
  94.2 0.7 pad_maximum_fusion
  94.9 4.1 %index_grad_query.3 = (f32[128,2048]{1,0:T(8,128)}, f32[1,128]{1,0:T(1,128)}) custom-call(f32[520,128]{1,0:T(8,128)S(1)} %collective-permute-done.8.refs_0_, f32[520,128]{1,0:T(8,128)S(1)} %collective-permute-done.9.refs_1_, f32[512,128]{1,0:T(8,128)S(1)} %collective-permute-done.10.refs_2_, f32[512,128]{1,0:T(8,128)S(1)} %collective-permute-done.11.refs_3_, ...), custom_call_target="tpu_custom_call" | custom-call | flops 1073741824 | bytes 3145728 | tf_op jit(solution)/shard_map/index_grad_query/pallas_call | solution.py:435
  (30 shorter events, 0.4 us)
Async XLA Ops:
  0.6 25.3 %copy-start = (bf16[512,128]{1,0:T(8,128)(2,1)S(1)}, bf16[512,128]{1,0:T(8,128)(2,1)}, u32[]{:S(2)}) copy-start(bf16[512,128]{1,0:T(8,128)(2,1)} %ik_ref.1) | copy-start | bytes 393220
  13.0 5.3 %collective-permute-start = (f32[32,512]{1,0:T(8,128)S(1)}, f32[32,512]{1,0:T(8,128)S(1)}, u32[]{:S(2)}, u32[]{:S(2)}) collective-permute-start(f32[32,512]{1,0:T(8,128)S(1)} %get-tuple-element.25), channel_id=1, source_target_pairs={{0,16},{8,24},{16,0},{24,8},{1,17},{9,25},{17,1},{25,9},{2,18},{10... | collective-permute-start | bytes 196616 | tf_op jit(solution)/shard_map/ppermute | solution.py:454
  18.3 7.7 %collective-permute-start.1 = (f32[32,512]{1,0:T(8,128)S(1)}, f32[32,512]{1,0:T(8,128)S(1)}, u32[]{:S(2)}, u32[]{:S(2)}) collective-permute-start(f32[32,512]{1,0:T(8,128)S(1)} %multiply_add_fusion.refs_0_), channel_id=1, source_target_pairs={{0,8},{8,0},{16,24},{24,16},{1,9},{9,1},{17,25},{25,17},{2,10},{10... | collective-permute-start | bytes 196616 | tf_op jit(solution)/shard_map/ppermute | solution.py:454
  23.8 17.8 %collective-permute-start.6 = (f32[1,128]{1,0:T(1,128)S(1)}, f32[1,128]{1,0:T(1,128)S(1)}, u32[]{:S(2)}, u32[]{:S(2)}) collective-permute-start(f32[1,128]{1,0:T(1,128)S(1)} %get-tuple-element.31), channel_id=1, source_target_pairs={{0,16},{8,24},{16,0},{24,8},{1,17},{9,25},{17,1},{25,9},{2,18},{10... | collective-permute-start | bytes 1544 | tf_op jit(solution)/shard_map/ppermute | solution.py:454
  25.9 55.6 %collective-permute-start.10 = (f32[512,128]{1,0:T(8,128)S(1)}, f32[512,128]{1,0:T(8,128)S(1)}, u32[]{:S(2)}, u32[]{:S(2)}) collective-permute-start(f32[512,128]{1,0:T(8,128)S(1)} %convert_element_type.7.refs_2_), channel_id=1, source_target_pairs={{0,16},{8,24},{16,0},{24,8},{1,17},{9,25},{17,1},{25,9},{2,18},{10... | collective-permute-start | bytes 786440 | tf_op jit(solution)/shard_map/ppermute | solution.py:454
  29.1 9.0 %collective-permute-start.4 = (f32[256,128]{1,0:T(8,128)S(1)}, f32[256,128]{1,0:T(8,128)S(1)}, u32[]{:S(2)}, u32[]{:S(2)}) collective-permute-start(f32[256,128]{1,0:T(8,128)S(1)} %get-tuple-element.29), channel_id=1, source_target_pairs={{0,2},{2,0},{4,6},{6,4},{1,3},{3,1},{5,7},{7,5},{8,10},{10,8},{12,... | collective-permute-start | bytes 393224 | tf_op jit(solution)/shard_map/ppermute | solution.py:454
  31.2 10.3 %collective-permute-start.2 = (f32[256,128]{1,0:T(8,128)S(1)}, f32[256,128]{1,0:T(8,128)S(1)}, u32[]{:S(2)}, u32[]{:S(2)}) collective-permute-start(f32[256,128]{1,0:T(8,128)S(1)} %get-tuple-element.27), channel_id=1, source_target_pairs={{0,6},{2,4},{4,2},{6,0},{1,7},{3,5},{5,3},{7,1},{8,14},{10,12},{12... | collective-permute-start | bytes 393224 | tf_op jit(solution)/shard_map/ppermute | solution.py:454
  38.1 11.0 %collective-permute-start.5 = (f32[512,128]{1,0:T(8,128)S(1)}, f32[512,128]{1,0:T(8,128)S(1)}, u32[]{:S(2)}, u32[]{:S(2)}) collective-permute-start(f32[512,128]{1,0:T(8,128)S(1)} %pad_add_fusion), channel_id=1, source_target_pairs={{0,6},{2,4},{4,2},{6,0},{1,7},{3,5},{5,3},{7,1},{8,14},{10,12},{12... | collective-permute-start | bytes 786440 | tf_op jit(solution)/shard_map/ppermute | solution.py:454
  41.5 11.3 %collective-permute-start.3 = (f32[512,128]{1,0:T(8,128)S(1)}, f32[512,128]{1,0:T(8,128)S(1)}, u32[]{:S(2)}, u32[]{:S(2)}) collective-permute-start(f32[512,128]{1,0:T(8,128)S(1)} %pad_add_fusion.1), channel_id=1, source_target_pairs={{0,2},{2,0},{4,6},{6,4},{1,3},{3,1},{5,7},{7,5},{8,10},{10,8},{12,... | collective-permute-start | bytes 786440 | tf_op jit(solution)/shard_map/ppermute | solution.py:454
  41.6 3.1 %collective-permute-start.7 = (f32[1,128]{1,0:T(1,128)S(1)}, f32[1,128]{1,0:T(1,128)S(1)}, u32[]{:S(2)}, u32[]{:S(2)}) collective-permute-start(f32[1,128]{1,0:T(1,128)S(1)} %multiply_add_fusion.1.refs_3_.refs_6_), channel_id=1, source_target_pairs={{0,8},{8,0},{16,24},{24,16},{1,9},{9,1},{17,25},{25,17},{2,10},{10... | collective-permute-start | bytes 1544 | tf_op jit(solution)/shard_map/ppermute | solution.py:454
  57.1 8.2 %collective-permute-start.14 = (f32[256,128]{1,0:T(8,128)S(1)}, f32[256,128]{1,0:T(8,128)S(1)}, u32[]{:S(2)}, u32[]{:S(2)}) collective-permute-start(f32[256,128]{1,0:T(8,128)S(1)} %get-tuple-element.39), channel_id=1, source_target_pairs={{0,6},{2,4},{4,2},{6,0},{1,7},{3,5},{5,3},{7,1},{8,14},{10,12},{12... | collective-permute-start | bytes 393224 | tf_op jit(solution)/shard_map/ppermute | solution.py:454
  59.0 24.3 %collective-permute-start.8 = (f32[520,128]{1,0:T(8,128)S(1)}, f32[520,128]{1,0:T(8,128)S(1)}, u32[]{:S(2)}, u32[]{:S(2)}) collective-permute-start(f32[520,128]{1,0:T(8,128)S(1)} %get-tuple-element.34.refs_0_), channel_id=1, source_target_pairs={{0,16},{8,24},{16,0},{24,8},{1,17},{9,25},{17,1},{25,9},{2,18},{10... | collective-permute-start | bytes 798728 | tf_op jit(solution)/shard_map/ppermute | solution.py:454
  60.5 6.2 %collective-permute-start.17 = (f32[256,128]{1,0:T(8,128)S(1)}, f32[256,128]{1,0:T(8,128)S(1)}, u32[]{:S(2)}, u32[]{:S(2)}) collective-permute-start(f32[256,128]{1,0:T(8,128)S(1)} %get-tuple-element.40), channel_id=1, source_target_pairs={{0,2},{2,0},{4,6},{6,4},{1,3},{3,1},{5,7},{7,5},{8,10},{10,8},{12,... | collective-permute-start | bytes 393224 | tf_op jit(solution)/shard_map/ppermute | solution.py:454
  60.5 28.6 %collective-permute-start.13 = (f32[512,128]{1,0:T(8,128)S(1)}, f32[512,128]{1,0:T(8,128)S(1)}, u32[]{:S(2)}, u32[]{:S(2)}) collective-permute-start(f32[512,128]{1,0:T(8,128)S(1)} %convert_element_type.7.refs_2_), channel_id=1, source_target_pairs={{0,8},{8,0},{16,24},{24,16},{1,9},{9,1},{17,25},{25,17},{2,10},{10... | collective-permute-start | bytes 786440 | tf_op jit(solution)/shard_map/ppermute | solution.py:454
  65.4 23.8 %collective-permute-start.12 = (f32[520,128]{1,0:T(8,128)S(1)}, f32[520,128]{1,0:T(8,128)S(1)}, u32[]{:S(2)}, u32[]{:S(2)}) collective-permute-start(f32[520,128]{1,0:T(8,128)S(1)} %get-tuple-element.34.refs_0_), channel_id=1, source_target_pairs={{0,8},{8,0},{16,24},{24,16},{1,9},{9,1},{17,25},{25,17},{2,10},{10... | collective-permute-start | bytes 798728 | tf_op jit(solution)/shard_map/ppermute | solution.py:454
  66.7 17.8 %collective-permute-start.15 = (f32[256,128]{1,0:T(8,128)S(1)}, f32[256,128]{1,0:T(8,128)S(1)}, u32[]{:S(2)}, u32[]{:S(2)}) collective-permute-start(f32[256,128]{1,0:T(8,128)S(1)} %add.46), channel_id=1, source_target_pairs={{0,1},{1,0},{2,3},{3,2},{4,5},{5,4},{6,7},{7,6},{8,9},{9,8},{10,11... | collective-permute-start | bytes 393224 | tf_op jit(solution)/shard_map/ppermute | solution.py:454
  81.5 6.8 %collective-permute-start.18 = (f32[256,128]{1,0:T(8,128)S(1)}, f32[256,128]{1,0:T(8,128)S(1)}, u32[]{:S(2)}, u32[]{:S(2)}) collective-permute-start(f32[256,128]{1,0:T(8,128)S(1)} %add.49), channel_id=1, source_target_pairs={{0,6},{2,4},{4,2},{6,0},{1,7},{3,5},{5,3},{7,1},{8,14},{10,12},{12... | collective-permute-start | bytes 393224 | tf_op jit(solution)/shard_map/ppermute | solution.py:454
  83.3 11.6 %collective-permute-start.9 = (f32[520,128]{1,0:T(8,128)S(1)}, f32[520,128]{1,0:T(8,128)S(1)}, u32[]{:S(2)}, u32[]{:S(2)}) collective-permute-start(f32[520,128]{1,0:T(8,128)S(1)} %collective-permute-done.8.refs_0_), channel_id=1, source_target_pairs={{0,8},{8,0},{16,24},{24,16},{1,9},{9,1},{17,25},{25,17},{2,10},{10... | collective-permute-start | bytes 798728 | tf_op jit(solution)/shard_map/ppermute | solution.py:454
  84.5 10.4 %collective-permute-start.11 = (f32[512,128]{1,0:T(8,128)S(1)}, f32[512,128]{1,0:T(8,128)S(1)}, u32[]{:S(2)}, u32[]{:S(2)}) collective-permute-start(f32[512,128]{1,0:T(8,128)S(1)} %collective-permute-done.10.refs_2_), channel_id=1, source_target_pairs={{0,8},{8,0},{16,24},{24,16},{1,9},{9,1},{17,25},{25,17},{2,10},{10... | collective-permute-start | bytes 786440 | tf_op jit(solution)/shard_map/ppermute | solution.py:454
  88.3 5.0 %collective-permute-start.16 = (f32[256,128]{1,0:T(8,128)S(1)}, f32[256,128]{1,0:T(8,128)S(1)}, u32[]{:S(2)}, u32[]{:S(2)}) collective-permute-start(f32[256,128]{1,0:T(8,128)S(1)} %add.47), channel_id=1, source_target_pairs={{0,2},{2,0},{4,6},{6,4},{1,3},{3,1},{5,7},{7,5},{8,10},{10,8},{12,... | collective-permute-start | bytes 393224 | tf_op jit(solution)/shard_map/ppermute | solution.py:454
  89.1 5.0 %collective-permute-start.19 = (f32[256,128]{1,0:T(8,128)S(1)}, f32[256,128]{1,0:T(8,128)S(1)}, u32[]{:S(2)}, u32[]{:S(2)}) collective-permute-start(f32[256,128]{1,0:T(8,128)S(1)} %add.50), channel_id=1, source_target_pairs={{0,1},{1,0},{2,3},{3,2},{4,5},{5,4},{6,7},{7,6},{8,9},{9,8},{10,11... | collective-permute-start | bytes 393224 | tf_op jit(solution)/shard_map/ppermute | solution.py:454

commit v8 on v7

--- a/solution.py
+++ b/solution.py
@@ -50,24 +50,37 @@
     return top + jnp.log2(functools.reduce(jnp.add, [jnp.exp2(p - top) for p in parts]))
 
 
-def key_limit_column(count_ref, row, keys):
+def packed_sizes(keys):
+    return [keys * part // 32 for part in (18, 20, 22, 32)]
+
+
+def for_packed(live, keys, run):
+    below = 0
+    for size in packed_sizes(keys):
+        pl.when((live > below) & (live <= size))(functools.partial(run, size))
+        below = size
+
+
+def packing(count_ref, keys):
     lane = lax.broadcasted_iota(jnp.int32, (1, keys), 1)
-    block = lane // KBLOCK
-    limit = jnp.zeros((1, keys), jnp.int32)
+    block, place = lane // KBLOCK, lane % KBLOCK
+    rank = jnp.full((1, keys), -1, jnp.int32)
+    base = jnp.int32(0)
     for b in range(keys // KBLOCK):
-        limit = jnp.where(block == b, count_ref[b], limit)
-    live = (lane % KBLOCK) < limit
-    row = jnp.where(live, row, BIG)
-    return jnp.transpose(jnp.broadcast_to(row, (8, keys)))[:, :1]
+        here = count_ref[b]
+        rank = jnp.where((block == b) & (place < here), base + place, rank)
+        base = base + here
+    return rank, base
 
 
 def main_keys(nope, parity, even_ref, odd_ref):
+    count = nope.shape[0]
     if parity == 0:
-        return jnp.concatenate([nope, even_ref[...]], axis=1)
+        return jnp.concatenate([nope, even_ref[:count, :]], axis=1)
     turned = jnp.concatenate([nope[:, DROPE:], nope[:, :DROPE]], axis=1)
     low = lax.broadcasted_iota(jnp.int32, turned.shape, 1) < DROPE
     first = jnp.where(low, jnp.zeros_like(turned), turned)
-    second = jnp.where(low, turned, odd_ref[...])
+    second = jnp.where(low, turned, odd_ref[:count, :])
     return jnp.concatenate([first, second], axis=1)
 
 
@@ -75,10 +88,10 @@
     return pl.ds(pl.multiple_of(index * width, LANES), width)
 
 
-def stats_kernel(per, count_hbm, q_hbm, kn_hbm, rope_hbm, qpos_hbm, kpos_hbm, iq_hbm,
-                 lse_ref, q_ref, kk_ref, bias_ref, iq_ref,
+def stats_kernel(per, count_hbm, q_hbm, kn_hbm, rope_hbm, qpos_hbm, kpos_hbm, iq_hbm, ik_hbm,
+                 lse_ref, q_ref, kk_ref, bias_ref, iq_ref, ik_ref, spread_ref, live_ref,
                  kn_ref, rope_ref, qpos_ref, kpos_ref, even_ref, odd_ref, none_ref, bad_ref,
-                 count_ref, small_sem, q_sem, kn_sem, iq_sem):
+                 pack_ref, raw_ref, count_ref, small_sem, q_sem, kn_sem, iq_sem):
     keys = kn_ref.shape[0]
     groups, rows = q_ref.shape[0], q_ref.shape[1]
     pairs = q_ref.shape[2] // PAIR
@@ -87,7 +100,8 @@
     small = [
         pltpu.make_async_copy(src, dst, small_sem.at[i])
         for i, (src, dst) in enumerate(
-            ((count_hbm, count_ref), (kpos_hbm, kpos_ref), (qpos_hbm, qpos_ref), (rope_hbm, rope_ref))
+            ((count_hbm, count_ref), (kpos_hbm, kpos_ref), (qpos_hbm, qpos_ref), (rope_hbm, rope_ref),
+             (ik_hbm, raw_ref))
         )
     ]
 
@@ -108,11 +122,21 @@
     for copy in small:
         copy.wait()
 
-    rope = jnp.transpose(rope_ref[...].astype(f32)).astype(bf16)
+    rank, live = packing(count_ref, keys)
+    row = lax.broadcasted_iota(jnp.int32, (keys, keys), 0)
+    chosen = row == rank
+    pack_ref[...] = jnp.where(chosen, 1.0, 0.0).astype(bf16)
+    position = jnp.sum(jnp.where(chosen, kpos_ref[...].astype(f32), 0.0), axis=1, keepdims=True)
+    column = jnp.where(row[:, :1] < live, position.astype(jnp.int32), BIG)
+    rank_column = jnp.transpose(jnp.broadcast_to(rank, (8, keys)))[:, :1]
+    lane = lax.broadcasted_iota(jnp.int32, (keys, keys), 1)
+    spread_ref[...] = jnp.where(lane == rank_column, 1.0, 0.0).astype(bf16)
+    live_ref[...] = jnp.broadcast_to(live, live_ref.shape)
+    ik_ref[...] = dot_nn(pack_ref[...], raw_ref[...])
+    rope = dot_nt(pack_ref[...], rope_ref[...]).astype(bf16)
     zero = jnp.zeros_like(rope)
     even_ref[...] = jnp.concatenate([rope, zero], axis=1)
     odd_ref[...] = jnp.concatenate([zero, rope], axis=1)
-    column = key_limit_column(count_ref, kpos_ref[...], keys)
     for g in range(groups):
         valid = column <= qpos_ref[g : g + 1, :]
         bias = jnp.where(valid, 0.0, NEG)
@@ -124,22 +148,23 @@
 
     def scores(kk, q3, c):
         q = q3.reshape(2 * rows, 2 * LANES)
-        return dot_nt(kk, q) * SCALE_MAIN + bias_ref[:, halves[c]]
+        return dot_nt(kk, q) * SCALE_MAIN + bias_ref[: kk.shape[0], halves[c]]
 
     def query(pair, a, c):
         at = pl.ds(pl.multiple_of(pair * PAIR + a * LANES, LANES), 2 * LANES)
         return q_ref[2 * c : 2 * c + 2, :, at]
 
-    def step(i, carry):
+    def step(size, i, carry):
         for p in range(per):
             pair = i * per + p
             for copy in large(pair):
                 copy.wait()
         for p in range(per):
             pair = i * per + p
+            both = dot_nn(pack_ref[:size, :], kn_ref[:, lanes_at(pair, 2 * DNOPE)]).astype(bf16)
             for a in range(2):
-                kk = main_keys(kn_ref[:, lanes_at(2 * pair + a, DNOPE)], a, even_ref, odd_ref)
-                kk_ref[:, lanes_at(2 * pair + a, 2 * LANES)] = kk
+                kk = main_keys(both[:, a * DNOPE : (a + 1) * DNOPE], a, even_ref, odd_ref)
+                kk_ref[:size, lanes_at(2 * pair + a, 2 * LANES)] = kk
                 for c, cols in enumerate(halves):
                     s = scores(kk, query(pair, a, c), c)
                     total = jnp.sum(jnp.exp2(s), axis=0, keepdims=True)
@@ -149,7 +174,10 @@
                     lse_ref[pl.ds(2 * pair + a, 1), cols] = jnp.where(skip, NEG, jnp.log2(total))
         return carry
 
-    lax.fori_loop(0, pairs // per, step, 0)
+    def run(size):
+        lax.fori_loop(0, pairs // per, functools.partial(step, size), 0)
+
+    for_packed(live, keys, run)
     index_copy.wait()
 
     @pl.when(jnp.max(bad_ref[...]) > 0)
@@ -158,7 +186,7 @@
             for a in range(2):
                 kk = kk_ref[:, lanes_at(2 * pair + a, 2 * LANES)]
                 for c, cols in enumerate(halves):
-                    s = scores(kk, query(pair, a, c), c)
+                    s = jnp.where(bias_ref[:, cols] < 0, NEG, scores(kk, query(pair, a, c), c))
                     top = jnp.max(s, axis=0, keepdims=True)
                     total = jnp.sum(jnp.exp2(s - top), axis=0, keepdims=True)
                     lse_ref[pl.ds(2 * pair + a, 1), cols] = top + jnp.log2(total)
@@ -167,21 +195,24 @@
         lax.fori_loop(0, pairs, again, 0)
 
 
-def main_stats(main_query, key_nope, rope_t, query_pos, key_pos, key_count, index_query):
+def main_stats(main_query, key_nope, rope_t, query_pos, key_pos, key_count, index_query, index_key):
     groups, rows, width = main_query.shape
     heads = width // DQK
     keys = key_nope.shape[0]
     total = groups * rows
     return pl.pallas_call(
         functools.partial(stats_kernel, 2),
-        in_specs=[pl.BlockSpec(memory_space=pltpu.HBM)] * 7,
-        out_specs=[IN_VMEM] * 5,
+        in_specs=[pl.BlockSpec(memory_space=pltpu.HBM)] * 8,
+        out_specs=[IN_VMEM] * 8,
         out_shape=[
             jax.ShapeDtypeStruct((heads, total), f32),
             jax.ShapeDtypeStruct(main_query.shape, bf16),
             jax.ShapeDtypeStruct((keys, heads * 2 * LANES), bf16),
             jax.ShapeDtypeStruct((keys, total), f32),
             jax.ShapeDtypeStruct(index_query.shape, bf16),
+            jax.ShapeDtypeStruct(index_key.shape, f32),
+            jax.ShapeDtypeStruct((keys, keys), bf16),
+            jax.ShapeDtypeStruct((8, LANES), jnp.int32),
         ],
         scratch_shapes=[
             pltpu.VMEM(key_nope.shape, bf16),
@@ -192,8 +223,10 @@
             pltpu.VMEM((keys, LANES), bf16),
             pltpu.VMEM((1, total), f32),
             pltpu.VMEM((1, total), f32),
+            pltpu.VMEM((keys, keys), bf16),
+            pltpu.VMEM(index_key.shape, bf16),
             pltpu.SMEM(key_count.shape, jnp.int32),
-            pltpu.SemaphoreType.DMA((4,)),
+            pltpu.SemaphoreType.DMA((5,)),
             pltpu.SemaphoreType.DMA((heads // 2,)),
             pltpu.SemaphoreType.DMA((heads // 2,)),
             pltpu.SemaphoreType.DMA,
@@ -203,10 +236,10 @@
             heads * total * keys * 512, main_query.size * 2 + key_nope.size * 2, heads * total * keys
         ),
         name="main_stats",
-    )(key_count, main_query, key_nope, rope_t, query_pos, key_pos, index_query)
-
-
-def target_kernel(n_lse, masks, per, parts, q_ref, kk_ref, bias_ref, *refs):
+    )(key_count, main_query, key_nope, rope_t, query_pos, key_pos, index_query, index_key)
+
+
+def target_kernel(n_lse, masks, per, parts, q_ref, kk_ref, bias_ref, live_ref, *refs):
     lse_refs = refs[:n_lse]
     out_refs = refs[n_lse:-1]
     glob_ref = refs[-1]
@@ -228,12 +261,12 @@
     for ref in out_refs:
         ref[...] = jnp.zeros_like(ref)
 
-    def step(i, carry):
+    def step(rows_kept, i, carry):
         for p in range(per):
             pair = i * per + p
             acc = None
             for a in range(2):
-                kk = kk_ref[:, lanes_at(2 * pair + a, 2 * LANES)]
+                kk = kk_ref[:rows_kept, lanes_at(2 * pair + a, 2 * LANES)]
                 at = pl.ds(pl.multiple_of(pair * PAIR + a * LANES, LANES), 2 * LANES)
                 qs = [q_ref[g, :, at] for g in ids]
                 q = qs[0] if n_groups == 1 else jnp.concatenate(qs, axis=0)
@@ -241,22 +274,27 @@
                 e = jnp.exp2(dot_nt(kk, q) * SCALE_MAIN - lse)
                 acc = e if acc is None else acc + e
             for g, at, ref in tiles:
-                ref[...] += acc[at, g * rows : (g + 1) * rows]
+                some = acc[at, g * rows : (g + 1) * rows]
+                if some.shape[0]:
+                    ref[: some.shape[0], :] += some
         return carry
 
-    lax.fori_loop(0, pairs // per, step, 0)
+    def run(rows_kept):
+        lax.fori_loop(0, pairs // per, functools.partial(step, rows_kept), 0)
+
+    for_packed(jnp.max(live_ref[...]), keys, run)
     for g, at, ref in tiles:
         ref[...] = jnp.where(bias_ref[at, lanes_at(ids[g], rows)] < 0, 0.0, ref[...])
 
 
-def head_sums(masks, q, kk, bias, lses, parts=1):
+def head_sums(masks, q, kk, bias, live, lses, parts=1):
     _, rows, width = q.shape
     heads = width // DQK
     keys = kk.shape[0]
     n = len(masks)
     return pl.pallas_call(
         functools.partial(target_kernel, len(lses), masks, 4 // n, parts),
-        in_specs=[IN_VMEM] * (3 + len(lses)),
+        in_specs=[IN_VMEM] * (4 + len(lses)),
         out_specs=[IN_VMEM] * (n * parts),
         out_shape=[jax.ShapeDtypeStruct((keys // parts, rows), f32)] * (n * parts),
         scratch_shapes=[pltpu.VMEM((heads, n * rows), f32)],
@@ -265,27 +303,33 @@
             heads * n * rows * keys * 512, heads * n * rows * keys // 16, heads * n * rows * keys
         ),
         name="head_sums",
-    )(q, kk, bias, *lses)
-
-
-def logits_kernel(per, iq_ref, ik_ref, wt_ref, bias_ref, logits_ref, lse_ref, wm_ref, w_ref):
+    )(q, kk, bias, live, *lses)
+
+
+def logits_kernel(per, iq_ref, wide_ref, wt_ref, bias_ref, live_ref,
+                  logits_ref, lse_ref, wm_ref, w_ref, ik_ref):
+    keys = wide_ref.shape[0]
     rows, width = iq_ref.shape
     w_ref[...] = wt_ref[...].astype(f32)
+    ik_ref[...] = wide_ref[...].astype(bf16)
     logits_ref[...] = jnp.zeros_like(logits_ref)
 
-    def step(i, carry):
+    def step(size, i, carry):
         for p in range(per):
             first = 2 * (i * per + p)
             q = jnp.concatenate([iq_ref[:, lanes_at(first + a, ID)] for a in range(2)], axis=0)
-            z = dot_nt(ik_ref[...], q)
+            z = dot_nt(ik_ref[:size, :], q)
             w = jnp.concatenate([w_ref[pl.ds(first + a, 1), :] for a in range(2)], axis=1)
             masked = jnp.where(z > 0, w, 0.0)
-            wm_ref[:, lanes_at(i * per + p, 2 * rows)] = masked.astype(bf16)
+            wm_ref[:size, lanes_at(i * per + p, 2 * rows)] = masked.astype(bf16)
             r = z * masked
-            logits_ref[...] += r[:, :rows] + r[:, rows:]
+            logits_ref[:size, :] += r[:, :rows] + r[:, rows:]
         return carry
 
-    lax.fori_loop(0, width // (2 * ID * per), step, 0)
+    def run(size):
+        lax.fori_loop(0, width // (2 * ID * per), functools.partial(step, size), 0)
+
+    for_packed(jnp.max(live_ref[...]), keys, run)
     logits = logits_ref[...] * SCALE_INDEX
     logits_ref[...] = logits
     valid = bias_ref[:, lanes_at(lax.axis_index("head"), rows)] == 0
@@ -294,7 +338,7 @@
     lse_ref[...] = top + jnp.log2(jnp.sum(jnp.exp2(s - top), axis=0, keepdims=True))
 
 
-def index_logits(index_query, index_key, weight_t, bias):
+def index_logits(index_query, index_key, weight_t, bias, live):
     rows, width = index_query.shape
     keys = index_key.shape[0]
     whole = lambda i: (0, 0)
@@ -303,8 +347,9 @@
         grid=(1,),
         in_specs=[
             IN_VMEM,
-            pl.BlockSpec(index_key.shape, whole),
+            IN_VMEM,
             pl.BlockSpec(weight_t.shape, whole),
+            IN_VMEM,
             IN_VMEM,
         ],
         out_specs=[IN_VMEM] * 3,
@@ -313,17 +358,21 @@
             jax.ShapeDtypeStruct((1, rows), f32),
             jax.ShapeDtypeStruct((keys, (width // ID) * rows), bf16),
         ],
-        scratch_shapes=[pltpu.VMEM((width // ID, rows), f32)],
+        scratch_shapes=[
+            pltpu.VMEM((width // ID, rows), f32),
+            pltpu.VMEM(index_key.shape, bf16),
+        ],
         compiler_params=pltpu.CompilerParams(vmem_limit_bytes=16 * 1024 * 1024),
         cost_estimate=cost(2 * keys * rows * width, rows * width * 2 + keys * rows * width // ID * 2),
         name="index_logits",
-    )(index_query, index_key, weight_t, bias)
+    )(index_query, index_key, weight_t, bias, live)
 
 
 def grad_key_kernel(n_parts, n_lse, per, *refs):
     parts = refs[:n_parts]
     lses = refs[n_parts : n_parts + n_lse]
-    logits_ref, wm_ref, iq_ref, bias_ref, cot_ref, sg_ref, lo_ref, hi_ref = refs[n_parts + n_lse :]
+    (logits_ref, wm_ref, iq_ref, bias_ref, live_ref, spread_ref, cot_ref,
+     sg_ref, lo_ref, hi_ref, sum_ref) = refs[n_parts + n_lse :]
     keys, rows = logits_ref.shape
     width = iq_ref.shape[1]
 
@@ -337,33 +386,43 @@
     terms = jnp.where(live, target * (jnp.log(jnp.where(live, target, 1.0)) - logits), 0.0)
     kl = jnp.sum(terms, axis=0, keepdims=True)
     sg_ref[keys:, :] = jnp.broadcast_to(kl, (8, rows))
-    lo_ref[...] = jnp.zeros_like(lo_ref)
-    hi_ref[...] = jnp.zeros_like(hi_ref)
-
-    def step(i, carry):
+    sum_ref[...] = jnp.zeros_like(sum_ref)
+
+    def step(size, i, carry):
         for p in range(per):
             dz = []
             qs = []
             for a in range(2):
                 j = 2 * (i * per + p) + a
-                wm = wm_ref[:, lanes_at(j, rows)].astype(f32)
-                dz.append((sg_ref[:keys, :] * wm).astype(bf16))
+                wm = wm_ref[:size, lanes_at(j, rows)].astype(f32)
+                dz.append((sg_ref[:size, :] * wm).astype(bf16))
                 qs.append(iq_ref[:, lanes_at(j, ID)])
-            g = dot_nn(jnp.concatenate(dz, axis=1), jnp.concatenate(qs, axis=0))
-            lo_ref[...] += g[: keys // 2]
-            hi_ref[...] += g[keys // 2 :]
+            sum_ref[:size, :] += dot_nn(jnp.concatenate(dz, axis=1), jnp.concatenate(qs, axis=0))
         return carry
 
-    lax.fori_loop(0, width // (2 * ID * per), step, 0)
-
-
-def index_grad_key(parts, lses, logits, wm, index_query, bias, cotangent):
+    def run(size):
+        lax.fori_loop(0, width // (2 * ID * per), functools.partial(step, size), 0)
+
+    for_packed(jnp.max(live_ref[...]), keys, run)
+    rest = sum_ref[...]
+    pieces = []
+    for _ in range(3):
+        piece = rest.astype(bf16)
+        pieces.append(piece)
+        rest = rest - piece.astype(f32)
+    placed = dot_nn(spread_ref[...], jnp.concatenate(pieces, axis=1))
+    placed = placed[:, :ID] + placed[:, ID : 2 * ID] + placed[:, 2 * ID :]
+    lo_ref[...] = placed[: keys // 2]
+    hi_ref[...] = placed[keys // 2 :]
+
+
+def index_grad_key(parts, lses, logits, wm, index_query, bias, live, spread, cotangent):
     rows, width = index_query.shape
     keys = logits.shape[0]
     return pl.pallas_call(
-        functools.partial(grad_key_kernel, len(parts), len(lses), 8),
+        functools.partial(grad_key_kernel, len(parts), len(lses), 4),
         grid=(1,),
-        in_specs=[IN_VMEM] * (len(parts) + len(lses) + 4)
+        in_specs=[IN_VMEM] * (len(parts) + len(lses) + 6)
         + [pl.BlockSpec((1, rows), lambda i: (0, 0))],
         out_specs=[IN_VMEM] * 3,
         out_shape=[
@@ -371,10 +430,11 @@
             jax.ShapeDtypeStruct((keys // 2, ID), f32),
             jax.ShapeDtypeStruct((keys // 2, ID), f32),
         ],
+        scratch_shapes=[pltpu.VMEM((keys, ID), f32)],
         compiler_params=pltpu.CompilerParams(vmem_limit_bytes=16 * 1024 * 1024),
         cost_estimate=cost(2 * keys * rows * width, rows * width * 2 + keys * rows * width // ID * 2),
         name="index_grad_key",
-    )(*parts, *lses, logits, wm, index_query, bias, cotangent)
+    )(*parts, *lses, logits, wm, index_query, bias, live, spread, cotangent)
 
 
 def grad_query_kernel(n_shards, first, n_lse, *refs):
@@ -496,33 +556,35 @@
             return [value, near, far, across]
         return list(lax.all_gather(value, "key"))
 
-    lse, q, kk, bias, iq = main_stats(
-        main_query, key_nope, rope_t, query_pos, key_row, key_count, index_query
+    lse, q, kk, bias, iq, wide, spread, live = main_stats(
+        main_query, key_nope, rope_t, query_pos, key_row, key_count, index_query, narrow
     )
     lses = butterfly_lse(lse, n_key)
-    logits, index_lse, wm = index_logits(iq, narrow, weight_t, bias)
+    logits, index_lse, wm = index_logits(iq, wide, weight_t, bias, live)
     index_lses = butterfly_lse(index_lse, n_key)
-    iks = gathered(index_key.astype(f32))
+    iks = gathered(wide)
 
     half = keys // 2
     if n_head == 4 and groups == 4:
-        low, high = head_sums([2], q, kk, bias, lses, parts=2)
+        low, high = head_sums([2], q, kk, bias, live, lses, parts=2)
         low = swap(low, "head", 1, 4)
         high = swap(high, "head", 3, 4)
-        up, down = head_sums([1, 3], q, kk, bias, lses)
+        up, down = head_sums([1, 3], q, kk, bias, live, lses)
         up = up + jnp.pad(high, ((half, 0), (0, 0)))
         down = down + jnp.pad(low, ((0, half), (0, 0)))
         from_up = swap(up, "head", 1, 4)
         from_down = swap(down, "head", 3, 4)
-        own = head_sums([0], q, kk, bias, lses)[0]
+        own = head_sums([0], q, kk, bias, live, lses)[0]
         parts = [own, from_up, from_down]
     else:
         z = lax.axis_index("head")
-        tiles = jnp.stack([head_sums([g], q, kk, bias, lses)[0] for g in range(groups)])
+        tiles = jnp.stack([head_sums([g], q, kk, bias, live, lses)[0] for g in range(groups)])
         tiles = tiles[jnp.bitwise_xor(jnp.arange(groups), z)]
         parts = [lax.psum_scatter(tiles, "head", scatter_dimension=0, tiled=True)[0]]
 
-    sg, *grad_key = index_grad_key(parts, index_lses, logits, wm, iq, bias, cotangent)
+    sg, *grad_key = index_grad_key(
+        parts, index_lses, logits, wm, iq, bias, live, spread, cotangent
+    )
     grad_key = summed_copies(grad_key, n_head, n_query)
     sgs = gathered(sg)
     carry = None

time: 99.4 us -> 103 us (1.036)
  waiting for transfers between devices: 23 us -> 27.9 us
  Pallas kernels: 40 us -> 36.8 us
  starting transfers between devices: 34.2 us -> 36 us
    ppermute x20, waiting for transfers between devices: 23 us -> 27.9 us  [swap(): return lax.ppermute(value, axis, [(i, i ^ mask) for i in range(size)])]
    pallas_call x3, Pallas kernels: 10.4 us -> 7.96 us  [head_sums(): pl.pallas_call(functools.partial(target_kernel, len(lses), masks, 4 // n,...]
    ppermute x20, starting transfers between devices: 34.2 us -> 36 us  [swap(): return lax.ppermute(value, axis, [(i, i ^ mask) for i in range(size)])]
    pallas_call x1, Pallas kernels: 5.44 us -> 4.09 us  [index_logits(): pl.pallas_call(functools.partial(logits_kernel, 4), grid=(1,), in_specs=[...]
  transfers between devices with their start and end apart: 20 -> 20, of which waited for: 9 -> 9; matrix products, arithmetic and copies ran while one was open for 1% -> 1% of each run, Pallas kernels for 24% -> 20%
where the time goes in v8:
time: 103 us; the launch traced here: 102 us
  Pallas kernels  36.8 us (36%)
  starting transfers between devices  36 us (35%)
  waiting for transfers between devices  27.9 us (27%)
    ppermute x20, starting transfers between devices, swap(): return lax.ppermute(value, axis, [(i, i ^ mask) for i in range(size)])  36 us
    ppermute x20, waiting for transfers between devices, swap(): return lax.ppermute(value, axis, [(i, i ^ mask) for i in range(size)])  27.9 us
    pallas_call x1, Pallas kernels, main_stats(): pl.pallas_call(functools.partial(stats_kernel, 2), in_specs=[pl.BlockSpec...  12.7 us
    pallas_call x3, Pallas kernels, head_sums(): pl.pallas_call(functools.partial(target_kernel, len(lses), masks, 4 // n,...  7.96 us
    pallas_call x2, Pallas kernels, index_grad_query(): pl.pallas_call(functools.partial(grad_query_kernel, n, first, len(lses)),...  7.57 us
    pallas_call x1, Pallas kernels, index_grad_key(): pl.pallas_call(functools.partial(grad_key_kernel, len(parts), len(lses),...  4.44 us
    pallas_call x1, Pallas kernels, index_logits(): pl.pallas_call(functools.partial(logits_kernel, 4), grid=(1,), in_specs=[...  4.09 us
  transfers between devices with their start and end apart: 20, of which 9 were waited for; matrix products, arithmetic and copies ran while one was open for 1% of the time, Pallas kernels for 20%

profile of v8, /device:TPU:0, one launch (start us, length us, event | category | flops | bytes accessed | tf_op | source)
XLA Modules:
  0.0 102.3 jit_solution(16244220409441696088)
XLA Ops:
  0.6 12.7 %main_stats.1 = (f32[32,512]{1,0:T(8,128)S(1)}, bf16[4,128,6144]{2,1,0:T(8,128)(2,1)S(1)}, bf16[512,8192]{1,0:T(8,128)(2,1)S(1)}, f32[512,512]{1,0:T(8,128)S(1)}...) custom-call(s32[16]{0:T(128)} %count_hbm.1, ...), custom_call_target="tpu_custom_call" | custom-call | flops 4294967296 | bytes 10485760 | tf_op jit(solution)/shard_map/main_stats/pallas_call | solution.py:203
  13.4 3.0 %collective-permute-start = (f32[32,512]{1,0:T(8,128)S(1)}, f32[32,512]{1,0:T(8,128)S(1)}, u32[]{:S(2)}, u32[]{:S(2)}) collective-permute-start(f32[32,512]{1,0:T(8,128)S(1)} %get-tuple-element.29), channel_id=1, source_target_pairs={{0,16},{8,24},{16,0},{24,8},{1,17},{9,25},{17,1},{25,9},{2,18},{10... | collective-permute-start | bytes 196616 | tf_op jit(solution)/shard_map/ppermute | solution.py:514
  16.4 0.1 collective-permute-start.10
  16.5 2.5 %collective-permute-done = f32[32,512]{1,0:T(8,128)S(1)} collective-permute-done((f32[32,512]{1,0:T(8,128)S(1)}, f32[32,512]{1,0:T(8,128)S(1)}, u32[]{:S(2)}, u32[]{:S(2)}) %collective-permute-start) | collective-permute-done | bytes 65568 | tf_op jit(solution)/shard_map/ppermute | solution.py:514
  19.0 0.1 collective-permute-start.1
  19.1 4.1 %index_logits.1 = (f32[512,128]{1,0:T(8,128)S(1)}, f32[1,128]{1,0:T(1,128)S(1)}, bf16[512,8192]{1,0:T(8,128)(2,1)S(1)}) custom-call(bf16[128,8192]{1,0:T(8,128)(2,1)S(1)} %get-tuple-element.34.iq_ref.refs_7_.refs_4_, f32[512,128]{1,0:T(8,128)S(1)} %get-tuple-element.35.wide_ref.refs_2_, bf16[64,128]{1,0:T(8,128)(2,1)} %bitcast.5, ...), custom_call_target="tpu_custom_call" | custom-call | flops 1073741824 | bytes 10485760 | tf_op jit(solution)/shard_map/index_logits/pallas_call | solution.py:345
  23.2 2.5 %collective-permute-start.6 = (f32[1,128]{1,0:T(1,128)S(1)}, f32[1,128]{1,0:T(1,128)S(1)}, u32[]{:S(2)}, u32[]{:S(2)}) collective-permute-start(f32[1,128]{1,0:T(1,128)S(1)} %get-tuple-element.36), channel_id=1, source_target_pairs={{0,16},{8,24},{16,0},{24,8},{1,17},{9,25},{17,1},{25,9},{2,18},{10... | collective-permute-start | bytes 1544 | tf_op jit(solution)/shard_map/ppermute | solution.py:514
  25.6 2.2 %head_sums.5 = (f32[256,128]{1,0:T(8,128)S(1)}, f32[256,128]{1,0:T(8,128)S(1)}) custom-call(bf16[4,128,6144]{2,1,0:T(8,128)(2,1)S(1)} %get-tuple-element.25.q_ref, bf16[512,8192]{1,0:T(8,128)(2,1)S(1)} %get-tuple-element.26.kk_ref, f32[512,512]{1,0:T(8,128)S(1)} %get-tuple-element.27.bias_ref.refs_8_, s32[8,128]{1,0:T(8,128)S(1)} %get-tuple-element.28.live_ref.refs_9_, ...), custom_call_target="tpu_custom_call" | custom-call | flops 1073741824 | bytes 131072 | tf_op jit(solution)/shard_map/head_sums/pallas_call | solution.py:295
  27.9 3.7 %collective-permute-start.2 = (f32[256,128]{1,0:T(8,128)S(1)}, f32[256,128]{1,0:T(8,128)S(1)}, u32[]{:S(2)}, u32[]{:S(2)}) collective-permute-start(f32[256,128]{1,0:T(8,128)S(1)} %get-tuple-element.31), channel_id=1, source_target_pairs={{0,6},{2,4},{4,2},{6,0},{1,7},{3,5},{5,3},{7,1},{8,14},{10,12},{12... | collective-permute-start | bytes 393224 | tf_op jit(solution)/shard_map/ppermute | solution.py:514
  31.6 3.5 %head_sums.4 = (f32[512,128]{1,0:T(8,128)S(1)}, f32[512,128]{1,0:T(8,128)S(1)}) custom-call(bf16[4,128,6144]{2,1,0:T(8,128)(2,1)S(1)} %get-tuple-element.25.q_ref, bf16[512,8192]{1,0:T(8,128)(2,1)S(1)} %get-tuple-element.26.kk_ref, f32[512,512]{1,0:T(8,128)S(1)} %get-tuple-element.27.bias_ref.refs_8_, s32[8,128]{1,0:T(8,128)S(1)} %get-tuple-element.28.live_ref.refs_9_, ...), custom_call_target="tpu_custom_call" | custom-call | flops 2147483648 | bytes 262144 | tf_op jit(solution)/shard_map/head_sums/pallas_call | solution.py:295
  35.1 3.5 %collective-permute-done.4 = f32[256,128]{1,0:T(8,128)S(1)} collective-permute-done((f32[256,128]{1,0:T(8,128)S(1)}, f32[256,128]{1,0:T(8,128)S(1)}, u32[]{:S(2)}, u32[]{:S(2)}) %collective-permute-start.4) | collective-permute-done | bytes 131104 | tf_op jit(solution)/shard_map/ppermute | solution.py:514
  38.6 1.8 %collective-permute-start.5 = (f32[512,128]{1,0:T(8,128)S(1)}, f32[512,128]{1,0:T(8,128)S(1)}, u32[]{:S(2)}, u32[]{:S(2)}) collective-permute-start(f32[512,128]{1,0:T(8,128)S(1)} %pad_add_fusion), channel_id=1, source_target_pairs={{0,6},{2,4},{4,2},{6,0},{1,7},{3,5},{5,3},{7,1},{8,14},{10,12},{12... | collective-permute-start | bytes 786440 | tf_op jit(solution)/shard_map/ppermute | solution.py:514
  40.4 0.1 collective-permute-start.3
  40.6 2.2 %head_sums.3.refs_0_ = f32[512,128]{1,0:T(8,128)S(1)} custom-call(bf16[4,128,6144]{2,1,0:T(8,128)(2,1)S(1)} %get-tuple-element.25.q_ref, bf16[512,8192]{1,0:T(8,128)(2,1)S(1)} %get-tuple-element.26.kk_ref, f32[512,512]{1,0:T(8,128)S(1)} %get-tuple-element.27.bias_ref.refs_8_, s32[8,128]{1,0:T(8,128)S(1)} %get-tuple-element.28.live_ref.refs_9_, ...), custom_call_target="tpu_custom_call" | custom-call | flops 1073741824 | bytes 131072 | tf_op jit(solution)/shard_map/head_sums/pallas_call | solution.py:295
  42.8 6.9 %collective-permute-done.5.refs_2_ = f32[512,128]{1,0:T(8,128)S(1)} collective-permute-done((f32[512,128]{1,0:T(8,128)S(1)}, f32[512,128]{1,0:T(8,128)S(1)}, u32[]{:S(2)}, u32[]{:S(2)}) %collective-permute-start.5) | collective-permute-done | bytes 262176 | tf_op jit(solution)/shard_map/ppermute | solution.py:514
  49.7 3.6 %collective-permute-done.3.refs_1_ = f32[512,128]{1,0:T(8,128)S(1)} collective-permute-done((f32[512,128]{1,0:T(8,128)S(1)}, f32[512,128]{1,0:T(8,128)S(1)}, u32[]{:S(2)}, u32[]{:S(2)}) %collective-permute-start.3) | collective-permute-done | bytes 262176 | tf_op jit(solution)/shard_map/ppermute | solution.py:514
  53.3 4.4 %index_grad_key.1 = (f32[520,128]{1,0:T(8,128)S(1)}, f32[256,128]{1,0:T(8,128)S(1)}, f32[256,128]{1,0:T(8,128)S(1)}) custom-call(f32[512,128]{1,0:T(8,128)S(1)} %head_sums.3.refs_0_, f32[512,128]{1,0:T(8,128)S(1)} %collective-permute-done.3.refs_1_, f32[512,128]{1,0:T(8,128)S(1)} %collective-permute-done.5.refs_2_, ...), custom_call_target="tpu_custom_call" | custom-call | flops 1073741824 | bytes 10485760 | tf_op jit(solution)/shard_map/index_grad_key/pallas_call | solution.py:422
  57.7 2.1 %collective-permute-start.14 = (f32[256,128]{1,0:T(8,128)S(1)}, f32[256,128]{1,0:T(8,128)S(1)}, u32[]{:S(2)}, u32[]{:S(2)}) collective-permute-start(f32[256,128]{1,0:T(8,128)S(1)} %get-tuple-element.45), channel_id=1, source_target_pairs={{0,6},{2,4},{4,2},{6,0},{1,7},{3,5},{5,3},{7,1},{8,14},{10,12},{12... | collective-permute-start | bytes 393224 | tf_op jit(solution)/shard_map/ppermute | solution.py:514
  59.8 1.0 %collective-permute-start.8 = (f32[520,128]{1,0:T(8,128)S(1)}, f32[520,128]{1,0:T(8,128)S(1)}, u32[]{:S(2)}, u32[]{:S(2)}) collective-permute-start(f32[520,128]{1,0:T(8,128)S(1)} %get-tuple-element.40.refs_0_), channel_id=1, source_target_pairs={{0,16},{8,24},{16,0},{24,8},{1,17},{9,25},{17,1},{25,9},{2,18},{10... | collective-permute-start | bytes 798728 | tf_op jit(solution)/shard_map/ppermute | solution.py:514
  60.9 4.5 %collective-permute-done.14 = f32[256,128]{1,0:T(8,128)S(1)} collective-permute-done((f32[256,128]{1,0:T(8,128)S(1)}, f32[256,128]{1,0:T(8,128)S(1)}, u32[]{:S(2)}, u32[]{:S(2)}) %collective-permute-start.14) | collective-permute-done | bytes 131104 | tf_op jit(solution)/shard_map/ppermute | solution.py:514
  65.4 1.8 %collective-permute-done.17 = f32[256,128]{1,0:T(8,128)S(1)} collective-permute-done((f32[256,128]{1,0:T(8,128)S(1)}, f32[256,128]{1,0:T(8,128)S(1)}, u32[]{:S(2)}, u32[]{:S(2)}) %collective-permute-start.17) | collective-permute-done | bytes 131104 | tf_op jit(solution)/shard_map/ppermute | solution.py:514
  67.3 16.8 %collective-permute-start.15 = (f32[256,128]{1,0:T(8,128)S(1)}, f32[256,128]{1,0:T(8,128)S(1)}, u32[]{:S(2)}, u32[]{:S(2)}) collective-permute-start(f32[256,128]{1,0:T(8,128)S(1)} %add.46), channel_id=1, source_target_pairs={{0,1},{1,0},{2,3},{3,2},{4,5},{5,4},{6,7},{7,6},{8,9},{9,8},{10,11... | collective-permute-start | bytes 393224 | tf_op jit(solution)/shard_map/ppermute | solution.py:514
  84.1 2.7 %collective-permute-start.18 = (f32[256,128]{1,0:T(8,128)S(1)}, f32[256,128]{1,0:T(8,128)S(1)}, u32[]{:S(2)}, u32[]{:S(2)}) collective-permute-start(f32[256,128]{1,0:T(8,128)S(1)} %add.49), channel_id=1, source_target_pairs={{0,6},{2,4},{4,2},{6,0},{1,7},{3,5},{5,3},{7,1},{8,14},{10,12},{12... | collective-permute-start | bytes 393224 | tf_op jit(solution)/shard_map/ppermute | solution.py:514
  86.8 0.3 collective-permute-done.15
  87.1 0.2 collective-permute-start.11
  87.3 3.6 %collective-permute-done.18 = f32[256,128]{1,0:T(8,128)S(1)} collective-permute-done((f32[256,128]{1,0:T(8,128)S(1)}, f32[256,128]{1,0:T(8,128)S(1)}, u32[]{:S(2)}, u32[]{:S(2)}) %collective-permute-start.18) | collective-permute-done | bytes 131104 | tf_op jit(solution)/shard_map/ppermute | solution.py:514
  90.9 1.5 %collective-permute-start.16 = (f32[256,128]{1,0:T(8,128)S(1)}, f32[256,128]{1,0:T(8,128)S(1)}, u32[]{:S(2)}, u32[]{:S(2)}) collective-permute-start(f32[256,128]{1,0:T(8,128)S(1)} %add.47), channel_id=1, source_target_pairs={{0,2},{2,0},{4,6},{6,4},{1,3},{3,1},{5,7},{7,5},{8,10},{10,8},{12,... | collective-permute-start | bytes 393224 | tf_op jit(solution)/shard_map/ppermute | solution.py:514
  92.5 0.3 collective-permute-start.19
  92.8 3.5 %index_grad_query.2 = (f32[128,2048]{1,0:T(8,128)S(1)}, f32[1,128]{1,0:T(1,128)S(1)}) custom-call(f32[520,128]{1,0:T(8,128)S(1)} %get-tuple-element.40.refs_0_, f32[520,128]{1,0:T(8,128)S(1)} %collective-permute-done.12.refs_1_, f32[512,128]{1,0:T(8,128)S(1)} %get-tuple-element.35.wide_ref.refs_2_, f32[512,128]{1,0:T(8,128)S(1)} %collective-permute-done.13.refs_3_, ...), custom_call_target="tpu_custom_call" | custom-call | flops 1073741824 | bytes 3145728 | tf_op jit(solution)/shard_map/index_grad_query/pallas_call | solution.py:495
  96.3 1.2 %collective-permute-done.19 = f32[256,128]{1,0:T(8,128)S(1)} collective-permute-done((f32[256,128]{1,0:T(8,128)S(1)}, f32[256,128]{1,0:T(8,128)S(1)}, u32[]{:S(2)}, u32[]{:S(2)}) %collective-permute-start.19) | collective-permute-done | bytes 131104 | tf_op jit(solution)/shard_map/ppermute | solution.py:514
  97.5 0.7 pad_maximum_fusion
  98.2 4.1 %index_grad_query.3 = (f32[128,2048]{1,0:T(8,128)}, f32[1,128]{1,0:T(1,128)}) custom-call(f32[520,128]{1,0:T(8,128)S(1)} %collective-permute-done.8.refs_0_, f32[520,128]{1,0:T(8,128)S(1)} %collective-permute-done.9.refs_1_, f32[512,128]{1,0:T(8,128)S(1)} %collective-permute-done.10.refs_2_, f32[512,128]{1,0:T(8,128)S(1)} %collective-permute-done.11.refs_3_, ...), custom_call_target="tpu_custom_call" | custom-call | flops 1073741824 | bytes 3145728 | tf_op jit(solution)/shard_map/index_grad_query/pallas_call | solution.py:495
  (27 shorter events, 0.3 us)
Async XLA Ops:
  13.4 5.6 %collective-permute-start = (f32[32,512]{1,0:T(8,128)S(1)}, f32[32,512]{1,0:T(8,128)S(1)}, u32[]{:S(2)}, u32[]{:S(2)}) collective-permute-start(f32[32,512]{1,0:T(8,128)S(1)} %get-tuple-element.29), channel_id=1, source_target_pairs={{0,16},{8,24},{16,0},{24,8},{1,17},{9,25},{17,1},{25,9},{2,18},{10... | collective-permute-start | bytes 196616 | tf_op jit(solution)/shard_map/ppermute | solution.py:514
  16.4 67.7 %collective-permute-start.10 = (f32[512,128]{1,0:T(8,128)S(1)}, f32[512,128]{1,0:T(8,128)S(1)}, u32[]{:S(2)}, u32[]{:S(2)}) collective-permute-start(f32[512,128]{1,0:T(8,128)S(1)} %get-tuple-element.35.wide_ref.refs_2_), channel_id=1, source_target_pairs={{0,16},{8,24},{16,0},{24,8},{1,17},{9,25},{17,1},{25,9},{2,18},{10... | collective-permute-start | bytes 786440 | tf_op jit(solution)/shard_map/ppermute | solution.py:514
  19.0 6.6 %collective-permute-start.1 = (f32[32,512]{1,0:T(8,128)S(1)}, f32[32,512]{1,0:T(8,128)S(1)}, u32[]{:S(2)}, u32[]{:S(2)}) collective-permute-start(f32[32,512]{1,0:T(8,128)S(1)} %multiply_add_fusion.refs_0_), channel_id=1, source_target_pairs={{0,8},{8,0},{16,24},{24,16},{1,9},{9,1},{17,25},{25,17},{2,10},{10... | collective-permute-start | bytes 196616 | tf_op jit(solution)/shard_map/ppermute | solution.py:514
  23.2 17.3 %collective-permute-start.6 = (f32[1,128]{1,0:T(1,128)S(1)}, f32[1,128]{1,0:T(1,128)S(1)}, u32[]{:S(2)}, u32[]{:S(2)}) collective-permute-start(f32[1,128]{1,0:T(1,128)S(1)} %get-tuple-element.36), channel_id=1, source_target_pairs={{0,16},{8,24},{16,0},{24,8},{1,17},{9,25},{17,1},{25,9},{2,18},{10... | collective-permute-start | bytes 1544 | tf_op jit(solution)/shard_map/ppermute | solution.py:514
  27.9 12.5 %collective-permute-start.2 = (f32[256,128]{1,0:T(8,128)S(1)}, f32[256,128]{1,0:T(8,128)S(1)}, u32[]{:S(2)}, u32[]{:S(2)}) collective-permute-start(f32[256,128]{1,0:T(8,128)S(1)} %get-tuple-element.31), channel_id=1, source_target_pairs={{0,6},{2,4},{4,2},{6,0},{1,7},{3,5},{5,3},{7,1},{8,14},{10,12},{12... | collective-permute-start | bytes 393224 | tf_op jit(solution)/shard_map/ppermute | solution.py:514
  31.6 7.0 %collective-permute-start.4 = (f32[256,128]{1,0:T(8,128)S(1)}, f32[256,128]{1,0:T(8,128)S(1)}, u32[]{:S(2)}, u32[]{:S(2)}) collective-permute-start(f32[256,128]{1,0:T(8,128)S(1)} %get-tuple-element.33), channel_id=1, source_target_pairs={{0,2},{2,0},{4,6},{6,4},{1,3},{3,1},{5,7},{7,5},{8,10},{10,8},{12,... | collective-permute-start | bytes 393224 | tf_op jit(solution)/shard_map/ppermute | solution.py:514
  38.6 11.1 %collective-permute-start.5 = (f32[512,128]{1,0:T(8,128)S(1)}, f32[512,128]{1,0:T(8,128)S(1)}, u32[]{:S(2)}, u32[]{:S(2)}) collective-permute-start(f32[512,128]{1,0:T(8,128)S(1)} %pad_add_fusion), channel_id=1, source_target_pairs={{0,6},{2,4},{4,2},{6,0},{1,7},{3,5},{5,3},{7,1},{8,14},{10,12},{12... | collective-permute-start | bytes 786440 | tf_op jit(solution)/shard_map/ppermute | solution.py:514
  40.4 12.9 %collective-permute-start.3 = (f32[512,128]{1,0:T(8,128)S(1)}, f32[512,128]{1,0:T(8,128)S(1)}, u32[]{:S(2)}, u32[]{:S(2)}) collective-permute-start(f32[512,128]{1,0:T(8,128)S(1)} %pad_add_fusion.1), channel_id=1, source_target_pairs={{0,2},{2,0},{4,6},{6,4},{1,3},{3,1},{5,7},{7,5},{8,10},{10,8},{12,... | collective-permute-start | bytes 786440 | tf_op jit(solution)/shard_map/ppermute | solution.py:514
  40.5 2.3 %collective-permute-start.7 = (f32[1,128]{1,0:T(1,128)S(1)}, f32[1,128]{1,0:T(1,128)S(1)}, u32[]{:S(2)}, u32[]{:S(2)}) collective-permute-start(f32[1,128]{1,0:T(1,128)S(1)} %multiply_add_fusion.1.refs_3_.refs_6_), channel_id=1, source_target_pairs={{0,8},{8,0},{16,24},{24,16},{1,9},{9,1},{17,25},{25,17},{2,10},{10... | collective-permute-start | bytes 1544 | tf_op jit(solution)/shard_map/ppermute | solution.py:514
  57.7 7.7 %collective-permute-start.14 = (f32[256,128]{1,0:T(8,128)S(1)}, f32[256,128]{1,0:T(8,128)S(1)}, u32[]{:S(2)}, u32[]{:S(2)}) collective-permute-start(f32[256,128]{1,0:T(8,128)S(1)} %get-tuple-element.45), channel_id=1, source_target_pairs={{0,6},{2,4},{4,2},{6,0},{1,7},{3,5},{5,3},{7,1},{8,14},{10,12},{12... | collective-permute-start | bytes 393224 | tf_op jit(solution)/shard_map/ppermute | solution.py:514
  59.8 26.9 %collective-permute-start.8 = (f32[520,128]{1,0:T(8,128)S(1)}, f32[520,128]{1,0:T(8,128)S(1)}, u32[]{:S(2)}, u32[]{:S(2)}) collective-permute-start(f32[520,128]{1,0:T(8,128)S(1)} %get-tuple-element.40.refs_0_), channel_id=1, source_target_pairs={{0,16},{8,24},{16,0},{24,8},{1,17},{9,25},{17,1},{25,9},{2,18},{10... | collective-permute-start | bytes 798728 | tf_op jit(solution)/shard_map/ppermute | solution.py:514
  60.9 6.4 %collective-permute-start.17 = (f32[256,128]{1,0:T(8,128)S(1)}, f32[256,128]{1,0:T(8,128)S(1)}, u32[]{:S(2)}, u32[]{:S(2)}) collective-permute-start(f32[256,128]{1,0:T(8,128)S(1)} %get-tuple-element.46), channel_id=1, source_target_pairs={{0,2},{2,0},{4,6},{6,4},{1,3},{3,1},{5,7},{7,5},{8,10},{10,8},{12,... | collective-permute-start | bytes 393224 | tf_op jit(solution)/shard_map/ppermute | solution.py:514
  60.9 31.6 %collective-permute-start.13 = (f32[512,128]{1,0:T(8,128)S(1)}, f32[512,128]{1,0:T(8,128)S(1)}, u32[]{:S(2)}, u32[]{:S(2)}) collective-permute-start(f32[512,128]{1,0:T(8,128)S(1)} %get-tuple-element.35.wide_ref.refs_2_), channel_id=1, source_target_pairs={{0,8},{8,0},{16,24},{24,16},{1,9},{9,1},{17,25},{25,17},{2,10},{10... | collective-permute-start | bytes 786440 | tf_op jit(solution)/shard_map/ppermute | solution.py:514
  65.4 27.4 %collective-permute-start.12 = (f32[520,128]{1,0:T(8,128)S(1)}, f32[520,128]{1,0:T(8,128)S(1)}, u32[]{:S(2)}, u32[]{:S(2)}) collective-permute-start(f32[520,128]{1,0:T(8,128)S(1)} %get-tuple-element.40.refs_0_), channel_id=1, source_target_pairs={{0,8},{8,0},{16,24},{24,16},{1,9},{9,1},{17,25},{25,17},{2,10},{10... | collective-permute-start | bytes 798728 | tf_op jit(solution)/shard_map/ppermute | solution.py:514
  67.3 19.8 %collective-permute-start.15 = (f32[256,128]{1,0:T(8,128)S(1)}, f32[256,128]{1,0:T(8,128)S(1)}, u32[]{:S(2)}, u32[]{:S(2)}) collective-permute-start(f32[256,128]{1,0:T(8,128)S(1)} %add.46), channel_id=1, source_target_pairs={{0,1},{1,0},{2,3},{3,2},{4,5},{5,4},{6,7},{7,6},{8,9},{9,8},{10,11... | collective-permute-start | bytes 393224 | tf_op jit(solution)/shard_map/ppermute | solution.py:514
  84.1 6.8 %collective-permute-start.18 = (f32[256,128]{1,0:T(8,128)S(1)}, f32[256,128]{1,0:T(8,128)S(1)}, u32[]{:S(2)}, u32[]{:S(2)}) collective-permute-start(f32[256,128]{1,0:T(8,128)S(1)} %add.49), channel_id=1, source_target_pairs={{0,6},{2,4},{4,2},{6,0},{1,7},{3,5},{5,3},{7,1},{8,14},{10,12},{12... | collective-permute-start | bytes 393224 | tf_op jit(solution)/shard_map/ppermute | solution.py:514
  86.8 11.5 %collective-permute-start.9 = (f32[520,128]{1,0:T(8,128)S(1)}, f32[520,128]{1,0:T(8,128)S(1)}, u32[]{:S(2)}, u32[]{:S(2)}) collective-permute-start(f32[520,128]{1,0:T(8,128)S(1)} %collective-permute-done.8.refs_0_), channel_id=1, source_target_pairs={{0,8},{8,0},{16,24},{24,16},{1,9},{9,1},{17,25},{25,17},{2,10},{10... | collective-permute-start | bytes 798728 | tf_op jit(solution)/shard_map/ppermute | solution.py:514
  87.1 11.1 %collective-permute-start.11 = (f32[512,128]{1,0:T(8,128)S(1)}, f32[512,128]{1,0:T(8,128)S(1)}, u32[]{:S(2)}, u32[]{:S(2)}) collective-permute-start(f32[512,128]{1,0:T(8,128)S(1)} %collective-permute-done.10.refs_2_), channel_id=1, source_target_pairs={{0,8},{8,0},{16,24},{24,16},{1,9},{9,1},{17,25},{25,17},{2,10},{10... | collective-permute-start | bytes 786440 | tf_op jit(solution)/shard_map/ppermute | solution.py:514
  90.9 5.4 %collective-permute-start.16 = (f32[256,128]{1,0:T(8,128)S(1)}, f32[256,128]{1,0:T(8,128)S(1)}, u32[]{:S(2)}, u32[]{:S(2)}) collective-permute-start(f32[256,128]{1,0:T(8,128)S(1)} %add.47), channel_id=1, source_target_pairs={{0,2},{2,0},{4,6},{6,4},{1,3},{3,1},{5,7},{7,5},{8,10},{10,8},{12,... | collective-permute-start | bytes 393224 | tf_op jit(solution)/shard_map/ppermute | solution.py:514
  92.5 5.0 %collective-permute-start.19 = (f32[256,128]{1,0:T(8,128)S(1)}, f32[256,128]{1,0:T(8,128)S(1)}, u32[]{:S(2)}, u32[]{:S(2)}) collective-permute-start(f32[256,128]{1,0:T(8,128)S(1)} %add.50), channel_id=1, source_target_pairs={{0,1},{1,0},{2,3},{3,2},{4,5},{5,4},{6,7},{7,6},{8,9},{9,8},{10,11... | collective-permute-start | bytes 393224 | tf_op jit(solution)/shard_map/ppermute | solution.py:514

commit v9 on v8

--- a/solution.py
+++ b/solution.py
@@ -89,9 +89,9 @@
 
 
 def stats_kernel(per, count_hbm, q_hbm, kn_hbm, rope_hbm, qpos_hbm, kpos_hbm, iq_hbm, ik_hbm,
-                 lse_ref, q_ref, kk_ref, bias_ref, iq_ref, ik_ref, spread_ref, live_ref,
+                 lse_ref, q_ref, kk_ref, bias_ref, iq_ref, ik_ref, rank_ref, live_ref,
                  kn_ref, rope_ref, qpos_ref, kpos_ref, even_ref, odd_ref, none_ref, bad_ref,
-                 pack_ref, raw_ref, count_ref, small_sem, q_sem, kn_sem, iq_sem):
+                 pack_ref, raw_ref, one_ref, two_ref, count_ref, small_sem, q_sem, kn_sem, iq_sem):
     keys = kn_ref.shape[0]
     groups, rows = q_ref.shape[0], q_ref.shape[1]
     pairs = q_ref.shape[2] // PAIR
@@ -126,14 +126,23 @@
     row = lax.broadcasted_iota(jnp.int32, (keys, keys), 0)
     chosen = row == rank
     pack_ref[...] = jnp.where(chosen, 1.0, 0.0).astype(bf16)
-    position = jnp.sum(jnp.where(chosen, kpos_ref[...].astype(f32), 0.0), axis=1, keepdims=True)
+    rank_ref[...] = jnp.broadcast_to(rank, rank_ref.shape)
+    live_ref[...] = jnp.broadcast_to(live, live_ref.shape)
+    position = kpos_ref[...].astype(f32)
+    digits = [rope_ref[...].astype(f32)]
+    for unit in (2048.0, 32.0, 1.0):
+        digit = jnp.floor(position / unit)
+        position = position - digit * unit
+        digits.append(digit)
+    digits.append(jnp.zeros((LANES - DROPE - 3, keys), f32))
+    packed = dot_nt(pack_ref[...], jnp.concatenate(digits, axis=0).astype(bf16))
+    position = (
+        packed[:, DROPE : DROPE + 1] * 2048.0
+        + packed[:, DROPE + 1 : DROPE + 2] * 32.0
+        + packed[:, DROPE + 2 : DROPE + 3]
+    )
     column = jnp.where(row[:, :1] < live, position.astype(jnp.int32), BIG)
-    rank_column = jnp.transpose(jnp.broadcast_to(rank, (8, keys)))[:, :1]
-    lane = lax.broadcasted_iota(jnp.int32, (keys, keys), 1)
-    spread_ref[...] = jnp.where(lane == rank_column, 1.0, 0.0).astype(bf16)
-    live_ref[...] = jnp.broadcast_to(live, live_ref.shape)
-    ik_ref[...] = dot_nn(pack_ref[...], raw_ref[...])
-    rope = dot_nt(pack_ref[...], rope_ref[...]).astype(bf16)
+    rope = packed[:, :DROPE].astype(bf16)
     zero = jnp.zeros_like(rope)
     even_ref[...] = jnp.concatenate([rope, zero], axis=1)
     odd_ref[...] = jnp.concatenate([zero, rope], axis=1)
@@ -154,17 +163,29 @@
         at = pl.ds(pl.multiple_of(pair * PAIR + a * LANES, LANES), 2 * LANES)
         return q_ref[2 * c : 2 * c + 2, :, at]
 
-    def step(size, i, carry):
+    steps = pairs // per
+
+    def arrive(i):
         for p in range(per):
-            pair = i * per + p
-            for copy in large(pair):
+            for copy in large(i * per + p):
                 copy.wait()
+
+    def build(size, buf, i):
         for p in range(per):
             pair = i * per + p
             both = dot_nn(pack_ref[:size, :], kn_ref[:, lanes_at(pair, 2 * DNOPE)]).astype(bf16)
             for a in range(2):
                 kk = main_keys(both[:, a * DNOPE : (a + 1) * DNOPE], a, even_ref, odd_ref)
                 kk_ref[:size, lanes_at(2 * pair + a, 2 * LANES)] = kk
+                at = (2 * p + a) * 2 * LANES
+                buf[:size, at : at + 2 * LANES] = kk
+
+    def process(size, buf, i):
+        for p in range(per):
+            pair = i * per + p
+            for a in range(2):
+                at = (2 * p + a) * 2 * LANES
+                kk = buf[:size, at : at + 2 * LANES]
                 for c, cols in enumerate(halves):
                     s = scores(kk, query(pair, a, c), c)
                     total = jnp.sum(jnp.exp2(s), axis=0, keepdims=True)
@@ -172,12 +193,23 @@
                     skip = none_ref[:, cols] > 0
                     bad_ref[:, cols] += jnp.where(fine | skip, 0.0, 1.0)
                     lse_ref[pl.ds(2 * pair + a, 1), cols] = jnp.where(skip, NEG, jnp.log2(total))
+
+    def step(size, i, carry):
+        arrive(2 * i + 1)
+        pl.when(2 * i + 2 < steps)(lambda: arrive(2 * i + 2))
+        process(size, one_ref, 2 * i)
+        build(size, two_ref, 2 * i + 1)
+        process(size, two_ref, 2 * i + 1)
+        build(size, one_ref, jnp.minimum(2 * i + 2, steps - 1))
         return carry
 
     def run(size):
-        lax.fori_loop(0, pairs // per, functools.partial(step, size), 0)
-
+        build(size, one_ref, 0)
+        lax.fori_loop(0, steps // 2, functools.partial(step, size), 0)
+
+    arrive(0)
     for_packed(live, keys, run)
+    ik_ref[...] = dot_nn(pack_ref[...], raw_ref[...])
     index_copy.wait()
 
     @pl.when(jnp.max(bad_ref[...]) > 0)
@@ -211,7 +243,7 @@
             jax.ShapeDtypeStruct((keys, total), f32),
             jax.ShapeDtypeStruct(index_query.shape, bf16),
             jax.ShapeDtypeStruct(index_key.shape, f32),
-            jax.ShapeDtypeStruct((keys, keys), bf16),
+            jax.ShapeDtypeStruct((8, keys), jnp.int32),
             jax.ShapeDtypeStruct((8, LANES), jnp.int32),
         ],
         scratch_shapes=[
@@ -225,6 +257,8 @@
             pltpu.VMEM((1, total), f32),
             pltpu.VMEM((keys, keys), bf16),
             pltpu.VMEM(index_key.shape, bf16),
+            pltpu.VMEM((keys, 8 * LANES), bf16),
+            pltpu.VMEM((keys, 8 * LANES), bf16),
             pltpu.SMEM(key_count.shape, jnp.int32),
             pltpu.SemaphoreType.DMA((5,)),
             pltpu.SemaphoreType.DMA((heads // 2,)),
@@ -237,6 +271,26 @@
         ),
         name="main_stats",
     )(key_count, main_query, key_nope, rope_t, query_pos, key_pos, index_query, index_key)
+
+
+def spread_kernel(rank_ref, spread_ref):
+    keys = rank_ref.shape[1]
+    column = jnp.transpose(rank_ref[...])[:, :1]
+    lane = lax.broadcasted_iota(jnp.int32, (keys, keys), 1)
+    spread_ref[...] = jnp.where(lane == column, 1.0, 0.0).astype(bf16)
+
+
+def spread_matrix(rank):
+    keys = rank.shape[1]
+    return pl.pallas_call(
+        spread_kernel,
+        in_specs=[IN_VMEM],
+        out_specs=IN_VMEM,
+        out_shape=jax.ShapeDtypeStruct((keys, keys), bf16),
+        compiler_params=pltpu.CompilerParams(vmem_limit_bytes=8 * 1024 * 1024),
+        cost_estimate=cost(keys * keys * 4, keys * keys * 2),
+        name="spread_matrix",
+    )(rank)
 
 
 def target_kernel(n_lse, masks, per, parts, q_ref, kk_ref, bias_ref, live_ref, *refs):
@@ -420,7 +474,7 @@
     rows, width = index_query.shape
     keys = logits.shape[0]
     return pl.pallas_call(
-        functools.partial(grad_key_kernel, len(parts), len(lses), 4),
+        functools.partial(grad_key_kernel, len(parts), len(lses), 8),
         grid=(1,),
         in_specs=[IN_VMEM] * (len(parts) + len(lses) + 6)
         + [pl.BlockSpec((1, rows), lambda i: (0, 0))],
@@ -556,7 +610,7 @@
             return [value, near, far, across]
         return list(lax.all_gather(value, "key"))
 
-    lse, q, kk, bias, iq, wide, spread, live = main_stats(
+    lse, q, kk, bias, iq, wide, rank, live = main_stats(
         main_query, key_nope, rope_t, query_pos, key_row, key_count, index_query, narrow
     )
     lses = butterfly_lse(lse, n_key)
@@ -582,6 +636,7 @@
         tiles = tiles[jnp.bitwise_xor(jnp.arange(groups), z)]
         parts = [lax.psum_scatter(tiles, "head", scatter_dimension=0, tiled=True)[0]]
 
+    spread = spread_matrix(rank)
     sg, *grad_key = index_grad_key(
         parts, index_lses, logits, wm, iq, bias, live, spread, cotangent
     )

time: 103 us -> 102 us (level)
  no operation moved by 1% of the time
where the time goes in v9:
time: 102 us
  Pallas kernels  36.5 us (36%)
  starting transfers between devices  35.9 us (35%)
  waiting for transfers between devices  27.9 us (27%)
    ppermute x20, starting transfers between devices, swap(): return lax.ppermute(value, axis, [(i, i ^ mask) for i in range(size)])  35.9 us
    ppermute x20, waiting for transfers between devices, swap(): return lax.ppermute(value, axis, [(i, i ^ mask) for i in range(size)])  27.9 us
    pallas_call x1, Pallas kernels, main_stats(): pl.pallas_call(functools.partial(stats_kernel, 2), in_specs=[pl.BlockSpec...  12.4 us
    pallas_call x3, Pallas kernels, head_sums(): pl.pallas_call(functools.partial(target_kernel, len(lses), masks, 4 // n,...  8 us
    pallas_call x2, Pallas kernels, index_grad_query(): pl.pallas_call(functools.partial(grad_query_kernel, n, first, len(lses)),...  7.56 us
    pallas_call x1, Pallas kernels, index_logits(): pl.pallas_call(functools.partial(logits_kernel, 4), grid=(1,), in_specs=[...  4.11 us
    pallas_call x1, Pallas kernels, index_grad_key(): pl.pallas_call(functools.partial(grad_key_kernel, len(parts), len(lses),...  4.1 us
  transfers between devices with their start and end apart: 20, of which 9 were waited for; matrix products, arithmetic and copies ran while one was open for 1% of the time, Pallas kernels for 20%

profile of v9, /device:TPU:0, one launch (start us, length us, event | category | flops | bytes accessed | tf_op | source)
XLA Modules:
  0.0 102.0 jit_solution(15851471115430671696)
XLA Ops:
  0.6 12.4 %main_stats.1 = (f32[32,512]{1,0:T(8,128)S(1)}, bf16[4,128,6144]{2,1,0:T(8,128)(2,1)S(1)}, bf16[512,8192]{1,0:T(8,128)(2,1)S(1)}, f32[512,512]{1,0:T(8,128)S(1)}...) custom-call(s32[16]{0:T(128)} %count_hbm.1, ...), custom_call_target="tpu_custom_call" | custom-call | flops 4294967296 | bytes 10485760 | tf_op jit(solution)/shard_map/main_stats/pallas_call | solution.py:235
  13.1 3.0 %collective-permute-start = (f32[32,512]{1,0:T(8,128)S(1)}, f32[32,512]{1,0:T(8,128)S(1)}, u32[]{:S(2)}, u32[]{:S(2)}) collective-permute-start(f32[32,512]{1,0:T(8,128)S(1)} %get-tuple-element.29), channel_id=1, source_target_pairs={{0,16},{8,24},{16,0},{24,8},{1,17},{9,25},{17,1},{25,9},{2,18},{10... | collective-permute-start | bytes 196616 | tf_op jit(solution)/shard_map/ppermute | solution.py:568
  16.1 0.1 collective-permute-start.10
  16.2 2.4 %collective-permute-done = f32[32,512]{1,0:T(8,128)S(1)} collective-permute-done((f32[32,512]{1,0:T(8,128)S(1)}, f32[32,512]{1,0:T(8,128)S(1)}, u32[]{:S(2)}, u32[]{:S(2)}) %collective-permute-start) | collective-permute-done | bytes 65568 | tf_op jit(solution)/shard_map/ppermute | solution.py:568
  18.7 4.1 %index_logits.1 = (f32[512,128]{1,0:T(8,128)S(1)}, f32[1,128]{1,0:T(1,128)S(1)}, bf16[512,8192]{1,0:T(8,128)(2,1)S(1)}) custom-call(bf16[128,8192]{1,0:T(8,128)(2,1)S(1)} %get-tuple-element.34.iq_ref.refs_7_.refs_4_, f32[512,128]{1,0:T(8,128)S(1)} %get-tuple-element.35.wide_ref.refs_2_, bf16[64,128]{1,0:T(8,128)(2,1)} %bitcast.5, ...), custom_call_target="tpu_custom_call" | custom-call | flops 1073741824 | bytes 10485760 | tf_op jit(solution)/shard_map/index_logits/pallas_call | solution.py:399
  22.8 2.5 %collective-permute-start.6 = (f32[1,128]{1,0:T(1,128)S(1)}, f32[1,128]{1,0:T(1,128)S(1)}, u32[]{:S(2)}, u32[]{:S(2)}) collective-permute-start(f32[1,128]{1,0:T(1,128)S(1)} %get-tuple-element.36), channel_id=1, source_target_pairs={{0,16},{8,24},{16,0},{24,8},{1,17},{9,25},{17,1},{25,9},{2,18},{10... | collective-permute-start | bytes 1544 | tf_op jit(solution)/shard_map/ppermute | solution.py:568
  25.3 0.3 spread_matrix.1.refs_10_
  25.6 2.4 %head_sums.5 = (f32[256,128]{1,0:T(8,128)S(1)}, f32[256,128]{1,0:T(8,128)S(1)}) custom-call(bf16[4,128,6144]{2,1,0:T(8,128)(2,1)S(1)} %get-tuple-element.25.q_ref, bf16[512,8192]{1,0:T(8,128)(2,1)S(1)} %get-tuple-element.26.kk_ref, f32[512,512]{1,0:T(8,128)S(1)} %get-tuple-element.27.bias_ref.refs_8_, s32[8,128]{1,0:T(8,128)S(1)} %get-tuple-element.28.live_ref.refs_9_, ...), custom_call_target="tpu_custom_call" | custom-call | flops 1073741824 | bytes 131072 | tf_op jit(solution)/shard_map/head_sums/pallas_call | solution.py:349
  28.1 3.7 %collective-permute-start.2 = (f32[256,128]{1,0:T(8,128)S(1)}, f32[256,128]{1,0:T(8,128)S(1)}, u32[]{:S(2)}, u32[]{:S(2)}) collective-permute-start(f32[256,128]{1,0:T(8,128)S(1)} %get-tuple-element.31), channel_id=1, source_target_pairs={{0,6},{2,4},{4,2},{6,0},{1,7},{3,5},{5,3},{7,1},{8,14},{10,12},{12... | collective-permute-start | bytes 393224 | tf_op jit(solution)/shard_map/ppermute | solution.py:568
  31.7 3.3 %head_sums.4 = (f32[512,128]{1,0:T(8,128)S(1)}, f32[512,128]{1,0:T(8,128)S(1)}) custom-call(bf16[4,128,6144]{2,1,0:T(8,128)(2,1)S(1)} %get-tuple-element.25.q_ref, bf16[512,8192]{1,0:T(8,128)(2,1)S(1)} %get-tuple-element.26.kk_ref, f32[512,512]{1,0:T(8,128)S(1)} %get-tuple-element.27.bias_ref.refs_8_, s32[8,128]{1,0:T(8,128)S(1)} %get-tuple-element.28.live_ref.refs_9_, ...), custom_call_target="tpu_custom_call" | custom-call | flops 2147483648 | bytes 262144 | tf_op jit(solution)/shard_map/head_sums/pallas_call | solution.py:349
  35.1 3.7 %collective-permute-done.4 = f32[256,128]{1,0:T(8,128)S(1)} collective-permute-done((f32[256,128]{1,0:T(8,128)S(1)}, f32[256,128]{1,0:T(8,128)S(1)}, u32[]{:S(2)}, u32[]{:S(2)}) %collective-permute-start.4) | collective-permute-done | bytes 131104 | tf_op jit(solution)/shard_map/ppermute | solution.py:568
  38.7 1.8 %collective-permute-start.5 = (f32[512,128]{1,0:T(8,128)S(1)}, f32[512,128]{1,0:T(8,128)S(1)}, u32[]{:S(2)}, u32[]{:S(2)}) collective-permute-start(f32[512,128]{1,0:T(8,128)S(1)} %pad_add_fusion), channel_id=1, source_target_pairs={{0,6},{2,4},{4,2},{6,0},{1,7},{3,5},{5,3},{7,1},{8,14},{10,12},{12... | collective-permute-start | bytes 786440 | tf_op jit(solution)/shard_map/ppermute | solution.py:568
  40.5 0.1 collective-permute-start.3
  40.7 2.2 %head_sums.3.refs_0_ = f32[512,128]{1,0:T(8,128)S(1)} custom-call(bf16[4,128,6144]{2,1,0:T(8,128)(2,1)S(1)} %get-tuple-element.25.q_ref, bf16[512,8192]{1,0:T(8,128)(2,1)S(1)} %get-tuple-element.26.kk_ref, f32[512,512]{1,0:T(8,128)S(1)} %get-tuple-element.27.bias_ref.refs_8_, s32[8,128]{1,0:T(8,128)S(1)} %get-tuple-element.28.live_ref.refs_9_, ...), custom_call_target="tpu_custom_call" | custom-call | flops 1073741824 | bytes 131072 | tf_op jit(solution)/shard_map/head_sums/pallas_call | solution.py:349
  43.0 6.8 %collective-permute-done.5.refs_2_ = f32[512,128]{1,0:T(8,128)S(1)} collective-permute-done((f32[512,128]{1,0:T(8,128)S(1)}, f32[512,128]{1,0:T(8,128)S(1)}, u32[]{:S(2)}, u32[]{:S(2)}) %collective-permute-start.5) | collective-permute-done | bytes 262176 | tf_op jit(solution)/shard_map/ppermute | solution.py:568
  49.8 3.5 %collective-permute-done.3.refs_1_ = f32[512,128]{1,0:T(8,128)S(1)} collective-permute-done((f32[512,128]{1,0:T(8,128)S(1)}, f32[512,128]{1,0:T(8,128)S(1)}, u32[]{:S(2)}, u32[]{:S(2)}) %collective-permute-start.3) | collective-permute-done | bytes 262176 | tf_op jit(solution)/shard_map/ppermute | solution.py:568
  53.3 4.1 %index_grad_key.1 = (f32[520,128]{1,0:T(8,128)S(1)}, f32[256,128]{1,0:T(8,128)S(1)}, f32[256,128]{1,0:T(8,128)S(1)}) custom-call(f32[512,128]{1,0:T(8,128)S(1)} %head_sums.3.refs_0_, f32[512,128]{1,0:T(8,128)S(1)} %collective-permute-done.3.refs_1_, f32[512,128]{1,0:T(8,128)S(1)} %collective-permute-done.5.refs_2_, ...), custom_call_target="tpu_custom_call" | custom-call | flops 1073741824 | bytes 10485760 | tf_op jit(solution)/shard_map/index_grad_key/pallas_call | solution.py:476
  57.4 2.1 %collective-permute-start.14 = (f32[256,128]{1,0:T(8,128)S(1)}, f32[256,128]{1,0:T(8,128)S(1)}, u32[]{:S(2)}, u32[]{:S(2)}) collective-permute-start(f32[256,128]{1,0:T(8,128)S(1)} %get-tuple-element.45), channel_id=1, source_target_pairs={{0,6},{2,4},{4,2},{6,0},{1,7},{3,5},{5,3},{7,1},{8,14},{10,12},{12... | collective-permute-start | bytes 393224 | tf_op jit(solution)/shard_map/ppermute | solution.py:568
  59.6 1.1 %collective-permute-start.8 = (f32[520,128]{1,0:T(8,128)S(1)}, f32[520,128]{1,0:T(8,128)S(1)}, u32[]{:S(2)}, u32[]{:S(2)}) collective-permute-start(f32[520,128]{1,0:T(8,128)S(1)} %get-tuple-element.40.refs_0_), channel_id=1, source_target_pairs={{0,16},{8,24},{16,0},{24,8},{1,17},{9,25},{17,1},{25,9},{2,18},{10... | collective-permute-start | bytes 798728 | tf_op jit(solution)/shard_map/ppermute | solution.py:568
  60.6 4.5 %collective-permute-done.14 = f32[256,128]{1,0:T(8,128)S(1)} collective-permute-done((f32[256,128]{1,0:T(8,128)S(1)}, f32[256,128]{1,0:T(8,128)S(1)}, u32[]{:S(2)}, u32[]{:S(2)}) %collective-permute-start.14) | collective-permute-done | bytes 131104 | tf_op jit(solution)/shard_map/ppermute | solution.py:568
  65.1 1.9 %collective-permute-done.17 = f32[256,128]{1,0:T(8,128)S(1)} collective-permute-done((f32[256,128]{1,0:T(8,128)S(1)}, f32[256,128]{1,0:T(8,128)S(1)}, u32[]{:S(2)}, u32[]{:S(2)}) %collective-permute-start.17) | collective-permute-done | bytes 131104 | tf_op jit(solution)/shard_map/ppermute | solution.py:568
  67.0 16.6 %collective-permute-start.15 = (f32[256,128]{1,0:T(8,128)S(1)}, f32[256,128]{1,0:T(8,128)S(1)}, u32[]{:S(2)}, u32[]{:S(2)}) collective-permute-start(f32[256,128]{1,0:T(8,128)S(1)} %add.46), channel_id=1, source_target_pairs={{0,1},{1,0},{2,3},{3,2},{4,5},{5,4},{6,7},{7,6},{8,9},{9,8},{10,11... | collective-permute-start | bytes 393224 | tf_op jit(solution)/shard_map/ppermute | solution.py:568
  83.7 2.7 %collective-permute-start.18 = (f32[256,128]{1,0:T(8,128)S(1)}, f32[256,128]{1,0:T(8,128)S(1)}, u32[]{:S(2)}, u32[]{:S(2)}) collective-permute-start(f32[256,128]{1,0:T(8,128)S(1)} %add.49), channel_id=1, source_target_pairs={{0,6},{2,4},{4,2},{6,0},{1,7},{3,5},{5,3},{7,1},{8,14},{10,12},{12... | collective-permute-start | bytes 393224 | tf_op jit(solution)/shard_map/ppermute | solution.py:568
  86.4 0.4 collective-permute-done.15
  86.7 0.2 collective-permute-start.11
  86.9 3.6 %collective-permute-done.18 = f32[256,128]{1,0:T(8,128)S(1)} collective-permute-done((f32[256,128]{1,0:T(8,128)S(1)}, f32[256,128]{1,0:T(8,128)S(1)}, u32[]{:S(2)}, u32[]{:S(2)}) %collective-permute-start.18) | collective-permute-done | bytes 131104 | tf_op jit(solution)/shard_map/ppermute | solution.py:568
  90.5 1.5 %collective-permute-start.16 = (f32[256,128]{1,0:T(8,128)S(1)}, f32[256,128]{1,0:T(8,128)S(1)}, u32[]{:S(2)}, u32[]{:S(2)}) collective-permute-start(f32[256,128]{1,0:T(8,128)S(1)} %add.47), channel_id=1, source_target_pairs={{0,2},{2,0},{4,6},{6,4},{1,3},{3,1},{5,7},{7,5},{8,10},{10,8},{12,... | collective-permute-start | bytes 393224 | tf_op jit(solution)/shard_map/ppermute | solution.py:568
  92.1 0.3 collective-permute-start.19
  92.4 3.5 %index_grad_query.2 = (f32[128,2048]{1,0:T(8,128)S(1)}, f32[1,128]{1,0:T(1,128)S(1)}) custom-call(f32[520,128]{1,0:T(8,128)S(1)} %get-tuple-element.40.refs_0_, f32[520,128]{1,0:T(8,128)S(1)} %collective-permute-done.12.refs_1_, f32[512,128]{1,0:T(8,128)S(1)} %get-tuple-element.35.wide_ref.refs_2_, f32[512,128]{1,0:T(8,128)S(1)} %collective-permute-done.13.refs_3_, ...), custom_call_target="tpu_custom_call" | custom-call | flops 1073741824 | bytes 3145728 | tf_op jit(solution)/shard_map/index_grad_query/pallas_call | solution.py:549
  96.0 1.2 %collective-permute-done.19 = f32[256,128]{1,0:T(8,128)S(1)} collective-permute-done((f32[256,128]{1,0:T(8,128)S(1)}, f32[256,128]{1,0:T(8,128)S(1)}, u32[]{:S(2)}, u32[]{:S(2)}) %collective-permute-start.19) | collective-permute-done | bytes 131104 | tf_op jit(solution)/shard_map/ppermute | solution.py:568
  97.1 0.7 pad_maximum_fusion
  97.9 4.1 %index_grad_query.3 = (f32[128,2048]{1,0:T(8,128)}, f32[1,128]{1,0:T(1,128)}) custom-call(f32[520,128]{1,0:T(8,128)S(1)} %collective-permute-done.8.refs_0_, f32[520,128]{1,0:T(8,128)S(1)} %collective-permute-done.9.refs_1_, f32[512,128]{1,0:T(8,128)S(1)} %collective-permute-done.10.refs_2_, f32[512,128]{1,0:T(8,128)S(1)} %collective-permute-done.11.refs_3_, ...), custom_call_target="tpu_custom_call" | custom-call | flops 1073741824 | bytes 3145728 | tf_op jit(solution)/shard_map/index_grad_query/pallas_call | solution.py:549
  (28 shorter events, 0.4 us)
Async XLA Ops:
  13.1 5.5 %collective-permute-start = (f32[32,512]{1,0:T(8,128)S(1)}, f32[32,512]{1,0:T(8,128)S(1)}, u32[]{:S(2)}, u32[]{:S(2)}) collective-permute-start(f32[32,512]{1,0:T(8,128)S(1)} %get-tuple-element.29), channel_id=1, source_target_pairs={{0,16},{8,24},{16,0},{24,8},{1,17},{9,25},{17,1},{25,9},{2,18},{10... | collective-permute-start | bytes 196616 | tf_op jit(solution)/shard_map/ppermute | solution.py:568
  16.1 67.6 %collective-permute-start.10 = (f32[512,128]{1,0:T(8,128)S(1)}, f32[512,128]{1,0:T(8,128)S(1)}, u32[]{:S(2)}, u32[]{:S(2)}) collective-permute-start(f32[512,128]{1,0:T(8,128)S(1)} %get-tuple-element.35.wide_ref.refs_2_), channel_id=1, source_target_pairs={{0,16},{8,24},{16,0},{24,8},{1,17},{9,25},{17,1},{25,9},{2,18},{10... | collective-permute-start | bytes 786440 | tf_op jit(solution)/shard_map/ppermute | solution.py:568
  18.6 7.0 %collective-permute-start.1 = (f32[32,512]{1,0:T(8,128)S(1)}, f32[32,512]{1,0:T(8,128)S(1)}, u32[]{:S(2)}, u32[]{:S(2)}) collective-permute-start(f32[32,512]{1,0:T(8,128)S(1)} %multiply_add_fusion.refs_0_), channel_id=1, source_target_pairs={{0,8},{8,0},{16,24},{24,16},{1,9},{9,1},{17,25},{25,17},{2,10},{10... | collective-permute-start | bytes 196616 | tf_op jit(solution)/shard_map/ppermute | solution.py:568
  22.8 17.8 %collective-permute-start.6 = (f32[1,128]{1,0:T(1,128)S(1)}, f32[1,128]{1,0:T(1,128)S(1)}, u32[]{:S(2)}, u32[]{:S(2)}) collective-permute-start(f32[1,128]{1,0:T(1,128)S(1)} %get-tuple-element.36), channel_id=1, source_target_pairs={{0,16},{8,24},{16,0},{24,8},{1,17},{9,25},{17,1},{25,9},{2,18},{10... | collective-permute-start | bytes 1544 | tf_op jit(solution)/shard_map/ppermute | solution.py:568
  28.1 12.5 %collective-permute-start.2 = (f32[256,128]{1,0:T(8,128)S(1)}, f32[256,128]{1,0:T(8,128)S(1)}, u32[]{:S(2)}, u32[]{:S(2)}) collective-permute-start(f32[256,128]{1,0:T(8,128)S(1)} %get-tuple-element.31), channel_id=1, source_target_pairs={{0,6},{2,4},{4,2},{6,0},{1,7},{3,5},{5,3},{7,1},{8,14},{10,12},{12... | collective-permute-start | bytes 393224 | tf_op jit(solution)/shard_map/ppermute | solution.py:568
  31.7 7.0 %collective-permute-start.4 = (f32[256,128]{1,0:T(8,128)S(1)}, f32[256,128]{1,0:T(8,128)S(1)}, u32[]{:S(2)}, u32[]{:S(2)}) collective-permute-start(f32[256,128]{1,0:T(8,128)S(1)} %get-tuple-element.33), channel_id=1, source_target_pairs={{0,2},{2,0},{4,6},{6,4},{1,3},{3,1},{5,7},{7,5},{8,10},{10,8},{12,... | collective-permute-start | bytes 393224 | tf_op jit(solution)/shard_map/ppermute | solution.py:568
  38.7 11.1 %collective-permute-start.5 = (f32[512,128]{1,0:T(8,128)S(1)}, f32[512,128]{1,0:T(8,128)S(1)}, u32[]{:S(2)}, u32[]{:S(2)}) collective-permute-start(f32[512,128]{1,0:T(8,128)S(1)} %pad_add_fusion), channel_id=1, source_target_pairs={{0,6},{2,4},{4,2},{6,0},{1,7},{3,5},{5,3},{7,1},{8,14},{10,12},{12... | collective-permute-start | bytes 786440 | tf_op jit(solution)/shard_map/ppermute | solution.py:568
  40.5 12.8 %collective-permute-start.3 = (f32[512,128]{1,0:T(8,128)S(1)}, f32[512,128]{1,0:T(8,128)S(1)}, u32[]{:S(2)}, u32[]{:S(2)}) collective-permute-start(f32[512,128]{1,0:T(8,128)S(1)} %pad_add_fusion.1), channel_id=1, source_target_pairs={{0,2},{2,0},{4,6},{6,4},{1,3},{3,1},{5,7},{7,5},{8,10},{10,8},{12,... | collective-permute-start | bytes 786440 | tf_op jit(solution)/shard_map/ppermute | solution.py:568
  40.7 2.3 %collective-permute-start.7 = (f32[1,128]{1,0:T(1,128)S(1)}, f32[1,128]{1,0:T(1,128)S(1)}, u32[]{:S(2)}, u32[]{:S(2)}) collective-permute-start(f32[1,128]{1,0:T(1,128)S(1)} %multiply_add_fusion.1.refs_3_.refs_6_), channel_id=1, source_target_pairs={{0,8},{8,0},{16,24},{24,16},{1,9},{9,1},{17,25},{25,17},{2,10},{10... | collective-permute-start | bytes 1544 | tf_op jit(solution)/shard_map/ppermute | solution.py:568
  57.4 7.7 %collective-permute-start.14 = (f32[256,128]{1,0:T(8,128)S(1)}, f32[256,128]{1,0:T(8,128)S(1)}, u32[]{:S(2)}, u32[]{:S(2)}) collective-permute-start(f32[256,128]{1,0:T(8,128)S(1)} %get-tuple-element.45), channel_id=1, source_target_pairs={{0,6},{2,4},{4,2},{6,0},{1,7},{3,5},{5,3},{7,1},{8,14},{10,12},{12... | collective-permute-start | bytes 393224 | tf_op jit(solution)/shard_map/ppermute | solution.py:568
  59.6 26.8 %collective-permute-start.8 = (f32[520,128]{1,0:T(8,128)S(1)}, f32[520,128]{1,0:T(8,128)S(1)}, u32[]{:S(2)}, u32[]{:S(2)}) collective-permute-start(f32[520,128]{1,0:T(8,128)S(1)} %get-tuple-element.40.refs_0_), channel_id=1, source_target_pairs={{0,16},{8,24},{16,0},{24,8},{1,17},{9,25},{17,1},{25,9},{2,18},{10... | collective-permute-start | bytes 798728 | tf_op jit(solution)/shard_map/ppermute | solution.py:568
  60.6 6.4 %collective-permute-start.17 = (f32[256,128]{1,0:T(8,128)S(1)}, f32[256,128]{1,0:T(8,128)S(1)}, u32[]{:S(2)}, u32[]{:S(2)}) collective-permute-start(f32[256,128]{1,0:T(8,128)S(1)} %get-tuple-element.46), channel_id=1, source_target_pairs={{0,2},{2,0},{4,6},{6,4},{1,3},{3,1},{5,7},{7,5},{8,10},{10,8},{12,... | collective-permute-start | bytes 393224 | tf_op jit(solution)/shard_map/ppermute | solution.py:568
  60.6 31.4 %collective-permute-start.13 = (f32[512,128]{1,0:T(8,128)S(1)}, f32[512,128]{1,0:T(8,128)S(1)}, u32[]{:S(2)}, u32[]{:S(2)}) collective-permute-start(f32[512,128]{1,0:T(8,128)S(1)} %get-tuple-element.35.wide_ref.refs_2_), channel_id=1, source_target_pairs={{0,8},{8,0},{16,24},{24,16},{1,9},{9,1},{17,25},{25,17},{2,10},{10... | collective-permute-start | bytes 786440 | tf_op jit(solution)/shard_map/ppermute | solution.py:568
  65.1 27.3 %collective-permute-start.12 = (f32[520,128]{1,0:T(8,128)S(1)}, f32[520,128]{1,0:T(8,128)S(1)}, u32[]{:S(2)}, u32[]{:S(2)}) collective-permute-start(f32[520,128]{1,0:T(8,128)S(1)} %get-tuple-element.40.refs_0_), channel_id=1, source_target_pairs={{0,8},{8,0},{16,24},{24,16},{1,9},{9,1},{17,25},{25,17},{2,10},{10... | collective-permute-start | bytes 798728 | tf_op jit(solution)/shard_map/ppermute | solution.py:568
  67.0 19.7 %collective-permute-start.15 = (f32[256,128]{1,0:T(8,128)S(1)}, f32[256,128]{1,0:T(8,128)S(1)}, u32[]{:S(2)}, u32[]{:S(2)}) collective-permute-start(f32[256,128]{1,0:T(8,128)S(1)} %add.46), channel_id=1, source_target_pairs={{0,1},{1,0},{2,3},{3,2},{4,5},{5,4},{6,7},{7,6},{8,9},{9,8},{10,11... | collective-permute-start | bytes 393224 | tf_op jit(solution)/shard_map/ppermute | solution.py:568
  83.7 6.8 %collective-permute-start.18 = (f32[256,128]{1,0:T(8,128)S(1)}, f32[256,128]{1,0:T(8,128)S(1)}, u32[]{:S(2)}, u32[]{:S(2)}) collective-permute-start(f32[256,128]{1,0:T(8,128)S(1)} %add.49), channel_id=1, source_target_pairs={{0,6},{2,4},{4,2},{6,0},{1,7},{3,5},{5,3},{7,1},{8,14},{10,12},{12... | collective-permute-start | bytes 393224 | tf_op jit(solution)/shard_map/ppermute | solution.py:568
  86.4 11.5 %collective-permute-start.9 = (f32[520,128]{1,0:T(8,128)S(1)}, f32[520,128]{1,0:T(8,128)S(1)}, u32[]{:S(2)}, u32[]{:S(2)}) collective-permute-start(f32[520,128]{1,0:T(8,128)S(1)} %collective-permute-done.8.refs_0_), channel_id=1, source_target_pairs={{0,8},{8,0},{16,24},{24,16},{1,9},{9,1},{17,25},{25,17},{2,10},{10... | collective-permute-start | bytes 798728 | tf_op jit(solution)/shard_map/ppermute | solution.py:568
  86.7 11.1 %collective-permute-start.11 = (f32[512,128]{1,0:T(8,128)S(1)}, f32[512,128]{1,0:T(8,128)S(1)}, u32[]{:S(2)}, u32[]{:S(2)}) collective-permute-start(f32[512,128]{1,0:T(8,128)S(1)} %collective-permute-done.10.refs_2_), channel_id=1, source_target_pairs={{0,8},{8,0},{16,24},{24,16},{1,9},{9,1},{17,25},{25,17},{2,10},{10... | collective-permute-start | bytes 786440 | tf_op jit(solution)/shard_map/ppermute | solution.py:568
  90.5 5.4 %collective-permute-start.16 = (f32[256,128]{1,0:T(8,128)S(1)}, f32[256,128]{1,0:T(8,128)S(1)}, u32[]{:S(2)}, u32[]{:S(2)}) collective-permute-start(f32[256,128]{1,0:T(8,128)S(1)} %add.47), channel_id=1, source_target_pairs={{0,2},{2,0},{4,6},{6,4},{1,3},{3,1},{5,7},{7,5},{8,10},{10,8},{12,... | collective-permute-start | bytes 393224 | tf_op jit(solution)/shard_map/ppermute | solution.py:568
  92.1 5.0 %collective-permute-start.19 = (f32[256,128]{1,0:T(8,128)S(1)}, f32[256,128]{1,0:T(8,128)S(1)}, u32[]{:S(2)}, u32[]{:S(2)}) collective-permute-start(f32[256,128]{1,0:T(8,128)S(1)} %add.50), channel_id=1, source_target_pairs={{0,1},{1,0},{2,3},{3,2},{4,5},{5,4},{6,7},{7,6},{8,9},{9,8},{10,11... | collective-permute-start | bytes 393224 | tf_op jit(solution)/shard_map/ppermute | solution.py:568

commit v10 on v9

--- a/solution.py
+++ b/solution.py
@@ -431,7 +431,10 @@
     width = iq_ref.shape[1]
 
     valid = bias_ref[:, lanes_at(lax.axis_index("head"), rows)] == 0
-    target = functools.reduce(jnp.add, [p[...] for p in parts]) * (1.0 / H)
+    target = parts[0][...]
+    for i in range(1, n_parts, 2):
+        target = target + jnp.concatenate([p[...] for p in parts[i : i + 2]], axis=0)
+    target = target * (1.0 / H)
     logits = logits_ref[...]
     lse2 = combine_lse([r[...] for r in lses])
     qprob = jnp.where(valid, jnp.exp2(logits * LOG2E - lse2), 0.0)
@@ -618,18 +621,17 @@
     index_lses = butterfly_lse(index_lse, n_key)
     iks = gathered(wide)
 
-    half = keys // 2
     if n_head == 4 and groups == 4:
         low, high = head_sums([2], q, kk, bias, live, lses, parts=2)
         low = swap(low, "head", 1, 4)
         high = swap(high, "head", 3, 4)
-        up, down = head_sums([1, 3], q, kk, bias, live, lses)
-        up = up + jnp.pad(high, ((half, 0), (0, 0)))
-        down = down + jnp.pad(low, ((0, half), (0, 0)))
-        from_up = swap(up, "head", 1, 4)
-        from_down = swap(down, "head", 3, 4)
+        up_lo, up_hi, down_lo, down_hi = head_sums([1, 3], q, kk, bias, live, lses, parts=2)
+        up_lo = swap(up_lo, "head", 1, 4)
+        down_hi = swap(down_hi, "head", 3, 4)
+        up_hi = swap(up_hi + high, "head", 1, 4)
+        down_lo = swap(down_lo + low, "head", 3, 4)
         own = head_sums([0], q, kk, bias, live, lses)[0]
-        parts = [own, from_up, from_down]
+        parts = [own, up_lo, up_hi, down_lo, down_hi]
     else:
         z = lax.axis_index("head")
         tiles = jnp.stack([head_sums([g], q, kk, bias, live, lses)[0] for g in range(groups)])

time: 102 us -> 98.5 us (0.966)
  waiting for transfers between devices: 27.9 us -> 20.6 us
  starting transfers between devices: 35.9 us -> 39.3 us
    ppermute x20 -> x22, waiting for transfers between devices: 27.9 us -> 20.6 us  [swap(): return lax.ppermute(value, axis, [(i, i ^ mask) for i in range(size)])]
    ppermute x20 -> x22, starting transfers between devices: 35.9 us -> 39.3 us  [swap(): return lax.ppermute(value, axis, [(i, i ^ mask) for i in range(size)])]
  transfers between devices with their start and end apart: 20 -> 22, of which waited for: 9 -> 10; matrix products, arithmetic and copies ran while one was open for 1% -> 1% of each run, Pallas kernels for 20% -> 20%
where the time goes in v10:
time: 98.5 us; the launch traced here: 98 us
  starting transfers between devices  39.3 us (40%)
  Pallas kernels  36.4 us (37%)
  waiting for transfers between devices  20.6 us (21%)
    ppermute x22, starting transfers between devices, swap(): return lax.ppermute(value, axis, [(i, i ^ mask) for i in range(size)])  39.3 us
    ppermute x22, waiting for transfers between devices, swap(): return lax.ppermute(value, axis, [(i, i ^ mask) for i in range(size)])  20.6 us
    pallas_call x1, Pallas kernels, main_stats(): pl.pallas_call(functools.partial(stats_kernel, 2), in_specs=[pl.BlockSpec...  12.4 us
    pallas_call x3, Pallas kernels, head_sums(): pl.pallas_call(functools.partial(target_kernel, len(lses), masks, 4 // n,...  8.01 us
    pallas_call x2, Pallas kernels, index_grad_query(): pl.pallas_call(functools.partial(grad_query_kernel, n, first, len(lses)),...  7.56 us
    pallas_call x1, Pallas kernels, index_logits(): pl.pallas_call(functools.partial(logits_kernel, 4), grid=(1,), in_specs=[...  4.11 us
    pallas_call x1, Pallas kernels, index_grad_key(): pl.pallas_call(functools.partial(grad_key_kernel, len(parts), len(lses),...  4.09 us
  transfers between devices with their start and end apart: 22, of which 10 were waited for; matrix products, arithmetic and copies ran while one was open for 1% of the time, Pallas kernels for 20%

profile of v10, /device:TPU:0, one launch (start us, length us, event | category | flops | bytes accessed | tf_op | source)
XLA Modules:
  0.0 98.0 jit_solution(7023162144087848719)
XLA Ops:
  0.6 12.4 %main_stats.1 = (f32[32,512]{1,0:T(8,128)S(1)}, bf16[4,128,6144]{2,1,0:T(8,128)(2,1)S(1)}, bf16[512,8192]{1,0:T(8,128)(2,1)S(1)}, f32[512,512]{1,0:T(8,128)S(1)}...) custom-call(s32[16]{0:T(128)} %count_hbm.1, ...), custom_call_target="tpu_custom_call" | custom-call | flops 4294967296 | bytes 10485760 | tf_op jit(solution)/shard_map/main_stats/pallas_call | solution.py:235
  13.1 3.0 %collective-permute-start = (f32[32,512]{1,0:T(8,128)S(1)}, f32[32,512]{1,0:T(8,128)S(1)}, u32[]{:S(2)}, u32[]{:S(2)}) collective-permute-start(f32[32,512]{1,0:T(8,128)S(1)} %get-tuple-element.31), channel_id=1, source_target_pairs={{0,16},{8,24},{16,0},{24,8},{1,17},{9,25},{17,1},{25,9},{2,18},{10... | collective-permute-start | bytes 196616 | tf_op jit(solution)/shard_map/ppermute | solution.py:571
  16.1 2.5 %collective-permute-done = f32[32,512]{1,0:T(8,128)S(1)} collective-permute-done((f32[32,512]{1,0:T(8,128)S(1)}, f32[32,512]{1,0:T(8,128)S(1)}, u32[]{:S(2)}, u32[]{:S(2)}) %collective-permute-start) | collective-permute-done | bytes 65568 | tf_op jit(solution)/shard_map/ppermute | solution.py:571
  18.7 4.1 %index_logits.1 = (f32[512,128]{1,0:T(8,128)S(1)}, f32[1,128]{1,0:T(1,128)S(1)}, bf16[512,8192]{1,0:T(8,128)(2,1)S(1)}) custom-call(bf16[128,8192]{1,0:T(8,128)(2,1)S(1)} %get-tuple-element.38.iq_ref.refs_9_.refs_4_, f32[512,128]{1,0:T(8,128)S(1)} %get-tuple-element.39.wide_ref.refs_2_, bf16[64,128]{1,0:T(8,128)(2,1)} %bitcast.5, ...), custom_call_target="tpu_custom_call" | custom-call | flops 1073741824 | bytes 10485760 | tf_op jit(solution)/shard_map/index_logits/pallas_call | solution.py:399
  22.8 1.8 %collective-permute-start.8 = (f32[1,128]{1,0:T(1,128)S(1)}, f32[1,128]{1,0:T(1,128)S(1)}, u32[]{:S(2)}, u32[]{:S(2)}) collective-permute-start(f32[1,128]{1,0:T(1,128)S(1)} %get-tuple-element.40), channel_id=1, source_target_pairs={{0,16},{8,24},{16,0},{24,8},{1,17},{9,25},{17,1},{25,9},{2,18},{10... | collective-permute-start | bytes 1544 | tf_op jit(solution)/shard_map/ppermute | solution.py:571
  24.9 2.4 %head_sums.5 = (f32[256,128]{1,0:T(8,128)S(1)}, f32[256,128]{1,0:T(8,128)S(1)}) custom-call(bf16[4,128,6144]{2,1,0:T(8,128)(2,1)S(1)} %get-tuple-element.27.q_ref, bf16[512,8192]{1,0:T(8,128)(2,1)S(1)} %get-tuple-element.28.kk_ref, f32[512,512]{1,0:T(8,128)S(1)} %get-tuple-element.29.bias_ref.refs_10_, s32[8,128]{1,0:T(8,128)S(1)} %get-tuple-element.30.live_ref.refs_11_, ...), custom_call_target="tpu_custom_call" | custom-call | flops 1073741824 | bytes 131072 | tf_op jit(solution)/shard_map/head_sums/pallas_call | solution.py:349
  27.4 3.7 %collective-permute-start.3 = (f32[256,128]{1,0:T(8,128)S(1)}, f32[256,128]{1,0:T(8,128)S(1)}, u32[]{:S(2)}, u32[]{:S(2)}) collective-permute-start(f32[256,128]{1,0:T(8,128)S(1)} %get-tuple-element.34), channel_id=1, source_target_pairs={{0,6},{2,4},{4,2},{6,0},{1,7},{3,5},{5,3},{7,1},{8,14},{10,12},{12... | collective-permute-start | bytes 393224 | tf_op jit(solution)/shard_map/ppermute | solution.py:571
  31.0 3.3 %head_sums.4 = (f32[256,128]{1,0:T(8,128)S(1)}, f32[256,128]{1,0:T(8,128)S(1)}, f32[256,128]{1,0:T(8,128)S(1)}, f32[256,128]{1,0:T(8,128)S(1)}) custom-call(bf16[4,128,6144]{2,1,0:T(8,128)(2,1)S(1)} %get-tuple-element.27.q_ref, bf16[512,8192]{1,0:T(8,128)(2,1)S(1)} %get-tuple-element.28.kk_ref, f32[512,512]{1,0:T(8,128)S(1)} %get-tuple-element.29.bias_ref.refs_10_, ...), custom_call_target="tpu_custom_call" | custom-call | flops 2147483648 | bytes 262144 | tf_op jit(solution)/shard_map/head_sums/pallas_call | solution.py:349
  34.4 2.1 %collective-permute-start.2 = (f32[256,128]{1,0:T(8,128)S(1)}, f32[256,128]{1,0:T(8,128)S(1)}, u32[]{:S(2)}, u32[]{:S(2)}) collective-permute-start(f32[256,128]{1,0:T(8,128)S(1)} %get-tuple-element.32), channel_id=1, source_target_pairs={{0,2},{2,0},{4,6},{6,4},{1,3},{3,1},{5,7},{7,5},{8,10},{10,8},{12,... | collective-permute-start | bytes 393224 | tf_op jit(solution)/shard_map/ppermute | solution.py:571
  36.7 1.0 %collective-permute-start.4 = (f32[256,128]{1,0:T(8,128)S(1)}, f32[256,128]{1,0:T(8,128)S(1)}, u32[]{:S(2)}, u32[]{:S(2)}) collective-permute-start(f32[256,128]{1,0:T(8,128)S(1)} %add.38), channel_id=1, source_target_pairs={{0,2},{2,0},{4,6},{6,4},{1,3},{3,1},{5,7},{7,5},{8,10},{10,8},{12,... | collective-permute-start | bytes 393224 | tf_op jit(solution)/shard_map/ppermute | solution.py:571
  37.7 0.4 collective-permute-done.5
  38.1 2.4 %collective-permute-start.6 = (f32[256,128]{1,0:T(8,128)S(1)}, f32[256,128]{1,0:T(8,128)S(1)}, u32[]{:S(2)}, u32[]{:S(2)}) collective-permute-start(f32[256,128]{1,0:T(8,128)S(1)} %add.39), channel_id=1, source_target_pairs={{0,6},{2,4},{4,2},{6,0},{1,7},{3,5},{5,3},{7,1},{8,14},{10,12},{12... | collective-permute-start | bytes 393224 | tf_op jit(solution)/shard_map/ppermute | solution.py:571
  40.6 2.3 %head_sums.3.refs_0_ = f32[512,128]{1,0:T(8,128)S(1)} custom-call(bf16[4,128,6144]{2,1,0:T(8,128)(2,1)S(1)} %get-tuple-element.27.q_ref, bf16[512,8192]{1,0:T(8,128)(2,1)S(1)} %get-tuple-element.28.kk_ref, f32[512,512]{1,0:T(8,128)S(1)} %get-tuple-element.29.bias_ref.refs_10_, s32[8,128]{1,0:T(8,128)S(1)} %get-tuple-element.30.live_ref.refs_11_, ...), custom_call_target="tpu_custom_call" | custom-call | flops 1073741824 | bytes 131072 | tf_op jit(solution)/shard_map/head_sums/pallas_call | solution.py:349
  42.9 0.6 collective-permute-start.12
  43.4 1.2 %collective-permute-done.7.refs_4_ = f32[256,128]{1,0:T(8,128)S(1)} collective-permute-done((f32[256,128]{1,0:T(8,128)S(1)}, f32[256,128]{1,0:T(8,128)S(1)}, u32[]{:S(2)}, u32[]{:S(2)}) %collective-permute-start.7) | collective-permute-done | bytes 131104 | tf_op jit(solution)/shard_map/ppermute | solution.py:571
  44.7 2.8 %collective-permute-done.4.refs_2_ = f32[256,128]{1,0:T(8,128)S(1)} collective-permute-done((f32[256,128]{1,0:T(8,128)S(1)}, f32[256,128]{1,0:T(8,128)S(1)}, u32[]{:S(2)}, u32[]{:S(2)}) %collective-permute-start.4) | collective-permute-done | bytes 131104 | tf_op jit(solution)/shard_map/ppermute | solution.py:571
  47.5 1.8 %collective-permute-done.6.refs_3_ = f32[256,128]{1,0:T(8,128)S(1)} collective-permute-done((f32[256,128]{1,0:T(8,128)S(1)}, f32[256,128]{1,0:T(8,128)S(1)}, u32[]{:S(2)}, u32[]{:S(2)}) %collective-permute-start.6) | collective-permute-done | bytes 131104 | tf_op jit(solution)/shard_map/ppermute | solution.py:571
  49.3 4.1 %index_grad_key.1 = (f32[520,128]{1,0:T(8,128)S(1)}, f32[256,128]{1,0:T(8,128)S(1)}, f32[256,128]{1,0:T(8,128)S(1)}) custom-call(f32[512,128]{1,0:T(8,128)S(1)} %head_sums.3.refs_0_, f32[256,128]{1,0:T(8,128)S(1)} %collective-permute-done.2.refs_1_, f32[256,128]{1,0:T(8,128)S(1)} %collective-permute-done.4.refs_2_, ...), custom_call_target="tpu_custom_call" | custom-call | flops 1073741824 | bytes 10485760 | tf_op jit(solution)/shard_map/index_grad_key/pallas_call | solution.py:479
  53.4 3.5 %collective-permute-start.16 = (f32[256,128]{1,0:T(8,128)S(1)}, f32[256,128]{1,0:T(8,128)S(1)}, u32[]{:S(2)}, u32[]{:S(2)}) collective-permute-start(f32[256,128]{1,0:T(8,128)S(1)} %get-tuple-element.49), channel_id=1, source_target_pairs={{0,6},{2,4},{4,2},{6,0},{1,7},{3,5},{5,3},{7,1},{8,14},{10,12},{12... | collective-permute-start | bytes 393224 | tf_op jit(solution)/shard_map/ppermute | solution.py:571
  56.9 0.5 collective-permute-start.10
  57.4 4.2 %collective-permute-done.16 = f32[256,128]{1,0:T(8,128)S(1)} collective-permute-done((f32[256,128]{1,0:T(8,128)S(1)}, f32[256,128]{1,0:T(8,128)S(1)}, u32[]{:S(2)}, u32[]{:S(2)}) %collective-permute-start.16) | collective-permute-done | bytes 131104 | tf_op jit(solution)/shard_map/ppermute | solution.py:571
  61.7 1.5 %collective-permute-done.19 = f32[256,128]{1,0:T(8,128)S(1)} collective-permute-done((f32[256,128]{1,0:T(8,128)S(1)}, f32[256,128]{1,0:T(8,128)S(1)}, u32[]{:S(2)}, u32[]{:S(2)}) %collective-permute-start.19) | collective-permute-done | bytes 131104 | tf_op jit(solution)/shard_map/ppermute | solution.py:571
  63.2 16.7 %collective-permute-start.17 = (f32[256,128]{1,0:T(8,128)S(1)}, f32[256,128]{1,0:T(8,128)S(1)}, u32[]{:S(2)}, u32[]{:S(2)}) collective-permute-start(f32[256,128]{1,0:T(8,128)S(1)} %add.42), channel_id=1, source_target_pairs={{0,1},{1,0},{2,3},{3,2},{4,5},{5,4},{6,7},{7,6},{8,9},{9,8},{10,11... | collective-permute-start | bytes 393224 | tf_op jit(solution)/shard_map/ppermute | solution.py:571
  79.9 2.0 %collective-permute-start.20 = (f32[256,128]{1,0:T(8,128)S(1)}, f32[256,128]{1,0:T(8,128)S(1)}, u32[]{:S(2)}, u32[]{:S(2)}) collective-permute-start(f32[256,128]{1,0:T(8,128)S(1)} %add.45), channel_id=1, source_target_pairs={{0,6},{2,4},{4,2},{6,0},{1,7},{3,5},{5,3},{7,1},{8,14},{10,12},{12... | collective-permute-start | bytes 393224 | tf_op jit(solution)/shard_map/ppermute | solution.py:571
  81.9 0.9 collective-permute-done.17
  82.8 4.0 %collective-permute-done.20 = f32[256,128]{1,0:T(8,128)S(1)} collective-permute-done((f32[256,128]{1,0:T(8,128)S(1)}, f32[256,128]{1,0:T(8,128)S(1)}, u32[]{:S(2)}, u32[]{:S(2)}) %collective-permute-start.20) | collective-permute-done | bytes 131104 | tf_op jit(solution)/shard_map/ppermute | solution.py:571
  86.8 1.3 %collective-permute-start.18 = (f32[256,128]{1,0:T(8,128)S(1)}, f32[256,128]{1,0:T(8,128)S(1)}, u32[]{:S(2)}, u32[]{:S(2)}) collective-permute-start(f32[256,128]{1,0:T(8,128)S(1)} %add.43), channel_id=1, source_target_pairs={{0,2},{2,0},{4,6},{6,4},{1,3},{3,1},{5,7},{7,5},{8,10},{10,8},{12,... | collective-permute-start | bytes 393224 | tf_op jit(solution)/shard_map/ppermute | solution.py:571
  88.2 0.3 collective-permute-start.21
  88.5 3.5 %index_grad_query.2 = (f32[128,2048]{1,0:T(8,128)S(1)}, f32[1,128]{1,0:T(1,128)S(1)}) custom-call(f32[520,128]{1,0:T(8,128)S(1)} %get-tuple-element.44.refs_0_, f32[520,128]{1,0:T(8,128)S(1)} %collective-permute-done.14.refs_1_, f32[512,128]{1,0:T(8,128)S(1)} %get-tuple-element.39.wide_ref.refs_2_, f32[512,128]{1,0:T(8,128)S(1)} %collective-permute-done.15.refs_3_, ...), custom_call_target="tpu_custom_call" | custom-call | flops 1073741824 | bytes 3145728 | tf_op jit(solution)/shard_map/index_grad_query/pallas_call | solution.py:552
  92.0 1.2 %collective-permute-done.21 = f32[256,128]{1,0:T(8,128)S(1)} collective-permute-done((f32[256,128]{1,0:T(8,128)S(1)}, f32[256,128]{1,0:T(8,128)S(1)}, u32[]{:S(2)}, u32[]{:S(2)}) %collective-permute-start.21) | collective-permute-done | bytes 131104 | tf_op jit(solution)/shard_map/ppermute | solution.py:571
  93.2 0.7 pad_maximum_fusion
  93.9 4.1 %index_grad_query.3 = (f32[128,2048]{1,0:T(8,128)}, f32[1,128]{1,0:T(1,128)}) custom-call(f32[520,128]{1,0:T(8,128)S(1)} %collective-permute-done.10.refs_0_, f32[520,128]{1,0:T(8,128)S(1)} %collective-permute-done.11.refs_1_, f32[512,128]{1,0:T(8,128)S(1)} %collective-permute-done.12.refs_2_, f32[512,128]{1,0:T(8,128)S(1)} %collective-permute-done.13.refs_3_, ...), custom_call_target="tpu_custom_call" | custom-call | flops 1073741824 | bytes 3145728 | tf_op jit(solution)/shard_map/index_grad_query/pallas_call | solution.py:552
  (32 shorter events, 0.9 us)
Async XLA Ops:
  13.1 5.5 %collective-permute-start = (f32[32,512]{1,0:T(8,128)S(1)}, f32[32,512]{1,0:T(8,128)S(1)}, u32[]{:S(2)}, u32[]{:S(2)}) collective-permute-start(f32[32,512]{1,0:T(8,128)S(1)} %get-tuple-element.31), channel_id=1, source_target_pairs={{0,16},{8,24},{16,0},{24,8},{1,17},{9,25},{17,1},{25,9},{2,18},{10... | collective-permute-start | bytes 196616 | tf_op jit(solution)/shard_map/ppermute | solution.py:571
  18.6 6.3 %collective-permute-start.1 = (f32[32,512]{1,0:T(8,128)S(1)}, f32[32,512]{1,0:T(8,128)S(1)}, u32[]{:S(2)}, u32[]{:S(2)}) collective-permute-start(f32[32,512]{1,0:T(8,128)S(1)} %multiply_add_fusion.refs_0_), channel_id=1, source_target_pairs={{0,8},{8,0},{16,24},{24,16},{1,9},{9,1},{17,25},{25,17},{2,10},{10... | collective-permute-start | bytes 196616 | tf_op jit(solution)/shard_map/ppermute | solution.py:571
  22.8 17.7 %collective-permute-start.8 = (f32[1,128]{1,0:T(1,128)S(1)}, f32[1,128]{1,0:T(1,128)S(1)}, u32[]{:S(2)}, u32[]{:S(2)}) collective-permute-start(f32[1,128]{1,0:T(1,128)S(1)} %get-tuple-element.40), channel_id=1, source_target_pairs={{0,16},{8,24},{16,0},{24,8},{1,17},{9,25},{17,1},{25,9},{2,18},{10... | collective-permute-start | bytes 1544 | tf_op jit(solution)/shard_map/ppermute | solution.py:571
  27.4 9.3 %collective-permute-start.3 = (f32[256,128]{1,0:T(8,128)S(1)}, f32[256,128]{1,0:T(8,128)S(1)}, u32[]{:S(2)}, u32[]{:S(2)}) collective-permute-start(f32[256,128]{1,0:T(8,128)S(1)} %get-tuple-element.34), channel_id=1, source_target_pairs={{0,6},{2,4},{4,2},{6,0},{1,7},{3,5},{5,3},{7,1},{8,14},{10,12},{12... | collective-permute-start | bytes 393224 | tf_op jit(solution)/shard_map/ppermute | solution.py:571
  31.0 7.1 %collective-permute-start.5 = (f32[256,128]{1,0:T(8,128)S(1)}, f32[256,128]{1,0:T(8,128)S(1)}, u32[]{:S(2)}, u32[]{:S(2)}) collective-permute-start(f32[256,128]{1,0:T(8,128)S(1)} %get-tuple-element.36), channel_id=1, source_target_pairs={{0,2},{2,0},{4,6},{6,4},{1,3},{3,1},{5,7},{7,5},{8,10},{10,8},{12,... | collective-permute-start | bytes 393224 | tf_op jit(solution)/shard_map/ppermute | solution.py:571
  34.4 9.1 %collective-permute-start.2 = (f32[256,128]{1,0:T(8,128)S(1)}, f32[256,128]{1,0:T(8,128)S(1)}, u32[]{:S(2)}, u32[]{:S(2)}) collective-permute-start(f32[256,128]{1,0:T(8,128)S(1)} %get-tuple-element.32), channel_id=1, source_target_pairs={{0,2},{2,0},{4,6},{6,4},{1,3},{3,1},{5,7},{7,5},{8,10},{10,8},{12,... | collective-permute-start | bytes 393224 | tf_op jit(solution)/shard_map/ppermute | solution.py:571
  36.4 8.2 %collective-permute-start.7 = (f32[256,128]{1,0:T(8,128)S(1)}, f32[256,128]{1,0:T(8,128)S(1)}, u32[]{:S(2)}, u32[]{:S(2)}) collective-permute-start(f32[256,128]{1,0:T(8,128)S(1)} %get-tuple-element.37), channel_id=1, source_target_pairs={{0,6},{2,4},{4,2},{6,0},{1,7},{3,5},{5,3},{7,1},{8,14},{10,12},{12... | collective-permute-start | bytes 393224 | tf_op jit(solution)/shard_map/ppermute | solution.py:571
  36.7 10.8 %collective-permute-start.4 = (f32[256,128]{1,0:T(8,128)S(1)}, f32[256,128]{1,0:T(8,128)S(1)}, u32[]{:S(2)}, u32[]{:S(2)}) collective-permute-start(f32[256,128]{1,0:T(8,128)S(1)} %add.38), channel_id=1, source_target_pairs={{0,2},{2,0},{4,6},{6,4},{1,3},{3,1},{5,7},{7,5},{8,10},{10,8},{12,... | collective-permute-start | bytes 393224 | tf_op jit(solution)/shard_map/ppermute | solution.py:571
  38.1 11.2 %collective-permute-start.6 = (f32[256,128]{1,0:T(8,128)S(1)}, f32[256,128]{1,0:T(8,128)S(1)}, u32[]{:S(2)}, u32[]{:S(2)}) collective-permute-start(f32[256,128]{1,0:T(8,128)S(1)} %add.39), channel_id=1, source_target_pairs={{0,6},{2,4},{4,2},{6,0},{1,7},{3,5},{5,3},{7,1},{8,14},{10,12},{12... | collective-permute-start | bytes 393224 | tf_op jit(solution)/shard_map/ppermute | solution.py:571
  40.5 2.3 %collective-permute-start.9 = (f32[1,128]{1,0:T(1,128)S(1)}, f32[1,128]{1,0:T(1,128)S(1)}, u32[]{:S(2)}, u32[]{:S(2)}) collective-permute-start(f32[1,128]{1,0:T(1,128)S(1)} %multiply_add_fusion.1.refs_5_.refs_6_), channel_id=1, source_target_pairs={{0,8},{8,0},{16,24},{24,16},{1,9},{9,1},{17,25},{25,17},{2,10},{10... | collective-permute-start | bytes 1544 | tf_op jit(solution)/shard_map/ppermute | solution.py:571
  42.9 37.0 %collective-permute-start.12 = (f32[512,128]{1,0:T(8,128)S(1)}, f32[512,128]{1,0:T(8,128)S(1)}, u32[]{:S(2)}, u32[]{:S(2)}) collective-permute-start(f32[512,128]{1,0:T(8,128)S(1)} %get-tuple-element.39.wide_ref.refs_2_), channel_id=1, source_target_pairs={{0,16},{8,24},{16,0},{24,8},{1,17},{9,25},{17,1},{25,9},{2,18},{10... | collective-permute-start | bytes 786440 | tf_op jit(solution)/shard_map/ppermute | solution.py:571
  53.4 8.2 %collective-permute-start.16 = (f32[256,128]{1,0:T(8,128)S(1)}, f32[256,128]{1,0:T(8,128)S(1)}, u32[]{:S(2)}, u32[]{:S(2)}) collective-permute-start(f32[256,128]{1,0:T(8,128)S(1)} %get-tuple-element.49), channel_id=1, source_target_pairs={{0,6},{2,4},{4,2},{6,0},{1,7},{3,5},{5,3},{7,1},{8,14},{10,12},{12... | collective-permute-start | bytes 393224 | tf_op jit(solution)/shard_map/ppermute | solution.py:571
  56.9 25.0 %collective-permute-start.10 = (f32[520,128]{1,0:T(8,128)S(1)}, f32[520,128]{1,0:T(8,128)S(1)}, u32[]{:S(2)}, u32[]{:S(2)}) collective-permute-start(f32[520,128]{1,0:T(8,128)S(1)} %get-tuple-element.44.refs_0_), channel_id=1, source_target_pairs={{0,16},{8,24},{16,0},{24,8},{1,17},{9,25},{17,1},{25,9},{2,18},{10... | collective-permute-start | bytes 798728 | tf_op jit(solution)/shard_map/ppermute | solution.py:571
  57.4 5.8 %collective-permute-start.19 = (f32[256,128]{1,0:T(8,128)S(1)}, f32[256,128]{1,0:T(8,128)S(1)}, u32[]{:S(2)}, u32[]{:S(2)}) collective-permute-start(f32[256,128]{1,0:T(8,128)S(1)} %get-tuple-element.50), channel_id=1, source_target_pairs={{0,2},{2,0},{4,6},{6,4},{1,3},{3,1},{5,7},{7,5},{8,10},{10,8},{12,... | collective-permute-start | bytes 393224 | tf_op jit(solution)/shard_map/ppermute | solution.py:571
  57.4 30.7 %collective-permute-start.15 = (f32[512,128]{1,0:T(8,128)S(1)}, f32[512,128]{1,0:T(8,128)S(1)}, u32[]{:S(2)}, u32[]{:S(2)}) collective-permute-start(f32[512,128]{1,0:T(8,128)S(1)} %get-tuple-element.39.wide_ref.refs_2_), channel_id=1, source_target_pairs={{0,8},{8,0},{16,24},{24,16},{1,9},{9,1},{17,25},{25,17},{2,10},{10... | collective-permute-start | bytes 786440 | tf_op jit(solution)/shard_map/ppermute | solution.py:571
  61.7 26.9 %collective-permute-start.14 = (f32[520,128]{1,0:T(8,128)S(1)}, f32[520,128]{1,0:T(8,128)S(1)}, u32[]{:S(2)}, u32[]{:S(2)}) collective-permute-start(f32[520,128]{1,0:T(8,128)S(1)} %get-tuple-element.44.refs_0_), channel_id=1, source_target_pairs={{0,8},{8,0},{16,24},{24,16},{1,9},{9,1},{17,25},{25,17},{2,10},{10... | collective-permute-start | bytes 798728 | tf_op jit(solution)/shard_map/ppermute | solution.py:571
  63.2 19.6 %collective-permute-start.17 = (f32[256,128]{1,0:T(8,128)S(1)}, f32[256,128]{1,0:T(8,128)S(1)}, u32[]{:S(2)}, u32[]{:S(2)}) collective-permute-start(f32[256,128]{1,0:T(8,128)S(1)} %add.42), channel_id=1, source_target_pairs={{0,1},{1,0},{2,3},{3,2},{4,5},{5,4},{6,7},{7,6},{8,9},{9,8},{10,11... | collective-permute-start | bytes 393224 | tf_op jit(solution)/shard_map/ppermute | solution.py:571
  79.9 6.9 %collective-permute-start.20 = (f32[256,128]{1,0:T(8,128)S(1)}, f32[256,128]{1,0:T(8,128)S(1)}, u32[]{:S(2)}, u32[]{:S(2)}) collective-permute-start(f32[256,128]{1,0:T(8,128)S(1)} %add.45), channel_id=1, source_target_pairs={{0,6},{2,4},{4,2},{6,0},{1,7},{3,5},{5,3},{7,1},{8,14},{10,12},{12... | collective-permute-start | bytes 393224 | tf_op jit(solution)/shard_map/ppermute | solution.py:571
  81.9 12.0 %collective-permute-start.11 = (f32[520,128]{1,0:T(8,128)S(1)}, f32[520,128]{1,0:T(8,128)S(1)}, u32[]{:S(2)}, u32[]{:S(2)}) collective-permute-start(f32[520,128]{1,0:T(8,128)S(1)} %collective-permute-done.10.refs_0_), channel_id=1, source_target_pairs={{0,8},{8,0},{16,24},{24,16},{1,9},{9,1},{17,25},{25,17},{2,10},{10... | collective-permute-start | bytes 798728 | tf_op jit(solution)/shard_map/ppermute | solution.py:571
  82.8 11.1 %collective-permute-start.13 = (f32[512,128]{1,0:T(8,128)S(1)}, f32[512,128]{1,0:T(8,128)S(1)}, u32[]{:S(2)}, u32[]{:S(2)}) collective-permute-start(f32[512,128]{1,0:T(8,128)S(1)} %collective-permute-done.12.refs_2_), channel_id=1, source_target_pairs={{0,8},{8,0},{16,24},{24,16},{1,9},{9,1},{17,25},{25,17},{2,10},{10... | collective-permute-start | bytes 786440 | tf_op jit(solution)/shard_map/ppermute | solution.py:571
  86.8 5.1 %collective-permute-start.18 = (f32[256,128]{1,0:T(8,128)S(1)}, f32[256,128]{1,0:T(8,128)S(1)}, u32[]{:S(2)}, u32[]{:S(2)}) collective-permute-start(f32[256,128]{1,0:T(8,128)S(1)} %add.43), channel_id=1, source_target_pairs={{0,2},{2,0},{4,6},{6,4},{1,3},{3,1},{5,7},{7,5},{8,10},{10,8},{12,... | collective-permute-start | bytes 393224 | tf_op jit(solution)/shard_map/ppermute | solution.py:571
  88.2 5.0 %collective-permute-start.21 = (f32[256,128]{1,0:T(8,128)S(1)}, f32[256,128]{1,0:T(8,128)S(1)}, u32[]{:S(2)}, u32[]{:S(2)}) collective-permute-start(f32[256,128]{1,0:T(8,128)S(1)} %add.46), channel_id=1, source_target_pairs={{0,1},{1,0},{2,3},{3,2},{4,5},{5,4},{6,7},{7,6},{8,9},{9,8},{10,11... | collective-permute-start | bytes 393224 | tf_op jit(solution)/shard_map/ppermute | solution.py:571
